TPU v7x, 32 devices: a whole 2x2x4 slice. The times are simulated.
32 devices in a mesh: dp: 2 (over x), rows: 4 (over y, core), cols: 4 (over z).
Axes of the slice: x: 2, y: 2, z: 4, core: 2. Of those that a mesh axis runs over, the one named last changes fastest.
Arguments:
- tokens: bfloat16 [768, 4096], P('cols', ('dp', 'rows')), may hold values from -6 to 6
- segment_ids: int32 [4096], P(('dp', 'rows')), may hold values from -1 to 256, as said below
- first_gain: float32 [768], P('cols'), may hold values from 0.5 to 1.5
- first_bias: float32 [768], P('cols'), may hold values from -3 to 3
- qkv_weight: bfloat16 [768, 2304], P('rows', 'cols'), may hold values from -2 to 2
- qv_bias: float32 [1536], P('cols'), may hold values from -3 to 3
- mix_weight: bfloat16 [768, 768], P('cols', 'rows'), may hold values from -0.875 to 0.875
- mix_bias: float32 [768], P('cols'), may hold values from -3 to 3
- second_gain: float32 [768], P('cols'), may hold values from 0.5 to 1.5
- second_bias: float32 [768], P('cols'), may hold values from -3 to 3
- up_weight: bfloat16 [768, 3072], P('rows', 'cols'), may hold values from -0.21875 to 0.21875
- up_bias: float32 [3072], P('cols'), may hold values from -3 to 3
- down_weight: bfloat16 [768, 3072], P('rows', 'cols'), may hold values from -0.109375 to 0.109375
- down_bias: float32 [768], P('cols'), may hold values from -3 to 3
- cotangent: bfloat16 [768, 4096], P('cols', ('dp', 'rows')), may hold values from -6 to 6
Outputs:
- output: bfloat16 [768, 4096], P('cols', ('dp', 'rows'))
- grad_tokens: float32 [768, 4096], P('cols', ('dp', 'rows'))
- grad_first_gain: float32 [768], P('cols')
- grad_first_bias: float32 [768], P('cols')
- grad_qkv_weight: float32 [768, 2304], P('rows', 'cols')
- grad_qv_bias: float32 [1536], P('cols')
- grad_mix_weight: float32 [768, 768], P('cols', 'rows')
- grad_mix_bias: float32 [768], P('cols')
- grad_second_gain: float32 [768], P('cols')
- grad_second_bias: float32 [768], P('cols')
- grad_up_weight: float32 [768, 3072], P('rows', 'cols')
- grad_up_bias: float32 [3072], P('cols')
- grad_down_weight: float32 [768, 3072], P('rows', 'cols')
- grad_down_bias: float32 [768], P('cols')
Inputs may be any that keep to these rules, and one draw needn't show every extreme that they name: `segment_ids`: within each aligned block of 512 slots the live slots come first and carry segment numbers 0, 1, 2, ... that never fall; padding slots carry -1; each segment has at most 256 slots and some segment exactly 256; the first 256 slots of a block hold no second segment; between 128 and 512 slots of a block are live, some block is full and some block half full.
All inputs are finite; a program needn't handle non-finite values.
Results may differ from a plain program's by a relative error of at most 0.0085.
Values may be sent and summed in bfloat16 or wider, within the bound.
No kernel may reach another device: no remote copies, remote signals or barrier semaphores. Data moves between devices by JAX's collectives and lax.ppermute only.
A program may use at most 64 MiB of HBM per device.

v0:
```python
import math

import jax
import jax.numpy as jnp
from jax import lax
from jax.sharding import PartitionSpec as P

D = 768
HD = 64


EPS = 1e-05
NEG = -1e30
ROOT = 0.7978845608028654
CUBIC = 0.044715


def gelu_value(pre_act):
    inner_arg = ROOT * (pre_act + CUBIC * pre_act * pre_act * pre_act)
    return 0.5 * pre_act * (1.0 + jnp.tanh(inner_arg))


def gelu_slope(pre_act):
    inner_arg = ROOT * (pre_act + CUBIC * pre_act * pre_act * pre_act)
    tanh_val = jnp.tanh(inner_arg)
    return 0.5 * (1.0 + tanh_val) + 0.5 * pre_act * (1.0 - tanh_val * tanh_val) * ROOT * (
        1.0 + 3.0 * CUBIC * pre_act * pre_act
    )


def allowed_pairs(seg_rows, seg_keys, block_start):
    query_pos = block_start + jnp.arange(seg_rows.shape[0], dtype=jnp.int32)
    key_pos = jnp.arange(seg_keys.shape[0], dtype=jnp.int32)
    earlier = key_pos[None, :] < query_pos[:, None]
    same_seg = (seg_rows[:, None] == seg_keys[None, :]) & (seg_rows[:, None] >= 0)
    return earlier & same_seg | (key_pos[None, :] == query_pos[:, None])


def product(form, left, right):
    return jnp.einsum(form, left, right, preferred_element_type=jnp.float32)


def matmul(left, right):
    return jnp.dot(left, right, preferred_element_type=jnp.float32)


def attend(query_vecs, key_vecs, value_vecs, seg_ids):
    row_count, head_count, head_width = query_vecs.shape
    block_rows = min(512, row_count)
    block_count = row_count // block_rows
    score_scale = 1.0 / math.sqrt(head_width)

    def one_block(item):
        query_block, seg_block, block_start = item
        scores = product("qhd,khd->hqk", query_block, key_vecs) * score_scale
        allowed = allowed_pairs(seg_block, seg_ids, block_start)
        scores = jnp.where(allowed[None], scores, NEG)
        row_max = jnp.max(scores, axis=-1, keepdims=True)
        log_total = row_max + jnp.log(jnp.sum(jnp.exp(scores - row_max), axis=-1, keepdims=True))
        attn_probs = jnp.exp(scores - log_total).astype(jnp.bfloat16)
        attended = product("hqk,khd->qhd", attn_probs, value_vecs).astype(jnp.bfloat16)
        return (attended, log_total[:, :, 0])

    starts = jnp.arange(block_count, dtype=jnp.int32) * block_rows
    attended, log_totals = lax.map(
        one_block,
        (
            query_vecs.reshape(block_count, block_rows, head_count, head_width),
            seg_ids.reshape(block_count, block_rows),
            starts,
        ),
    )
    return (attended.reshape(row_count, head_count, head_width), log_totals)


def attend_back(query_vecs, key_vecs, value_vecs, attended, grad_att, seg_ids, log_totals):
    row_count, head_count, head_width = query_vecs.shape
    block_rows = min(512, row_count)
    block_count = row_count // block_rows
    score_scale = 1.0 / math.sqrt(head_width)
    deltas = jnp.sum(grad_att.astype(jnp.float32) * attended.astype(jnp.float32), axis=-1)

    def one_block(carry, item):
        grad_keys, grad_values = carry
        query_block, grad_block, delta_block, seg_block, total_block, block_start = item
        scores = product("qhd,khd->hqk", query_block, key_vecs) * score_scale
        allowed = allowed_pairs(seg_block, seg_ids, block_start)
        scores = jnp.where(allowed[None], scores, NEG)
        attn_probs = jnp.exp(scores - total_block[:, :, None])
        rounded = attn_probs.astype(jnp.bfloat16)
        grad_values = grad_values + product("hqk,qhd->khd", rounded, grad_block)
        grad_probs = product("qhd,khd->hqk", grad_block, value_vecs)
        grad_scores = (attn_probs * (grad_probs - delta_block.T[:, :, None]) * score_scale).astype(
            jnp.bfloat16
        )
        grad_query = product("hqk,khd->qhd", grad_scores, key_vecs)
        grad_keys = grad_keys + product("hqk,qhd->khd", grad_scores, query_block)
        return ((grad_keys, grad_values), grad_query)

    starts = jnp.arange(block_count, dtype=jnp.int32) * block_rows
    empty = jnp.zeros(key_vecs.shape, jnp.float32)
    shape_blocks = (block_count, block_rows, head_count, head_width)
    (grad_keys, grad_values), grad_query = lax.scan(
        one_block,
        (empty, empty),
        (
            query_vecs.reshape(shape_blocks),
            grad_att.reshape(shape_blocks),
            deltas.reshape(block_count, block_rows, head_count),
            seg_ids.reshape(block_count, block_rows),
            log_totals,
            starts,
        ),
    )
    return (grad_query.reshape(row_count, head_count, head_width), grad_keys, grad_values)


def row_sums(first, second):
    return lax.psum((jnp.sum(first, axis=-1), jnp.sum(second, axis=-1)), "cols")


def norm_forward(values, norm_gain, norm_bias):
    row_total, row_squares = row_sums(values, values * values)
    row_mean = (row_total / D)[:, None]
    row_var = (row_squares / D)[:, None] - row_mean * row_mean
    inv_std = lax.rsqrt(row_var + EPS)
    normed = (values - row_mean) * inv_std
    return ((normed * norm_gain + norm_bias).astype(jnp.bfloat16), normed, inv_std)


def norm_back(grad_out, normed, inv_std, norm_gain):
    scaled = grad_out * norm_gain
    row_total, row_paired = row_sums(scaled, scaled * normed)
    return inv_std * (scaled - (row_total / D)[:, None] - normed * (row_paired / D)[:, None])


def widen(values):
    return lax.all_gather(values, "cols", axis=1, tiled=True)


def widen_grad(values):
    return lax.all_gather(values, "cols", axis=1, tiled=True)


def combine(partial_sum):
    return lax.psum_scatter(partial_sum, "cols", scatter_dimension=1, tiled=True)


def narrow(partial_sum):
    return lax.psum_scatter(partial_sum, "cols", scatter_dimension=1, tiled=True)


def block_rows_sum(qkv_grad, up_grad, mix_grad, down_grad):
    qkv_part, up_part = (
        lax.psum_scatter(qkv_grad, "rows", scatter_dimension=0, tiled=True),
        lax.psum_scatter(up_grad, "rows", scatter_dimension=0, tiled=True),
    )
    mix_part, down_part = (
        lax.psum_scatter(mix_grad, "rows", scatter_dimension=1, tiled=True),
        lax.psum_scatter(down_grad, "rows", scatter_dimension=0, tiled=True),
    )
    return (qkv_part, up_part, mix_part, down_part)


def body(
    tokens,
    segment_ids,
    first_gain,
    first_bias,
    qkv_weight,
    qv_bias,
    mix_weight,
    mix_bias,
    second_gain,
    second_bias,
    up_weight,
    up_bias,
    down_weight,
    down_bias,
    cotangent,
):
    row_count = tokens.shape[1]
    heads_here = qkv_weight.shape[1] // (3 * HD)
    qkv_whole, up_whole = (
        lax.all_gather(qkv_weight, "rows", axis=0, tiled=True),
        lax.all_gather(up_weight, "rows", axis=0, tiled=True),
    )
    mix_whole, down_whole = (
        lax.all_gather(mix_weight, "rows", axis=1, tiled=True),
        lax.all_gather(down_weight, "rows", axis=0, tiled=True),
    )
    inputs = tokens.astype(jnp.float32).T
    normed_one, hat_one, inv_one = norm_forward(inputs, first_gain, first_bias)
    wide_one = widen(normed_one)
    projected = matmul(wide_one, qkv_whole).reshape(row_count, 3, heads_here, HD)
    bias_parts = qv_bias.reshape(2, heads_here, HD)
    query_vecs = (projected[:, 0] + bias_parts[0]).astype(jnp.bfloat16)
    key_vecs = projected[:, 1].astype(jnp.bfloat16)
    value_vecs = (projected[:, 2] + bias_parts[1]).astype(jnp.bfloat16)
    attended, log_totals = attend(query_vecs, key_vecs, value_vecs, segment_ids)
    attended_flat = attended.reshape(row_count, heads_here * HD)
    hidden = inputs + combine(matmul(attended_flat, mix_whole)) + mix_bias
    normed_two, hat_two, inv_two = norm_forward(hidden, second_gain, second_bias)
    wide_two = widen(normed_two)
    pre_act = matmul(wide_two, up_whole) + up_bias
    active = gelu_value(pre_act).astype(jnp.bfloat16)
    final_sum = (
        hidden
        + combine(jnp.einsum("tu,fu->tf", active, down_whole, preferred_element_type=jnp.float32))
        + down_bias
    )
    output = final_sum.T.astype(jnp.bfloat16)
    live_mask = (segment_ids >= 0).astype(jnp.float32)
    grad_final = cotangent.astype(jnp.float32).T * live_mask[:, None]
    grad_wide = widen_grad(grad_final.astype(jnp.bfloat16))
    grad_down = jnp.einsum("tf,tu->fu", grad_wide, active, preferred_element_type=jnp.float32)
    grad_down_b = jnp.sum(grad_final, axis=0)
    grad_pre = (matmul(grad_wide, down_whole) * gelu_slope(pre_act)).astype(jnp.bfloat16)
    grad_up = matmul(wide_two.T, grad_pre)
    grad_up_b = jnp.sum(grad_pre.astype(jnp.float32), axis=0)
    grad_second_in = narrow(matmul(grad_pre, up_whole.T))
    grad_second_gain = jnp.sum(grad_second_in * hat_two, axis=0)
    grad_second_bias = jnp.sum(grad_second_in, axis=0)
    grad_hidden = grad_final + norm_back(grad_second_in, hat_two, inv_two, second_gain)
    grad_hidden_wide = widen_grad(grad_hidden.astype(jnp.bfloat16))
    grad_mix = matmul(attended_flat.T, grad_hidden_wide)
    grad_mix_b = jnp.sum(grad_hidden, axis=0)
    grad_att = (
        matmul(grad_hidden_wide, mix_whole.T)
        .astype(jnp.bfloat16)
        .reshape(row_count, heads_here, HD)
    )
    grad_query, grad_keys, grad_values = attend_back(
        query_vecs, key_vecs, value_vecs, attended, grad_att, segment_ids, log_totals
    )
    grad_qv = jnp.stack(
        [jnp.sum(grad_query, axis=0), jnp.sum(grad_values, axis=0)], axis=0
    ).reshape(2 * heads_here * HD)
    grad_projected = (
        jnp.stack([grad_query, grad_keys, grad_values], axis=1)
        .reshape(row_count, 3 * heads_here * HD)
        .astype(jnp.bfloat16)
    )
    grad_qkv = matmul(wide_one.T, grad_projected)
    grad_first_in = narrow(matmul(grad_projected, qkv_whole.T))
    grad_first_gain = jnp.sum(grad_first_in * hat_one, axis=0)
    grad_first_bias = jnp.sum(grad_first_in, axis=0)
    grad_tokens = (grad_hidden + norm_back(grad_first_in, hat_one, inv_one, first_gain)).T
    small_sums = lax.psum(
        (
            grad_first_gain,
            grad_first_bias,
            grad_qv,
            grad_mix_b,
            grad_second_gain,
            grad_second_bias,
            grad_up_b,
            grad_down_b,
        ),
        ("dp", "rows"),
    )
    qkv_part, up_part, mix_part, down_part = block_rows_sum(grad_qkv, grad_up, grad_mix, grad_down)
    qkv_part, up_part, mix_part, down_part = lax.psum(
        (qkv_part, up_part, mix_part, down_part), "dp"
    )
    return (
        output,
        grad_tokens,
        small_sums[0],
        small_sums[1],
        qkv_part,
        small_sums[2],
        mix_part,
        small_sums[3],
        small_sums[4],
        small_sums[5],
        up_part,
        small_sums[6],
        down_part,
        small_sums[7],
    )


def solution(mesh):
    return jax.shard_map(
        body,
        mesh=mesh,
        in_specs=(
            P("cols", ("dp", "rows")),
            P(("dp", "rows")),
            P("cols"),
            P("cols"),
            P("rows", "cols"),
            P("cols"),
            P("cols", "rows"),
            P("cols"),
            P("cols"),
            P("cols"),
            P("rows", "cols"),
            P("cols"),
            P("rows", "cols"),
            P("cols"),
            P("cols", ("dp", "rows")),
        ),
        out_specs=(
            P("cols", ("dp", "rows")),
            P("cols", ("dp", "rows")),
            P("cols"),
            P("cols"),
            P("rows", "cols"),
            P("cols"),
            P("cols", "rows"),
            P("cols"),
            P("cols"),
            P("cols"),
            P("rows", "cols"),
            P("cols"),
            P("rows", "cols"),
            P("cols"),
        ),
        check_vma=False,
    )
```

profile of v0, /device:TPU:0, one launch (start us, length us, event | category | flops | bytes accessed | tf_op | source)
XLA Modules:
  0.0 463.5 jit_solution(14573244544184651740)
XLA Ops:
  10.1 13.5 %all-reduce.4 = (f32[512]{0:T(512)S(1)}, f32[512]{0:T(512)S(1)}) all-reduce(f32[512]{0:T(512)S(1)} %fusion.28, f32[512]{0:T(512)S(1)} %convert_reduce_fusion.1), channel_id=1, replica_groups=mesh['dp'=2,'rows'=4,'cols'=4] {'cols'}, use_global_device_ids=true, to_apply=%region_3.0 | all-reduce | flops 1024 | bytes 8192 | tf_op jit(solution)/shard_map/psum | solution.py:119
  24.7 16.6 %all_gather.24 = bf16[512,768]{0,1:T(8,128)(2,1)S(1)} all-gather(bf16[512,192]{0,1:T(8,128)(2,1)S(1)} %fusion.21), channel_id=1, replica_groups=mesh['dp'=2,'rows'=4,'cols'=4] {'cols'}, dimensions={1}, use_global_device_ids=true | all-gather | bytes 983040 | tf_op jit(solution)/shard_map/all_gather | solution.py:138
  41.3 9.7 %all_gather.25 = bf16[768,576]{1,0:T(8,128)(2,1)S(1)} all-gather(bf16[192,576]{1,0:T(8,128)(2,1)S(1)} %copy-done.16), channel_id=1, replica_groups=mesh['dp'=2,'rows'=4,'cols'=4] {'rows'}, dimensions={0}, use_global_device_ids=true | all-gather | bytes 1105920 | tf_op jit(solution)/shard_map/all_gather | solution.py:185
  55.4 6.6 %all_gather.26 = bf16[192,768]{0,1:T(8,128)(2,1)S(1)} all-gather(bf16[192,192]{0,1:T(8,128)(2,1)S(1)} %copy.40), channel_id=1, replica_groups=mesh['dp'=2,'rows'=4,'cols'=4] {'rows'}, dimensions={1}, use_global_device_ids=true | all-gather | bytes 368640 | tf_op jit(solution)/shard_map/all_gather | solution.py:189
  62.0 2.2 convolution_convert_fusion.2
  68.6 30.1 %all_gather.30 = bf16[512,768]{0,1:T(8,128)(2,1)} all-gather(bf16[512,192]{0,1:T(8,128)(2,1)S(1)} %get-tuple-element.115), channel_id=1, replica_groups=mesh['dp'=2,'rows'=4,'cols'=4] {'cols'}, dimensions={1}, use_global_device_ids=true | all-gather | bytes 983040 | tf_op jit(solution)/shard_map/all_gather | solution.py:142
  98.7 13.4 %reduce-scatter.11.cloned.1.call-done = f32[512,192]{0,1:T(8,128)} async-done(((f32[512,768]{0,1:T(8,128)}), f32[512,192]{0,1:T(8,128)}) %reduce-scatter.11.cloned.1.call-update) | async-done | bytes 393232 | tf_op jit(solution)/shard_map/reduce_scatter | solution.py:146
  113.9 10.4 %all-reduce.3 = (f32[512]{0:T(512)}, f32[512]{0:T(512)}) all-reduce(f32[512]{0:T(512)S(1)} %get-tuple-element.83, f32[512]{0:T(512)S(1)} %get-tuple-element.82), channel_id=1, replica_groups=mesh['dp'=2,'rows'=4,'cols'=4] {'cols'}, use_global_device_ids=true, to_apply=%region_10.11 | all-reduce | flops 1024 | bytes 8192 | tf_op jit(solution)/shard_map/psum | solution.py:119
  126.1 17.7 %all_gather.27 = bf16[512,768]{0,1:T(8,128)(2,1)} all-gather(bf16[512,192]{0,1:T(8,128)(2,1)S(1)} %add_convert_fusion.1), channel_id=1, replica_groups=mesh['dp'=2,'rows'=4,'cols'=4] {'cols'}, dimensions={1}, use_global_device_ids=true | all-gather | bytes 983040 | tf_op jit(solution)/shard_map/all_gather | solution.py:138
  143.8 3.5 convolution_add_fusion
  147.3 4.2 convert_reduce_fusion
  152.4 2.0 fusion.58
  154.4 3.8 fusion.47
  158.3 30.7 %reduce-scatter.15.cloned.1.call-done = f32[512,192]{0,1:T(8,128)} async-done(((f32[512,768]{0,1:T(8,128)}), f32[512,192]{0,1:T(8,128)}) %reduce-scatter.15.cloned.1.call-update) | async-done | bytes 393232 | tf_op jit(solution)/shard_map/reduce_scatter | solution.py:150
  189.0 1.9 multiply_reduce_fusion
  190.9 10.4 %all-reduce.2 = (f32[512]{0:T(512)}, f32[512]{0:T(512)}) all-reduce(f32[512]{0:T(512)} %get-tuple-element.63, f32[512]{0:T(512)} %get-tuple-element.67), channel_id=1, replica_groups=mesh['dp'=2,'rows'=4,'cols'=4] {'cols'}, use_global_device_ids=true, to_apply=%region_16.17 | all-reduce | flops 1024 | bytes 8192 | tf_op jit(solution)/shard_map/psum | solution.py:119
  203.8 21.8 %reduce-scatter.13.cloned.1.call-done = f32[512,192]{0,1:T(8,128)} async-done(((f32[512,768]{0,1:T(8,128)}), f32[512,192]{0,1:T(8,128)}) %reduce-scatter.13.cloned.1.call-update) | async-done | bytes 393232 | tf_op jit(solution)/shard_map/reduce_scatter | solution.py:146
  225.7 2.9 fusion.49
  229.3 18.0 %all_gather.31 = bf16[512,768]{0,1:T(8,128)(2,1)S(1)} all-gather(bf16[512,192]{0,1:T(8,128)(2,1)S(1)} %convert_element_type.92), channel_id=1, replica_groups=mesh['dp'=2,'rows'=4,'cols'=4] {'cols'}, dimensions={1}, use_global_device_ids=true | all-gather | bytes 983040 | tf_op jit(solution)/shard_map/all_gather | solution.py:142
  249.5 3.6 fusion.60
  253.3 4.1 fusion.46
  259.3 2.0 multiply_convert_fusion
  264.6 2.1 fusion.59
  267.9 1.9 fusion.62
  269.9 2.0 reduce-scatter.25.cloned.1.call-done
  273.7 33.6 %reduce-scatter.21.cloned.1.call-done = f32[192,768]{1,0:T(8,128)} async-done(((f32[768,768]{1,0:T(8,128)}), f32[192,768]{1,0:T(8,128)}) %reduce-scatter.21.cloned.1.call-update) | async-done | bytes 589840 | tf_op jit(solution)/shard_map/reduce_scatter | solution.py:156
  307.3 35.3 %reduce-scatter.23.cloned.1.call-done = f32[192,768]{1,0:T(8,128)} async-done(((f32[768,768]{1,0:T(8,128)}), f32[192,768]{1,0:T(8,128)}) %reduce-scatter.23.cloned.1.call-update) | async-done | bytes 589840 | tf_op jit(solution)/shard_map/reduce_scatter | solution.py:160
  342.6 33.0 %reduce-scatter.19.cloned.1.call-done = f32[192,576]{1,0:T(8,128)} async-done(((f32[768,576]{1,0:T(8,128)}), f32[192,576]{1,0:T(8,128)}) %reduce-scatter.19.cloned.1.call-update) | async-done | bytes 442384 | tf_op jit(solution)/shard_map/reduce_scatter | solution.py:155
  375.7 37.5 %reduce-scatter.17.cloned.1.call-done = f32[512,192]{0,1:T(8,128)} async-done(((f32[512,768]{0,1:T(8,128)}), f32[512,192]{0,1:T(8,128)}) %reduce-scatter.17.cloned.1.call-update) | async-done | bytes 393232 | tf_op jit(solution)/shard_map/reduce_scatter | solution.py:150
  414.5 24.9 %all-reduce = (f32[192]{0:T(256)}, f32[192]{0:T(256)}, f32[384]{0:T(512)}, f32[192]{0:T(256)}, f32[192]{0:T(256)}, /*index=5*/f32[192]{0:T(256)}, f32[768]{0:T(1024)}, f32[192]{0:T(256)}) all-reduce(f32[192]{0:T(256)S(1)} %get-tuple-element.64, ...), channel_id=1, replica_groups=mesh['dp'=2,'rows'=4,'cols'=4] {'dp','rows'}, use_global_device_ids=true, to_apply=%region_24.25 | all-reduce | flops 2304 | bytes 18432 | tf_op jit(solution)/shard_map/psum | solution.py:249
  439.4 9.9 %all-reduce.1 = (f32[512]{0:T(512)S(1)}, f32[512]{0:T(512)S(1)}) all-reduce(f32[512]{0:T(512)S(1)} %get-tuple-element.65, f32[512]{0:T(512)S(1)} %get-tuple-element.66), channel_id=1, replica_groups=mesh['dp'=2,'rows'=4,'cols'=4] {'cols'}, use_global_device_ids=true, to_apply=%region_22.23 | all-reduce | flops 1024 | bytes 8192 | tf_op jit(solution)/shard_map/psum | solution.py:119
  451.2 1.9 copy.56
  (128 shorter events, 37.0 us)
Async XLA Ops:
  8.0 33.2 %copy-start.16 = (bf16[192,576]{1,0:T(8,128)(2,1)S(1)}, bf16[192,576]{1,0:T(8,128)(2,1)}, u32[]{:S(2)}) copy-start(bf16[192,576]{1,0:T(8,128)(2,1)} %param.19) | copy-start | bytes 663556
  8.0 42.9 %copy-start.18 = (s32[512]{0:T(512)S(1)}, s32[512]{0:T(512)}, u32[]{:S(2)}) copy-start(s32[512]{0:T(512)} %param.16) | copy-start | bytes 6148
  8.0 104.0 %reduce-scatter.11.cloned.1.call-start = ((), (), s32[]{:S(2)}) async-start(), calls=%async_computation.8 | async-start | bytes 1966080 | tf_op jit(solution)/shard_map/reduce_scatter | solution.py:146
  9.1 42.9 %copy-start.30 = (f32[384]{0:T(512)S(1)}, f32[384]{0:T(512)}, u32[]{:S(2)}) copy-start(f32[384]{0:T(512)} %param.20) | copy-start | bytes 4612
  41.3 11.6 %copy-start.4 = (bf16[512,768]{0,1:T(8,128)(2,1)}, bf16[512,768]{0,1:T(8,128)(2,1)S(1)}, u32[]{:S(2)}) copy-start(bf16[512,768]{0,1:T(8,128)(2,1)S(1)} %all_gather.24) | copy-start | bytes 2359300
  50.9 1.9 copy-start
  50.9 16.0 %copy-start.21 = (f32[512]{0:T(512)}, f32[512]{0:T(512)S(1)}, u32[]{:S(2)}) copy-start(f32[512]{0:T(512)S(1)} %get-tuple-element.106) | copy-start | bytes 6148
  55.3 8.9 %copy-start.29 = (f32[3,64]{1,0:T(4,128)}, f32[3,64]{1,0:T(4,128)S(1)}, u32[]{:S(2)}) copy-start(f32[3,64]{1,0:T(4,128)S(1)} %add.180) | copy-start | bytes 2308
  62.0 2.2 copy-start.10
  65.7 46.3 %copy-start.2 = (bf16[192,512]{1,0:T(8,128)(2,1)S(1)}, bf16[192,512]{1,0:T(8,128)(2,1)}, u32[]{:S(2)}) copy-start(bf16[192,512]{1,0:T(8,128)(2,1)} %param.15) | copy-start | bytes 589828
  65.7 78.0 %all-gather.3.cloned.1.call-start = ((), (), s32[]{:S(2)}) async-start(), calls=%async_computation.9 | async-start | bytes 1474560 | tf_op jit(solution)/shard_map/all_gather | solution.py:186
  66.3 80.9 %all-gather.5.cloned.1.call-start = ((), (), s32[]{:S(2)}) async-start(), calls=%async_computation.10 | async-start | bytes 1474560 | tf_op jit(solution)/shard_map/all_gather | solution.py:190
  66.9 122.1 %reduce-scatter.15.cloned.1.call-start = ((), (), s32[]{:S(2)}) async-start(), calls=%async_computation.12 | async-start | bytes 1966080 | tf_op jit(solution)/shard_map/reduce_scatter | solution.py:150
  147.3 5.1 %copy-start.31 = (bf16[768,768]{1,0:T(8,128)(2,1)S(1)}, bf16[768,768]{1,0:T(8,128)(2,1)}, u32[]{:S(2)}) copy-start(bf16[768,768]{1,0:T(8,128)(2,1)} %all-gather.3.cloned.1.call-done) | copy-start | bytes 3538948
  154.4 71.3 %reduce-scatter.13.cloned.1.call-start = ((), (), s32[]{:S(2)}) async-start(), calls=%async_computation.11 | async-start | bytes 1966080 | tf_op jit(solution)/shard_map/reduce_scatter | solution.py:146
  158.2 113.7 %reduce-scatter.25.cloned.1.call-start = ((), (), s32[]{:S(2)}) async-start(), calls=%async_computation.17 | async-start | bytes 983040
  249.5 57.8 %reduce-scatter.21.cloned.1.call-start = ((), (), s32[]{:S(2)}) async-start(), calls=%async_computation.15 | async-start | bytes 2949120 | tf_op jit(solution)/shard_map/reduce_scatter | solution.py:156
  253.1 89.5 %reduce-scatter.23.cloned.1.call-start = ((), (), s32[]{:S(2)}) async-start(), calls=%async_computation.16 | async-start | bytes 2949120 | tf_op jit(solution)/shard_map/reduce_scatter | solution.py:160
  257.4 1.9 copy-start.23
  257.4 118.2 %reduce-scatter.19.cloned.1.call-start = ((), (), s32[]{:S(2)}) async-start(), calls=%async_computation.14 | async-start | bytes 2457600 | tf_op jit(solution)/shard_map/reduce_scatter | solution.py:155
  259.3 2.0 copy-start.20
  266.7 146.5 %reduce-scatter.17.cloned.1.call-start = ((), (), s32[]{:S(2)}) async-start(), calls=%async_computation.13 | async-start | bytes 1966080 | tf_op jit(solution)/shard_map/reduce_scatter | solution.py:150
  269.8 143.4 %copy-start.22 = (f32[192]{0:T(256)S(1)}, f32[192]{0:T(256)}, u32[]{:S(2)}) copy-start(f32[192]{0:T(256)} %param.17) | copy-start | bytes 2308
  269.8 144.6 %copy-start.24 = (f32[192]{0:T(256)S(1)}, f32[192]{0:T(256)}, u32[]{:S(2)}) copy-start(f32[192]{0:T(256)} %get-tuple-element.104) | copy-start | bytes 2308
  269.8 144.6 %copy-start.25 = (f32[192]{0:T(256)S(1)}, f32[192]{0:T(256)}, u32[]{:S(2)}) copy-start(f32[192]{0:T(256)} %get-tuple-element.114) | copy-start | bytes 2308
  269.9 144.6 %copy-start.26 = (f32[192]{0:T(256)S(1)}, f32[192]{0:T(256)}, u32[]{:S(2)}) copy-start(f32[192]{0:T(256)} %get-tuple-element.62) | copy-start | bytes 2308
  269.9 144.6 %copy-start.27 = (f32[192]{0:T(256)S(1)}, f32[192]{0:T(256)}, u32[]{:S(2)}) copy-start(f32[192]{0:T(256)} %get-tuple-element.80) | copy-start | bytes 2308
  269.9 144.6 %copy-start.28 = (f32[768]{0:T(1024)S(1)}, f32[768]{0:T(1024)}, u32[]{:S(2)}) copy-start(f32[768]{0:T(1024)} %get-tuple-element.124) | copy-start | bytes 9220
  269.9 179.4 %copy-start.9 = (f32[512,192]{0,1:T(8,128)S(1)}, f32[512,192]{0,1:T(8,128)}, u32[]{:S(2)}) copy-start(f32[512,192]{0,1:T(8,128)} %copy-done.8) | copy-start | bytes 1179652
  269.9 181.3 %all-reduce.8.cloned.1.call-start = ((), (), s32[]{:S(2)}) async-start(), calls=%async_computation.18 | async-start | bytes 3735552 | tf_op jit(solution)/shard_map/psum | solution.py:263
  451.2 3.6 copy-start.15
  451.2 4.4 copy-start.14
  (11 other events, 13.7 us)
Sparse Core Ops, SparseCore 0:
  65.8 46.1 reduce-scatter.10
  154.5 34.4 reduce-scatter.14
  191.3 34.2 reduce-scatter.12
  375.7 58.2 all-reduce.7
Sparse Core Ops, SparseCore 1:
  67.8 15.7 all-gather.2
  84.9 17.3 all-gather.4
  249.5 22.4 reduce-scatter.24
  274.5 32.7 reduce-scatter.20
  309.8 32.7 reduce-scatter.22
  345.1 30.4 reduce-scatter.18
  377.7 35.4 reduce-scatter.16
where the time goes:
time: 465 us; the launch traced here: 464 us
  waiting for transfers between devices  209 us (45%)
  blocking collectives  168 us (36%)
  matrix products  37.3 us (8%)
  other arithmetic  21.4 us (5%)
  between operations  15.7 us (3%)
  local copies, waits for them, and re-layouts  12.4 us (3%)
    reduce_scatter x2, waiting for transfers between devices, narrow(): lax.psum_scatter(partial_sum, 'cols', scatter_dimension=1, tiled=True)  68.2 us
    all_gather x2, blocking collectives, widen_grad(): return lax.all_gather(values, 'cols', axis=1, tiled=True)  48.1 us
    psum x4, blocking collectives, row_sums(): return lax.psum((jnp.sum(first, axis=-1), jnp.sum(second, axis=-1)), 'cols')  44.1 us
    reduce_scatter x1, waiting for transfers between devices, block_rows_sum(): lax.psum_scatter(down_grad, 'rows', scatter_dimension=0, tiled=True)  35.3 us
    reduce_scatter x2, waiting for transfers between devices, combine(): lax.psum_scatter(partial_sum, 'cols', scatter_dimension=1, tiled=True)  35.2 us
    all_gather x2, blocking collectives, widen(): return lax.all_gather(values, 'cols', axis=1, tiled=True)  34.2 us
    reduce_scatter x1, waiting for transfers between devices, block_rows_sum(): lax.psum_scatter(up_grad, 'rows', scatter_dimension=0, tiled=True)  33.6 us
    reduce_scatter x1, waiting for transfers between devices, block_rows_sum(): lax.psum_scatter(qkv_grad, 'rows', scatter_dimension=0, tiled=True)  33 us
  transfers between devices with their start and end apart: 11, of which 8 were waited for; matrix products, arithmetic and copies ran while one was open for 9% of the time, Pallas kernels for 0%

commit v1 on v0

v1 whole, which is shorter than its diff:
```python
import functools
import math

import jax
import jax.numpy as jnp
from jax import lax
from jax.experimental import pallas as pl
from jax.experimental.pallas import tpu as pltpu
from jax.sharding import PartitionSpec as P

HD = 64
MAXLEN = 256
EPS = 1e-05
NEG = -1e30
ROOT = 0.7978845608028654
CUBIC = 0.044715
F32 = jnp.float32
BF16 = jnp.bfloat16


def dot(left, right, dims):
    return lax.dot_general(left, right, (dims, ((), ())), preferred_element_type=F32)


def mm(left, right):
    return dot(left, right, ((1,), (0,)))


def mm_t(left, right):
    return dot(left, right, ((0,), (0,)))


def mm_nt(left, right):
    return dot(left, right, ((1,), (1,)))


def gelu_both(pre_act):
    inner_arg = ROOT * (pre_act + CUBIC * pre_act * pre_act * pre_act)
    tanh_val = jnp.tanh(inner_arg)
    value = 0.5 * pre_act * (1.0 + tanh_val)
    slope = 0.5 * (1.0 + tanh_val) + 0.5 * pre_act * (1.0 - tanh_val * tanh_val) * ROOT * (
        1.0 + 3.0 * CUBIC * pre_act * pre_act
    )
    return value, slope


def allowed_mask(seg_row, seg_col, width):
    key_pos = lax.broadcasted_iota(jnp.int32, (width, width), 0)
    query_pos = lax.broadcasted_iota(jnp.int32, (width, width), 1)
    same_seg = (seg_col == seg_row) & (seg_row >= 0)
    return (key_pos < query_pos) & same_seg | (key_pos == query_pos)


def attend_kernel(width, heads, qkv_ref, bias_ref, row_ref, col_ref, qkv_out, att_out, total_out):
    head_rows = heads * HD
    biased = qkv_ref[...] + bias_ref[...]
    qkv_out[...] = biased.astype(BF16)
    scale = 1.0 / math.sqrt(HD)
    for half in range(qkv_ref.shape[1] // width):
        cols = pl.ds(half * width, width)
        allowed = allowed_mask(row_ref[:, cols], col_ref[cols, :], width)
        for head in range(heads):
            query = qkv_out[pl.ds(head * HD, HD), cols]
            keys = qkv_out[pl.ds(head_rows + head * HD, HD), cols]
            values = qkv_out[pl.ds(2 * head_rows + head * HD, HD), cols]
            scores = jnp.where(allowed, mm_t(keys, query) * scale, NEG)
            top = jnp.max(scores, axis=0, keepdims=True)
            log_total = top + jnp.log(jnp.sum(jnp.exp(scores - top), axis=0, keepdims=True))
            probs = jnp.exp(scores - log_total).astype(BF16)
            att_out[pl.ds(head * HD, HD), cols] = mm(values, probs).astype(BF16)
            total_out[pl.ds(head, 1), cols] = log_total


def attend(projected, bias_col, seg_row, seg_col, heads):
    rows, tokens = projected.shape
    width = min(MAXLEN, tokens)
    return pl.pallas_call(
        functools.partial(attend_kernel, width, heads),
        out_shape=(
            jax.ShapeDtypeStruct((rows, tokens), BF16),
            jax.ShapeDtypeStruct((heads * HD, tokens), BF16),
            jax.ShapeDtypeStruct((heads, tokens), F32),
        ),
        name="attend",
    )(projected, bias_col, seg_row, seg_col)


def attend_back_kernel(
    width, heads, qkv_ref, att_ref, grad_ref, total_ref, row_ref, col_ref, out_ref, sums_ref
):
    head_rows = heads * HD
    scale = 1.0 / math.sqrt(HD)
    for head in range(heads):
        sum_query = jnp.zeros((HD, 1), F32)
        sum_value = jnp.zeros((HD, 1), F32)
        for half in range(qkv_ref.shape[1] // width):
            cols = pl.ds(half * width, width)
            allowed = allowed_mask(row_ref[:, cols], col_ref[cols, :], width)
            query = qkv_ref[pl.ds(head * HD, HD), cols]
            keys = qkv_ref[pl.ds(head_rows + head * HD, HD), cols]
            values = qkv_ref[pl.ds(2 * head_rows + head * HD, HD), cols]
            grad = grad_ref[pl.ds(head * HD, HD), cols]
            attended = att_ref[pl.ds(head * HD, HD), cols]
            delta = jnp.sum(grad.astype(F32) * attended.astype(F32), axis=0, keepdims=True)
            scores = jnp.where(allowed, mm_t(keys, query) * scale, NEG)
            probs = jnp.exp(scores - total_ref[pl.ds(head, 1), cols])
            grad_values = mm_nt(grad, probs.astype(BF16))
            grad_probs = mm_t(values, grad)
            grad_scores = (probs * (grad_probs - delta) * scale).astype(BF16)
            grad_query = mm(keys, grad_scores)
            grad_keys = mm_nt(query, grad_scores)
            out_ref[pl.ds(head * HD, HD), cols] = grad_query.astype(BF16)
            out_ref[pl.ds(head_rows + head * HD, HD), cols] = grad_keys.astype(BF16)
            out_ref[pl.ds(2 * head_rows + head * HD, HD), cols] = grad_values.astype(BF16)
            sum_query += jnp.sum(grad_query, axis=1, keepdims=True)
            sum_value += jnp.sum(grad_values, axis=1, keepdims=True)
        sums_ref[pl.ds(head * HD, HD), :] = sum_query
        sums_ref[pl.ds(head_rows + head * HD, HD), :] = sum_value


def attend_back(qkv, attended, grad_att, totals, seg_row, seg_col, heads):
    rows, tokens = qkv.shape
    width = min(MAXLEN, tokens)
    return pl.pallas_call(
        functools.partial(attend_back_kernel, width, heads),
        out_shape=(
            jax.ShapeDtypeStruct((rows, tokens), BF16),
            jax.ShapeDtypeStruct((2 * heads * HD, 1), F32),
        ),
        name="attend_back",
    )(qkv, attended, grad_att, totals, seg_row, seg_col)


def bits_of(size):
    bits, bit = [], 1
    while bit < size:
        bits.append(bit)
        bit *= 2
    return bits


def swap(values, axis, size, bit):
    return lax.ppermute(values, axis, [(at, at ^ bit) for at in range(size)])


def shift(values, axis, size, step):
    return lax.ppermute(values, axis, [(at, (at + step) % size) for at in range(size)])


def whole_sum(values, axis_sizes):
    for axis, size in axis_sizes:
        for bit in bits_of(size):
            values = values + swap(values, axis, size, bit)
    return values


def put(target, piece, start, axis):
    return lax.dynamic_update_slice_in_dim(target, piece, start, axis)


def take(source, start, length, axis):
    return lax.dynamic_slice_in_dim(source, start, length, axis)


def make_body(n_dp, n_rows, n_cols):
    row_bits = bits_of(n_rows)[::-1]
    order = [0]
    for bit in row_bits:
        order = order + [value ^ bit for value in order]

    def body(
        tokens,
        segment_ids,
        first_gain,
        first_bias,
        qkv_weight,
        qv_bias,
        mix_weight,
        mix_bias,
        second_gain,
        second_bias,
        up_weight,
        up_bias,
        down_weight,
        down_bias,
        cotangent,
    ):
        feat, count = tokens.shape
        width = feat * n_cols
        part = count // n_cols
        heads = qkv_weight.shape[1] // (3 * HD)
        at_row = lax.axis_index("rows")
        at_col = lax.axis_index("cols")
        places = jnp.array([order.index(value) for value in range(n_rows)], jnp.int32)

        def place(block):
            return places[at_row ^ block]

        def col_of(step):
            return (at_col + step) % n_cols

        def to_rel(values):
            pieces = [take(values, (at_row ^ value) * feat, feat, 0) for value in order]
            return jnp.concatenate(pieces, axis=0)

        def to_nat(values):
            pieces = [take(values, place(block) * feat, feat, 0) for block in range(n_rows)]
            return jnp.concatenate(pieces, axis=0)

        def rows_whole(shard):
            for bit in row_bits:
                shard = jnp.concatenate([shard, swap(shard, "rows", n_rows, bit)], axis=0)
            return shard

        def rows_reduce(grad):
            for bit in row_bits[::-1]:
                half = grad.shape[0] // 2
                sent = swap(grad[half:].astype(BF16), "rows", n_rows, bit)
                grad = grad[:half] + sent.astype(F32)
            for bit in bits_of(n_dp):
                grad = grad + swap(grad.astype(BF16), "dp", n_dp, bit).astype(F32)
            return grad

        def col_blocks(own, start_of):
            whole = jnp.zeros((own.shape[0] * n_cols,) + own.shape[1:], own.dtype)
            whole = put(whole, own, start_of(at_col), 0)
            for step in range(1, n_cols):
                whole = put(whole, shift(own, "cols", n_cols, step), start_of(col_of(-step)), 0)
            return whole

        def col_exchange(piece_for):
            got = [(piece_for(at_col), at_col)]
            for step in range(1, n_cols):
                got.append((shift(piece_for(col_of(step)), "cols", n_cols, step), col_of(-step)))
            return got

        tok_whole = lax.all_gather(tokens, "cols", axis=0, tiled=True)
        qkv_rel = rows_whole(qkv_weight)
        mix_cols = col_blocks(mix_weight, lambda col: col * feat)
        mix_rel = rows_whole(mix_cols.T)
        up_rel = rows_whole(up_weight)
        down_rel = rows_whole(down_weight)
        cot_rel = col_blocks(cotangent, lambda col: place(col) * feat)

        seg_row = segment_ids.reshape(1, count)
        seg_col = segment_ids.reshape(count, 1)
        live = seg_row >= 0

        norms = jnp.stack([first_gain, first_bias, mix_bias, second_gain, second_bias], axis=1)
        norms = to_rel(lax.all_gather(norms, "cols", axis=0, tiled=True))
        gain_one, bias_one, bias_mix, gain_two, bias_two = [norms[:, k : k + 1] for k in range(5)]

        inputs = to_rel(tok_whole).astype(F32)
        mean_one = jnp.mean(inputs, axis=0, keepdims=True)
        inv_one = lax.rsqrt(jnp.mean(inputs * inputs, axis=0, keepdims=True) - mean_one * mean_one + EPS)
        hat_one = (inputs - mean_one) * inv_one
        normed_one = (hat_one * gain_one + bias_one).astype(BF16)
        projected = mm_t(qkv_rel, normed_one)
        head_rows = heads * HD
        bias_col = jnp.concatenate(
            [qv_bias[:head_rows], jnp.zeros((head_rows,), F32), qv_bias[head_rows:]]
        ).reshape(3 * head_rows, 1)
        qkv, attended, totals = attend(projected, bias_col, seg_row, seg_col, heads)

        att_whole = lax.all_gather(attended, "cols", axis=0, tiled=True)
        hidden = inputs + mm(mix_rel, att_whole) + bias_mix
        mean_two = jnp.mean(hidden, axis=0, keepdims=True)
        inv_two = lax.rsqrt(jnp.mean(hidden * hidden, axis=0, keepdims=True) - mean_two * mean_two + EPS)
        hat_two = (hidden - mean_two) * inv_two
        normed_two = (hat_two * gain_two + bias_two).astype(BF16)

        pre_act = mm_t(up_rel, normed_two) + up_bias[:, None]
        value, slope = gelu_both(pre_act)
        active = value.astype(BF16)
        grad_final_b = jnp.where(live, cot_rel, jnp.zeros_like(cot_rel))
        grad_pre = (mm_t(down_rel, grad_final_b) * slope).astype(BF16)
        part_two = mm(up_rel, grad_pre).astype(BF16)
        got = col_exchange(lambda col: take(part_two, col * part, part, 1))
        grad_two = sum(piece.astype(F32) for piece, _ in got)

        grad_down = rows_reduce(mm_nt(grad_final_b, active))
        grad_up = rows_reduce(mm_nt(normed_two, grad_pre))

        part_out = mm(down_rel, active).astype(BF16)
        got = col_exchange(lambda col: take(part_out, place(col) * feat, feat, 0))
        own_hidden = take(hidden, place(at_col) * feat, feat, 0)
        output = own_hidden + down_bias[:, None] + sum(piece.astype(F32) for piece, _ in got)

        own_at = at_col * part
        own_hat = (take(hidden, own_at, part, 1) - take(mean_two, own_at, part, 1)) * take(
            inv_two, own_at, part, 1
        )
        scaled = grad_two * gain_two
        grad_hidden = take(grad_final_b, own_at, part, 1).astype(F32) + take(inv_two, own_at, part, 1) * (
            scaled
            - jnp.mean(scaled, axis=0, keepdims=True)
            - own_hat * jnp.mean(scaled * own_hat, axis=0, keepdims=True)
        )
        grad_hidden_b = grad_hidden.astype(BF16)
        grad_att_all = mm_t(mix_rel, grad_hidden_b).astype(BF16)
        got = col_exchange(lambda col: take(grad_att_all, col * feat, feat, 0))
        grad_att = jnp.zeros((feat, count), BF16)
        for piece, col in got:
            grad_att = put(grad_att, piece, col * part, 1)
        got = col_exchange(lambda col: grad_hidden_b)
        grad_hidden_all = jnp.zeros((width, count), BF16)
        for piece, col in got:
            grad_hidden_all = put(grad_hidden_all, piece, col * part, 1)

        grad_proj, qv_sums = attend_back(qkv, attended, grad_att, totals, seg_row, seg_col, heads)
        grad_one_part = mm(qkv_rel, grad_proj)
        grad_qkv = rows_reduce(mm_nt(normed_one, grad_proj))
        grad_mix = rows_reduce(mm_nt(grad_hidden_all, attended))

        scaled = grad_one_part * gain_one
        stats = jnp.concatenate(
            [
                jnp.sum(scaled, axis=0, keepdims=True),
                jnp.sum(scaled * hat_one, axis=0, keepdims=True),
            ],
            axis=0,
        )
        stats = whole_sum(stats, [("cols", n_cols)]) / width
        grad_one_b = grad_one_part.astype(BF16)
        got = col_exchange(lambda col: take(grad_one_b, place(col) * feat, feat, 0))
        grad_one = sum(piece.astype(F32) for piece, _ in got)
        own_place = place(at_col) * feat
        hat_own = (tokens.astype(F32) - mean_one) * inv_one
        grad_tokens = take(grad_hidden_all, own_place, feat, 0).astype(F32) + inv_one * (
            grad_one * first_gain[:, None] - stats[:1] - hat_own * stats[1:]
        )

        token_sums = jnp.stack(
            [
                jnp.sum(grad_two * own_hat, axis=1),
                jnp.sum(grad_two, axis=1),
                jnp.sum(grad_hidden, axis=1),
            ],
            axis=1,
        )
        token_sums = whole_sum(to_nat(token_sums), [("cols", n_cols)])
        token_sums = take(token_sums, at_col * feat, feat, 0)
        own_final = jnp.where(live, cotangent.astype(F32), 0.0)
        early = jnp.concatenate(
            [
                token_sums.T.reshape(-1),
                jnp.sum(own_final, axis=1),
                jnp.sum(grad_pre.astype(F32), axis=1),
            ]
        )
        late = jnp.concatenate(
            [qv_sums.reshape(-1), jnp.sum(grad_one * hat_own, axis=1), jnp.sum(grad_one, axis=1)]
        )
        axes = [("rows", n_rows), ("dp", n_dp)]
        early = whole_sum(early, axes)
        late = whole_sum(late, axes)
        n_qv = 2 * head_rows
        return (
            output.astype(BF16),
            grad_tokens,
            late[n_qv : n_qv + feat],
            late[n_qv + feat :],
            grad_qkv,
            late[:n_qv],
            grad_mix.T,
            early[2 * feat : 3 * feat],
            early[:feat],
            early[feat : 2 * feat],
            grad_up,
            early[4 * feat :],
            grad_down,
            early[3 * feat : 4 * feat],
        )

    return body


def solution(mesh):
    sizes = mesh.shape
    return jax.shard_map(
        make_body(sizes["dp"], sizes["rows"], sizes["cols"]),
        mesh=mesh,
        in_specs=(
            P("cols", ("dp", "rows")),
            P(("dp", "rows")),
            P("cols"),
            P("cols"),
            P("rows", "cols"),
            P("cols"),
            P("cols", "rows"),
            P("cols"),
            P("cols"),
            P("cols"),
            P("rows", "cols"),
            P("cols"),
            P("rows", "cols"),
            P("cols"),
            P("cols", ("dp", "rows")),
        ),
        out_specs=(
            P("cols", ("dp", "rows")),
            P("cols", ("dp", "rows")),
            P("cols"),
            P("cols"),
            P("rows", "cols"),
            P("cols"),
            P("cols", "rows"),
            P("cols"),
            P("cols"),
            P("cols"),
            P("rows", "cols"),
            P("cols"),
            P("rows", "cols"),
            P("cols"),
        ),
        check_vma=False,
    )
```

time: 465 us -> 265 us (0.57)
  waiting for transfers between devices: 209 us -> 88.9 us
  blocking collectives: 168 us -> 48.4 us
  starting transfers between devices: 0.65 us -> 52 us
  matrix products: 37.3 us -> 15.4 us
  local copies, waits for them, and re-layouts: 12.4 us -> 24.5 us
  Pallas kernels: 0 us -> 8.29 us
  between operations: 15.7 us -> 9.07 us
    reduce_scatter x7 -> x0, waiting for transfers between devices: 205 us -> none  [the longest x2 68.2 us: narrow(): lax.psum_scatter(partial_sum, 'cols', scatter_dimension=1, tiled=True)]
    ppermute x0 -> x51, waiting for transfers between devices: none -> 88.9 us  [the longest x21 46.6 us: shift(): lax.ppermute(values, axis, [(at, (at + step) % size) for at in range(size)])]
    psum x5 -> x0, blocking collectives: 69 us -> none  [the longest x4 44.1 us: row_sums(): return lax.psum((jnp.sum(first, axis=-1), jnp.sum(second, axis=-1)), 'cols')]
    ppermute x0 -> x51, starting transfers between devices: none -> 52 us  [the longest x21 29.2 us: shift(): lax.ppermute(values, axis, [(at, (at + step) % size) for at in range(size)])]
    all_gather x6 -> x3, blocking collectives: 98.5 us -> 48.4 us  [the longest x1 18.3 us: body(): att_whole = lax.all_gather(attended, 'cols', axis=0, tiled=True)]
    dot_general x17 -> x12, matrix products: 36.1 us -> 15.4 us  [dot(): lax.dot_general(left, right, (dims, ((), ())), preferred_element_type=F32)]
    reduce_sum x9 -> x5, other arithmetic: 12.3 us -> 1.41 us  [the longest x1 0.43 us: body(): jnp.sum(grad_two * own_hat, axis=1)]
    pallas_call x0 -> x2, Pallas kernels: none -> 8.29 us  [the longest x1 4.24 us: attend(): pl.pallas_call(functools.partial(attend_kernel, width, heads), out_shape=...]
  transfers between devices with their start and end apart: 11 -> 51, of which waited for: 8 -> 25; matrix products, arithmetic and copies ran while one was open for 9% -> 16% of each run, Pallas kernels for 0% -> 3%
where the time goes in v1:
time: 265 us; the launch traced here: 264 us
  waiting for transfers between devices  88.9 us (34%)
  starting transfers between devices  52 us (20%)
  blocking collectives  48.4 us (18%)
  local copies, waits for them, and re-layouts  24.5 us (9%)
  other arithmetic  17.2 us (6%)
  matrix products  15.4 us (6%)
  between operations  9.07 us (3%)
  Pallas kernels  8.29 us (3%)
    ppermute x21, waiting for transfers between devices, shift(): lax.ppermute(values, axis, [(at, (at + step) % size) for at in range(size)])  46.6 us
    ppermute x30, waiting for transfers between devices, swap(): return lax.ppermute(values, axis, [(at, at ^ bit) for at in range(size)])  42.3 us
    ppermute x21, starting transfers between devices, shift(): lax.ppermute(values, axis, [(at, (at + step) % size) for at in range(size)])  29.2 us
    ppermute x30, starting transfers between devices, swap(): return lax.ppermute(values, axis, [(at, at ^ bit) for at in range(size)])  22.8 us
    all_gather x1, blocking collectives, body(): att_whole = lax.all_gather(attended, 'cols', axis=0, tiled=True)  18.3 us
    all_gather x1, blocking collectives, body(): tok_whole = lax.all_gather(tokens, 'cols', axis=0, tiled=True)  17 us
    dot_general x12, matrix products, dot(): lax.dot_general(left, right, (dims, ((), ())), preferred_element_type=F32)  15.4 us
    all_gather x1, blocking collectives, body(): norms = to_rel(lax.all_gather(norms, 'cols', axis=0, tiled=True))  13.1 us
  transfers between devices with their start and end apart: 51, of which 25 were waited for; matrix products, arithmetic and copies ran while one was open for 16% of the time, Pallas kernels for 3%

profile of v1, /device:TPU:0, one launch (start us, length us, event | category | flops | bytes accessed | tf_op | source)
XLA Modules:
  0.0 263.7 jit_solution(15795832271704118032)
XLA Ops:
  0.7 3.1 %collective-permute-start = (bf16[192,192]{1,0:T(8,128)(2,1)}, bf16[192,192]{1,0:T(8,128)(2,1)S(1)}, u32[]{:S(2)}, u32[]{:S(2)}) collective-permute-start(bf16[192,192]{1,0:T(8,128)(2,1)} %param.22), channel_id=1, source_target_pairs={{0,1},{1,2},{2,3},{3,0},{4,5},{5,6},{6,7},{7,4},{8,9},{9,10},{10,1... | collective-permute-start | bytes 221192 | tf_op jit(solution)/shard_map/ppermute | solution.py:147
  3.8 2.6 collective-permute-start.1
  15.1 13.1 %all-gather = f32[4,192,5]{1,2,0:T(8,128)S(1)} all-gather(f32[1,192,5]{1,2,0:T(8,128)S(1)} %bitcast.53), channel_id=1, replica_groups=mesh['dp'=2,'rows'=4,'cols'=4] {'cols'}, dimensions={0}, use_global_device_ids=true | all-gather | bytes 19200 | tf_op jit(solution)/shard_map/all_gather | solution.py:250
  36.7 17.0 %all_gather.9 = bf16[768,512]{1,0:T(8,128)(2,1)S(1)} all-gather(bf16[192,512]{1,0:T(8,128)(2,1)S(1)} %copy-done), channel_id=1, replica_groups=mesh['dp'=2,'rows'=4,'cols'=4] {'cols'}, dimensions={0}, use_global_device_ids=true | all-gather | bytes 983040 | tf_op jit(solution)/shard_map/all_gather | solution.py:237
  56.4 2.8 %collective-permute-start.2 = (bf16[192,192]{1,0:T(8,128)(2,1)S(1)}, bf16[192,192]{1,0:T(8,128)(2,1)S(1)}, u32[]{:S(2)}, u32[]{:S(2)}) collective-permute-start(bf16[192,192]{1,0:T(8,128)(2,1)S(1)} %copy-done.24), channel_id=1, source_target_pairs={{0,3},{1,0},{2,1},{3,2},{4,7},{5,4},{6,5},{7,6},{8,11},{9,8},{10,9... | collective-permute-start | bytes 221192 | tf_op jit(solution)/shard_map/ppermute | solution.py:147
  59.3 4.4 %collective-permute-done.2 = bf16[192,192]{1,0:T(8,128)(2,1)S(1)} collective-permute-done((bf16[192,192]{1,0:T(8,128)(2,1)S(1)}, bf16[192,192]{1,0:T(8,128)(2,1)S(1)}, u32[]{:S(2)}, u32[]{:S(2)}) %collective-permute-start.2) | collective-permute-done | bytes 73760 | tf_op jit(solution)/shard_map/ppermute | solution.py:147
  63.8 3.0 %collective-permute-done.14 = bf16[192,512]{1,0:T(8,128)(2,1)S(1)} collective-permute-done((bf16[192,512]{1,0:T(8,128)(2,1)S(1)}, bf16[192,512]{1,0:T(8,128)(2,1)S(1)}, u32[]{:S(2)}, u32[]{:S(2)}) %collective-permute-start.14) | collective-permute-done | bytes 196640 | tf_op jit(solution)/shard_map/ppermute | solution.py:147
  66.8 2.0 collective-permute-start.16
  68.8 2.9 %collective-permute-done.15 = bf16[192,512]{1,0:T(8,128)(2,1)S(1)} collective-permute-done((bf16[192,512]{1,0:T(8,128)(2,1)S(1)}, bf16[192,512]{1,0:T(8,128)(2,1)S(1)}, u32[]{:S(2)}, u32[]{:S(2)}) %collective-permute-start.15) | collective-permute-done | bytes 196640 | tf_op jit(solution)/shard_map/ppermute | solution.py:147
  83.5 4.2 %attend.1 = (bf16[576,512]{1,0:T(8,128)(2,1)}, bf16[192,512]{1,0:T(8,128)(2,1)}, f32[3,512]{1,0:T(4,128)}) custom-call(f32[576,512]{1,0:T(8,128)} %fusion.28.qkv_ref, f32[576,1]{1,0:T(8,128)} %reshape.152.bias_ref, s32[1,512]{1,0:T(1,128)} %bitcast.50, s32[512,1]{1,0:T(8,128)} %copy.42.col_ref), custom_call_target="tpu_custom_call" | custom-call | tf_op jit(solution)/shard_map/attend/pallas_call | solution.py:77
  87.7 18.3 %all_gather.11 = bf16[768,512]{1,0:T(8,128)(2,1)S(1)} all-gather(bf16[192,512]{1,0:T(8,128)(2,1)} %get-tuple-element.19.att_ref), channel_id=1, replica_groups=mesh['dp'=2,'rows'=4,'cols'=4] {'cols'}, dimensions={0}, use_global_device_ids=true | all-gather | bytes 983040 | tf_op jit(solution)/shard_map/all_gather | solution.py:265
  108.0 2.3 fusion.32
  116.5 2.2 collective-permute-start.19
  120.5 3.6 %collective-permute-done.19 = bf16[768,128]{1,0:T(8,128)(2,1)S(1)} collective-permute-done((bf16[768,128]{1,0:T(8,128)(2,1)S(1)}, bf16[768,128]{1,0:T(8,128)(2,1)S(1)}, u32[]{:S(2)}, u32[]{:S(2)}) %collective-permute-start.19) | collective-permute-done | bytes 196640 | tf_op jit(solution)/shard_map/ppermute | solution.py:147
  124.1 10.8 %collective-permute-done.18 = bf16[768,128]{1,0:T(8,128)(2,1)S(1)} collective-permute-done((bf16[768,128]{1,0:T(8,128)(2,1)S(1)}, bf16[768,128]{1,0:T(8,128)(2,1)S(1)}, u32[]{:S(2)}, u32[]{:S(2)}) %collective-permute-start.18) | collective-permute-done | bytes 196640 | tf_op jit(solution)/shard_map/ppermute | solution.py:147
  137.0 3.4 %collective-permute-start.13 = (bf16[192,512]{1,0:T(8,128)(2,1)S(1)}, bf16[192,512]{1,0:T(8,128)(2,1)}, u32[]{:S(2)}, u32[]{:S(2)}) collective-permute-start(bf16[192,512]{1,0:T(8,128)(2,1)S(1)} %get-tuple-element.110), channel_id=1, source_target_pairs={{0,3},{1,0},{2,1},{3,2},{4,7},{5,4},{6,5},{7,6},{8,11},{9,8},{10,9... | collective-permute-start | bytes 589832 | tf_op jit(solution)/shard_map/ppermute | solution.py:147
  142.9 2.3 collective-permute-start.41
  145.9 10.6 %collective-permute-done.41 = f32[768,3]{0,1:T(4,128)S(1)} collective-permute-done((f32[768,3]{0,1:T(4,128)S(1)}, f32[768,3]{0,1:T(4,128)S(1)}, u32[]{:S(2)}, u32[]{:S(2)}) %collective-permute-start.41) | collective-permute-done | bytes 9248 | tf_op jit(solution)/shard_map/ppermute | solution.py:143
  158.9 3.2 %collective-permute-done.43 = f32[1536]{0:T(1024)S(1)} collective-permute-done((f32[1536]{0:T(1024)S(1)}, f32[1536]{0:T(1024)S(1)}, u32[]{:S(2)}, u32[]{:S(2)}) %collective-permute-start.43) | collective-permute-done | bytes 6176 | tf_op jit(solution)/shard_map/ppermute | solution.py:143
  163.3 3.4 %collective-permute-start.21 = (bf16[768,128]{1,0:T(8,128)(2,1)}, bf16[768,128]{1,0:T(8,128)(2,1)}, u32[]{:S(2)}, u32[]{:S(2)}) collective-permute-start(bf16[768,128]{1,0:T(8,128)(2,1)} %get-tuple-element.100), channel_id=1, source_target_pairs={{0,2},{1,3},{2,0},{3,1},{4,6},{5,7},{6,4},{7,5},{8,10},{9,11},{10,... | collective-permute-start | bytes 589832 | tf_op jit(solution)/shard_map/ppermute | solution.py:147
  168.2 2.1 add_convert_fusion.1
  171.7 4.9 %collective-permute-done.23 = bf16[192,128]{1,0:T(8,128)(2,1)S(1)} collective-permute-done((bf16[192,128]{1,0:T(8,128)(2,1)S(1)}, bf16[192,128]{1,0:T(8,128)(2,1)S(1)}, u32[]{:S(2)}, u32[]{:S(2)}) %collective-permute-start.23) | collective-permute-done | bytes 49184 | tf_op jit(solution)/shard_map/ppermute | solution.py:147
  176.6 5.8 %collective-permute-done.24 = bf16[192,128]{1,0:T(8,128)(2,1)S(1)} collective-permute-done((bf16[192,128]{1,0:T(8,128)(2,1)S(1)}, bf16[192,128]{1,0:T(8,128)(2,1)S(1)}, u32[]{:S(2)}, u32[]{:S(2)}) %collective-permute-start.24) | collective-permute-done | bytes 49184 | tf_op jit(solution)/shard_map/ppermute | solution.py:147
  184.0 4.1 %attend_back.1 = (bf16[576,512]{1,0:T(8,128)(2,1)}, f32[384,1]{1,0:T(8,128)}) custom-call(bf16[576,512]{1,0:T(8,128)(2,1)} %get-tuple-element.20.qkv_ref, bf16[192,512]{1,0:T(8,128)(2,1)} %get-tuple-element.19.att_ref, bf16[192,512]{1,0:T(8,128)(2,1)} %copy-done.12, f32[3,512]{1,0:T(4,128)} %get-tuple-element.21.total_ref, s32[1,512]{1,0:T(1,128)} %bitcast.51, ...), custom_call_target="tpu_custom_call" | custom-call | tf_op jit(solution)/shard_map/attend_back/pallas_call | solution.py:124
  188.1 2.3 multiply_reduce_fusion.1
  191.9 2.2 collective-permute-done.29
  204.2 3.9 %collective-permute-start.22 = (bf16[768,128]{1,0:T(8,128)(2,1)}, bf16[768,128]{1,0:T(8,128)(2,1)S(1)}, u32[]{:S(2)}, u32[]{:S(2)}) collective-permute-start(bf16[768,128]{1,0:T(8,128)(2,1)} %get-tuple-element.100), channel_id=1, source_target_pairs={{0,3},{1,0},{2,1},{3,2},{4,7},{5,4},{6,5},{7,6},{8,11},{9,8},{10,9... | collective-permute-start | bytes 589832 | tf_op jit(solution)/shard_map/ppermute | solution.py:147
  208.0 7.2 %collective-permute-done.27 = bf16[192,512]{1,0:T(8,128)(2,1)S(1)} collective-permute-done((bf16[192,512]{1,0:T(8,128)(2,1)S(1)}, bf16[192,512]{1,0:T(8,128)(2,1)S(1)}, u32[]{:S(2)}, u32[]{:S(2)}) %collective-permute-start.27) | collective-permute-done | bytes 196640 | tf_op jit(solution)/shard_map/ppermute | solution.py:147
  218.7 2.7 %collective-permute-done.32 = f32[768]{0:T(1024)S(1)} collective-permute-done((f32[768]{0:T(1024)S(1)}, f32[768]{0:T(1024)S(1)}, u32[]{:S(2)}, u32[]{:S(2)}) %collective-permute-start.32) | collective-permute-done | bytes 3104 | tf_op jit(solution)/shard_map/ppermute | solution.py:143
  234.4 2.5 collective-permute-done.39
  240.7 7.9 %collective-permute-done.35 = bf16[192,576]{0,1:T(8,128)(2,1)S(1)} collective-permute-done((bf16[192,576]{0,1:T(8,128)(2,1)S(1)}, bf16[192,576]{0,1:T(8,128)(2,1)S(1)}, u32[]{:S(2)}, u32[]{:S(2)}) %collective-permute-start.35) | collective-permute-done | bytes 221216 | tf_op jit(solution)/shard_map/ppermute | solution.py:143
  251.6 7.0 %collective-permute-done.36 = bf16[192,576]{0,1:T(8,128)(2,1)S(1)} collective-permute-done((bf16[192,576]{0,1:T(8,128)(2,1)S(1)}, bf16[192,576]{0,1:T(8,128)(2,1)S(1)}, u32[]{:S(2)}, u32[]{:S(2)}) %collective-permute-start.36) | collective-permute-done | bytes 221216 | tf_op jit(solution)/shard_map/ppermute | solution.py:143
  (283 shorter events, 86.8 us)
Async XLA Ops:
  0.7 55.7 %collective-permute-start = (bf16[192,192]{1,0:T(8,128)(2,1)}, bf16[192,192]{1,0:T(8,128)(2,1)S(1)}, u32[]{:S(2)}, u32[]{:S(2)}) collective-permute-start(bf16[192,192]{1,0:T(8,128)(2,1)} %param.22), channel_id=1, source_target_pairs={{0,1},{1,2},{2,3},{3,0},{4,5},{5,6},{6,7},{7,4},{8,9},{9,10},{10,1... | collective-permute-start | bytes 221192 | tf_op jit(solution)/shard_map/ppermute | solution.py:147
  3.8 55.4 %collective-permute-start.1 = (bf16[192,192]{1,0:T(8,128)(2,1)}, bf16[192,192]{1,0:T(8,128)(2,1)S(1)}, u32[]{:S(2)}, u32[]{:S(2)}) collective-permute-start(bf16[192,192]{1,0:T(8,128)(2,1)} %param.22), channel_id=1, source_target_pairs={{0,2},{1,3},{2,0},{3,1},{4,6},{5,7},{6,4},{7,5},{8,10},{9,11},{10,... | collective-permute-start | bytes 221192 | tf_op jit(solution)/shard_map/ppermute | solution.py:147
  6.4 67.6 %collective-permute-start.7 = (bf16[192,768]{1,0:T(8,128)(2,1)}, bf16[192,768]{1,0:T(8,128)(2,1)S(1)}, u32[]{:S(2)}, u32[]{:S(2)}) collective-permute-start(bf16[192,768]{1,0:T(8,128)(2,1)} %param.28), channel_id=1, source_target_pairs={{0,8},{4,12},{8,0},{12,4},{1,9},{5,13},{9,1},{13,5},{2,10},{6,14},... | collective-permute-start | bytes 884744 | tf_op jit(solution)/shard_map/ppermute | solution.py:143
  7.9 67.6 %collective-permute-start.9 = (bf16[192,768]{1,0:T(8,128)(2,1)}, bf16[192,768]{1,0:T(8,128)(2,1)S(1)}, u32[]{:S(2)}, u32[]{:S(2)}) collective-permute-start(bf16[192,768]{1,0:T(8,128)(2,1)} %param.26), channel_id=1, source_target_pairs={{0,8},{4,12},{8,0},{12,4},{1,9},{5,13},{9,1},{13,5},{2,10},{6,14},... | collective-permute-start | bytes 884744 | tf_op jit(solution)/shard_map/ppermute | solution.py:143
  8.4 65.3 %collective-permute-start.5 = (bf16[192,576]{1,0:T(8,128)(2,1)}, bf16[192,576]{1,0:T(8,128)(2,1)S(1)}, u32[]{:S(2)}, u32[]{:S(2)}) collective-permute-start(bf16[192,576]{1,0:T(8,128)(2,1)} %param.20), channel_id=1, source_target_pairs={{0,8},{4,12},{8,0},{12,4},{1,9},{5,13},{9,1},{13,5},{2,10},{6,14},... | collective-permute-start | bytes 663560 | tf_op jit(solution)/shard_map/ppermute | solution.py:143
  63.8 7.9 %collective-permute-start.15 = (bf16[192,512]{1,0:T(8,128)(2,1)S(1)}, bf16[192,512]{1,0:T(8,128)(2,1)S(1)}, u32[]{:S(2)}, u32[]{:S(2)}) collective-permute-start(bf16[192,512]{1,0:T(8,128)(2,1)S(1)} %copy-done.13), channel_id=1, source_target_pairs={{0,2},{1,3},{2,0},{3,1},{4,6},{5,7},{6,4},{7,5},{8,10},{9,11},{10,... | collective-permute-start | bytes 589832 | tf_op jit(solution)/shard_map/ppermute | solution.py:147
  71.7 7.8 %collective-permute-start.3 = (bf16[192,768]{0,1:T(8,128)(2,1)S(1)}, bf16[192,768]{0,1:T(8,128)(2,1)S(1)}, u32[]{:S(2)}, u32[]{:S(2)}) collective-permute-start(bf16[192,768]{0,1:T(8,128)(2,1)S(1)} %bitcast.46), channel_id=1, source_target_pairs={{0,8},{4,12},{8,0},{12,4},{1,9},{5,13},{9,1},{13,5},{2,10},{6,14},... | collective-permute-start | bytes 884744 | tf_op jit(solution)/shard_map/ppermute | solution.py:143
  75.5 30.4 %collective-permute-start.8 = (bf16[384,768]{1,0:T(8,128)(2,1)}, bf16[384,768]{1,0:T(8,128)(2,1)S(1)}, u32[]{:S(2)}, u32[]{:S(2)}) collective-permute-start(bf16[384,768]{1,0:T(8,128)(2,1)} %pad_maximum_fusion.3), channel_id=1, source_target_pairs={{0,4},{4,0},{8,12},{12,8},{1,5},{5,1},{9,13},{13,9},{2,6},{6,2},{1... | collective-permute-start | bytes 1769480 | tf_op jit(solution)/shard_map/ppermute | solution.py:143
  76.4 30.4 %collective-permute-start.10 = (bf16[384,768]{1,0:T(8,128)(2,1)}, bf16[384,768]{1,0:T(8,128)(2,1)}, u32[]{:S(2)}, u32[]{:S(2)}) collective-permute-start(bf16[384,768]{1,0:T(8,128)(2,1)} %pad_maximum_fusion.4), channel_id=1, source_target_pairs={{0,4},{4,0},{8,12},{12,8},{1,5},{5,1},{9,13},{13,9},{2,6},{6,2},{1... | collective-permute-start | bytes 1769480 | tf_op jit(solution)/shard_map/ppermute | solution.py:143
  80.5 27.4 %collective-permute-start.4 = (bf16[384,768]{0,1:T(8,128)(2,1)}, bf16[384,768]{0,1:T(8,128)(2,1)}, u32[]{:S(2)}, u32[]{:S(2)}) collective-permute-start(bf16[384,768]{0,1:T(8,128)(2,1)} %pad_maximum_fusion.2), channel_id=1, source_target_pairs={{0,4},{4,0},{8,12},{12,8},{1,5},{5,1},{9,13},{13,9},{2,6},{6,2},{1... | collective-permute-start | bytes 1769480 | tf_op jit(solution)/shard_map/ppermute | solution.py:143
  118.7 16.1 %collective-permute-start.18 = (bf16[768,128]{1,0:T(8,128)(2,1)S(1)}, bf16[768,128]{1,0:T(8,128)(2,1)S(1)}, u32[]{:S(2)}, u32[]{:S(2)}) collective-permute-start(bf16[768,128]{1,0:T(8,128)(2,1)S(1)} %get-tuple-element.108), channel_id=1, source_target_pairs={{0,2},{1,3},{2,0},{3,1},{4,6},{5,7},{6,4},{7,5},{8,10},{9,11},{10,... | collective-permute-start | bytes 589832 | tf_op jit(solution)/shard_map/ppermute | solution.py:147
  118.7 16.1 %collective-permute-start.17 = (bf16[768,128]{1,0:T(8,128)(2,1)S(1)}, bf16[768,128]{1,0:T(8,128)(2,1)S(1)}, u32[]{:S(2)}, u32[]{:S(2)}) collective-permute-start(bf16[768,128]{1,0:T(8,128)(2,1)S(1)} %get-tuple-element.106), channel_id=1, source_target_pairs={{0,1},{1,2},{2,3},{3,0},{4,5},{5,6},{6,7},{7,4},{8,9},{9,10},{10,1... | collective-permute-start | bytes 589832 | tf_op jit(solution)/shard_map/ppermute | solution.py:147
  137.0 26.3 %collective-permute-start.13 = (bf16[192,512]{1,0:T(8,128)(2,1)S(1)}, bf16[192,512]{1,0:T(8,128)(2,1)}, u32[]{:S(2)}, u32[]{:S(2)}) collective-permute-start(bf16[192,512]{1,0:T(8,128)(2,1)S(1)} %get-tuple-element.110), channel_id=1, source_target_pairs={{0,3},{1,0},{2,1},{3,2},{4,7},{5,4},{6,5},{7,6},{8,11},{9,8},{10,9... | collective-permute-start | bytes 589832 | tf_op jit(solution)/shard_map/ppermute | solution.py:147
  140.4 26.2 %collective-permute-start.12 = (bf16[192,512]{1,0:T(8,128)(2,1)S(1)}, bf16[192,512]{1,0:T(8,128)(2,1)}, u32[]{:S(2)}, u32[]{:S(2)}) collective-permute-start(bf16[192,512]{1,0:T(8,128)(2,1)S(1)} %get-tuple-element.111), channel_id=1, source_target_pairs={{0,2},{1,3},{2,0},{3,1},{4,6},{5,7},{6,4},{7,5},{8,10},{9,11},{10,... | collective-permute-start | bytes 589832 | tf_op jit(solution)/shard_map/ppermute | solution.py:147
  140.4 26.3 %collective-permute-start.11 = (bf16[192,512]{1,0:T(8,128)(2,1)S(1)}, bf16[192,512]{1,0:T(8,128)(2,1)}, u32[]{:S(2)}, u32[]{:S(2)}) collective-permute-start(bf16[192,512]{1,0:T(8,128)(2,1)S(1)} %get-tuple-element.109), channel_id=1, source_target_pairs={{0,1},{1,2},{2,3},{3,0},{4,5},{5,6},{6,7},{7,4},{8,9},{9,10},{10,1... | collective-permute-start | bytes 589832 | tf_op jit(solution)/shard_map/ppermute | solution.py:147
  141.9 84.9 %collective-permute-start.45 = (bf16[384,768]{1,0:T(8,128)(2,1)}, bf16[384,768]{1,0:T(8,128)(2,1)}, u32[]{:S(2)}, u32[]{:S(2)}) collective-permute-start(bf16[384,768]{1,0:T(8,128)(2,1)} %slice.196), channel_id=1, source_target_pairs={{0,4},{4,0},{8,12},{12,8},{1,5},{5,1},{9,13},{13,9},{2,6},{6,2},{1... | collective-permute-start | bytes 1769480 | tf_op jit(solution)/shard_map/ppermute | solution.py:143
  142.9 13.6 %collective-permute-start.41 = (f32[768,3]{0,1:T(4,128)S(1)}, f32[768,3]{0,1:T(4,128)S(1)}, u32[]{:S(2)}, u32[]{:S(2)}) collective-permute-start(f32[768,3]{0,1:T(4,128)S(1)} %fusion.56), channel_id=1, source_target_pairs={{0,2},{1,3},{2,0},{3,1},{4,6},{5,7},{6,4},{7,5},{8,10},{9,11},{10,... | collective-permute-start | bytes 27656 | tf_op jit(solution)/shard_map/ppermute | solution.py:143
  162.2 39.9 %collective-permute-start.20 = (bf16[768,128]{1,0:T(8,128)(2,1)}, bf16[768,128]{1,0:T(8,128)(2,1)}, u32[]{:S(2)}, u32[]{:S(2)}) collective-permute-start(bf16[768,128]{1,0:T(8,128)(2,1)} %get-tuple-element.100), channel_id=1, source_target_pairs={{0,1},{1,2},{2,3},{3,0},{4,5},{5,6},{6,7},{7,4},{8,9},{9,10},{10,1... | collective-permute-start | bytes 589832 | tf_op jit(solution)/shard_map/ppermute | solution.py:147
  163.3 39.8 %collective-permute-start.21 = (bf16[768,128]{1,0:T(8,128)(2,1)}, bf16[768,128]{1,0:T(8,128)(2,1)}, u32[]{:S(2)}, u32[]{:S(2)}) collective-permute-start(bf16[768,128]{1,0:T(8,128)(2,1)} %get-tuple-element.100), channel_id=1, source_target_pairs={{0,2},{1,3},{2,0},{3,1},{4,6},{5,7},{6,4},{7,5},{8,10},{9,11},{10,... | collective-permute-start | bytes 589832 | tf_op jit(solution)/shard_map/ppermute | solution.py:147
  166.7 9.9 %collective-permute-start.23 = (bf16[192,128]{1,0:T(8,128)(2,1)S(1)}, bf16[192,128]{1,0:T(8,128)(2,1)S(1)}, u32[]{:S(2)}, u32[]{:S(2)}) collective-permute-start(bf16[192,128]{1,0:T(8,128)(2,1)S(1)} %get-tuple-element.118), channel_id=1, source_target_pairs={{0,1},{1,2},{2,3},{3,0},{4,5},{5,6},{6,7},{7,4},{8,9},{9,10},{10,1... | collective-permute-start | bytes 147464 | tf_op jit(solution)/shard_map/ppermute | solution.py:147
  170.4 12.0 %collective-permute-start.24 = (bf16[192,128]{1,0:T(8,128)(2,1)S(1)}, bf16[192,128]{1,0:T(8,128)(2,1)S(1)}, u32[]{:S(2)}, u32[]{:S(2)}) collective-permute-start(bf16[192,128]{1,0:T(8,128)(2,1)S(1)} %get-tuple-element.117), channel_id=1, source_target_pairs={{0,2},{1,3},{2,0},{3,1},{4,6},{5,7},{6,4},{7,5},{8,10},{9,11},{10,... | collective-permute-start | bytes 147464 | tf_op jit(solution)/shard_map/ppermute | solution.py:147
  199.6 15.6 %collective-permute-start.27 = (bf16[192,512]{1,0:T(8,128)(2,1)S(1)}, bf16[192,512]{1,0:T(8,128)(2,1)S(1)}, u32[]{:S(2)}, u32[]{:S(2)}) collective-permute-start(bf16[192,512]{1,0:T(8,128)(2,1)S(1)} %get-tuple-element.105), channel_id=1, source_target_pairs={{0,2},{1,3},{2,0},{3,1},{4,6},{5,7},{6,4},{7,5},{8,10},{9,11},{10,... | collective-permute-start | bytes 589832 | tf_op jit(solution)/shard_map/ppermute | solution.py:147
  202.0 13.2 %collective-permute-start.26 = (bf16[192,512]{1,0:T(8,128)(2,1)S(1)}, bf16[192,512]{1,0:T(8,128)(2,1)S(1)}, u32[]{:S(2)}, u32[]{:S(2)}) collective-permute-start(bf16[192,512]{1,0:T(8,128)(2,1)S(1)} %get-tuple-element.103), channel_id=1, source_target_pairs={{0,1},{1,2},{2,3},{3,0},{4,5},{5,6},{6,7},{7,4},{8,9},{9,10},{10,1... | collective-permute-start | bytes 589832 | tf_op jit(solution)/shard_map/ppermute | solution.py:147
  203.1 26.7 %collective-permute-start.48 = (bf16[384,768]{1,0:T(8,128)(2,1)S(1)}, bf16[384,768]{1,0:T(8,128)(2,1)S(1)}, u32[]{:S(2)}, u32[]{:S(2)}) collective-permute-start(bf16[384,768]{1,0:T(8,128)(2,1)S(1)} %copy-done.19), channel_id=1, source_target_pairs={{0,4},{4,0},{8,12},{12,8},{1,5},{5,1},{9,13},{13,9},{2,6},{6,2},{1... | collective-permute-start | bytes 1769480 | tf_op jit(solution)/shard_map/ppermute | solution.py:143
  204.2 13.5 %collective-permute-start.22 = (bf16[768,128]{1,0:T(8,128)(2,1)}, bf16[768,128]{1,0:T(8,128)(2,1)S(1)}, u32[]{:S(2)}, u32[]{:S(2)}) collective-permute-start(bf16[768,128]{1,0:T(8,128)(2,1)} %get-tuple-element.100), channel_id=1, source_target_pairs={{0,3},{1,0},{2,1},{3,2},{4,7},{5,4},{6,5},{7,6},{8,11},{9,8},{10,9... | collective-permute-start | bytes 589832 | tf_op jit(solution)/shard_map/ppermute | solution.py:147
  215.2 18.5 %collective-permute-start.34 = (bf16[384,576]{0,1:T(8,128)(2,1)}, bf16[384,576]{0,1:T(8,128)(2,1)S(1)}, u32[]{:S(2)}, u32[]{:S(2)}) collective-permute-start(bf16[384,576]{0,1:T(8,128)(2,1)} %slice.197), channel_id=1, source_target_pairs={{0,4},{4,0},{8,12},{12,8},{1,5},{5,1},{9,13},{13,9},{2,6},{6,2},{1... | collective-permute-start | bytes 1327112 | tf_op jit(solution)/shard_map/ppermute | solution.py:143
  228.3 10.2 %collective-permute-start.46 = (bf16[192,768]{1,0:T(8,128)(2,1)S(1)}, bf16[192,768]{1,0:T(8,128)(2,1)S(1)}, u32[]{:S(2)}, u32[]{:S(2)}) collective-permute-start(bf16[192,768]{1,0:T(8,128)(2,1)S(1)} %slice.199), channel_id=1, source_target_pairs={{0,8},{4,12},{8,0},{12,4},{1,9},{5,13},{9,1},{13,5},{2,10},{6,14},... | collective-permute-start | bytes 884744 | tf_op jit(solution)/shard_map/ppermute | solution.py:143
  230.0 20.3 %collective-permute-start.49 = (bf16[192,768]{1,0:T(8,128)(2,1)S(1)}, bf16[192,768]{1,0:T(8,128)(2,1)S(1)}, u32[]{:S(2)}, u32[]{:S(2)}) collective-permute-start(bf16[192,768]{1,0:T(8,128)(2,1)S(1)} %slice.198), channel_id=1, source_target_pairs={{0,8},{4,12},{8,0},{12,4},{1,9},{5,13},{9,1},{13,5},{2,10},{6,14},... | collective-permute-start | bytes 884744 | tf_op jit(solution)/shard_map/ppermute | solution.py:143
  234.0 14.7 %collective-permute-start.35 = (bf16[192,576]{0,1:T(8,128)(2,1)S(1)}, bf16[192,576]{0,1:T(8,128)(2,1)S(1)}, u32[]{:S(2)}, u32[]{:S(2)}) collective-permute-start(bf16[192,576]{0,1:T(8,128)(2,1)S(1)} %slice.200), channel_id=1, source_target_pairs={{0,8},{4,12},{8,0},{12,4},{1,9},{5,13},{9,1},{13,5},{2,10},{6,14},... | collective-permute-start | bytes 663560 | tf_op jit(solution)/shard_map/ppermute | solution.py:143
  239.3 20.4 %collective-permute-start.47 = (bf16[192,768]{1,0:T(8,128)(2,1)}, bf16[192,768]{1,0:T(8,128)(2,1)}, u32[]{:S(2)}, u32[]{:S(2)}) collective-permute-start(bf16[192,768]{1,0:T(8,128)(2,1)} %fusion.16), channel_id=1, source_target_pairs={{0,16},{16,0},{1,17},{17,1},{2,18},{18,2},{3,19},{19,3},{4,20},{20... | collective-permute-start | bytes 884744 | tf_op jit(solution)/shard_map/ppermute | solution.py:143
  248.7 9.9 %collective-permute-start.36 = (bf16[192,576]{0,1:T(8,128)(2,1)S(1)}, bf16[192,576]{0,1:T(8,128)(2,1)S(1)}, u32[]{:S(2)}, u32[]{:S(2)}) collective-permute-start(bf16[192,576]{0,1:T(8,128)(2,1)S(1)} %fusion.15), channel_id=1, source_target_pairs={{0,16},{16,0},{1,17},{17,1},{2,18},{18,2},{3,19},{19,3},{4,20},{20... | collective-permute-start | bytes 663560 | tf_op jit(solution)/shard_map/ppermute | solution.py:143
  251.0 10.8 %collective-permute-start.50 = (bf16[192,768]{1,0:T(8,128)(2,1)}, bf16[192,768]{1,0:T(8,128)(2,1)}, u32[]{:S(2)}, u32[]{:S(2)}) collective-permute-start(bf16[192,768]{1,0:T(8,128)(2,1)} %fusion.17), channel_id=1, source_target_pairs={{0,16},{16,0},{1,17},{17,1},{2,18},{18,2},{3,19},{19,3},{4,20},{20... | collective-permute-start | bytes 884744 | tf_op jit(solution)/shard_map/ppermute | solution.py:143
  (62 other events, 585.0 us)

commit v2 on v1

--- a/solution.py
+++ b/solution.py
@@ -207,20 +207,6 @@
             pieces = [take(values, place(block) * feat, feat, 0) for block in range(n_rows)]
             return jnp.concatenate(pieces, axis=0)
 
-        def rows_whole(shard):
-            for bit in row_bits:
-                shard = jnp.concatenate([shard, swap(shard, "rows", n_rows, bit)], axis=0)
-            return shard
-
-        def rows_reduce(grad):
-            for bit in row_bits[::-1]:
-                half = grad.shape[0] // 2
-                sent = swap(grad[half:].astype(BF16), "rows", n_rows, bit)
-                grad = grad[:half] + sent.astype(F32)
-            for bit in bits_of(n_dp):
-                grad = grad + swap(grad.astype(BF16), "dp", n_dp, bit).astype(F32)
-            return grad
-
         def col_blocks(own, start_of):
             whole = jnp.zeros((own.shape[0] * n_cols,) + own.shape[1:], own.dtype)
             whole = put(whole, own, start_of(at_col), 0)
@@ -234,21 +220,56 @@
                 got.append((shift(piece_for(col_of(step)), "cols", n_cols, step), col_of(-step)))
             return got
 
+        def col_halving(piece_for):
+            bits = bits_of(n_cols)
+            held = [at_col ^ value for value in range(n_cols)]
+            held = [piece_for(col) for col in held]
+            for bit in bits:
+                keep = [held[at] for at in range(len(held)) if not at & 1]
+                give = [held[at] for at in range(len(held)) if at & 1]
+                got = swap(jnp.concatenate(give, axis=0).astype(BF16), "cols", n_cols, bit)
+                got = jnp.split(got, len(give), axis=0)
+                held = [mine.astype(F32) + theirs.astype(F32) for mine, theirs in zip(keep, got)]
+            return held[0]
+
+        def after(value, *others):
+            return lax.optimization_barrier((value,) + others)[0]
+
+        def split_three(values):
+            high = lax.reduce_precision(values, 8, 7)
+            middle = lax.reduce_precision(values - high, 8, 7)
+            low = values - high - middle
+            return [part_of.astype(BF16) for part_of in (high, middle, low)]
+
+        n_qkv = qkv_weight.shape[1]
+        n_hid = up_weight.shape[1]
+        pair = jnp.concatenate([up_weight, down_weight], axis=1)
+        if n_rows > 1:
+            qkv_half = jnp.concatenate([qkv_weight, swap(qkv_weight, "rows", n_rows, row_bits[0])], axis=0)
+            pair_half = jnp.concatenate([pair, swap(pair, "rows", n_rows, row_bits[0])], axis=0)
+        norms = jnp.stack([first_gain, first_bias, mix_bias, second_gain, second_bias], axis=1)
+        norms = jnp.concatenate(split_three(norms), axis=1)
         tok_whole = lax.all_gather(tokens, "cols", axis=0, tiled=True)
-        qkv_rel = rows_whole(qkv_weight)
-        mix_cols = col_blocks(mix_weight, lambda col: col * feat)
-        mix_rel = rows_whole(mix_cols.T)
-        up_rel = rows_whole(up_weight)
-        down_rel = rows_whole(down_weight)
-        cot_rel = col_blocks(cotangent, lambda col: place(col) * feat)
+        packed = after(jnp.concatenate([mix_weight, norms], axis=1), tok_whole)
+        packed = lax.all_gather(packed, "cols", axis=0, tiled=True)
+        mix_cols = packed[:, :feat].T
+        norms = packed[:, feat:].astype(F32)
+        n_norm = norms.shape[1] // 3
+        norms = to_rel(norms[:, :n_norm] + norms[:, n_norm : 2 * n_norm] + norms[:, 2 * n_norm :])
+        gain_one, bias_one, bias_mix, gain_two, bias_two = [norms[:, k : k + 1] for k in range(n_norm)]
+
+        def rest_whole(half, bits):
+            for bit in bits:
+                half = jnp.concatenate([half, swap(half, "rows", n_rows, bit)], axis=0)
+            return half
+
+        qkv_rel = rest_whole(qkv_half, row_bits[1:])
+        mix_half = jnp.concatenate([mix_cols, swap(mix_cols, "rows", n_rows, row_bits[0])], axis=0)
+        cot_rel = col_blocks(after(cotangent, packed), lambda col: place(col) * feat)
 
         seg_row = segment_ids.reshape(1, count)
         seg_col = segment_ids.reshape(count, 1)
         live = seg_row >= 0
-
-        norms = jnp.stack([first_gain, first_bias, mix_bias, second_gain, second_bias], axis=1)
-        norms = to_rel(lax.all_gather(norms, "cols", axis=0, tiled=True))
-        gain_one, bias_one, bias_mix, gain_two, bias_two = [norms[:, k : k + 1] for k in range(5)]
 
         inputs = to_rel(tok_whole).astype(F32)
         mean_one = jnp.mean(inputs, axis=0, keepdims=True)
@@ -260,6 +281,9 @@
         bias_col = jnp.concatenate(
             [qv_bias[:head_rows], jnp.zeros((head_rows,), F32), qv_bias[head_rows:]]
         ).reshape(3 * head_rows, 1)
+        rest = jnp.concatenate([after(pair_half, projected), mix_half], axis=1)
+        rest = rest_whole(rest, row_bits[1:])
+        up_rel, down_rel, mix_rel = rest[:, :n_hid], rest[:, n_hid : 2 * n_hid], rest[:, 2 * n_hid :]
         qkv, attended, totals = attend(projected, bias_col, seg_row, seg_col, heads)
 
         att_whole = lax.all_gather(attended, "cols", axis=0, tiled=True)
@@ -278,13 +302,24 @@
         got = col_exchange(lambda col: take(part_two, col * part, part, 1))
         grad_two = sum(piece.astype(F32) for piece, _ in got)
 
-        grad_down = rows_reduce(mm_nt(grad_final_b, active))
-        grad_up = rows_reduce(mm_nt(normed_two, grad_pre))
-
-        part_out = mm(down_rel, active).astype(BF16)
-        got = col_exchange(lambda col: take(part_out, place(col) * feat, feat, 0))
-        own_hidden = take(hidden, place(at_col) * feat, feat, 0)
-        output = own_hidden + down_bias[:, None] + sum(piece.astype(F32) for piece, _ in got)
+        def reduce_core(grad):
+            half = grad.shape[0] // 2
+            return grad[:half] + swap(grad[half:].astype(BF16), "rows", n_rows, row_bits[-1]).astype(F32)
+
+        def reduce_rest(grad, bits):
+            for bit in bits:
+                half = grad.shape[0] // 2
+                grad = grad[:half] + swap(grad[half:].astype(BF16), "rows", n_rows, bit).astype(F32)
+            return grad
+
+        def reduce_dp(grad):
+            for bit in bits_of(n_dp):
+                grad = grad + swap(grad.astype(BF16), "dp", n_dp, bit).astype(F32)
+            return grad
+
+        grads_ff = jnp.concatenate([mm_nt(grad_final_b, active), mm_nt(normed_two, grad_pre)], axis=1)
+        grads_ff = reduce_core(grads_ff)
+        part_out = mm(down_rel, active)
 
         own_at = at_col * part
         own_hat = (take(hidden, own_at, part, 1) - take(mean_two, own_at, part, 1)) * take(
@@ -302,74 +337,78 @@
         grad_att = jnp.zeros((feat, count), BF16)
         for piece, col in got:
             grad_att = put(grad_att, piece, col * part, 1)
-        got = col_exchange(lambda col: grad_hidden_b)
-        grad_hidden_all = jnp.zeros((width, count), BF16)
-        for piece, col in got:
-            grad_hidden_all = put(grad_hidden_all, piece, col * part, 1)
+
+        grads_ff = reduce_rest(after(grads_ff, grad_att_all), row_bits[::-1][1:])
+        grads_mix = mm_nt(grad_hidden_b, take(att_whole, own_at, part, 1))
+        grads_mix = reduce_core(grads_mix)
+        part_out = after(part_out, grad_att_all)
+        out_sum = col_halving(lambda col: take(part_out, place(col) * feat, feat, 0))
+        own_hidden = take(hidden, place(at_col) * feat, feat, 0)
+        output = own_hidden + down_bias[:, None] + out_sum
 
         grad_proj, qv_sums = attend_back(qkv, attended, grad_att, totals, seg_row, seg_col, heads)
+        grads_ff = reduce_dp(after(grads_ff, grad_proj))
         grad_one_part = mm(qkv_rel, grad_proj)
-        grad_qkv = rows_reduce(mm_nt(normed_one, grad_proj))
-        grad_mix = rows_reduce(mm_nt(grad_hidden_all, attended))
 
         scaled = grad_one_part * gain_one
-        stats = jnp.concatenate(
-            [
-                jnp.sum(scaled, axis=0, keepdims=True),
-                jnp.sum(scaled * hat_one, axis=0, keepdims=True),
-            ],
-            axis=0,
-        )
-        stats = whole_sum(stats, [("cols", n_cols)]) / width
-        grad_one_b = grad_one_part.astype(BF16)
-        got = col_exchange(lambda col: take(grad_one_b, place(col) * feat, feat, 0))
-        grad_one = sum(piece.astype(F32) for piece, _ in got)
-        own_place = place(at_col) * feat
-        hat_own = (tokens.astype(F32) - mean_one) * inv_one
-        grad_tokens = take(grad_hidden_all, own_place, feat, 0).astype(F32) + inv_one * (
-            grad_one * first_gain[:, None] - stats[:1] - hat_own * stats[1:]
-        )
-
-        token_sums = jnp.stack(
+        share = put(jnp.zeros((width, count), F32), grad_hidden, own_at, 1) + inv_one * (
+            scaled
+            - jnp.mean(scaled, axis=0, keepdims=True)
+            - hat_one * jnp.mean(scaled * hat_one, axis=0, keepdims=True)
+        )
+        share_b = share.astype(BF16)
+        got = col_exchange(lambda col: take(share_b, place(col) * feat, feat, 0))
+        grad_tokens = sum(piece.astype(F32) for piece, _ in got)
+
+        grads_mix = reduce_rest(grads_mix, row_bits[::-1][1:])
+        grads_mix = jnp.stack([take(grads_mix, col * feat, feat, 1) for col in range(n_cols)])
+        grads_mix = col_halving(lambda col: lax.dynamic_index_in_dim(grads_mix, col, 0, keepdims=False))
+        grads_qkv = reduce_core(mm_nt(normed_one, grad_proj))
+        grads_qkv = reduce_rest(grads_qkv, row_bits[::-1][1:])
+        grads_last = reduce_dp(jnp.concatenate([grads_qkv, grads_mix], axis=1))
+
+        wide_sums = jnp.stack(
             [
                 jnp.sum(grad_two * own_hat, axis=1),
                 jnp.sum(grad_two, axis=1),
                 jnp.sum(grad_hidden, axis=1),
+                jnp.sum(grad_one_part * hat_one, axis=1),
+                jnp.sum(grad_one_part, axis=1),
             ],
             axis=1,
         )
-        token_sums = whole_sum(to_nat(token_sums), [("cols", n_cols)])
-        token_sums = take(token_sums, at_col * feat, feat, 0)
+        wide_sums = whole_sum(to_nat(wide_sums), [("cols", n_cols)])
+        wide_sums = take(wide_sums, at_col * feat, feat, 0).T.reshape(-1)
         own_final = jnp.where(live, cotangent.astype(F32), 0.0)
-        early = jnp.concatenate(
+        n_qv = 2 * head_rows
+        sums = jnp.concatenate(
             [
-                token_sums.T.reshape(-1),
+                wide_sums,
                 jnp.sum(own_final, axis=1),
                 jnp.sum(grad_pre.astype(F32), axis=1),
+                qv_sums.reshape(-1),
             ]
         )
-        late = jnp.concatenate(
-            [qv_sums.reshape(-1), jnp.sum(grad_one * hat_own, axis=1), jnp.sum(grad_one, axis=1)]
-        )
-        axes = [("rows", n_rows), ("dp", n_dp)]
-        early = whole_sum(early, axes)
-        late = whole_sum(late, axes)
-        n_qv = 2 * head_rows
+        sums = whole_sum(sums, [("rows", n_rows), ("dp", n_dp)])
+        cuts = [0]
+        for length in (feat, feat, feat, feat, feat, feat, n_hid, n_qv):
+            cuts.append(cuts[-1] + length)
+        sums = [sums[at:end] for at, end in zip(cuts[:-1], cuts[1:])]
         return (
             output.astype(BF16),
             grad_tokens,
-            late[n_qv : n_qv + feat],
-            late[n_qv + feat :],
-            grad_qkv,
-            late[:n_qv],
-            grad_mix.T,
-            early[2 * feat : 3 * feat],
-            early[:feat],
-            early[feat : 2 * feat],
-            grad_up,
-            early[4 * feat :],
-            grad_down,
-            early[3 * feat : 4 * feat],
+            sums[3],
+            sums[4],
+            grads_last[:, :n_qkv],
+            sums[7],
+            grads_last[:, n_qkv:].T,
+            sums[2],
+            sums[0],
+            sums[1],
+            grads_ff[:, n_hid:],
+            sums[6],
+            grads_ff[:, :n_hid],
+            sums[5],
         )
 
     return body

time: 265 us -> 256 us (0.966)
  waiting for transfers between devices: 88.9 us -> 50.8 us
  other arithmetic: 17.2 us -> 37.8 us
  local copies, waits for them, and re-layouts: 24.5 us -> 36.5 us
  starting transfers between devices: 52 us -> 40 us
  blocking collectives: 48.4 us -> 53.7 us
    ppermute x21 -> x12, waiting for transfers between devices: 46.6 us -> 25.6 us  [shift(): lax.ppermute(values, axis, [(at, (at + step) % size) for at in range(size)])]
    ppermute x30 -> x22, waiting for transfers between devices: 42.3 us -> 25.2 us  [swap(): return lax.ppermute(values, axis, [(at, at ^ bit) for at in range(size)])]
    ppermute x21 -> x12, starting transfers between devices: 29.2 us -> 15.1 us  [shift(): lax.ppermute(values, axis, [(at, (at + step) % size) for at in range(size)])]
    concatenate x6 -> x8, other arithmetic: 2.94 us -> 13.7 us  [the longest x1 6.46 us: rest_whole(): half = jnp.concatenate([half, swap(half, 'rows', n_rows, bit)], axis=0)]
    all_gather x1, blocking collectives: 17 us -> 20.6 us  [body(): tok_whole = lax.all_gather(tokens, 'cols', axis=0, tiled=True)]
    another operation x3 -> x6, local copies, waits for them, and re-layouts: 0.01 us -> 3.1 us  [body(): jnp.stack([jnp.sum(grad_two * own_hat, axis=1), jnp.sum(grad_two, axis=1)...]
    mul x0 -> x1, other arithmetic: none -> 3.07 us  [body(): inv_one * (scaled - jnp.mean(scaled, axis=0, keepdims=True) - hat_one * j...]
    ppermute x0 -> x2, local copies, waits for them, and re-layouts: none -> 2.67 us  [swap(): return lax.ppermute(values, axis, [(at, at ^ bit) for at in range(size)])]
  transfers between devices with their start and end apart: 51 -> 34, of which waited for: 25 -> 16; matrix products, arithmetic and copies ran while one was open for 16% -> 26% of each run, Pallas kernels for 3% -> 3%
where the time goes in v2:
time: 256 us; the launch traced here: 255 us
  blocking collectives  53.7 us (21%)
  waiting for transfers between devices  50.8 us (20%)
  starting transfers between devices  40 us (16%)
  other arithmetic  37.8 us (15%)
  local copies, waits for them, and re-layouts  36.5 us (14%)
  matrix products  16.8 us (7%)
  between operations  10.6 us (4%)
  Pallas kernels  8.58 us (3%)
    ppermute x12, waiting for transfers between devices, shift(): lax.ppermute(values, axis, [(at, (at + step) % size) for at in range(size)])  25.6 us
    ppermute x22, waiting for transfers between devices, swap(): return lax.ppermute(values, axis, [(at, at ^ bit) for at in range(size)])  25.2 us
    ppermute x22, starting transfers between devices, swap(): return lax.ppermute(values, axis, [(at, at ^ bit) for at in range(size)])  24.9 us
    all_gather x1, blocking collectives, body(): tok_whole = lax.all_gather(tokens, 'cols', axis=0, tiled=True)  20.6 us
    all_gather x1, blocking collectives, body(): att_whole = lax.all_gather(attended, 'cols', axis=0, tiled=True)  18.5 us
    dot_general x12, matrix products, dot(): lax.dot_general(left, right, (dims, ((), ())), preferred_element_type=F32)  16.8 us
    ppermute x12, starting transfers between devices, shift(): lax.ppermute(values, axis, [(at, (at + step) % size) for at in range(size)])  15.1 us
    all_gather x1, blocking collectives, body(): packed = lax.all_gather(packed, 'cols', axis=0, tiled=True)  14.5 us
  transfers between devices with their start and end apart: 34, of which 16 were waited for; matrix products, arithmetic and copies ran while one was open for 26% of the time, Pallas kernels for 3%

profile of v2, /device:TPU:0, one launch (start us, length us, event | category | flops | bytes accessed | tf_op | source)
XLA Modules:
  0.0 254.7 jit_solution(14417510862356323736)
XLA Ops:
  0.7 3.1 %collective-permute-start.1 = (bf16[192,576]{1,0:T(8,128)(2,1)}, bf16[192,576]{1,0:T(8,128)(2,1)}, u32[]{:S(2)}, u32[]{:S(2)}) collective-permute-start(bf16[192,576]{1,0:T(8,128)(2,1)} %param.20), channel_id=1, source_target_pairs={{0,8},{4,12},{8,0},{12,4},{1,9},{5,13},{9,1},{13,5},{2,10},{6,14},... | collective-permute-start | bytes 663560 | tf_op jit(solution)/shard_map/ppermute | solution.py:143
  7.0 20.6 %all_gather.9 = bf16[768,512]{1,0:T(8,128)(2,1)S(1)} all-gather(bf16[192,512]{1,0:T(8,128)(2,1)} %param.16), channel_id=1, replica_groups=mesh['dp'=2,'rows'=4,'cols'=4] {'cols'}, dimensions={0}, use_global_device_ids=true | all-gather | bytes 983040 | tf_op jit(solution)/shard_map/all_gather | solution.py:252
  27.8 14.5 %all_gather.10 = bf16[768,207]{1,0:T(8,128)(2,1)S(1)} all-gather(bf16[192,207]{1,0:T(8,128)(2,1)S(1)} %pad_maximum_fusion.11), channel_id=1, replica_groups=mesh['dp'=2,'rows'=4,'cols'=4] {'cols'}, dimensions={0}, use_global_device_ids=true | all-gather | bytes 397440 | tf_op jit(solution)/shard_map/all_gather | solution.py:254
  46.5 1.8 pad_maximum_fusion.8
  55.2 1.9 fusion.46.qkv_ref
  74.4 3.0 %collective-permute-done.6 = bf16[192,512]{1,0:T(8,128)(2,1)S(1)} collective-permute-done((bf16[192,512]{1,0:T(8,128)(2,1)S(1)}, bf16[192,512]{1,0:T(8,128)(2,1)S(1)}, u32[]{:S(2)}, u32[]{:S(2)}) %collective-permute-start.6) | collective-permute-done | bytes 196640 | tf_op jit(solution)/shard_map/ppermute | solution.py:147
  77.6 4.5 %attend.1 = (bf16[576,512]{1,0:T(8,128)(2,1)}, bf16[192,512]{1,0:T(8,128)(2,1)}, f32[3,512]{1,0:T(4,128)}) custom-call(f32[576,512]{1,0:T(8,128)} %fusion.46.qkv_ref, f32[576,1]{1,0:T(8,128)} %reshape.163.bias_ref, s32[1,512]{1,0:T(1,128)} %bitcast.56, s32[512,1]{1,0:T(8,128)} %copy.83.col_ref), custom_call_target="tpu_custom_call" | custom-call | tf_op jit(solution)/shard_map/attend/pallas_call | solution.py:77
  82.1 18.5 %all_gather.11 = bf16[768,512]{1,0:T(8,128)(2,1)S(1)} all-gather(bf16[192,512]{1,0:T(8,128)(2,1)} %get-tuple-element.27.att_ref), channel_id=1, replica_groups=mesh['dp'=2,'rows'=4,'cols'=4] {'cols'}, dimensions={0}, use_global_device_ids=true | all-gather | bytes 983040 | tf_op jit(solution)/shard_map/all_gather | solution.py:289
  100.7 6.5 %pad_maximum_fusion = bf16[768,2304]{1,0:T(8,128)(2,1)S(1)} fusion(bf16[384,2304]{1,0:T(8,128)(2,1)} %collective-permute-done.4, bf16[384,768]{1,0:T(8,128)(2,1)S(1)} %copy.81, bf16[384,1536]{1,0:T(8,128)(2,1)S(1)} %pad_maximum_fusion.3), kind=kLoop, calls=%fused_computation.2 | loop fusion | flops 10616832 | bytes 7077888 | tf_op jit(solution)/shard_map/concatenate | solution.py:263
  109.3 2.2 convert_reduce_fusion.1
  114.7 3.7 %collective-permute-start.10 = (bf16[768,128]{1,0:T(8,128)(2,1)S(1)}, bf16[768,128]{1,0:T(8,128)(2,1)S(1)}, u32[]{:S(2)}, u32[]{:S(2)}) collective-permute-start(bf16[768,128]{1,0:T(8,128)(2,1)S(1)} %get-tuple-element.139), channel_id=1, source_target_pairs={{0,3},{1,0},{2,1},{3,2},{4,7},{5,4},{6,5},{7,6},{8,11},{9,8},{10,9... | collective-permute-start | bytes 589832 | tf_op jit(solution)/shard_map/ppermute | solution.py:147
  120.6 3.7 %collective-permute-done.8 = bf16[768,128]{1,0:T(8,128)(2,1)S(1)} collective-permute-done((bf16[768,128]{1,0:T(8,128)(2,1)S(1)}, bf16[768,128]{1,0:T(8,128)(2,1)S(1)}, u32[]{:S(2)}, u32[]{:S(2)}) %collective-permute-start.8) | collective-permute-done | bytes 196640 | tf_op jit(solution)/shard_map/ppermute | solution.py:147
  124.3 8.1 %collective-permute-done.9 = bf16[768,128]{1,0:T(8,128)(2,1)S(1)} collective-permute-done((bf16[768,128]{1,0:T(8,128)(2,1)S(1)}, bf16[768,128]{1,0:T(8,128)(2,1)S(1)}, u32[]{:S(2)}, u32[]{:S(2)}) %collective-permute-start.9) | collective-permute-done | bytes 196640 | tf_op jit(solution)/shard_map/ppermute | solution.py:147
  138.0 3.9 %collective-permute-start.15 = (bf16[192,128]{1,0:T(8,128)(2,1)S(1)}, bf16[192,128]{1,0:T(8,128)(2,1)S(1)}, u32[]{:S(2)}, u32[]{:S(2)}) collective-permute-start(bf16[192,128]{1,0:T(8,128)(2,1)S(1)} %get-tuple-element.149), channel_id=1, source_target_pairs={{0,3},{1,0},{2,1},{3,2},{4,7},{5,4},{6,5},{7,6},{8,11},{9,8},{10,9... | collective-permute-start | bytes 147464 | tf_op jit(solution)/shard_map/ppermute | solution.py:147
  143.6 3.4 %collective-permute-done.14 = bf16[192,128]{1,0:T(8,128)(2,1)S(1)} collective-permute-done((bf16[192,128]{1,0:T(8,128)(2,1)S(1)}, bf16[192,128]{1,0:T(8,128)(2,1)S(1)}, u32[]{:S(2)}, u32[]{:S(2)}) %collective-permute-start.14) | collective-permute-done | bytes 49184 | tf_op jit(solution)/shard_map/ppermute | solution.py:147
  148.2 4.1 %attend_back.1 = (bf16[576,512]{1,0:T(8,128)(2,1)}, f32[384,1]{1,0:T(8,128)}) custom-call(bf16[576,512]{1,0:T(8,128)(2,1)} %get-tuple-element.30.qkv_ref, bf16[192,512]{1,0:T(8,128)(2,1)} %get-tuple-element.27.att_ref, bf16[192,512]{1,0:T(8,128)(2,1)} %constant_dynamic-update-slice_fusion.grad_ref, f32[3,512]{1,0:T(4,128)} %get-tuple-element.31.total_ref, ...), custom_call_target="tpu_custom_call" | custom-call | tf_op jit(solution)/shard_map/attend_back/pallas_call | solution.py:124
  152.3 4.1 %fusion.20 = (f32[768]{0:T(1024)S(1)}, f32[512]{0:T(512)S(1)}, f32[512]{0:T(512)}, f32[768]{0:T(1024)S(1)}, f32[768,512]{1,0:T(8,128)}) fusion(f32[512]{0:T(512)} %copy-done.32, f32[512]{0:T(512)} %copy-done.31, bf16[192,512]{1,0:T(8,128)(2,1)S(1)} %copy-done.13, bf16[192,512]{1,0:T(8,128)(2,1)S(1)} %copy-done.15, bf16[192,512]{1,0:T(8,128)(2,1)S(1)} %copy-done.17, ...), kind=kOutput, calls=%fused_computation.31 | convolution fusion | flops 459666944 | bytes 3851264 | tf_op jit(solution)/shard_map/dot_general | solution.py:22
  161.1 3.1 %collective-permute-done.19 = f32[768,5]{0,1:T(8,128)S(1)} collective-permute-done((f32[768,5]{0,1:T(8,128)S(1)}, f32[768,5]{0,1:T(8,128)S(1)}, u32[]{:S(2)}, u32[]{:S(2)}) %collective-permute-start.19) | collective-permute-done | bytes 15392 | tf_op jit(solution)/shard_map/ppermute | solution.py:143
  165.5 3.1 %fusion.19 = f32[768,512]{1,0:T(8,128)} fusion(f32[768,512]{1,0:T(8,128)} %get-tuple-element.187, f32[512]{0:T(512)} %broadcast_multiply_fusion, f32[512]{0:T(512)S(1)} %broadcast_multiply_fusion.1, f32[768]{0:T(1024)S(1)} %get-tuple-element.121, f32[512]{0:T(512)} %copy-done.32, f32[512]{0:T(512)} %copy-done.31, bf16[192,512]{1,0:T(8,128)(2,1)S(1)} %copy-done.13, ...), kind=kLoop, calls=%fused_computation.30 | loop fusion | flops 5898240 | bytes 3943424 | tf_op jit(solution)/shard_map/mul | solution.py:354
  172.5 2.0 fusion.44
  176.3 1.9 collective-permute-done.22
  180.1 3.5 %collective-permute-start.18 = (bf16[192,512]{1,0:T(8,128)(2,1)S(1)}, bf16[192,512]{1,0:T(8,128)(2,1)S(1)}, u32[]{:S(2)}, u32[]{:S(2)}) collective-permute-start(bf16[192,512]{1,0:T(8,128)(2,1)S(1)} %get-tuple-element.136), channel_id=1, source_target_pairs={{0,3},{1,0},{2,1},{3,2},{4,7},{5,4},{6,5},{7,6},{8,11},{9,8},{10,9... | collective-permute-start | bytes 589832 | tf_op jit(solution)/shard_map/ppermute | solution.py:147
  186.2 3.2 %collective-permute-done.16 = bf16[192,512]{1,0:T(8,128)(2,1)S(1)} collective-permute-done((bf16[192,512]{1,0:T(8,128)(2,1)S(1)}, bf16[192,512]{1,0:T(8,128)(2,1)S(1)}, u32[]{:S(2)}, u32[]{:S(2)}) %collective-permute-start.16) | collective-permute-done | bytes 196640 | tf_op jit(solution)/shard_map/ppermute | solution.py:147
  189.4 7.1 %collective-permute-start.11 = (bf16[384,512]{1,0:T(8,128)(2,1)S(1)}, bf16[384,512]{1,0:T(8,128)(2,1)S(1)}, u32[]{:S(2)}, u32[]{:S(2)}) collective-permute-start(bf16[384,512]{1,0:T(8,128)(2,1)S(1)} %copy-done.23), channel_id=1, source_target_pairs={{0,1},{1,0},{2,3},{3,2},{4,5},{5,4},{6,7},{7,6},{8,9},{9,8},{10,11... | collective-permute-start | bytes 1179656 | tf_op jit(solution)/shard_map/ppermute | solution.py:143
  196.5 3.6 %collective-permute-done.17 = bf16[192,512]{1,0:T(8,128)(2,1)S(1)} collective-permute-done((bf16[192,512]{1,0:T(8,128)(2,1)S(1)}, bf16[192,512]{1,0:T(8,128)(2,1)S(1)}, u32[]{:S(2)}, u32[]{:S(2)}) %collective-permute-start.17) | collective-permute-done | bytes 196640 | tf_op jit(solution)/shard_map/ppermute | solution.py:147
  205.4 2.0 collective-permute-start.12
  208.5 2.1 collective-permute-start.25
  210.7 3.7 %collective-permute-done.27 = bf16[192,768]{0,1:T(8,128)(2,1)S(1)} collective-permute-done((bf16[192,768]{0,1:T(8,128)(2,1)S(1)}, bf16[192,768]{0,1:T(8,128)(2,1)S(1)}, u32[]{:S(2)}, u32[]{:S(2)}) %collective-permute-start.27) | collective-permute-done | bytes 294944 | tf_op jit(solution)/shard_map/ppermute | solution.py:143
  224.4 4.6 %collective-permute-done.29 = bf16[192,192]{0,1:T(8,128)(2,1)S(1)} collective-permute-done((bf16[192,192]{0,1:T(8,128)(2,1)S(1)}, bf16[192,192]{0,1:T(8,128)(2,1)S(1)}, u32[]{:S(2)}, u32[]{:S(2)}) %collective-permute-start.29) | collective-permute-done | bytes 73760 | tf_op jit(solution)/shard_map/ppermute | solution.py:143
  230.4 3.9 %collective-permute-done.32 = bf16[192,1536]{1,0:T(8,128)(2,1)} collective-permute-done((bf16[192,1536]{1,0:T(8,128)(2,1)}, bf16[192,1536]{1,0:T(8,128)(2,1)}, u32[]{:S(2)}, u32[]{:S(2)}) %collective-permute-start.32) | collective-permute-done | bytes 589856 | tf_op jit(solution)/shard_map/ppermute | solution.py:143
  238.9 2.0 add_convert_fusion.1
  243.7 7.3 %collective-permute-done.33 = bf16[192,1536]{1,0:T(8,128)(2,1)} collective-permute-done((bf16[192,1536]{1,0:T(8,128)(2,1)}, bf16[192,1536]{1,0:T(8,128)(2,1)}, u32[]{:S(2)}, u32[]{:S(2)}) %collective-permute-start.33) | collective-permute-done | bytes 589856 | tf_op jit(solution)/shard_map/ppermute | solution.py:143
  (245 shorter events, 83.5 us)
Async XLA Ops:
  0.7 45.8 %collective-permute-start.1 = (bf16[192,576]{1,0:T(8,128)(2,1)}, bf16[192,576]{1,0:T(8,128)(2,1)}, u32[]{:S(2)}, u32[]{:S(2)}) collective-permute-start(bf16[192,576]{1,0:T(8,128)(2,1)} %param.20), channel_id=1, source_target_pairs={{0,8},{4,12},{8,0},{12,4},{1,9},{5,13},{9,1},{13,5},{2,10},{6,14},... | collective-permute-start | bytes 663560 | tf_op jit(solution)/shard_map/ppermute | solution.py:143
  5.7 46.0 %collective-permute-start = (bf16[192,1536]{1,0:T(8,128)(2,1)S(1)}, bf16[192,1536]{1,0:T(8,128)(2,1)}, u32[]{:S(2)}, u32[]{:S(2)}) collective-permute-start(bf16[192,1536]{1,0:T(8,128)(2,1)S(1)} %constant_dynamic-update-slice_fusion.7), channel_id=1, source_target_pairs={{0,8},{4,12},{8,0},{12,4},{1,9},{5,13},{9,1},{13,5},{2,10},{6,14},... | collective-permute-start | bytes 1769480 | tf_op jit(solution)/shard_map/ppermute | solution.py:143
  42.3 7.9 %collective-permute-start.3 = (bf16[192,768]{0,1:T(8,128)(2,1)S(1)}, bf16[192,768]{0,1:T(8,128)(2,1)}, u32[]{:S(2)}, u32[]{:S(2)}) collective-permute-start(bf16[192,768]{0,1:T(8,128)(2,1)S(1)} %slice_bitcast_fusion), channel_id=1, source_target_pairs={{0,8},{4,12},{8,0},{12,4},{1,9},{5,13},{9,1},{13,5},{2,10},{6,14},... | collective-permute-start | bytes 884744 | tf_op jit(solution)/shard_map/ppermute | solution.py:143
  48.2 4.7 %collective-permute-start.2 = (bf16[384,576]{1,0:T(8,128)(2,1)}, bf16[384,576]{1,0:T(8,128)(2,1)}, u32[]{:S(2)}, u32[]{:S(2)}) collective-permute-start(bf16[384,576]{1,0:T(8,128)(2,1)} %pad_maximum_fusion.8), channel_id=1, source_target_pairs={{0,4},{4,0},{8,12},{12,8},{1,5},{5,1},{9,13},{13,9},{2,6},{6,2},{1... | collective-permute-start | bytes 1327112 | tf_op jit(solution)/shard_map/ppermute | solution.py:143
  58.4 42.2 %collective-permute-start.4 = (bf16[384,2304]{1,0:T(8,128)(2,1)}, bf16[384,2304]{1,0:T(8,128)(2,1)}, u32[]{:S(2)}, u32[]{:S(2)}) collective-permute-start(bf16[384,2304]{1,0:T(8,128)(2,1)} %pad_maximum_fusion.2), channel_id=1, source_target_pairs={{0,4},{4,0},{8,12},{12,8},{1,5},{5,1},{9,13},{13,9},{2,6},{6,2},{1... | collective-permute-start | bytes 5308424 | tf_op jit(solution)/shard_map/ppermute | solution.py:143
  58.6 18.9 %collective-permute-start.7 = (bf16[192,512]{1,0:T(8,128)(2,1)S(1)}, bf16[192,512]{1,0:T(8,128)(2,1)S(1)}, u32[]{:S(2)}, u32[]{:S(2)}) collective-permute-start(bf16[192,512]{1,0:T(8,128)(2,1)S(1)} %copy-done.22), channel_id=1, source_target_pairs={{0,3},{1,0},{2,1},{3,2},{4,7},{5,4},{6,5},{7,6},{8,11},{9,8},{10,9... | collective-permute-start | bytes 589832 | tf_op jit(solution)/shard_map/ppermute | solution.py:147
  60.2 17.3 %collective-permute-start.6 = (bf16[192,512]{1,0:T(8,128)(2,1)S(1)}, bf16[192,512]{1,0:T(8,128)(2,1)S(1)}, u32[]{:S(2)}, u32[]{:S(2)}) collective-permute-start(bf16[192,512]{1,0:T(8,128)(2,1)S(1)} %copy-done.22), channel_id=1, source_target_pairs={{0,2},{1,3},{2,0},{3,1},{4,6},{5,7},{6,4},{7,5},{8,10},{9,11},{10,... | collective-permute-start | bytes 589832 | tf_op jit(solution)/shard_map/ppermute | solution.py:147
  60.2 14.2 %collective-permute-start.5 = (bf16[192,512]{1,0:T(8,128)(2,1)S(1)}, bf16[192,512]{1,0:T(8,128)(2,1)S(1)}, u32[]{:S(2)}, u32[]{:S(2)}) collective-permute-start(bf16[192,512]{1,0:T(8,128)(2,1)S(1)} %copy-done.22), channel_id=1, source_target_pairs={{0,1},{1,2},{2,3},{3,0},{4,5},{5,6},{6,7},{7,4},{8,9},{9,10},{10,1... | collective-permute-start | bytes 589832 | tf_op jit(solution)/shard_map/ppermute | solution.py:147
  114.5 9.7 %collective-permute-start.8 = (bf16[768,128]{1,0:T(8,128)(2,1)S(1)}, bf16[768,128]{1,0:T(8,128)(2,1)S(1)}, u32[]{:S(2)}, u32[]{:S(2)}) collective-permute-start(bf16[768,128]{1,0:T(8,128)(2,1)S(1)} %get-tuple-element.138), channel_id=1, source_target_pairs={{0,1},{1,2},{2,3},{3,0},{4,5},{5,6},{6,7},{7,4},{8,9},{9,10},{10,1... | collective-permute-start | bytes 589832 | tf_op jit(solution)/shard_map/ppermute | solution.py:147
  114.7 9.6 %collective-permute-start.10 = (bf16[768,128]{1,0:T(8,128)(2,1)S(1)}, bf16[768,128]{1,0:T(8,128)(2,1)S(1)}, u32[]{:S(2)}, u32[]{:S(2)}) collective-permute-start(bf16[768,128]{1,0:T(8,128)(2,1)S(1)} %get-tuple-element.139), channel_id=1, source_target_pairs={{0,3},{1,0},{2,1},{3,2},{4,7},{5,4},{6,5},{7,6},{8,11},{9,8},{10,9... | collective-permute-start | bytes 589832 | tf_op jit(solution)/shard_map/ppermute | solution.py:147
  118.4 13.9 %collective-permute-start.9 = (bf16[768,128]{1,0:T(8,128)(2,1)S(1)}, bf16[768,128]{1,0:T(8,128)(2,1)S(1)}, u32[]{:S(2)}, u32[]{:S(2)}) collective-permute-start(bf16[768,128]{1,0:T(8,128)(2,1)S(1)} %get-tuple-element.140), channel_id=1, source_target_pairs={{0,2},{1,3},{2,0},{3,1},{4,6},{5,7},{6,4},{7,5},{8,10},{9,11},{10,... | collective-permute-start | bytes 589832 | tf_op jit(solution)/shard_map/ppermute | solution.py:147
  119.6 95.8 %collective-permute-start.31 = (bf16[384,1536]{0,1:T(8,128)(2,1)}, bf16[384,1536]{0,1:T(8,128)(2,1)}, u32[]{:S(2)}, u32[]{:S(2)}) collective-permute-start(bf16[384,1536]{0,1:T(8,128)(2,1)} %fusion.2), channel_id=1, source_target_pairs={{0,4},{4,0},{8,12},{12,8},{1,5},{5,1},{9,13},{13,9},{2,6},{6,2},{1... | collective-permute-start | bytes 3538952 | tf_op jit(solution)/shard_map/ppermute | solution.py:143
  136.6 6.4 %collective-permute-start.13 = (bf16[192,128]{1,0:T(8,128)(2,1)S(1)}, bf16[192,128]{1,0:T(8,128)(2,1)S(1)}, u32[]{:S(2)}, u32[]{:S(2)}) collective-permute-start(bf16[192,128]{1,0:T(8,128)(2,1)S(1)} %get-tuple-element.151), channel_id=1, source_target_pairs={{0,1},{1,2},{2,3},{3,0},{4,5},{5,6},{6,7},{7,4},{8,9},{9,10},{10,1... | collective-permute-start | bytes 147464 | tf_op jit(solution)/shard_map/ppermute | solution.py:147
  138.0 9.5 %collective-permute-start.15 = (bf16[192,128]{1,0:T(8,128)(2,1)S(1)}, bf16[192,128]{1,0:T(8,128)(2,1)S(1)}, u32[]{:S(2)}, u32[]{:S(2)}) collective-permute-start(bf16[192,128]{1,0:T(8,128)(2,1)S(1)} %get-tuple-element.149), channel_id=1, source_target_pairs={{0,3},{1,0},{2,1},{3,2},{4,7},{5,4},{6,5},{7,6},{8,11},{9,8},{10,9... | collective-permute-start | bytes 147464 | tf_op jit(solution)/shard_map/ppermute | solution.py:147
  142.0 5.0 %collective-permute-start.14 = (bf16[192,128]{1,0:T(8,128)(2,1)S(1)}, bf16[192,128]{1,0:T(8,128)(2,1)S(1)}, u32[]{:S(2)}, u32[]{:S(2)}) collective-permute-start(bf16[192,128]{1,0:T(8,128)(2,1)S(1)} %get-tuple-element.150), channel_id=1, source_target_pairs={{0,2},{1,3},{2,0},{3,1},{4,6},{5,7},{6,4},{7,5},{8,10},{9,11},{10,... | collective-permute-start | bytes 147464 | tf_op jit(solution)/shard_map/ppermute | solution.py:147
  142.9 58.1 %collective-permute-start.26 = (bf16[384,768]{0,1:T(8,128)(2,1)}, bf16[384,768]{0,1:T(8,128)(2,1)}, u32[]{:S(2)}, u32[]{:S(2)}) collective-permute-start(bf16[384,768]{0,1:T(8,128)(2,1)} %slice.232), channel_id=1, source_target_pairs={{0,4},{4,0},{8,12},{12,8},{1,5},{5,1},{9,13},{13,9},{2,6},{6,2},{1... | collective-permute-start | bytes 1769480 | tf_op jit(solution)/shard_map/ppermute | solution.py:143
  160.4 3.8 %collective-permute-start.19 = (f32[768,5]{0,1:T(8,128)S(1)}, f32[768,5]{0,1:T(8,128)S(1)}, u32[]{:S(2)}, u32[]{:S(2)}) collective-permute-start(f32[768,5]{0,1:T(8,128)S(1)} %pad_maximum_fusion.12), channel_id=1, source_target_pairs={{0,1},{1,0},{2,3},{3,2},{4,5},{5,4},{6,7},{7,6},{8,9},{9,8},{10,11... | collective-permute-start | bytes 46088 | tf_op jit(solution)/shard_map/ppermute | solution.py:143
  164.9 5.3 %collective-permute-start.20 = (f32[768,5]{0,1:T(8,128)}, f32[768,5]{0,1:T(8,128)}, u32[]{:S(2)}, u32[]{:S(2)}) collective-permute-start(f32[768,5]{0,1:T(8,128)} %fusion.65), channel_id=1, source_target_pairs={{0,2},{1,3},{2,0},{3,1},{4,6},{5,7},{6,4},{7,5},{8,10},{9,11},{10,... | collective-permute-start | bytes 46088 | tf_op jit(solution)/shard_map/ppermute | solution.py:143
  178.2 5.5 %collective-permute-start.23 = (f32[2304]{0:T(1024)S(1)}, f32[2304]{0:T(1024)S(1)}, u32[]{:S(2)}, u32[]{:S(2)}) collective-permute-start(f32[2304]{0:T(1024)S(1)} %add.485), channel_id=1, source_target_pairs={{0,16},{16,0},{1,17},{17,1},{2,18},{18,2},{3,19},{19,3},{4,20},{20... | collective-permute-start | bytes 27656 | tf_op jit(solution)/shard_map/ppermute | solution.py:143
  179.8 9.7 %collective-permute-start.16 = (bf16[192,512]{1,0:T(8,128)(2,1)S(1)}, bf16[192,512]{1,0:T(8,128)(2,1)S(1)}, u32[]{:S(2)}, u32[]{:S(2)}) collective-permute-start(bf16[192,512]{1,0:T(8,128)(2,1)S(1)} %get-tuple-element.135), channel_id=1, source_target_pairs={{0,1},{1,2},{2,3},{3,0},{4,5},{5,6},{6,7},{7,4},{8,9},{9,10},{10,1... | collective-permute-start | bytes 589832 | tf_op jit(solution)/shard_map/ppermute | solution.py:147
  180.1 16.4 %collective-permute-start.18 = (bf16[192,512]{1,0:T(8,128)(2,1)S(1)}, bf16[192,512]{1,0:T(8,128)(2,1)S(1)}, u32[]{:S(2)}, u32[]{:S(2)}) collective-permute-start(bf16[192,512]{1,0:T(8,128)(2,1)S(1)} %get-tuple-element.136), channel_id=1, source_target_pairs={{0,3},{1,0},{2,1},{3,2},{4,7},{5,4},{6,5},{7,6},{8,11},{9,8},{10,9... | collective-permute-start | bytes 589832 | tf_op jit(solution)/shard_map/ppermute | solution.py:147
  183.7 16.4 %collective-permute-start.17 = (bf16[192,512]{1,0:T(8,128)(2,1)S(1)}, bf16[192,512]{1,0:T(8,128)(2,1)S(1)}, u32[]{:S(2)}, u32[]{:S(2)}) collective-permute-start(bf16[192,512]{1,0:T(8,128)(2,1)S(1)} %get-tuple-element.137), channel_id=1, source_target_pairs={{0,2},{1,3},{2,0},{3,1},{4,6},{5,7},{6,4},{7,5},{8,10},{9,11},{10,... | collective-permute-start | bytes 589832 | tf_op jit(solution)/shard_map/ppermute | solution.py:147
  189.4 14.8 %collective-permute-start.11 = (bf16[384,512]{1,0:T(8,128)(2,1)S(1)}, bf16[384,512]{1,0:T(8,128)(2,1)S(1)}, u32[]{:S(2)}, u32[]{:S(2)}) collective-permute-start(bf16[384,512]{1,0:T(8,128)(2,1)S(1)} %copy-done.23), channel_id=1, source_target_pairs={{0,1},{1,0},{2,3},{3,2},{4,5},{5,4},{6,7},{7,6},{8,9},{9,8},{10,11... | collective-permute-start | bytes 1179656 | tf_op jit(solution)/shard_map/ppermute | solution.py:143
  196.5 10.9 %collective-permute-start.24 = (bf16[384,576]{0,1:T(8,128)(2,1)S(1)}, bf16[384,576]{0,1:T(8,128)(2,1)S(1)}, u32[]{:S(2)}, u32[]{:S(2)}) collective-permute-start(bf16[384,576]{0,1:T(8,128)(2,1)S(1)} %slice.233), channel_id=1, source_target_pairs={{0,4},{4,0},{8,12},{12,8},{1,5},{5,1},{9,13},{13,9},{2,6},{6,2},{1... | collective-permute-start | bytes 1327112 | tf_op jit(solution)/shard_map/ppermute | solution.py:143
  202.3 12.1 %collective-permute-start.27 = (bf16[192,768]{0,1:T(8,128)(2,1)S(1)}, bf16[192,768]{0,1:T(8,128)(2,1)S(1)}, u32[]{:S(2)}, u32[]{:S(2)}) collective-permute-start(bf16[192,768]{0,1:T(8,128)(2,1)S(1)} %slice.234), channel_id=1, source_target_pairs={{0,8},{4,12},{8,0},{12,4},{1,9},{5,13},{9,1},{13,5},{2,10},{6,14},... | collective-permute-start | bytes 884744 | tf_op jit(solution)/shard_map/ppermute | solution.py:143
  205.4 33.5 %collective-permute-start.12 = (bf16[192,512]{1,0:T(8,128)(2,1)S(1)}, bf16[192,512]{1,0:T(8,128)(2,1)}, u32[]{:S(2)}, u32[]{:S(2)}) collective-permute-start(bf16[192,512]{1,0:T(8,128)(2,1)S(1)} %add_convert_fusion.2), channel_id=1, source_target_pairs={{0,2},{1,3},{2,0},{3,1},{4,6},{5,7},{6,4},{7,5},{8,10},{9,11},{10,... | collective-permute-start | bytes 589832 | tf_op jit(solution)/shard_map/ppermute | solution.py:143
  208.5 14.9 %collective-permute-start.25 = (bf16[192,576]{0,1:T(8,128)(2,1)}, bf16[192,576]{0,1:T(8,128)(2,1)}, u32[]{:S(2)}, u32[]{:S(2)}) collective-permute-start(bf16[192,576]{0,1:T(8,128)(2,1)} %slice.235), channel_id=1, source_target_pairs={{0,8},{4,12},{8,0},{12,4},{1,9},{5,13},{9,1},{13,5},{2,10},{6,14},... | collective-permute-start | bytes 663560 | tf_op jit(solution)/shard_map/ppermute | solution.py:143
  215.4 6.9 %collective-permute-start.28 = (bf16[384,192]{0,1:T(8,128)(2,1)}, bf16[384,192]{0,1:T(8,128)(2,1)S(1)}, u32[]{:S(2)}, u32[]{:S(2)}) collective-permute-start(bf16[384,192]{0,1:T(8,128)(2,1)} %pad_maximum_fusion.10), channel_id=1, source_target_pairs={{0,1},{1,0},{2,3},{3,2},{4,5},{5,4},{6,7},{7,6},{8,9},{9,8},{10,11... | collective-permute-start | bytes 442376 | tf_op jit(solution)/shard_map/ppermute | solution.py:143
  220.8 13.5 %collective-permute-start.32 = (bf16[192,1536]{1,0:T(8,128)(2,1)}, bf16[192,1536]{1,0:T(8,128)(2,1)}, u32[]{:S(2)}, u32[]{:S(2)}) collective-permute-start(bf16[192,1536]{1,0:T(8,128)(2,1)} %copy.87), channel_id=1, source_target_pairs={{0,8},{4,12},{8,0},{12,4},{1,9},{5,13},{9,1},{13,5},{2,10},{6,14},... | collective-permute-start | bytes 1769480 | tf_op jit(solution)/shard_map/ppermute | solution.py:143
  222.4 6.6 %collective-permute-start.29 = (bf16[192,192]{0,1:T(8,128)(2,1)S(1)}, bf16[192,192]{0,1:T(8,128)(2,1)S(1)}, u32[]{:S(2)}, u32[]{:S(2)}) collective-permute-start(bf16[192,192]{0,1:T(8,128)(2,1)S(1)} %fusion.31), channel_id=1, source_target_pairs={{0,2},{1,3},{2,0},{3,1},{4,6},{5,7},{6,4},{7,5},{8,10},{9,11},{10,... | collective-permute-start | bytes 221192 | tf_op jit(solution)/shard_map/ppermute | solution.py:143
  229.9 11.1 %collective-permute-start.30 = (bf16[192,768]{0,1:T(8,128)(2,1)}, bf16[192,768]{0,1:T(8,128)(2,1)}, u32[]{:S(2)}, u32[]{:S(2)}) collective-permute-start(bf16[192,768]{0,1:T(8,128)(2,1)} %fusion.30), channel_id=1, source_target_pairs={{0,16},{16,0},{1,17},{17,1},{2,18},{18,2},{3,19},{19,3},{4,20},{20... | collective-permute-start | bytes 884744 | tf_op jit(solution)/shard_map/ppermute | solution.py:143
  238.4 12.6 %collective-permute-start.33 = (bf16[192,1536]{1,0:T(8,128)(2,1)}, bf16[192,1536]{1,0:T(8,128)(2,1)}, u32[]{:S(2)}, u32[]{:S(2)}) collective-permute-start(bf16[192,1536]{1,0:T(8,128)(2,1)} %copy.89), channel_id=1, source_target_pairs={{0,16},{16,0},{1,17},{17,1},{2,18},{18,2},{3,19},{19,3},{4,20},{20... | collective-permute-start | bytes 1769480 | tf_op jit(solution)/shard_map/ppermute | solution.py:143
  (39 other events, 566.7 us)

commit v3 on v1

v3 whole, which is shorter than its diff:
```python
import functools
import math

import jax
import jax.numpy as jnp
from jax import lax
from jax.experimental import pallas as pl
from jax.experimental.pallas import tpu as pltpu
from jax.sharding import PartitionSpec as P

HD = 64
MAXLEN = 256
EPS = 1e-05
NEG = -1e30
ROOT = 0.7978845608028654
CUBIC = 0.044715
F32 = jnp.float32
BF16 = jnp.bfloat16


def dot(left, right, dims):
    return lax.dot_general(left, right, (dims, ((), ())), preferred_element_type=F32)


def mm(left, right):
    return dot(left, right, ((1,), (0,)))


def mm_t(left, right):
    return dot(left, right, ((0,), (0,)))


def mm_nt(left, right):
    return dot(left, right, ((1,), (1,)))


def gelu_both(pre_act):
    inner_arg = ROOT * (pre_act + CUBIC * pre_act * pre_act * pre_act)
    tanh_val = jnp.tanh(inner_arg)
    value = 0.5 * pre_act * (1.0 + tanh_val)
    slope = 0.5 * (1.0 + tanh_val) + 0.5 * pre_act * (1.0 - tanh_val * tanh_val) * ROOT * (
        1.0 + 3.0 * CUBIC * pre_act * pre_act
    )
    return value, slope


def allowed_mask(seg_row, seg_col, width):
    key_pos = lax.broadcasted_iota(jnp.int32, (width, width), 0)
    query_pos = lax.broadcasted_iota(jnp.int32, (width, width), 1)
    same_seg = (seg_col == seg_row) & (seg_row >= 0)
    return (key_pos < query_pos) & same_seg | (key_pos == query_pos)


def block(index, size):
    return pl.ds(pl.multiple_of(index * size, size), size)


def norm_cols(tok_ref, count, which):
    cols = tok_ref[:, count : tok_ref.shape[1]].astype(F32)
    return [cols[:, k : k + 1] + cols[:, k + 5 : k + 6] + cols[:, k + 10 : k + 11] for k in which]


def run(kernel, name, outs, ins, scratch=(), flops=0):
    specs = [pl.BlockSpec(memory_space=pltpu.SMEM)]
    specs += [pl.BlockSpec(memory_space=pltpu.VMEM)] * (len(ins) - 1)
    size = sum(math.prod(value.shape) * value.dtype.itemsize for value in list(ins) + list(outs))
    return pl.pallas_call(
        kernel,
        out_shape=outs,
        in_specs=specs,
        out_specs=[pl.BlockSpec(memory_space=pltpu.VMEM)] * len(outs),
        scratch_shapes=list(scratch),
        name=name,
        cost_estimate=pl.CostEstimate(flops=flops, transcendentals=0, bytes_accessed=size),
    )(*ins)


def shaped(shape, dtype):
    return jax.ShapeDtypeStruct(shape, dtype)


def pack_kernel(here, tok, g1, b1, bm, g2, b2, qv, up, down, seg, packed, qkv_col, up_col, down_col, seg_col):
    feat, count = tok.shape
    rows = jnp.concatenate([ref[...] for ref in (g1, b1, bm, g2, b2)], axis=0)
    high = rows.astype(BF16).astype(F32)
    middle = (rows - high).astype(BF16).astype(F32)
    low = rows - high - middle
    used = 3 * rows.shape[0]
    filler = jnp.zeros((128 - used, feat), F32)
    packed[:, :count] = tok[...]
    packed[:, count:] = jnp.concatenate([high, middle, low, filler], axis=0).T.astype(BF16)

    def column(row):
        return jnp.broadcast_to(row, (128, row.shape[1])).T[:, :1]

    half = qv.shape[1] // 2
    qv_col = column(qv[...])
    qkv_col[:half, :] = qv_col[:half]
    qkv_col[half : 2 * half, :] = jnp.zeros((half, 1), F32)
    qkv_col[2 * half :, :] = qv_col[half:]
    up_col[...] = column(up[...])
    down_col[...] = column(down[...])
    seg_col[...] = column(seg[...].astype(F32)).astype(jnp.int32)


def first_kernel(order, heads, here, tok, w0, w1, w2, w3, bias, row, col, normed, stats, qkv, att, totals, w_all):
    feat = w0.shape[0]
    count = row.shape[1]
    for value, piece in zip(order, (w0, w1, w2, w3)):
        w_all[block(here[0] ^ value, feat), :] = piece[...]
    gain, shift = norm_cols(tok, count, (0, 1))
    values = tok[:, :count].astype(F32)
    mean = jnp.mean(values, axis=0, keepdims=True)
    inv = lax.rsqrt(jnp.mean(values * values, axis=0, keepdims=True) - mean * mean + EPS)
    stats[0:1, :] = mean
    stats[1:2, :] = inv
    normed[...] = ((values - mean) * inv * gain + shift).astype(BF16)
    qkv[...] = (mm_t(w_all[...], normed[...]) + bias[...]).astype(BF16)
    head_rows = heads * HD
    scale = 1.0 / math.sqrt(HD)
    width = min(MAXLEN, count)
    for half in range(count // width):
        cols = pl.ds(half * width, width)
        allowed = allowed_mask(row[:, cols], col[cols, :], width)
        for head in range(heads):
            query = qkv[pl.ds(head * HD, HD), cols]
            keys = qkv[pl.ds(head_rows + head * HD, HD), cols]
            held = qkv[pl.ds(2 * head_rows + head * HD, HD), cols]
            scores = jnp.where(allowed, mm_t(keys, query) * scale, NEG)
            top = jnp.max(scores, axis=0, keepdims=True)
            log_total = top + jnp.log(jnp.sum(jnp.exp(scores - top), axis=0, keepdims=True))
            probs = jnp.exp(scores - log_total).astype(BF16)
            att[pl.ds(head * HD, HD), cols] = mm(held, probs).astype(BF16)
            totals[pl.ds(head, 1), cols] = log_total


def mix_pack_kernel(here, m0, m1, m2, m3, out):
    for step, piece in enumerate((m0, m1, m2, m3)):
        out[block(here[1] ^ step, m0.shape[0]), :] = piece[...]


def middle_kernel(
    order, here, tok, att, m0, m1, m2, m3, u0, u1, u2, u3, d0, d1, d2, d3, c0, c1, c2, c3, row, up_col,
    normed, grad_pre, active, grad_final, p1, p2, p3, own_two, own_hat, own_inv, own_hidden, up_sum, down_all,
    up_all, hidden,
):
    feat, count = c0.shape
    part = own_two.shape[1]
    live = row[...] >= 0
    bias_mix, gain, shift = norm_cols(tok, count, (2, 3, 4))
    for value, piece in zip(order, (u0, u1, u2, u3)):
        up_all[block(here[0] ^ value, feat), :] = piece[...]
    for value, piece in zip(order, (d0, d1, d2, d3)):
        down_all[block(here[0] ^ value, feat), :] = piece[...]
    for step, piece in enumerate((c0, c1, c2, c3)):
        masked = jnp.where(live, piece[...].astype(F32), 0.0)
        grad_final[block(here[1] ^ step, feat), :] = masked.astype(BF16)
    for value, piece in zip(order, (m0, m1, m2, m3)):
        hidden[block(here[0] ^ value, feat), :] = mm_t(piece[...], att[...])
    hidden[...] = hidden[...] + tok[:, :count].astype(F32) + bias_mix
    values = hidden[...]
    mean = jnp.mean(values, axis=0, keepdims=True)
    inv = lax.rsqrt(jnp.mean(values * values, axis=0, keepdims=True) - mean * mean + EPS)
    own_hidden[...] = hidden[block(here[1], feat), :]
    hat = (values - mean) * inv
    normed[...] = (hat * gain + shift).astype(BF16)
    hidden[...] = hat
    own_inv[...] = jnp.broadcast_to(inv, (8, count))
    own_hat[...] = hidden[:, block(here[1], part)]
    value, slope = gelu_both(mm_t(up_all[...], normed[...]) + up_col[...])
    active[...] = value.astype(BF16)
    grad = mm_t(down_all[...], grad_final[...]) * slope
    grad_pre[...] = grad.astype(BF16)
    up_sum[...] = jnp.sum(grad_pre[...].astype(F32), axis=1, keepdims=True)
    hidden[...] = mm(up_all[...], grad_pre[...])
    own_two[...] = hidden[:, block(here[1], part)]
    for step, out in enumerate((p1, p2, p3)):
        out[...] = hidden[:, block(here[1] ^ (step + 1), part)].astype(BF16)


def ff_grads_kernel(order, here, grad_final, active, normed, grad_pre, down_all, send, keep, out_send, out_keep):
    feat = keep.shape[0] // 2
    hid = active.shape[0]
    for at, value in enumerate(order):
        rows = block(here[0] ^ value, feat)
        down = mm_nt(grad_final[rows, :], active[...])
        up = mm_nt(normed[rows, :], grad_pre[...])
        if at < 2:
            keep[pl.ds(at * feat, feat), :hid] = down
            keep[pl.ds(at * feat, feat), hid:] = up
        else:
            send[pl.ds((at - 2) * feat, feat), :hid] = down.astype(BF16)
            send[pl.ds((at - 2) * feat, feat), hid:] = up.astype(BF16)
    for step in range(4):
        out = mm(down_all[block(here[1] ^ step, feat), :], active[...])
        if step % 2:
            out_send[pl.ds(step // 2 * feat, feat), :] = out.astype(BF16)
        else:
            out_keep[pl.ds(step // 2 * feat, feat), :] = out


def second_back_kernel(
    order, here, tok, own_two, r1, r2, r3, own_hat, own_inv, grad_final, m0, m1, m2, m3,
    grad_hidden, grad_hidden_b, a0, a1, a2, a3, sums, all_att,
):
    feat = a0.shape[0]
    part = own_two.shape[1]
    (gain,) = norm_cols(tok, grad_final.shape[1], (3,))
    grad = own_two[...] + r1[...].astype(F32) + r2[...].astype(F32) + r3[...].astype(F32)
    hat = own_hat[...]
    lanes = block(here[1], part)
    inv = own_inv[:, lanes][:1]
    scaled = grad * gain
    out = grad_final[:, lanes].astype(F32) + inv * (
        scaled
        - jnp.mean(scaled, axis=0, keepdims=True)
        - hat * jnp.mean(scaled * hat, axis=0, keepdims=True)
    )
    grad_hidden[...] = out
    grad_hidden_b[...] = out.astype(BF16)
    total = jnp.zeros(all_att.shape, F32)
    for value, piece in zip(order, (m0, m1, m2, m3)):
        total += mm(piece[...], grad_hidden_b[block(here[0] ^ value, feat), :])
    all_att[...] = total.astype(BF16)
    for step, ref in enumerate((a0, a1, a2, a3)):
        ref[...] = all_att[block(here[1] ^ step, feat), :]
    sums[:, 0:1] = jnp.sum(grad * hat, axis=1, keepdims=True)
    sums[:, 1:2] = jnp.sum(grad, axis=1, keepdims=True)
    sums[:, 2:3] = jnp.sum(out, axis=1, keepdims=True)


def mix_grad_kernel(order, here, att, grad_hidden_b, send, keep):
    feat = send.shape[2]
    own = att[:, block(here[1], grad_hidden_b.shape[1])]
    for at, value in enumerate(order):
        grad = mm_nt(own, grad_hidden_b[block(here[0] ^ value, feat), :])
        if at < 2:
            keep[at] = grad
        else:
            send[at - 2] = grad.astype(BF16)


def first_back_kernel(
    order, heads, here, tok, stats, qkv, att, totals, a0, a1, a2, a3, row, col, w0, w1, w2, w3, grad_hidden,
    grad_proj, qv_sum, s0, s1, s2, s3, sums, grad_att, share,
):
    feat, count = att.shape
    part = a0.shape[1]
    head_rows = heads * HD
    scale = 1.0 / math.sqrt(HD)
    for step, piece in enumerate((a0, a1, a2, a3)):
        grad_att[:, block(here[1] ^ step, part)] = piece[...]
    width = min(MAXLEN, count)
    for half in range(count // width):
        cols = pl.ds(half * width, width)
        allowed = allowed_mask(row[:, cols], col[cols, :], width)
        for head in range(heads):
            query = qkv[pl.ds(head * HD, HD), cols]
            keys = qkv[pl.ds(head_rows + head * HD, HD), cols]
            held = qkv[pl.ds(2 * head_rows + head * HD, HD), cols]
            grad = grad_att[pl.ds(head * HD, HD), cols]
            attended = att[pl.ds(head * HD, HD), cols]
            delta = jnp.sum(grad.astype(F32) * attended.astype(F32), axis=0, keepdims=True)
            scores = jnp.where(allowed, mm_t(keys, query) * scale, NEG)
            probs = jnp.exp(scores - totals[pl.ds(head, 1), cols])
            grad_held = mm_nt(grad, probs.astype(BF16))
            grad_probs = mm_t(held, grad)
            grad_scores = (probs * (grad_probs - delta) * scale).astype(BF16)
            grad_query = mm(keys, grad_scores)
            grad_keys = mm_nt(query, grad_scores)
            grad_proj[pl.ds(head * HD, HD), cols] = grad_query.astype(BF16)
            grad_proj[pl.ds(head_rows + head * HD, HD), cols] = grad_keys.astype(BF16)
            grad_proj[pl.ds(2 * head_rows + head * HD, HD), cols] = grad_held.astype(BF16)
            for at, grown in ((head * HD, grad_query), (head_rows + head * HD, grad_held)):
                total = jnp.sum(grown, axis=1, keepdims=True)
                if half:
                    total = total + qv_sum[pl.ds(at, HD), :]
                qv_sum[pl.ds(at, HD), :] = total
    for value, piece in zip(order, (w0, w1, w2, w3)):
        share[block(here[0] ^ value, feat), :] = mm(piece[...], grad_proj[...])
    (gain,) = norm_cols(tok, count, (0,))
    inv = stats[1:2, :]
    hat = (tok[:, :count].astype(F32) - stats[0:1, :]) * inv
    grad = share[...]
    sums[:, 0:1] = jnp.sum(grad * hat, axis=1, keepdims=True)
    sums[:, 1:2] = jnp.sum(grad, axis=1, keepdims=True)
    scaled = grad * gain
    share[...] = inv * (
        scaled
        - jnp.mean(scaled, axis=0, keepdims=True)
        - hat * jnp.mean(scaled * hat, axis=0, keepdims=True)
    )
    share[:, block(here[1], part)] += grad_hidden[...]
    s0[...] = share[block(here[1], feat), :]
    for step, ref in enumerate((s1, s2, s3)):
        ref[...] = share[block(here[1] ^ (step + 1), feat), :].astype(BF16)


def qkv_grads_kernel(order, here, normed, grad_proj, send, keep):
    feat = keep.shape[0] // 2
    for at, value in enumerate(order):
        grad = mm_nt(normed[block(here[0] ^ value, feat), :], grad_proj[...])
        if at < 2:
            keep[pl.ds(at * feat, feat), :] = grad
        else:
            send[pl.ds((at - 2) * feat, feat), :] = grad.astype(BF16)


def sums_kernel(here, second, first, up_sum, qv_sum, cot, row, wide, rest):
    width = second.shape[0]
    feat = cot.shape[0]
    lane = lax.broadcasted_iota(jnp.int32, (width, 128), 1)

    def rows_of(columns):
        total = jnp.zeros((width, 128), F32)
        for at, column in columns:
            total = jnp.where(lane == at, column, total)
        return total.T[:8]

    wide[...] = rows_of([(k, second[:, k : k + 1]) for k in range(3)] + [(3 + k, first[:, k : k + 1]) for k in range(2)])
    down = jnp.sum(jnp.where(row[...] >= 0, cot[...].astype(F32), 0.0), axis=1, keepdims=True)
    down = jnp.concatenate([down, jnp.zeros((width - feat, 1), F32)], axis=0)
    held = jnp.concatenate([qv_sum[...], jnp.zeros((width - qv_sum.shape[0], 1), F32)], axis=0)
    rest[...] = rows_of([(5, up_sum[...]), (6, held), (7, down)])


def halve_kernel(here, keep, got, kept, send):
    half = kept.shape[0]
    kept[...] = keep[:half] + got[:half].astype(F32)
    send[...] = (keep[half:] + got[half:].astype(F32)).astype(BF16)


def bits_of(size):
    bits, bit = [], 1
    while bit < size:
        bits.append(bit)
        bit *= 2
    return bits


def swap(values, axis, size, bit):
    return lax.ppermute(values, axis, [(at, at ^ bit) for at in range(size)])


def after(value, *others):
    return lax.optimization_barrier((value,) + others)[0]


def make_body(n_dp, n_rows, n_cols):
    assert n_rows == 4 and n_cols == 4
    far, near = 2, 1
    order = (0, far, near, far ^ near)

    def over_rows(value, bit):
        return swap(value, "rows", n_rows, bit)

    def over_cols(value, bit):
        return swap(value, "cols", n_cols, bit)

    def over_dp(value):
        value = value.astype(BF16).astype(F32)
        for bit in bits_of(n_dp):
            value = value + swap(value.astype(BF16), "dp", n_dp, bit).astype(F32)
        return value

    def body(
        tokens,
        segment_ids,
        first_gain,
        first_bias,
        qkv_weight,
        qv_bias,
        mix_weight,
        mix_bias,
        second_gain,
        second_bias,
        up_weight,
        up_bias,
        down_weight,
        down_bias,
        cotangent,
    ):
        feat, count = tokens.shape
        width = feat * n_cols
        part = count // n_cols
        n_qkv = qkv_weight.shape[1]
        n_hid = up_weight.shape[1]
        heads = n_qkv // (3 * HD)
        head_rows = heads * HD
        here = jnp.stack([lax.axis_index("rows"), lax.axis_index("cols")]).astype(jnp.int32)
        row = segment_ids.reshape(1, count)

        def halve(keep, got):
            half = (keep.shape[0] // 2,) + keep.shape[1:]
            return run(halve_kernel, "halve", (shaped(half, F32), shaped(half, BF16)), (here, keep, got))

        qkv_y = over_rows(qkv_weight, far)
        qkv_c = over_rows(qkv_weight, near)
        packed, qkv_col, up_col, down_col, seg_col = run(
            pack_kernel,
            "pack",
            (
                shaped((feat, count + 128), BF16),
                shaped((n_qkv, 1), F32),
                shaped((n_hid, 1), F32),
                shaped((feat, 1), F32),
                shaped((count, 1), jnp.int32),
            ),
            (here, tokens)
            + tuple(
                value.reshape(1, -1)
                for value in (
                    first_gain, first_bias, mix_bias, second_gain, second_bias, qv_bias, up_bias, down_bias, segment_ids,
                )
            ),
        )
        tok = lax.all_gather(packed, "cols", axis=0, tiled=True)
        qkv_yc = over_rows(qkv_y, near)
        w_pieces = (qkv_weight, qkv_y, qkv_c, qkv_yc)

        mix_own, up_own, down_own, cot_own = [
            after(value, tok) for value in (mix_weight, up_weight, down_weight, cotangent)
        ]
        mix_z = [over_cols(mix_own, bit) for bit in (1, 2, 3)]
        up_y, down_y = over_rows(up_own, far), over_rows(down_own, far)
        up_c, down_c = over_rows(up_own, near), over_rows(down_own, near)
        cot_z = [over_cols(cot_own, bit) for bit in (1, 2, 3)]

        normed_one, stats, qkv, attended, totals = run(
            functools.partial(first_kernel, order, heads),
            "first",
            (
                shaped((width, count), BF16),
                shaped((2, count), F32),
                shaped((n_qkv, count), BF16),
                shaped((head_rows, count), BF16),
                shaped((heads, count), F32),
            ),
            (here, tok) + w_pieces + (qkv_col, row, seg_col),
            scratch=(pltpu.VMEM((width, n_qkv), BF16),),
            flops=2 * width * n_qkv * count,
        )
        (mix_all,) = run(
            mix_pack_kernel, "mix_pack", (shaped((width, feat), BF16),), (here, mix_weight) + tuple(mix_z)
        )
        mix_y, mix_c = over_rows(mix_all, far), over_rows(mix_all, near)

        att = lax.all_gather(attended, "cols", axis=0, tiled=True)
        up_yc, down_yc, mix_yc = over_rows(up_y, near), over_rows(down_y, near), over_rows(mix_y, near)
        m_pieces = (mix_all, mix_y, mix_c, mix_yc)

        wide_b = shaped((width, count), BF16)
        piece_b = shaped((width, part), BF16)
        piece_f = shaped((width, part), F32)
        (
            normed_two, grad_pre, active, grad_final, p1, p2, p3, own_two, own_hat, own_inv, own_hidden, up_sum, down_all,
        ) = run(
            functools.partial(middle_kernel, order),
            "middle",
            (
                wide_b, shaped((n_hid, count), BF16), shaped((n_hid, count), BF16), wide_b,
                piece_b, piece_b, piece_b, piece_f, piece_f,
                shaped((8, count), F32), shaped((feat, count), F32), shaped((n_hid, 1), F32), shaped((width, n_hid), BF16),
            ),
            (here, tok, att)
            + m_pieces
            + (up_weight, up_y, up_c, up_yc)
            + (down_weight, down_y, down_c, down_yc)
            + (cotangent,)
            + tuple(cot_z)
            + (row, up_col),
            scratch=(pltpu.VMEM((width, n_hid), BF16), pltpu.VMEM((width, count), F32)),
            flops=2 * width * count * (width + 3 * n_hid),
        )
        got = [over_cols(value, bit) for value, bit in zip((p1, p2, p3), (1, 2, 3))]

        ff_send, ff_keep, out_send, out_keep = run(
            functools.partial(ff_grads_kernel, order),
            "ff_grads",
            (
                shaped((2 * feat, 2 * n_hid), BF16), shaped((2 * feat, 2 * n_hid), F32),
                shaped((2 * feat, count), BF16), shaped((2 * feat, count), F32),
            ),
            (here, grad_final, active, normed_two, grad_pre, down_all),
            flops=2 * width * count * 3 * n_hid,
        )
        ff_keep, ff_send = halve(ff_keep, over_rows(ff_send, near))
        ff_got = over_rows(ff_send, far)

        grad_hidden, grad_hidden_b, a0, a1, a2, a3, second = run(
            functools.partial(second_back_kernel, order),
            "second_back",
            (
                piece_f, piece_b,
                shaped((feat, part), BF16), shaped((feat, part), BF16), shaped((feat, part), BF16), shaped((feat, part), BF16),
                shaped((width, 8), F32),
            ),
            (here, tok, own_two) + tuple(got) + (own_hat, own_inv, grad_final) + m_pieces,
            scratch=(pltpu.VMEM((width, part), BF16),),
            flops=2 * width * part * width,
        )
        b1, b2, b3 = [over_cols(value, bit) for value, bit in zip((a1, a2, a3), (1, 2, 3))]
        mix_send, mix_keep = run(
            functools.partial(mix_grad_kernel, order),
            "mix_grad",
            (shaped((2, width, feat), BF16), shaped((2, width, feat), F32)),
            (here, att, grad_hidden_b),
            flops=2 * width * part * width,
        )
        mix_keep, mix_send = halve(mix_keep, over_rows(mix_send, near))
        mix_got = over_rows(mix_send, far)

        grad_proj, qv_sum, s0, s1, s2, s3, first = run(
            functools.partial(first_back_kernel, order, heads),
            "first_back",
            (
                shaped((n_qkv, count), BF16), shaped((2 * head_rows, 1), F32),
                shaped((feat, count), F32), shaped((feat, count), BF16), shaped((feat, count), BF16), shaped((feat, count), BF16),
                shaped((width, 8), F32),
            ),
            (here, tok, stats, qkv, attended, totals, a0, b1, b2, b3, row, seg_col) + w_pieces + (grad_hidden,),
            scratch=(pltpu.VMEM((head_rows, count), BF16), pltpu.VMEM((width, count), F32)),
            flops=2 * width * n_qkv * count,
        )
        got = [over_cols(value, bit) for value, bit in zip((s1, s2, s3), (1, 2, 3))]

        qkv_send, qkv_keep = run(
            functools.partial(qkv_grads_kernel, order),
            "qkv_grads",
            (shaped((2 * feat, n_qkv), BF16), shaped((2 * feat, n_qkv), F32)),
            (here, normed_one, grad_proj),
            flops=2 * width * count * n_qkv,
        )
        qkv_keep, qkv_send = halve(qkv_keep, over_rows(qkv_send, near))
        grad_qkv = over_dp(qkv_keep + over_rows(qkv_send, far).astype(F32))
        grad_ff = over_dp(ff_keep + ff_got.astype(F32))

        wide, rest = run(
            sums_kernel, "sums", (shaped((8, width), F32), shaped((8, width), F32)),
            (here, second, first, up_sum, qv_sum, cotangent, row),
        )
        for bit in bits_of(n_cols):
            wide = wide + over_cols(wide, bit)
        sums = wide + rest
        for axis, size in (("rows", n_rows), ("dp", n_dp)):
            for bit in bits_of(size):
                sums = sums + swap(sums, axis, size, bit)

        at_col = lax.axis_index("cols")
        grad_mix = (mix_keep[0] + mix_got[0].astype(F32)).reshape(n_cols, feat, feat)

        def mix_block(step):
            return lax.dynamic_index_in_dim(grad_mix, at_col ^ step, 0, keepdims=False)

        mix_got = over_cols(jnp.stack([mix_block(1), mix_block(3)]).astype(BF16), 1).astype(F32)
        mix_low, mix_high = mix_block(0) + mix_got[0], mix_block(2) + mix_got[1]
        grad_mix = over_dp(mix_low + over_cols(mix_high.astype(BF16), 2).astype(F32))

        out_send = after(out_send, a1)
        out_keep, out_send = halve(out_keep, over_cols(out_send, 1))
        output = own_hidden + down_col + out_keep + over_cols(out_send, 2).astype(F32)

        grad_tokens = s0 + got[0].astype(F32) + got[1].astype(F32) + got[2].astype(F32)

        own = lax.dynamic_slice_in_dim(sums, at_col * feat, feat, 1)
        return (
            output.astype(BF16),
            grad_tokens,
            own[3],
            own[4],
            grad_qkv,
            sums[6, : 2 * head_rows],
            grad_mix,
            own[2],
            own[0],
            own[1],
            grad_ff[:, n_hid:],
            sums[5, :n_hid],
            grad_ff[:, :n_hid],
            sums[7, :feat],
        )

    return body


def solution(mesh):
    sizes = mesh.shape
    return jax.shard_map(
        make_body(sizes["dp"], sizes["rows"], sizes["cols"]),
        mesh=mesh,
        in_specs=(
            P("cols", ("dp", "rows")),
            P(("dp", "rows")),
            P("cols"),
            P("cols"),
            P("rows", "cols"),
            P("cols"),
            P("cols", "rows"),
            P("cols"),
            P("cols"),
            P("cols"),
            P("rows", "cols"),
            P("cols"),
            P("rows", "cols"),
            P("cols"),
            P("cols", ("dp", "rows")),
        ),
        out_specs=(
            P("cols", ("dp", "rows")),
            P("cols", ("dp", "rows")),
            P("cols"),
            P("cols"),
            P("rows", "cols"),
            P("cols"),
            P("cols", "rows"),
            P("cols"),
            P("cols"),
            P("cols"),
            P("rows", "cols"),
            P("cols"),
            P("rows", "cols"),
            P("cols"),
        ),
        check_vma=False,
    )
```

time: 265 us -> 251 us (0.947)
  Pallas kernels: 8.29 us -> 56.4 us
  matrix products: 15.4 us -> 0 us
  waiting for transfers between devices: 88.9 us -> 76 us
  local copies, waits for them, and re-layouts: 24.5 us -> 14.7 us
  other arithmetic: 17.2 us -> 7.51 us
  between operations: 9.07 us -> 1.06 us
  blocking collectives: 48.4 us -> 42.1 us
    pallas_call x2 -> x14, Pallas kernels: 8.29 us -> 56.4 us  [run(): pl.pallas_call(kernel, out_shape=outs, in_specs=specs, out_specs=[pl.Bloc...]
    ppermute x21 -> x0, waiting for transfers between devices: 46.6 us -> none  [shift(): lax.ppermute(values, axis, [(at, (at + step) % size) for at in range(size)])]
    ppermute x30 -> x45, waiting for transfers between devices: 42.3 us -> 76 us  [swap(): return lax.ppermute(values, axis, [(at, at ^ bit) for at in range(size)])]
    ppermute x30 -> x45, starting transfers between devices: 22.8 us -> 52.8 us  [swap(): return lax.ppermute(values, axis, [(at, at ^ bit) for at in range(size)])]
    ppermute x21 -> x0, starting transfers between devices: 29.2 us -> none  [shift(): lax.ppermute(values, axis, [(at, (at + step) % size) for at in range(size)])]
    dot_general x12 -> x0, matrix products: 15.4 us -> none  [dot(): lax.dot_general(left, right, (dims, ((), ())), preferred_element_type=F32)]
    all_gather x3 -> x2, blocking collectives: 48.4 us -> 42.1 us  [the longest x1 22.6 us: body(): tok = lax.all_gather(packed, 'cols', axis=0, tiled=True)]
    unnamed x95 -> x90, local copies, waits for them, and re-layouts: 10.9 us -> 6.62 us
  transfers between devices with their start and end apart: 51 -> 45, of which waited for: 25 -> 17; matrix products, arithmetic and copies ran while one was open for 16% -> 6% of each run, Pallas kernels for 3% -> 13%
where the time goes in v3:
time: 251 us
  waiting for transfers between devices  76 us (30%)
  Pallas kernels  56.4 us (22%)
  starting transfers between devices  52.8 us (21%)
  blocking collectives  42.1 us (17%)
  local copies, waits for them, and re-layouts  14.7 us (6%)
  other arithmetic  7.51 us (3%)
    ppermute x45, waiting for transfers between devices, swap(): return lax.ppermute(values, axis, [(at, at ^ bit) for at in range(size)])  76 us
    pallas_call x14, Pallas kernels, run(): pl.pallas_call(kernel, out_shape=outs, in_specs=specs, out_specs=[pl.Bloc...  56.4 us
    ppermute x45, starting transfers between devices, swap(): return lax.ppermute(values, axis, [(at, at ^ bit) for at in range(size)])  52.8 us
    all_gather x1, blocking collectives, body(): tok = lax.all_gather(packed, 'cols', axis=0, tiled=True)  22.6 us
    all_gather x1, blocking collectives, body(): att = lax.all_gather(attended, 'cols', axis=0, tiled=True)  19.5 us
    unnamed x90, local copies, waits for them, and re-layouts  6.62 us
  transfers between devices with their start and end apart: 45, of which 17 were waited for; matrix products, arithmetic and copies ran while one was open for 6% of the time, Pallas kernels for 13%

profile of v3, /device:TPU:0, one launch (start us, length us, event | category | flops | bytes accessed | tf_op | source)
XLA Modules:
  0.0 250.7 jit_solution(4475763683223229276)
XLA Ops:
  0.7 3.1 %collective-permute-start = (bf16[192,576]{1,0:T(8,128)(2,1)}, bf16[192,576]{1,0:T(8,128)(2,1)S(1)}, u32[]{:S(2)}, u32[]{:S(2)}) collective-permute-start(bf16[192,576]{1,0:T(8,128)(2,1)} %w0.3), channel_id=1, source_target_pairs={{0,8},{4,12},{8,0},{12,4},{1,9},{5,13},{9,1},{13,5},{2,10},{6,14},... | collective-permute-start | bytes 663560 | tf_op jit(solution)/shard_map/ppermute | solution.py:342
  6.9 2.3 pack.1
  9.2 22.6 %all_gather.6.tok = bf16[768,640]{1,0:T(8,128)(2,1)} all-gather(bf16[192,640]{1,0:T(8,128)(2,1)} %get-tuple-element.74), channel_id=1, replica_groups=mesh['dp'=2,'rows'=4,'cols'=4] {'cols'}, dimensions={0}, use_global_device_ids=true | all-gather | bytes 1228800 | tf_op jit(solution)/shard_map/all_gather | solution.py:417
  33.5 2.2 collective-permute-start.17
  35.8 2.6 %collective-permute-done.5.m3 = bf16[192,192]{1,0:T(8,128)(2,1)S(1)} collective-permute-done((bf16[192,192]{1,0:T(8,128)(2,1)S(1)}, bf16[192,192]{1,0:T(8,128)(2,1)S(1)}, u32[]{:S(2)}, u32[]{:S(2)}) %collective-permute-start.5) | collective-permute-done | bytes 73760 | tf_op jit(solution)/shard_map/ppermute | solution.py:342
  38.4 11.0 %collective-permute-start.4 = (bf16[192,192]{1,0:T(8,128)(2,1)S(1)}, bf16[192,192]{1,0:T(8,128)(2,1)S(1)}, u32[]{:S(2)}, u32[]{:S(2)}) collective-permute-start(bf16[192,192]{1,0:T(8,128)(2,1)S(1)} %copy-done.22), channel_id=1, source_target_pairs={{0,2},{1,3},{2,0},{3,1},{4,6},{5,7},{6,4},{7,5},{8,10},{9,11},{10,... | collective-permute-start | bytes 221192 | tf_op jit(solution)/shard_map/ppermute | solution.py:342
  49.4 8.9 %collective-permute-done.4.m2 = bf16[192,192]{1,0:T(8,128)(2,1)S(1)} collective-permute-done((bf16[192,192]{1,0:T(8,128)(2,1)S(1)}, bf16[192,192]{1,0:T(8,128)(2,1)S(1)}, u32[]{:S(2)}, u32[]{:S(2)}) %collective-permute-start.4) | collective-permute-done | bytes 73760 | tf_op jit(solution)/shard_map/ppermute | solution.py:342
  58.4 4.6 %collective-permute-done.3.m1 = bf16[192,192]{1,0:T(8,128)(2,1)S(1)} collective-permute-done((bf16[192,192]{1,0:T(8,128)(2,1)S(1)}, bf16[192,192]{1,0:T(8,128)(2,1)S(1)}, u32[]{:S(2)}, u32[]{:S(2)}) %collective-permute-start.3) | collective-permute-done | bytes 73760 | tf_op jit(solution)/shard_map/ppermute | solution.py:342
  68.9 5.8 %first.1 = (bf16[768,512]{1,0:T(8,128)(2,1)}, f32[2,512]{1,0:T(2,128)}, bf16[576,512]{1,0:T(8,128)(2,1)}, bf16[192,512]{1,0:T(8,128)(2,1)}, f32[3,512]{1,0:T(4,128)}) custom-call(s32[2]{0:T(128)} %pad_add_fusion.here, bf16[768,640]{1,0:T(8,128)(2,1)} %all_gather.6.tok, bf16[192,576]{1,0:T(8,128)(2,1)} %w0.3, bf16[192,576]{1,0:T(8,128)(2,1)} %copy-done.4, ...), custom_call_target="tpu_custom_call" | custom-call | flops 452984832 | bytes 3457288 | tf_op jit(solution)/shard_map/first/pallas_call | solution.py:67
  75.9 5.8 %collective-permute-done.12.d1 = bf16[192,768]{1,0:T(8,128)(2,1)S(1)} collective-permute-done((bf16[192,768]{1,0:T(8,128)(2,1)S(1)}, bf16[192,768]{1,0:T(8,128)(2,1)S(1)}, u32[]{:S(2)}, u32[]{:S(2)}) %collective-permute-start.12) | collective-permute-done | bytes 294944 | tf_op jit(solution)/shard_map/ppermute | solution.py:342
  81.7 7.3 %collective-permute-done.6.m1 = bf16[768,192]{1,0:T(8,128)(2,1)S(1)} collective-permute-done((bf16[768,192]{1,0:T(8,128)(2,1)}, bf16[768,192]{1,0:T(8,128)(2,1)S(1)}, u32[]{:S(2)}, u32[]{:S(2)}) %collective-permute-start.6) | collective-permute-done | bytes 294944 | tf_op jit(solution)/shard_map/ppermute | solution.py:342
  89.0 19.5 %all_gather.7.att = bf16[768,512]{1,0:T(8,128)(2,1)} all-gather(bf16[192,512]{1,0:T(8,128)(2,1)} %get-tuple-element.77.att), channel_id=1, replica_groups=mesh['dp'=2,'rows'=4,'cols'=4] {'cols'}, dimensions={0}, use_global_device_ids=true | all-gather | bytes 983040 | tf_op jit(solution)/shard_map/all_gather | solution.py:448
  110.1 9.1 %middle.1 = (bf16[768,512]{1,0:T(8,128)(2,1)}, bf16[768,512]{1,0:T(8,128)(2,1)}, bf16[768,512]{1,0:T(8,128)(2,1)}, bf16[768,512]{1,0:T(8,128)(2,1)}, bf16[768,12...) custom-call(s32[2]{0:T(128)} %pad_add_fusion.here, ...), custom_call_target="tpu_custom_call" | custom-call | flops 2415919104 | bytes 12214280 | tf_op jit(solution)/shard_map/middle/pallas_call | solution.py:67
  119.3 2.6 %collective-permute-start.19 = (bf16[768,128]{1,0:T(8,128)(2,1)}, bf16[768,128]{1,0:T(8,128)(2,1)S(1)}, u32[]{:S(2)}, u32[]{:S(2)}) collective-permute-start(bf16[768,128]{1,0:T(8,128)(2,1)} %get-tuple-element.94), channel_id=1, source_target_pairs={{0,2},{1,3},{2,0},{3,1},{4,6},{5,7},{6,4},{7,5},{8,10},{9,11},{10,... | collective-permute-start | bytes 589832 | tf_op jit(solution)/shard_map/ppermute | solution.py:342
  123.6 4.5 %collective-permute-done.18.r1 = bf16[768,128]{1,0:T(8,128)(2,1)S(1)} collective-permute-done((bf16[768,128]{1,0:T(8,128)(2,1)}, bf16[768,128]{1,0:T(8,128)(2,1)S(1)}, u32[]{:S(2)}, u32[]{:S(2)}) %collective-permute-start.18) | collective-permute-done | bytes 196640 | tf_op jit(solution)/shard_map/ppermute | solution.py:342
  128.2 7.9 %collective-permute-done.19.r2 = bf16[768,128]{1,0:T(8,128)(2,1)S(1)} collective-permute-done((bf16[768,128]{1,0:T(8,128)(2,1)}, bf16[768,128]{1,0:T(8,128)(2,1)S(1)}, u32[]{:S(2)}, u32[]{:S(2)}) %collective-permute-start.19) | collective-permute-done | bytes 196640 | tf_op jit(solution)/shard_map/ppermute | solution.py:342
  136.8 4.2 %second_back.1 = (f32[768,128]{1,0:T(8,128)}, bf16[768,128]{1,0:T(8,128)(2,1)}, bf16[192,128]{1,0:T(8,128)(2,1)}, bf16[192,128]{1,0:T(8,128)(2,1)}, bf16[192,128...) custom-call(s32[2]{0:T(128)} %pad_add_fusion.here, bf16[768,640]{1,0:T(8,128)(2,1)} %all_gather.6.tok, ...), custom_call_target="tpu_custom_call" | custom-call | flops 150994944 | bytes 5152776 | tf_op jit(solution)/shard_map/second_back/pallas_call | solution.py:67
  141.1 3.5 %collective-permute-start.24 = (bf16[192,128]{1,0:T(8,128)(2,1)}, bf16[192,128]{1,0:T(8,128)(2,1)S(1)}, u32[]{:S(2)}, u32[]{:S(2)}) collective-permute-start(bf16[192,128]{1,0:T(8,128)(2,1)} %get-tuple-element.106), channel_id=1, source_target_pairs={{0,2},{1,3},{2,0},{3,1},{4,6},{5,7},{6,4},{7,5},{8,10},{9,11},{10,... | collective-permute-start | bytes 147464 | tf_op jit(solution)/shard_map/ppermute | solution.py:342
  146.9 3.9 %collective-permute-done.25.a3 = bf16[192,128]{1,0:T(8,128)(2,1)S(1)} collective-permute-done((bf16[192,128]{1,0:T(8,128)(2,1)}, bf16[192,128]{1,0:T(8,128)(2,1)S(1)}, u32[]{:S(2)}, u32[]{:S(2)}) %collective-permute-start.25) | collective-permute-done | bytes 49184 | tf_op jit(solution)/shard_map/ppermute | solution.py:342
  151.6 6.8 %first_back.1 = (bf16[576,512]{1,0:T(8,128)(2,1)}, f32[384,1]{1,0:T(8,128)}, f32[192,512]{1,0:T(8,128)}, bf16[192,512]{1,0:T(8,128)(2,1)}, bf16[192,512]{1,0:T(8...) custom-call(s32[2]{0:T(128)} %pad_add_fusion.here, bf16[768,640]{1,0:T(8,128)(2,1)} %all_gather.6.tok, ...), custom_call_target="tpu_custom_call" | custom-call | flops 452984832 | bytes 4857352 | tf_op jit(solution)/shard_map/first_back/pallas_call | solution.py:67
  158.4 3.0 %sums.1 = (f32[8,768]{1,0:T(8,128)}, f32[8,768]{1,0:T(8,128)}) custom-call(s32[2]{0:T(128)} %pad_add_fusion.here, f32[768,8]{1,0:T(8,128)} %get-tuple-element.113.second, f32[768,8]{1,0:T(8,128)} %get-tuple-element.114.first, f32[768,1]{1,0:T(8,128)} %get-tuple-element.115.up_sum, f32[384,1]{1,0:T(8,128)} %get-tuple-element.116.qv_sum, ...), custom_call_target="tpu_custom_call" | custom-call | bytes 301576 | tf_op jit(solution)/shard_map/sums/pallas_call | solution.py:67
  161.4 3.0 %mix_grad.1 = (bf16[2,768,192]{2,1,0:T(8,128)(2,1)}, f32[2,768,192]{2,1,0:T(8,128)}) custom-call(s32[2]{0:T(128)} %pad_add_fusion.here, bf16[768,512]{1,0:T(8,128)(2,1)} %all_gather.7.att, bf16[768,128]{1,0:T(8,128)(2,1)} %get-tuple-element.125.grad_hidden_b), custom_call_target="tpu_custom_call" | custom-call | flops 150994944 | bytes 2752520 | tf_op jit(solution)/shard_map/mix_grad/pallas_call | solution.py:67
  166.0 2.4 collective-permute-start.30
  168.4 6.7 %ff_grads.1 = (bf16[384,1536]{1,0:T(8,128)(2,1)}, f32[384,1536]{1,0:T(8,128)}, bf16[384,512]{1,0:T(8,128)(2,1)}, f32[384,512]{1,0:T(8,128)}) custom-call(s32[2]{0:T(128)} %pad_add_fusion.here, bf16[768,512]{1,0:T(8,128)(2,1)} %get-tuple-element.85.grad_final, bf16[768,512]{1,0:T(8,128)(2,1)} %get-tuple-element.86.active, ...), custom_call_target="tpu_custom_call" | custom-call | flops 1811939328 | bytes 9043976 | tf_op jit(solution)/shard_map/ff_grads/pallas_call | solution.py:67
  182.3 3.1 %qkv_grads.1 = (bf16[384,576]{1,0:T(8,128)(2,1)}, f32[384,576]{1,0:T(8,128)}) custom-call(s32[2]{0:T(128)} %pad_add_fusion.here, bf16[768,512]{1,0:T(8,128)(2,1)} %get-tuple-element.119.normed, bf16[576,512]{1,0:T(8,128)(2,1)} %get-tuple-element.120.grad_proj), custom_call_target="tpu_custom_call" | custom-call | flops 452984832 | bytes 2703368 | tf_op jit(solution)/shard_map/qkv_grads/pallas_call | solution.py:67
  194.5 2.8 %halve.6 = (f32[1,768,192]{2,1,0:T(8,128)}, bf16[1,768,192]{2,1,0:T(8,128)(2,1)}) custom-call(s32[2]{0:T(128)} %pad_add_fusion.here, f32[2,768,192]{2,1,0:T(8,128)} %get-tuple-element.126.keep, bf16[2,768,192]{2,1,0:T(8,128)(2,1)} %copy.30.got), custom_call_target="tpu_custom_call" | custom-call | bytes 2654216 | tf_op jit(solution)/shard_map/halve/pallas_call | solution.py:67
  197.4 9.5 %collective-permute-done.27 = bf16[192,512]{1,0:T(8,128)(2,1)} collective-permute-done((bf16[192,512]{1,0:T(8,128)(2,1)S(1)}, bf16[192,512]{1,0:T(8,128)(2,1)}, u32[]{:S(2)}, u32[]{:S(2)}) %collective-permute-start.27) | collective-permute-done | bytes 196640 | tf_op jit(solution)/shard_map/ppermute | solution.py:342
  210.3 2.3 halve.5
  217.9 3.3 %halve.7 = (f32[192,1536]{1,0:T(8,128)}, bf16[192,1536]{1,0:T(8,128)(2,1)}) custom-call(s32[2]{0:T(128)} %pad_add_fusion.here, f32[384,1536]{1,0:T(8,128)} %get-tuple-element.130.keep, bf16[384,1536]{1,0:T(8,128)(2,1)} %copy-done.2), custom_call_target="tpu_custom_call" | custom-call | bytes 5308424 | tf_op jit(solution)/shard_map/halve/pallas_call | solution.py:67
  222.0 4.2 %collective-permute-start.39 = (bf16[2,192,192]{2,1,0:T(8,128)(2,1)S(1)}, bf16[2,192,192]{2,1,0:T(8,128)(2,1)S(1)}, u32[]{:S(2)}, u32[]{:S(2)}) collective-permute-start(bf16[2,192,192]{2,1,0:T(8,128)(2,1)S(1)} %pad_maximum_fusion), channel_id=1, source_target_pairs={{0,1},{1,0},{2,3},{3,2},{4,5},{5,4},{6,7},{7,6},{8,9},{9,8},{10,11... | collective-permute-start | bytes 442376 | tf_op jit(solution)/shard_map/ppermute | solution.py:342
  226.9 4.0 %collective-permute-done.39 = bf16[2,192,192]{2,1,0:T(8,128)(2,1)S(1)} collective-permute-done((bf16[2,192,192]{2,1,0:T(8,128)(2,1)S(1)}, bf16[2,192,192]{2,1,0:T(8,128)(2,1)S(1)}, u32[]{:S(2)}, u32[]{:S(2)}) %collective-permute-start.39) | collective-permute-done | bytes 147488 | tf_op jit(solution)/shard_map/ppermute | solution.py:342
  238.0 10.7 %collective-permute-done.41 = bf16[192,192]{1,0:T(8,128)(2,1)S(1)} collective-permute-done((bf16[192,192]{1,0:T(8,128)(2,1)S(1)}, bf16[192,192]{1,0:T(8,128)(2,1)S(1)}, u32[]{:S(2)}, u32[]{:S(2)}) %collective-permute-start.41) | collective-permute-done | bytes 73760 | tf_op jit(solution)/shard_map/ppermute | solution.py:342
  (192 shorter events, 56.2 us)
Async XLA Ops:
  0.7 48.7 %collective-permute-start = (bf16[192,576]{1,0:T(8,128)(2,1)}, bf16[192,576]{1,0:T(8,128)(2,1)S(1)}, u32[]{:S(2)}, u32[]{:S(2)}) collective-permute-start(bf16[192,576]{1,0:T(8,128)(2,1)} %w0.3), channel_id=1, source_target_pairs={{0,8},{4,12},{8,0},{12,4},{1,9},{5,13},{9,1},{13,5},{2,10},{6,14},... | collective-permute-start | bytes 663560 | tf_op jit(solution)/shard_map/ppermute | solution.py:342
  33.5 34.0 %collective-permute-start.1 = (bf16[192,576]{1,0:T(8,128)(2,1)S(1)}, bf16[192,576]{1,0:T(8,128)(2,1)S(1)}, u32[]{:S(2)}, u32[]{:S(2)}) collective-permute-start(bf16[192,576]{1,0:T(8,128)(2,1)S(1)} %copy-done.3), channel_id=1, source_target_pairs={{0,4},{4,0},{8,12},{12,8},{1,5},{5,1},{9,13},{13,9},{2,6},{6,2},{1... | collective-permute-start | bytes 663560 | tf_op jit(solution)/shard_map/ppermute | solution.py:342
  33.5 31.9 %collective-permute-start.17 = (bf16[192,512]{1,0:T(8,128)(2,1)S(1)}, bf16[192,512]{1,0:T(8,128)(2,1)S(1)}, u32[]{:S(2)}, u32[]{:S(2)}) collective-permute-start(bf16[192,512]{1,0:T(8,128)(2,1)S(1)} %copy-done.20), channel_id=1, source_target_pairs={{0,3},{1,2},{2,1},{3,0},{4,7},{5,6},{6,5},{7,4},{8,11},{9,10},{10,... | collective-permute-start | bytes 589832 | tf_op jit(solution)/shard_map/ppermute | solution.py:342
  35.8 30.3 %collective-permute-start.16 = (bf16[192,512]{1,0:T(8,128)(2,1)S(1)}, bf16[192,512]{1,0:T(8,128)(2,1)S(1)}, u32[]{:S(2)}, u32[]{:S(2)}) collective-permute-start(bf16[192,512]{1,0:T(8,128)(2,1)S(1)} %copy-done.20), channel_id=1, source_target_pairs={{0,2},{1,3},{2,0},{3,1},{4,6},{5,7},{6,4},{7,5},{8,10},{9,11},{10,... | collective-permute-start | bytes 589832 | tf_op jit(solution)/shard_map/ppermute | solution.py:342
  38.4 20.0 %collective-permute-start.4 = (bf16[192,192]{1,0:T(8,128)(2,1)S(1)}, bf16[192,192]{1,0:T(8,128)(2,1)S(1)}, u32[]{:S(2)}, u32[]{:S(2)}) collective-permute-start(bf16[192,192]{1,0:T(8,128)(2,1)S(1)} %copy-done.22), channel_id=1, source_target_pairs={{0,2},{1,3},{2,0},{3,1},{4,6},{5,7},{6,4},{7,5},{8,10},{9,11},{10,... | collective-permute-start | bytes 221192 | tf_op jit(solution)/shard_map/ppermute | solution.py:342
  49.4 18.7 %collective-permute-start.2 = (bf16[192,576]{1,0:T(8,128)(2,1)S(1)}, bf16[192,576]{1,0:T(8,128)(2,1)S(1)}, u32[]{:S(2)}, u32[]{:S(2)}) collective-permute-start(bf16[192,576]{1,0:T(8,128)(2,1)S(1)} %collective-permute-done.w1), channel_id=1, source_target_pairs={{0,4},{4,0},{8,12},{12,8},{1,5},{5,1},{9,13},{13,9},{2,6},{6,2},{1... | collective-permute-start | bytes 663560 | tf_op jit(solution)/shard_map/ppermute | solution.py:342
  63.0 12.3 %collective-permute-start.10 = (bf16[192,768]{1,0:T(8,128)(2,1)S(1)}, bf16[192,768]{1,0:T(8,128)(2,1)S(1)}, u32[]{:S(2)}, u32[]{:S(2)}) collective-permute-start(bf16[192,768]{1,0:T(8,128)(2,1)S(1)} %copy-done.31), channel_id=1, source_target_pairs={{0,4},{4,0},{8,12},{12,8},{1,5},{5,1},{9,13},{13,9},{2,6},{6,2},{1... | collective-permute-start | bytes 884744 | tf_op jit(solution)/shard_map/ppermute | solution.py:342
  65.5 9.9 %collective-permute-start.9 = (bf16[192,768]{1,0:T(8,128)(2,1)S(1)}, bf16[192,768]{1,0:T(8,128)(2,1)S(1)}, u32[]{:S(2)}, u32[]{:S(2)}) collective-permute-start(bf16[192,768]{1,0:T(8,128)(2,1)S(1)} %copy-done.31), channel_id=1, source_target_pairs={{0,8},{4,12},{8,0},{12,4},{1,9},{5,13},{9,1},{13,5},{2,10},{6,14},... | collective-permute-start | bytes 884744 | tf_op jit(solution)/shard_map/ppermute | solution.py:342
  66.1 15.6 %collective-permute-start.12 = (bf16[192,768]{1,0:T(8,128)(2,1)S(1)}, bf16[192,768]{1,0:T(8,128)(2,1)S(1)}, u32[]{:S(2)}, u32[]{:S(2)}) collective-permute-start(bf16[192,768]{1,0:T(8,128)(2,1)S(1)} %copy-done.32), channel_id=1, source_target_pairs={{0,8},{4,12},{8,0},{12,4},{1,9},{5,13},{9,1},{13,5},{2,10},{6,14},... | collective-permute-start | bytes 884744 | tf_op jit(solution)/shard_map/ppermute | solution.py:342
  67.6 21.4 %collective-permute-start.6 = (bf16[768,192]{1,0:T(8,128)(2,1)}, bf16[768,192]{1,0:T(8,128)(2,1)S(1)}, u32[]{:S(2)}, u32[]{:S(2)}) collective-permute-start(bf16[768,192]{1,0:T(8,128)(2,1)} %mix_pack.1.m0), channel_id=1, source_target_pairs={{0,8},{4,12},{8,0},{12,4},{1,9},{5,13},{9,1},{13,5},{2,10},{6,14},... | collective-permute-start | bytes 884744 | tf_op jit(solution)/shard_map/ppermute | solution.py:342
  74.7 33.9 %collective-permute-start.13 = (bf16[192,768]{1,0:T(8,128)(2,1)S(1)}, bf16[192,768]{1,0:T(8,128)(2,1)S(1)}, u32[]{:S(2)}, u32[]{:S(2)}) collective-permute-start(bf16[192,768]{1,0:T(8,128)(2,1)S(1)} %copy-done.32), channel_id=1, source_target_pairs={{0,4},{4,0},{8,12},{12,8},{1,5},{5,1},{9,13},{13,9},{2,6},{6,2},{1... | collective-permute-start | bytes 884744 | tf_op jit(solution)/shard_map/ppermute | solution.py:342
  75.3 33.2 %collective-permute-start.7 = (bf16[768,192]{1,0:T(8,128)(2,1)S(1)}, bf16[768,192]{1,0:T(8,128)(2,1)S(1)}, u32[]{:S(2)}, u32[]{:S(2)}) collective-permute-start(bf16[768,192]{1,0:T(8,128)(2,1)S(1)} %copy-done), channel_id=1, source_target_pairs={{0,4},{4,0},{8,12},{12,8},{1,5},{5,1},{9,13},{13,9},{2,6},{6,2},{1... | collective-permute-start | bytes 884744 | tf_op jit(solution)/shard_map/ppermute | solution.py:342
  75.4 33.1 %collective-permute-start.11 = (bf16[192,768]{1,0:T(8,128)(2,1)S(1)}, bf16[192,768]{1,0:T(8,128)(2,1)S(1)}, u32[]{:S(2)}, u32[]{:S(2)}) collective-permute-start(bf16[192,768]{1,0:T(8,128)(2,1)S(1)} %collective-permute-done.9.u1), channel_id=1, source_target_pairs={{0,4},{4,0},{8,12},{12,8},{1,5},{5,1},{9,13},{13,9},{2,6},{6,2},{1... | collective-permute-start | bytes 884744 | tf_op jit(solution)/shard_map/ppermute | solution.py:342
  81.7 26.9 %collective-permute-start.14 = (bf16[192,768]{1,0:T(8,128)(2,1)S(1)}, bf16[192,768]{1,0:T(8,128)(2,1)S(1)}, u32[]{:S(2)}, u32[]{:S(2)}) collective-permute-start(bf16[192,768]{1,0:T(8,128)(2,1)S(1)} %collective-permute-done.12.d1), channel_id=1, source_target_pairs={{0,4},{4,0},{8,12},{12,8},{1,5},{5,1},{9,13},{13,9},{2,6},{6,2},{1... | collective-permute-start | bytes 884744 | tf_op jit(solution)/shard_map/ppermute | solution.py:342
  89.0 19.6 %collective-permute-start.8 = (bf16[768,192]{1,0:T(8,128)(2,1)S(1)}, bf16[768,192]{1,0:T(8,128)(2,1)S(1)}, u32[]{:S(2)}, u32[]{:S(2)}) collective-permute-start(bf16[768,192]{1,0:T(8,128)(2,1)S(1)} %collective-permute-done.6.m1), channel_id=1, source_target_pairs={{0,4},{4,0},{8,12},{12,8},{1,5},{5,1},{9,13},{13,9},{2,6},{6,2},{1... | collective-permute-start | bytes 884744 | tf_op jit(solution)/shard_map/ppermute | solution.py:342
  119.2 9.0 %collective-permute-start.18 = (bf16[768,128]{1,0:T(8,128)(2,1)}, bf16[768,128]{1,0:T(8,128)(2,1)S(1)}, u32[]{:S(2)}, u32[]{:S(2)}) collective-permute-start(bf16[768,128]{1,0:T(8,128)(2,1)} %get-tuple-element.93), channel_id=1, source_target_pairs={{0,1},{1,0},{2,3},{3,2},{4,5},{5,4},{6,7},{7,6},{8,9},{9,8},{10,11... | collective-permute-start | bytes 589832 | tf_op jit(solution)/shard_map/ppermute | solution.py:342
  119.3 16.7 %collective-permute-start.19 = (bf16[768,128]{1,0:T(8,128)(2,1)}, bf16[768,128]{1,0:T(8,128)(2,1)S(1)}, u32[]{:S(2)}, u32[]{:S(2)}) collective-permute-start(bf16[768,128]{1,0:T(8,128)(2,1)} %get-tuple-element.94), channel_id=1, source_target_pairs={{0,2},{1,3},{2,0},{3,1},{4,6},{5,7},{6,4},{7,5},{8,10},{9,11},{10,... | collective-permute-start | bytes 589832 | tf_op jit(solution)/shard_map/ppermute | solution.py:342
  121.9 14.1 %collective-permute-start.20 = (bf16[768,128]{1,0:T(8,128)(2,1)}, bf16[768,128]{1,0:T(8,128)(2,1)S(1)}, u32[]{:S(2)}, u32[]{:S(2)}) collective-permute-start(bf16[768,128]{1,0:T(8,128)(2,1)} %get-tuple-element.95), channel_id=1, source_target_pairs={{0,3},{1,2},{2,1},{3,0},{4,7},{5,6},{6,5},{7,4},{8,11},{9,10},{10,... | collective-permute-start | bytes 589832 | tf_op jit(solution)/shard_map/ppermute | solution.py:342
  165.9 24.7 %collective-permute-start.37 = (bf16[2,768,192]{1,2,0:T(8,128)(2,1)S(1)}, bf16[2,768,192]{1,2,0:T(8,128)(2,1)S(1)}, u32[]{:S(2)}, u32[]{:S(2)}) collective-permute-start(bf16[2,768,192]{1,2,0:T(8,128)(2,1)S(1)} %copy.29), channel_id=1, source_target_pairs={{0,4},{4,0},{8,12},{12,8},{1,5},{5,1},{9,13},{13,9},{2,6},{6,2},{1... | collective-permute-start | bytes 1769480 | tf_op jit(solution)/shard_map/ppermute | solution.py:342
  166.0 9.7 %collective-permute-start.30 = (f32[8,768]{1,0:T(8,128)S(1)}, f32[8,768]{1,0:T(8,128)S(1)}, u32[]{:S(2)}, u32[]{:S(2)}) collective-permute-start(f32[8,768]{1,0:T(8,128)S(1)} %add.102), channel_id=1, source_target_pairs={{0,2},{1,3},{2,0},{3,1},{4,6},{5,7},{6,4},{7,5},{8,10},{9,11},{10,... | collective-permute-start | bytes 73736 | tf_op jit(solution)/shard_map/ppermute | solution.py:342
  175.1 13.6 %collective-permute-start.21 = (bf16[384,512]{1,0:T(8,128)(2,1)}, bf16[384,512]{1,0:T(8,128)(2,1)S(1)}, u32[]{:S(2)}, u32[]{:S(2)}) collective-permute-start(bf16[384,512]{1,0:T(8,128)(2,1)} %get-tuple-element.99), channel_id=1, source_target_pairs={{0,1},{1,0},{2,3},{3,2},{4,5},{5,4},{6,7},{7,6},{8,9},{9,8},{10,11... | collective-permute-start | bytes 1179656 | tf_op jit(solution)/shard_map/ppermute | solution.py:342
  177.8 39.1 %collective-permute-start.42 = (bf16[384,1536]{1,0:T(8,128)(2,1)}, bf16[384,1536]{1,0:T(8,128)(2,1)S(1)}, u32[]{:S(2)}, u32[]{:S(2)}) collective-permute-start(bf16[384,1536]{1,0:T(8,128)(2,1)} %get-tuple-element.131), channel_id=1, source_target_pairs={{0,4},{4,0},{8,12},{12,8},{1,5},{5,1},{9,13},{13,9},{2,6},{6,2},{1... | collective-permute-start | bytes 3538952 | tf_op jit(solution)/shard_map/ppermute | solution.py:342
  177.8 19.5 %collective-permute-start.26 = (bf16[192,512]{1,0:T(8,128)(2,1)}, bf16[192,512]{1,0:T(8,128)(2,1)S(1)}, u32[]{:S(2)}, u32[]{:S(2)}) collective-permute-start(bf16[192,512]{1,0:T(8,128)(2,1)} %get-tuple-element.110), channel_id=1, source_target_pairs={{0,1},{1,0},{2,3},{3,2},{4,5},{5,4},{6,7},{7,6},{8,9},{9,8},{10,11... | collective-permute-start | bytes 589832 | tf_op jit(solution)/shard_map/ppermute | solution.py:342
  185.4 21.5 %collective-permute-start.27 = (bf16[192,512]{1,0:T(8,128)(2,1)S(1)}, bf16[192,512]{1,0:T(8,128)(2,1)}, u32[]{:S(2)}, u32[]{:S(2)}) collective-permute-start(bf16[192,512]{1,0:T(8,128)(2,1)S(1)} %copy-done.40), channel_id=1, source_target_pairs={{0,2},{1,3},{2,0},{3,1},{4,6},{5,7},{6,4},{7,5},{8,10},{9,11},{10,... | collective-permute-start | bytes 589832 | tf_op jit(solution)/shard_map/ppermute | solution.py:342
  188.7 18.8 %collective-permute-start.28 = (bf16[192,512]{1,0:T(8,128)(2,1)S(1)}, bf16[192,512]{1,0:T(8,128)(2,1)}, u32[]{:S(2)}, u32[]{:S(2)}) collective-permute-start(bf16[192,512]{1,0:T(8,128)(2,1)S(1)} %copy-done.39), channel_id=1, source_target_pairs={{0,3},{1,2},{2,1},{3,0},{4,7},{5,6},{6,5},{7,4},{8,11},{9,10},{10,... | collective-permute-start | bytes 589832 | tf_op jit(solution)/shard_map/ppermute | solution.py:342
  190.6 18.9 %collective-permute-start.34 = (bf16[384,576]{1,0:T(8,128)(2,1)}, bf16[384,576]{1,0:T(8,128)(2,1)S(1)}, u32[]{:S(2)}, u32[]{:S(2)}) collective-permute-start(bf16[384,576]{1,0:T(8,128)(2,1)} %get-tuple-element.122), channel_id=1, source_target_pairs={{0,4},{4,0},{8,12},{12,8},{1,5},{5,1},{9,13},{13,9},{2,6},{6,2},{1... | collective-permute-start | bytes 1327112 | tf_op jit(solution)/shard_map/ppermute | solution.py:342
  197.4 16.6 %collective-permute-start.22 = (bf16[192,512]{1,0:T(8,128)(2,1)S(1)}, bf16[192,512]{1,0:T(8,128)(2,1)}, u32[]{:S(2)}, u32[]{:S(2)}) collective-permute-start(bf16[192,512]{1,0:T(8,128)(2,1)S(1)} %copy-done.44), channel_id=1, source_target_pairs={{0,2},{1,3},{2,0},{3,1},{4,6},{5,7},{6,4},{7,5},{8,10},{9,11},{10,... | collective-permute-start | bytes 589832 | tf_op jit(solution)/shard_map/ppermute | solution.py:342
  212.6 13.5 %collective-permute-start.35 = (bf16[192,576]{1,0:T(8,128)(2,1)}, bf16[192,576]{1,0:T(8,128)(2,1)S(1)}, u32[]{:S(2)}, u32[]{:S(2)}) collective-permute-start(bf16[192,576]{1,0:T(8,128)(2,1)} %get-tuple-element.124), channel_id=1, source_target_pairs={{0,8},{4,12},{8,0},{12,4},{1,9},{5,13},{9,1},{13,5},{2,10},{6,14},... | collective-permute-start | bytes 663560 | tf_op jit(solution)/shard_map/ppermute | solution.py:342
  221.3 13.1 %collective-permute-start.43 = (bf16[192,1536]{1,0:T(8,128)(2,1)}, bf16[192,1536]{1,0:T(8,128)(2,1)S(1)}, u32[]{:S(2)}, u32[]{:S(2)}) collective-permute-start(bf16[192,1536]{1,0:T(8,128)(2,1)} %get-tuple-element.133), channel_id=1, source_target_pairs={{0,8},{4,12},{8,0},{12,4},{1,9},{5,13},{9,1},{13,5},{2,10},{6,14},... | collective-permute-start | bytes 1769480 | tf_op jit(solution)/shard_map/ppermute | solution.py:342
  226.2 11.0 %collective-permute-start.36 = (bf16[192,576]{1,0:T(8,128)(2,1)S(1)}, bf16[192,576]{1,0:T(8,128)(2,1)S(1)}, u32[]{:S(2)}, u32[]{:S(2)}) collective-permute-start(bf16[192,576]{1,0:T(8,128)(2,1)S(1)} %add_convert_fusion.1), channel_id=1, source_target_pairs={{0,16},{16,0},{1,17},{17,1},{2,18},{18,2},{3,19},{19,3},{4,20},{20... | collective-permute-start | bytes 663560 | tf_op jit(solution)/shard_map/ppermute | solution.py:342
  234.5 14.9 %collective-permute-start.44 = (bf16[192,1536]{1,0:T(8,128)(2,1)S(1)}, bf16[192,1536]{1,0:T(8,128)(2,1)S(1)}, u32[]{:S(2)}, u32[]{:S(2)}) collective-permute-start(bf16[192,1536]{1,0:T(8,128)(2,1)S(1)} %add_convert_fusion), channel_id=1, source_target_pairs={{0,16},{16,0},{1,17},{17,1},{2,18},{18,2},{3,19},{19,3},{4,20},{20... | collective-permute-start | bytes 1769480 | tf_op jit(solution)/shard_map/ppermute | solution.py:342
  236.5 12.2 %collective-permute-start.41 = (bf16[192,192]{1,0:T(8,128)(2,1)S(1)}, bf16[192,192]{1,0:T(8,128)(2,1)S(1)}, u32[]{:S(2)}, u32[]{:S(2)}) collective-permute-start(bf16[192,192]{1,0:T(8,128)(2,1)S(1)} %fusion.3), channel_id=1, source_target_pairs={{0,16},{16,0},{1,17},{17,1},{2,18},{18,2},{3,19},{19,3},{4,20},{20... | collective-permute-start | bytes 221192 | tf_op jit(solution)/shard_map/ppermute | solution.py:342
  (58 other events, 595.3 us)

commit v4 on v3

v4 whole, which is shorter than its diff:
```python
import functools
import math

import jax
import jax.numpy as jnp
from jax import lax
from jax.experimental import pallas as pl
from jax.experimental.pallas import tpu as pltpu
from jax.sharding import PartitionSpec as P


HD = 64
MAXLEN = 256
EPS = 1e-05
NEG = -1e30
ROOT = 0.7978845608028654
CUBIC = 0.044715
F32 = jnp.float32
BF16 = jnp.bfloat16


def dot(left, right, dims):
    return lax.dot_general(left, right, (dims, ((), ())), preferred_element_type=F32)


def mm(left, right):
    return dot(left, right, ((1,), (0,)))


def mm_t(left, right):
    return dot(left, right, ((0,), (0,)))


def mm_nt(left, right):
    return dot(left, right, ((1,), (1,)))


def gelu_both(pre_act):
    inner_arg = ROOT * (pre_act + CUBIC * pre_act * pre_act * pre_act)
    tanh_val = jnp.tanh(inner_arg)
    value = 0.5 * pre_act * (1.0 + tanh_val)
    slope = 0.5 * (1.0 + tanh_val) + 0.5 * pre_act * (1.0 - tanh_val * tanh_val) * ROOT * (
        1.0 + 3.0 * CUBIC * pre_act * pre_act
    )
    return value, slope


def allowed_mask(seg_row, seg_col, width):
    key_pos = lax.broadcasted_iota(jnp.int32, (width, width), 0)
    query_pos = lax.broadcasted_iota(jnp.int32, (width, width), 1)
    same_seg = (seg_col == seg_row) & (seg_row >= 0)
    return (key_pos < query_pos) & same_seg | (key_pos == query_pos)


def block(index, size):
    return pl.ds(pl.multiple_of(index * size, size), size)


def norm_cols(tok_ref, count, which):
    start = tok_ref.shape[0] // 4 - 128
    cols = tok_ref[:, count : tok_ref.shape[1]].astype(F32)[:, start:]
    return [cols[:, k : k + 1] + cols[:, k + 5 : k + 6] + cols[:, k + 10 : k + 11] for k in which]


def run(kernel, outs, ins, scratch=(), flops=0):
    specs = [pl.BlockSpec(memory_space=pltpu.SMEM)]
    specs += [pl.BlockSpec(memory_space=pltpu.VMEM)] * (len(ins) - 1)
    size = sum(math.prod(value.shape) * value.dtype.itemsize for value in list(ins) + list(outs))
    return pl.pallas_call(
        kernel,
        out_shape=outs,
        in_specs=specs,
        out_specs=[pl.BlockSpec(memory_space=pltpu.VMEM)] * len(outs),
        scratch_shapes=list(scratch),
        cost_estimate=pl.CostEstimate(flops=flops, transcendentals=0, bytes_accessed=size),
    )(*ins)


def shaped(shape, dtype):
    return jax.ShapeDtypeStruct(shape, dtype)


def column(row):
    return jnp.broadcast_to(row, (128, row.shape[1])).T[:, :1]


def pack_kernel(here, tok, mix, cot, g1, b1, bm, g2, b2, down, seg, packed, packed_two, down_col, seg_col):
    feat, count = tok.shape
    rows = jnp.concatenate([ref[...] for ref in (g1, b1, bm, g2, b2)], axis=0)
    high = rows.astype(BF16).astype(F32)
    middle = (rows - high).astype(BF16).astype(F32)
    low = rows - high - middle
    used = 3 * rows.shape[0]
    norms = jnp.concatenate([high, middle, low, jnp.zeros((128 - used, feat), F32)], axis=0).T
    packed[:, :count] = tok[...]
    packed[:, count : count + 128] = jnp.concatenate(
        [mix[:, 128:].astype(F32), norms[:, : 128 - (feat - 128)]], axis=1
    ).astype(BF16)
    packed_two[:, :count] = cot[...]
    packed_two[:, count:] = mix[:, :128]
    down_col[...] = column(down[...])
    seg_col[...] = column(seg[...].astype(F32)).astype(jnp.int32)


def first_kernel(order, heads, here, tok, w0, w1, w2, w3, qv, row, col, normed, stats, qkv, att, totals, w_all):
    feat = w0.shape[0]
    count = row.shape[1]
    for value, piece in zip(order, (w0, w1, w2, w3)):
        w_all[block(here[0] ^ value, feat), :] = piece[...]
    gain, shift = norm_cols(tok, count, (0, 1))
    values = tok[:, :count].astype(F32)
    mean = jnp.mean(values, axis=0, keepdims=True)
    inv = lax.rsqrt(jnp.mean(values * values, axis=0, keepdims=True) - mean * mean + EPS)
    stats[0:1, :] = mean
    stats[1:2, :] = inv
    normed[...] = ((values - mean) * inv * gain + shift).astype(BF16)
    head_rows = heads * HD
    qv_col = column(qv[...].reshape(1, 2 * head_rows))
    bias = jnp.concatenate([qv_col[:head_rows], jnp.zeros((head_rows, 1), F32), qv_col[head_rows:]], axis=0)
    qkv[...] = (mm_t(w_all[...], normed[...]) + bias).astype(BF16)
    scale = 1.0 / math.sqrt(HD)
    width = min(MAXLEN, count)
    for half in range(count // width):
        cols = pl.ds(half * width, width)
        allowed = allowed_mask(row[:, cols], col[cols, :], width)
        for head in range(heads):
            query = qkv[pl.ds(head * HD, HD), cols]
            keys = qkv[pl.ds(head_rows + head * HD, HD), cols]
            held = qkv[pl.ds(2 * head_rows + head * HD, HD), cols]
            scores = jnp.where(allowed, mm_t(keys, query) * scale, NEG)
            top = jnp.max(scores, axis=0, keepdims=True)
            log_total = top + jnp.log(jnp.sum(jnp.exp(scores - top), axis=0, keepdims=True))
            probs = jnp.exp(scores - log_total).astype(BF16)
            att[pl.ds(head * HD, HD), cols] = mm(held, probs).astype(BF16)
            totals[pl.ds(head, 1), cols] = log_total


def mix_pack_kernel(tok, cot, out):
    out[:, :128] = cot[...]
    out[:, 128:] = tok[:, : out.shape[1] - 128]


def mix_pack(tok, cot, feat):
    width, lanes = tok.shape
    last = pl.BlockSpec((width, 128), lambda step: (0, lanes // 128 - 1))
    return pl.pallas_call(
        mix_pack_kernel,
        grid=(1,),
        out_shape=shaped((width, feat), BF16),
        in_specs=[last, last],
        out_specs=pl.BlockSpec((width, feat), lambda step: (0, 0)),
        name="mix_pack",
    )(tok, cot)


def middle_kernel(
    order, here, tok, att, m0, m1, m2, m3, u0, u1, u2, u3, d0, d1, d2, d3, cot, row, up,
    normed, grad_pre, active, grad_final, p1, p2, p3, own_two, own_hat, own_inv, own_hidden, up_sum, down_all,
    up_all, hidden,
):
    feat, count = own_hidden.shape
    part = own_two.shape[1]
    live = row[...] >= 0
    bias_mix, gain, shift = norm_cols(tok, count, (2, 3, 4))
    for value, piece in zip(order, (u0, u1, u2, u3)):
        up_all[block(here[0] ^ value, feat), :] = piece[...]
    for value, piece in zip(order, (d0, d1, d2, d3)):
        down_all[block(here[0] ^ value, feat), :] = piece[...]
    grad_final[...] = jnp.where(live, cot[:, :count].astype(F32), 0.0).astype(BF16)
    for value, piece in zip(order, (m0, m1, m2, m3)):
        hidden[block(here[0] ^ value, feat), :] = mm_t(piece[...], att[...])
    hidden[...] = hidden[...] + tok[:, :count].astype(F32) + bias_mix
    values = hidden[...]
    mean = jnp.mean(values, axis=0, keepdims=True)
    inv = lax.rsqrt(jnp.mean(values * values, axis=0, keepdims=True) - mean * mean + EPS)
    own_hidden[...] = hidden[block(here[1], feat), :]
    hat = (values - mean) * inv
    normed[...] = (hat * gain + shift).astype(BF16)
    hidden[...] = hat
    own_inv[...] = jnp.broadcast_to(inv, (8, count))
    own_hat[...] = hidden[:, block(here[1], part)]
    value, slope = gelu_both(mm_t(up_all[...], normed[...]) + column(up[...].reshape(1, up.shape[0])))
    active[...] = value.astype(BF16)
    grad = mm_t(down_all[...], grad_final[...]) * slope
    grad_pre[...] = grad.astype(BF16)
    up_sum[...] = jnp.sum(grad_pre[...].astype(F32), axis=1, keepdims=True)
    hidden[...] = mm(up_all[...], grad_pre[...])
    own_two[...] = hidden[:, block(here[1], part)]
    for step, out in enumerate((p1, p2, p3)):
        out[...] = hidden[:, block(here[1] ^ (step + 1), part)].astype(BF16)


def in_order(order, here, target, source):
    feat = target.shape[0] // len(order)
    for at, value in enumerate(order):
        target[pl.ds(at * feat, feat), :] = source[block(here[0] ^ value, feat), :]


def ff_grads_kernel(
    order, here, grad_final, active, normed, grad_pre, down_all, send, keep, out_send, out_keep, rows
):
    half = keep.shape[0]
    feat = half // 2
    hid = active.shape[0]
    in_order(order, here, rows, grad_final)
    down = mm_nt(rows[...], active[...])
    keep[:, :hid] = down[:half]
    send[:, :hid] = down[half:].astype(BF16)
    in_order(order, here, rows, normed)
    up = mm_nt(rows[...], grad_pre[...])
    keep[:, hid:] = up[:half]
    send[:, hid:] = up[half:].astype(BF16)
    for step in (0, 2):
        out_keep[pl.ds(step // 2 * feat, feat), :] = mm(down_all[block(here[1] ^ step, feat), :], active[...])
        out = mm(down_all[block(here[1] ^ (step + 1), feat), :], active[...])
        out_send[pl.ds(step // 2 * feat, feat), :] = out.astype(BF16)


def second_back_kernel(
    order, here, tok, own_two, r1, r2, r3, own_hat, own_inv, grad_final, m0, m1, m2, m3,
    grad_hidden, grad_hidden_b, sums, a0, a1, a2, a3, all_att,
):
    feat = a0.shape[0]
    part = own_two.shape[1]
    (gain,) = norm_cols(tok, grad_final.shape[1], (3,))
    grad = own_two[...] + r1[...].astype(F32) + r2[...].astype(F32) + r3[...].astype(F32)
    sums[:, 1:2] = jnp.sum(grad, axis=1, keepdims=True)
    hat = own_hat[...]
    lanes = block(here[1], part)
    inv = own_inv[:, lanes][:1]
    scaled = grad * gain
    out = grad_final[:, lanes].astype(F32) + inv * (
        scaled
        - jnp.mean(scaled, axis=0, keepdims=True)
        - hat * jnp.mean(scaled * hat, axis=0, keepdims=True)
    )
    grad_hidden[...] = out
    grad_hidden_b[...] = out.astype(BF16)
    sums[:, 0:1] = jnp.sum(grad * hat, axis=1, keepdims=True)
    sums[:, 2:3] = jnp.sum(out, axis=1, keepdims=True)
    total = jnp.zeros(all_att.shape, F32)
    for value, piece in zip(order, (m0, m1, m2, m3)):
        total += mm(piece[...], grad_hidden_b[block(here[0] ^ value, feat), :])
    all_att[...] = total.astype(BF16)
    for step, ref in enumerate((a0, a1, a2, a3)):
        ref[...] = all_att[block(here[1] ^ step, feat), :]


def first_back_kernel(
    order, heads, here, tok, stats, qkv, att, totals, a0, a1, a2, a3, row, col, w0, w1, w2, w3, grad_hidden, second,
    grad_proj, qv_sum, s0, s1, s2, s3, grad_att, share, sums,
):
    feat, count = att.shape
    part = a0.shape[1]
    head_rows = heads * HD
    scale = 1.0 / math.sqrt(HD)
    for step, piece in enumerate((a0, a1, a2, a3)):
        grad_att[:, block(here[1] ^ step, part)] = piece[...]
    width = min(MAXLEN, count)
    for half in range(count // width):
        cols = pl.ds(half * width, width)
        allowed = allowed_mask(row[:, cols], col[cols, :], width)
        for head in range(heads):
            query = qkv[pl.ds(head * HD, HD), cols]
            keys = qkv[pl.ds(head_rows + head * HD, HD), cols]
            held = qkv[pl.ds(2 * head_rows + head * HD, HD), cols]
            grad = grad_att[pl.ds(head * HD, HD), cols]
            attended = att[pl.ds(head * HD, HD), cols]
            delta = jnp.sum(grad.astype(F32) * attended.astype(F32), axis=0, keepdims=True)
            scores = jnp.where(allowed, mm_t(keys, query) * scale, NEG)
            probs = jnp.exp(scores - totals[pl.ds(head, 1), cols])
            grad_held = mm_nt(grad, probs.astype(BF16))
            grad_probs = mm_t(held, grad)
            grad_scores = (probs * (grad_probs - delta) * scale).astype(BF16)
            grad_query = mm(keys, grad_scores)
            grad_keys = mm_nt(query, grad_scores)
            grad_proj[pl.ds(head * HD, HD), cols] = grad_query.astype(BF16)
            grad_proj[pl.ds(head_rows + head * HD, HD), cols] = grad_keys.astype(BF16)
            grad_proj[pl.ds(2 * head_rows + head * HD, HD), cols] = grad_held.astype(BF16)
            for at, grown in ((head * HD, grad_query), (head_rows + head * HD, grad_held)):
                total = jnp.sum(grown, axis=1, keepdims=True)
                if half:
                    total = total + qv_sum[pl.ds(at, HD), :]
                qv_sum[pl.ds(at, HD), :] = total
    for value, piece in zip(order, (w0, w1, w2, w3)):
        share[block(here[0] ^ value, feat), :] = mm(piece[...], grad_proj[...])
    (gain,) = norm_cols(tok, count, (0,))
    inv = stats[1:2, :]
    hat = (tok[:, :count].astype(F32) - stats[0:1, :]) * inv
    grad = share[...]
    lane = lax.broadcasted_iota(jnp.int32, sums.shape, 1)
    columns = [second[:, k : k + 1] for k in range(3)]
    columns += [jnp.sum(grad * hat, axis=1, keepdims=True), jnp.sum(grad, axis=1, keepdims=True)]
    total = jnp.zeros(sums.shape, F32)
    for at, values in enumerate(columns):
        total = jnp.where(lane == at, values, total)
    sums[...] = total
    scaled = grad * gain
    share[...] = inv * (
        scaled
        - jnp.mean(scaled, axis=0, keepdims=True)
        - hat * jnp.mean(scaled * hat, axis=0, keepdims=True)
    )
    share[:, block(here[1], part)] += grad_hidden[...]
    for step, ref in enumerate((s0, s1, s2, s3)):
        rows = block(here[1] ^ step, feat)
        extra = ref.shape[0] - feat
        ref[:feat, :] = share[rows, :].astype(ref.dtype)
        ref[feat:, :feat] = sums[rows, :].T[:extra].astype(ref.dtype)


def last_grads(pair, here, normed, grad_proj, att, pieces, rows, hidden):
    feat, count = att.shape
    part = count // len(pieces)
    for at, value in enumerate(pair):
        source = block(here[0] ^ value, feat)
        target = pl.ds(at * feat, feat)
        rows[target, :] = normed[source, :]
        for step, ref in enumerate(pieces):
            hidden[target, block(here[1] ^ step, part)] = ref[source, :]
    return mm_nt(rows[...], grad_proj[...]), mm_nt(hidden[...], att[...])


def last_send_kernel(order, here, normed, grad_proj, att, h0, h1, h2, h3, send, rows, hidden):
    split = grad_proj.shape[0]
    qkv, mix = last_grads(order[2:], here, normed, grad_proj, att, (h0, h1, h2, h3), rows, hidden)
    send[:, :split] = qkv.astype(BF16)
    send[:, split:] = mix.astype(BF16)


def last_keep_kernel(order, here, normed, grad_proj, att, h0, h1, h2, h3, got, own, own_b, send, rows, hidden):
    feat = att.shape[0]
    split = grad_proj.shape[0]
    qkv, mix = last_grads(order[:2], here, normed, grad_proj, att, (h0, h1, h2, h3), rows, hidden)
    qkv += got[:, :split].astype(F32)
    mix += got[:, split:].astype(F32)
    own[:, :split] = qkv[:feat]
    own[:, split:] = mix[:feat]
    own_b[:, :split] = qkv[:feat].astype(BF16)
    own_b[:, split:] = mix[:feat].astype(BF16)
    send[:, :split] = qkv[feat:].astype(BF16)
    send[:, split:] = mix[feat:].astype(BF16)


def rest_kernel(here, up_sum, qv_sum, cot, row, rest):
    width = up_sum.shape[0]
    feat = cot.shape[0]
    down = jnp.sum(jnp.where(row[...] >= 0, cot[...].astype(F32), 0.0), axis=1, keepdims=True)
    down = jnp.concatenate([down, jnp.zeros((width - feat, 1), F32)], axis=0)
    held = jnp.concatenate([qv_sum[...], jnp.zeros((width - qv_sum.shape[0], 1), F32)], axis=0)
    lane = lax.broadcasted_iota(jnp.int32, (width, 128), 1)
    total = jnp.zeros((width, 128), F32)
    for at, values in ((5, up_sum[...]), (6, held), (7, down)):
        total = jnp.where(lane == at, values, total)
    rest[...] = total.T[:8]


def token_sum_kernel(here, s0, g1, g2, g3, rest, out, sums):
    feat = out.shape[0]
    total = s0[...]
    for ref in (g1, g2, g3):
        total += ref[...].astype(F32)
    out[...] = total[:feat]
    sums[...] = rest[...]
    sums[:5, :feat] = total[feat : feat + 5, :feat]


def last_sum_kernel(here, own, got_y, got_x, got_xy, qkv, mix):
    split = qkv.shape[1]
    total = own[...] + got_y[...].astype(F32) + got_x[...].astype(F32) + got_xy[...].astype(F32)
    qkv[...] = total[:, :split]
    mix[...] = total[:, split:].T


def halve_kernel(here, keep, got, kept, send):
    half = kept.shape[0]
    kept[...] = keep[:half] + got[:half].astype(F32)
    send[...] = (keep[half:] + got[half:].astype(F32)).astype(BF16)


def bits_of(size):
    bits, bit = [], 1
    while bit < size:
        bits.append(bit)
        bit *= 2
    return bits


def swap(values, axis, size, bit):
    return lax.ppermute(values, axis, [(at, at ^ bit) for at in range(size)])


def after(value, *others):
    return lax.optimization_barrier((value,) + others)[0]


def together(*values):
    return lax.optimization_barrier(values)


def make_body(n_dp, n_rows, n_cols):
    assert n_rows == 4 and n_cols == 4
    far, near = 2, 1
    order = (0, far, near, far ^ near)

    def over_rows(value, bit):
        return swap(value, "rows", n_rows, bit)

    def over_cols(value, bit):
        return swap(value, "cols", n_cols, bit)

    def all_over_cols(values):
        return [over_cols(value, bit) for value, bit in zip(values, (1, 2, 3))]

    def over_dp(value):
        value = value.astype(BF16).astype(F32)
        for bit in bits_of(n_dp):
            value = value + swap(value.astype(BF16), "dp", n_dp, bit).astype(F32)
        return value

    def body(
        tokens,
        segment_ids,
        first_gain,
        first_bias,
        qkv_weight,
        qv_bias,
        mix_weight,
        mix_bias,
        second_gain,
        second_bias,
        up_weight,
        up_bias,
        down_weight,
        down_bias,
        cotangent,
    ):
        feat, count = tokens.shape
        width = feat * n_cols
        part = count // n_cols
        n_qkv = qkv_weight.shape[1]
        n_hid = up_weight.shape[1]
        heads = n_qkv // (3 * HD)
        head_rows = heads * HD
        here = jnp.stack([lax.axis_index("rows"), lax.axis_index("cols")]).astype(jnp.int32)
        row = segment_ids.reshape(1, count)

        def halve(keep, got):
            half = (keep.shape[0] // 2,) + keep.shape[1:]
            return run(halve_kernel, (shaped(half, F32), shaped(half, BF16)), (here, keep, got))

        qkv_y = over_rows(qkv_weight, far)
        up_y, down_y = over_rows(up_weight, far), over_rows(down_weight, far)
        qkv_c, up_c, down_c = [over_rows(value, near) for value in (qkv_weight, up_weight, down_weight)]
        lanes = shaped((feat, count + 128), BF16)
        packed, packed_two, down_col, seg_col = run(
            pack_kernel,
            (lanes, lanes, shaped((feat, 1), F32), shaped((count, 1), jnp.int32)),
            (here, tokens, mix_weight, cotangent)
            + tuple(
                value.reshape(1, -1)
                for value in (first_gain, first_bias, mix_bias, second_gain, second_bias, down_bias, segment_ids)
            ),
        )
        tok = lax.all_gather(packed, "cols", axis=0, tiled=True)
        qkv_yc = over_rows(qkv_y, near)
        w_pieces = (qkv_weight, qkv_y, qkv_c, qkv_yc)
        cot = lax.all_gather(after(packed_two, tok), "cols", axis=0, tiled=True)
        mix_all = mix_pack(tok, cot, feat)
        mix_y, mix_c = over_rows(mix_all, far), over_rows(mix_all, near)
        up_yc, down_yc = over_rows(up_y, near), over_rows(down_y, near)

        normed_one, stats, qkv, attended, totals = run(
            functools.partial(first_kernel, order, heads),
            (
                shaped((width, count), BF16),
                shaped((2, count), F32),
                shaped((n_qkv, count), BF16),
                shaped((head_rows, count), BF16),
                shaped((heads, count), F32),
            ),
            (here, after(tok, mix_all)) + w_pieces + (qv_bias, row, seg_col),
            scratch=(pltpu.VMEM((width, n_qkv), BF16),),
            flops=2 * width * n_qkv * count,
        )
        att = lax.all_gather(attended, "cols", axis=0, tiled=True)
        mix_yc = over_rows(mix_y, near)
        m_pieces = (mix_all, mix_y, mix_c, mix_yc)

        wide_b = shaped((width, count), BF16)
        piece_b = shaped((width, part), BF16)
        piece_f = shaped((width, part), F32)
        (
            normed_two, grad_pre, active, grad_final, p1, p2, p3, own_two, own_hat, own_inv, own_hidden, up_sum, down_all,
        ) = run(
            functools.partial(middle_kernel, order),
            (
                wide_b, shaped((n_hid, count), BF16), shaped((n_hid, count), BF16), wide_b,
                piece_b, piece_b, piece_b, piece_f, piece_f,
                shaped((8, count), F32), shaped((feat, count), F32), shaped((n_hid, 1), F32), shaped((width, n_hid), BF16),
            ),
            (here, tok, att)
            + m_pieces
            + (up_weight, up_y, up_c, up_yc)
            + (down_weight, down_y, down_c, down_yc)
            + (cot, row, up_bias),
            scratch=(pltpu.VMEM((width, n_hid), BF16), pltpu.VMEM((width, count), F32)),
            flops=2 * width * count * (width + 3 * n_hid),
        )
        got = all_over_cols((p1, p2, p3))

        ff_send, ff_keep, out_send, out_keep = run(
            functools.partial(ff_grads_kernel, order),
            (
                shaped((2 * feat, 2 * n_hid), BF16), shaped((2 * feat, 2 * n_hid), F32),
                shaped((2 * feat, count), BF16), shaped((2 * feat, count), F32),
            ),
            (here, grad_final, active, normed_two, grad_pre, down_all),
            scratch=(pltpu.VMEM((width, count), BF16),),
            flops=2 * width * count * 3 * n_hid,
        )
        ff_keep, ff_send = halve(ff_keep, over_rows(ff_send, near))
        got[0], got[1], got[2], ff_keep, ff_send, out_send = together(*got, ff_keep, ff_send, out_send)
        ff_got = over_rows(ff_send, far)

        grad_hidden, grad_hidden_b, second, a0, a1, a2, a3 = run(
            functools.partial(second_back_kernel, order),
            (
                piece_f, piece_b, shaped((width, 8), F32),
                shaped((feat, part), BF16), shaped((feat, part), BF16), shaped((feat, part), BF16), shaped((feat, part), BF16),
            ),
            (here, tok, own_two) + tuple(got) + (own_hat, own_inv, grad_final) + m_pieces,
            scratch=(pltpu.VMEM((width, part), BF16),),
            flops=2 * width * part * width,
        )
        b1, b2, b3 = all_over_cols((a1, a2, a3))
        h_pieces = [grad_hidden_b] + all_over_cols((grad_hidden_b,) * 3)
        out_got = over_cols(after(out_send, grad_hidden_b), 1)
        ff_sum = ff_keep + ff_got.astype(F32)
        b1, b2, b3, ff_sum = together(b1, b2, b3, ff_sum)
        grad_ff = over_dp(ff_sum)

        grad_proj, qv_sum, s0, s1, s2, s3 = run(
            functools.partial(first_back_kernel, order, heads),
            (
                shaped((n_qkv, count), BF16), shaped((2 * head_rows, 1), F32),
                shaped((feat + 16, count), F32),
                shaped((feat + 16, count), BF16), shaped((feat + 16, count), BF16), shaped((feat + 16, count), BF16),
            ),
            (here, tok, stats, qkv, attended, totals, a0, b1, b2, b3, row, seg_col) + w_pieces + (grad_hidden, second),
            scratch=(pltpu.VMEM((head_rows, count), BF16), pltpu.VMEM((width, count), F32), pltpu.VMEM((width, 128), F32)),
            flops=2 * width * n_qkv * count,
        )
        got = all_over_cols((s1, s2, s3))

        last_ins = (here, normed_one, grad_proj, attended) + tuple(h_pieces)
        n_last = n_qkv + feat
        (last_send,) = run(
            functools.partial(last_send_kernel, order), (shaped((2 * feat, n_last), BF16),), last_ins,
            scratch=(pltpu.VMEM((2 * feat, count), BF16), pltpu.VMEM((2 * feat, count), BF16)),
            flops=width * count * n_last,
        )
        own, own_b, last_send = run(
            functools.partial(last_keep_kernel, order),
            (shaped((feat, n_last), F32), shaped((feat, n_last), BF16), shaped((feat, n_last), BF16)),
            last_ins + (over_rows(last_send, near),),
            scratch=(pltpu.VMEM((2 * feat, count), BF16), pltpu.VMEM((2 * feat, count), BF16)),
            flops=width * count * n_last,
        )
        pairs = [(at, at ^ 1) for at in range(n_dp)]
        far_dp = [(d * n_rows + r, (d ^ 1) * n_rows + (r ^ far)) for d in range(n_dp) for r in range(n_rows)]
        got_y = over_rows(last_send, far)
        if n_dp > 1:
            got_x = lax.ppermute(own_b, "dp", pairs)
            got_xy = lax.ppermute(last_send, ("dp", "rows"), far_dp)
        else:
            got_x = got_xy = jnp.zeros_like(got_y)
        grad_qkv, grad_mix = run(
            last_sum_kernel, (shaped((feat, n_qkv), F32), shaped((feat, feat), F32)), (here, own, got_y, got_x, got_xy)
        )
        for bit in bits_of(n_dp)[1:]:
            grad_qkv = grad_qkv + swap(grad_qkv.astype(BF16), "dp", n_dp, bit).astype(F32)
            grad_mix = grad_mix + swap(grad_mix.astype(BF16), "dp", n_dp, bit).astype(F32)

        (rest,) = run(rest_kernel, (shaped((8, width), F32),), (here, up_sum, qv_sum, cotangent, row))
        grad_tokens, sums = run(
            token_sum_kernel, (shaped((feat, count), F32), shaped((8, width), F32)), (here, s0) + tuple(got) + (rest,)
        )
        for axis, size in (("rows", n_rows), ("dp", n_dp)):
            for bit in bits_of(size):
                sums = sums + swap(sums, axis, size, bit)

        out_keep, out_send = halve(out_keep, out_got)
        output = own_hidden + down_col + out_keep + over_cols(out_send, 2).astype(F32)
        return (
            output.astype(BF16),
            grad_tokens,
            sums[3, :feat],
            sums[4, :feat],
            grad_qkv,
            sums[6, : 2 * head_rows],
            grad_mix,
            sums[2, :feat],
            sums[0, :feat],
            sums[1, :feat],
            grad_ff[:, n_hid:],
            sums[5, :n_hid],
            grad_ff[:, :n_hid],
            sums[7, :feat],
        )

    return body


def solution(mesh):
    sizes = mesh.shape
    body = make_body(sizes["dp"], sizes["rows"], sizes["cols"])

    return jax.shard_map(
        body,
        mesh=mesh,
        in_specs=(
            P("cols", ("dp", "rows")),
            P(("dp", "rows")),
            P("cols"),
            P("cols"),
            P("rows", "cols"),
            P("cols"),
            P("cols", "rows"),
            P("cols"),
            P("cols"),
            P("cols"),
            P("rows", "cols"),
            P("cols"),
            P("rows", "cols"),
            P("cols"),
            P("cols", ("dp", "rows")),
        ),
        out_specs=(
            P("cols", ("dp", "rows")),
            P("cols", ("dp", "rows")),
            P("cols"),
            P("cols"),
            P("rows", "cols"),
            P("cols"),
            P("cols", "rows"),
            P("cols"),
            P("cols"),
            P("cols"),
            P("rows", "cols"),
            P("cols"),
            P("rows", "cols"),
            P("cols"),
        ),
        check_vma=False,
    )
```

time: 251 us -> 234 us (0.932)
  blocking collectives: 42.1 us -> 62.9 us
  starting transfers between devices: 52.8 us -> 34.9 us
  waiting for transfers between devices: 76 us -> 66.9 us
  other arithmetic: 7.51 us -> 2.58 us
  local copies, waits for them, and re-layouts: 14.7 us -> 10 us
    all_gather x0 -> x1, blocking collectives: none -> 21 us  [body(): cot = lax.all_gather(after(packed_two, tok), 'cols', axis=0, tiled=True)]
    ppermute x45 -> x34, starting transfers between devices: 52.8 us -> 31.9 us  [swap(): return lax.ppermute(values, axis, [(at, at ^ bit) for at in range(size)])]
    ppermute x45 -> x34, waiting for transfers between devices: 76 us -> 55.5 us  [swap(): return lax.ppermute(values, axis, [(at, at ^ bit) for at in range(size)])]
    ppermute x0 -> x2, waiting for transfers between devices: none -> 11.3 us  [the longest x1 11.3 us: body(): got_x = lax.ppermute(own_b, 'dp', pairs)]
    pallas_call x14 -> x13, Pallas kernels: 56.4 us -> 53.3 us  [run(): pl.pallas_call(kernel, out_shape=outs, in_specs=specs, out_specs=[pl.Bloc...]
    ppermute x0 -> x2, starting transfers between devices: none -> 2.98 us  [the longest x1 2.44 us: body(): got_xy = lax.ppermute(last_send, ('dp', 'rows'), far_dp)]
    add x4 -> x1, other arithmetic: 3.03 us -> 0.11 us  [body(): ff_sum = ff_keep + ff_got.astype(F32)]
    reshape x2 -> x0, local copies, waits for them, and re-layouts: 2.51 us -> none  [body(): value.reshape(1, -1)]
  transfers between devices with their start and end apart: 45 -> 36, of which waited for: 17 -> 12; matrix products, arithmetic and copies ran while one was open for 6% -> 2% of each run, Pallas kernels for 13% -> 16%
where the time goes in v4:
time: 234 us; the launch traced here: 233 us
  waiting for transfers between devices  66.9 us (29%)
  blocking collectives  62.9 us (27%)
  Pallas kernels  55.2 us (24%)
  starting transfers between devices  34.9 us (15%)
  local copies, waits for them, and re-layouts  10 us (4%)
  other arithmetic  2.58 us (1%)
    ppermute x34, waiting for transfers between devices, swap(): return lax.ppermute(values, axis, [(at, at ^ bit) for at in range(size)])  55.5 us
    pallas_call x13, Pallas kernels, run(): pl.pallas_call(kernel, out_shape=outs, in_specs=specs, out_specs=[pl.Bloc...  53.3 us
    ppermute x34, starting transfers between devices, swap(): return lax.ppermute(values, axis, [(at, at ^ bit) for at in range(size)])  31.9 us
    all_gather x1, blocking collectives, body(): tok = lax.all_gather(packed, 'cols', axis=0, tiled=True)  22.9 us
    all_gather x1, blocking collectives, body(): cot = lax.all_gather(after(packed_two, tok), 'cols', axis=0, tiled=True)  21 us
    all_gather x1, blocking collectives, body(): att = lax.all_gather(attended, 'cols', axis=0, tiled=True)  19 us
    ppermute x1, waiting for transfers between devices, body(): got_x = lax.ppermute(own_b, 'dp', pairs)  11.3 us
    unnamed x82, local copies, waits for them, and re-layouts  7.12 us
  transfers between devices with their start and end apart: 36, of which 12 were waited for; matrix products, arithmetic and copies ran while one was open for 2% of the time, Pallas kernels for 16%

profile of v4, /device:TPU:0, one launch (start us, length us, event | category | flops | bytes accessed | tf_op | source)
XLA Modules:
  0.0 233.5 jit_solution(15864399856356214166)
XLA Ops:
  1.2 2.6 %collective-permute-start = (bf16[192,576]{1,0:T(8,128)(2,1)}, bf16[192,576]{1,0:T(8,128)(2,1)S(1)}, u32[]{:S(2)}, u32[]{:S(2)}) collective-permute-start(bf16[192,576]{1,0:T(8,128)(2,1)} %w0.3), channel_id=1, source_target_pairs={{0,8},{4,12},{8,0},{12,4},{1,9},{5,13},{9,1},{13,5},{2,10},{6,14},... | collective-permute-start | bytes 663560 | tf_op jit(solution)/shard_map/ppermute | solution.py:390
  4.0 1.9 collective-permute-start.9
  6.5 2.3 shard_map.254
  8.7 22.9 %all_gather.9.tok = bf16[768,640]{1,0:T(8,128)(2,1)} all-gather(bf16[192,640]{1,0:T(8,128)(2,1)} %get-tuple-element.77), channel_id=1, replica_groups=mesh['dp'=2,'rows'=4,'cols'=4] {'cols'}, dimensions={0}, use_global_device_ids=true | all-gather | bytes 1228800 | tf_op jit(solution)/shard_map/all_gather | solution.py:465
  31.6 21.0 %all_gather.10.cot = bf16[768,640]{1,0:T(8,128)(2,1)} all-gather(bf16[192,640]{1,0:T(8,128)(2,1)S(1)} %copy-done.20), channel_id=1, replica_groups=mesh['dp'=2,'rows'=4,'cols'=4] {'cols'}, dimensions={0}, use_global_device_ids=true | all-gather | bytes 1228800 | tf_op jit(solution)/shard_map/all_gather | solution.py:468
  52.6 1.9 mix_pack.1.m0
  57.3 5.7 %shard_map.255 = (bf16[768,512]{1,0:T(8,128)(2,1)}, f32[2,512]{1,0:T(2,128)}, bf16[576,512]{1,0:T(8,128)(2,1)}, bf16[192,512]{1,0:T(8,128)(2,1)}, f32[3,512]{1,0:T(4,128)}) custom-call(s32[2]{0:T(128)} %pad_add_fusion.here, bf16[768,640]{1,0:T(8,128)(2,1)} %all_gather.9.tok, bf16[192,576]{1,0:T(8,128)(2,1)} %w0.3, bf16[192,576]{1,0:T(8,128)(2,1)} %copy-done.4, ...), custom_call_target="tpu_custom_call" | custom-call | flops 452984832 | bytes 3456520 | tf_op jit(solution)/shard_map/pallas_call | solution.py:69
  64.2 19.0 %all_gather.11.att = bf16[768,512]{1,0:T(8,128)(2,1)} all-gather(bf16[192,512]{1,0:T(8,128)(2,1)} %get-tuple-element.82.att), channel_id=1, replica_groups=mesh['dp'=2,'rows'=4,'cols'=4] {'cols'}, dimensions={0}, use_global_device_ids=true | all-gather | bytes 983040 | tf_op jit(solution)/shard_map/all_gather | solution.py:486
  84.9 9.0 %shard_map.256 = (bf16[768,512]{1,0:T(8,128)(2,1)}, bf16[768,512]{1,0:T(8,128)(2,1)}, bf16[768,512]{1,0:T(8,128)(2,1)}, bf16[768,512]{1,0:T(8,128)(2,1)}, bf16[7...) custom-call(s32[2]{0:T(128)} %pad_add_fusion.here, ...), custom_call_target="tpu_custom_call" | custom-call | flops 2415919104 | bytes 12410888 | tf_op jit(solution)/shard_map/pallas_call | solution.py:69
  93.9 5.9 %shard_map.257 = (bf16[384,1536]{1,0:T(8,128)(2,1)}, f32[384,1536]{1,0:T(8,128)}, bf16[384,512]{1,0:T(8,128)(2,1)}, f32[384,512]{1,0:T(8,128)}) custom-call(s32[2]{0:T(128)} %pad_add_fusion.here, bf16[768,512]{1,0:T(8,128)(2,1)} %get-tuple-element.85.grad_final, bf16[768,512]{1,0:T(8,128)(2,1)} %get-tuple-element.86.active, ...), custom_call_target="tpu_custom_call" | custom-call | flops 1811939328 | bytes 9043976 | tf_op jit(solution)/shard_map/pallas_call | solution.py:69
  99.9 2.2 collective-permute-start.13
  102.2 2.1 collective-permute-start.14
  105.3 3.3 %shard_map.258 = (f32[192,1536]{1,0:T(8,128)}, bf16[192,1536]{1,0:T(8,128)(2,1)}) custom-call(s32[2]{0:T(128)} %pad_add_fusion.here, f32[384,1536]{1,0:T(8,128)} %get-tuple-element.94.keep, bf16[384,1536]{1,0:T(8,128)(2,1)} %copy-done.2), custom_call_target="tpu_custom_call" | custom-call | bytes 5308424 | tf_op jit(solution)/shard_map/pallas_call | solution.py:69
  108.6 2.1 collective-permute-done.12.r1
  110.7 6.4 %collective-permute-done.13.r2 = bf16[768,128]{1,0:T(8,128)(2,1)S(1)} collective-permute-done((bf16[768,128]{1,0:T(8,128)(2,1)S(1)}, bf16[768,128]{1,0:T(8,128)(2,1)S(1)}, u32[]{:S(2)}, u32[]{:S(2)}) %collective-permute-start.13) | collective-permute-done | bytes 196640 | tf_op jit(solution)/shard_map/ppermute | solution.py:390
  118.7 4.2 %shard_map.259 = (f32[768,128]{1,0:T(8,128)}, bf16[768,128]{1,0:T(8,128)(2,1)}, f32[768,8]{1,0:T(8,128)}, bf16[192,128]{1,0:T(8,128)(2,1)}, bf16[192,128]{1,0:T(...) custom-call(s32[2]{0:T(128)} %pad_add_fusion.here, bf16[768,640]{1,0:T(8,128)(2,1)} %all_gather.9.tok, ...), custom_call_target="tpu_custom_call" | custom-call | flops 150994944 | bytes 5152776 | tf_op jit(solution)/shard_map/pallas_call | solution.py:69
  123.0 4.2 %collective-permute-start.18 = (bf16[192,128]{1,0:T(8,128)(2,1)}, bf16[192,128]{1,0:T(8,128)(2,1)S(1)}, u32[]{:S(2)}, u32[]{:S(2)}) collective-permute-start(bf16[192,128]{1,0:T(8,128)(2,1)} %get-tuple-element.114), channel_id=1, source_target_pairs={{0,1},{1,0},{2,3},{3,2},{4,5},{5,4},{6,7},{7,6},{8,9},{9,8},{10,11... | collective-permute-start | bytes 147464 | tf_op jit(solution)/shard_map/ppermute | solution.py:390
  135.0 7.4 %shard_map.261 = (bf16[576,512]{1,0:T(8,128)(2,1)}, f32[384,1]{1,0:T(8,128)}, f32[208,512]{1,0:T(8,128)}, bf16[208,512]{1,0:T(8,128)(2,1)}, bf16[208,512]{1,0:T(8,128)(2,1)}, /*index=5*/bf16[208,512]{1,0:T(8,128)(2,1)}) custom-call(s32[2]{0:T(128)} %pad_add_fusion.here, bf16[768,640]{1,0:T(8,128)(2,1)} %all_gather.9.tok, f32[2,512]{1,0:T(2,128)} %get-tuple-element.110.stats, ...), custom_call_target="tpu_custom_call" | custom-call | flops 452984832 | bytes 4939272 | tf_op jit(solution)/shard_map/pallas_call | solution.py:69
  142.4 2.2 collective-permute-start.22
  145.0 2.1 collective-permute-start.24
  149.6 3.5 %collective-permute-done.22.g1 = bf16[208,512]{1,0:T(8,128)(2,1)S(1)} collective-permute-done((bf16[208,512]{1,0:T(8,128)(2,1)}, bf16[208,512]{1,0:T(8,128)(2,1)S(1)}, u32[]{:S(2)}, u32[]{:S(2)}) %collective-permute-start.22) | collective-permute-done | bytes 213024 | tf_op jit(solution)/shard_map/ppermute | solution.py:390
  153.1 2.2 shard_map.260
  155.3 16.5 %collective-permute-done.23.g2 = bf16[208,512]{1,0:T(8,128)(2,1)S(1)} collective-permute-done((bf16[208,512]{1,0:T(8,128)(2,1)}, bf16[208,512]{1,0:T(8,128)(2,1)S(1)}, u32[]{:S(2)}, u32[]{:S(2)}) %collective-permute-start.23) | collective-permute-done | bytes 213024 | tf_op jit(solution)/shard_map/ppermute | solution.py:390
  171.8 2.3 shard_map.262.rest
  174.7 2.1 shard_map.263
  180.5 7.3 %collective-permute-done.29.h2 = bf16[768,128]{1,0:T(8,128)(2,1)S(1)} collective-permute-done((bf16[768,128]{1,0:T(8,128)(2,1)S(1)}, bf16[768,128]{1,0:T(8,128)(2,1)S(1)}, u32[]{:S(2)}, u32[]{:S(2)}) %collective-permute-start.29) | collective-permute-done | bytes 196640 | tf_op jit(solution)/shard_map/ppermute | solution.py:390
  188.5 3.2 %shard_map.264 = bf16[384,768]{1,0:T(8,128)(2,1)} custom-call(s32[2]{0:T(128)} %pad_add_fusion.here, bf16[768,512]{1,0:T(8,128)(2,1)} %get-tuple-element.132.normed, bf16[576,512]{1,0:T(8,128)(2,1)} %get-tuple-element.133.grad_proj, bf16[192,512]{1,0:T(8,128)(2,1)} %get-tuple-element.82.att, bf16[768,128]{1,0:T(8,128)(2,1)} %get-tuple-element.106.h0, ...), custom_call_target="tpu_custom_call" | custom-call | flops 301989888 | bytes 2949128 | tf_op jit(solution)/shard_map/pallas_call | solution.py:69
  194.6 13.3 %collective-permute-done.27 = f32[8,768]{1,0:T(8,128)S(1)} collective-permute-done((f32[8,768]{1,0:T(8,128)S(1)}, f32[8,768]{1,0:T(8,128)S(1)}, u32[]{:S(2)}, u32[]{:S(2)}) %collective-permute-start.27) | collective-permute-done | bytes 24608 | tf_op jit(solution)/shard_map/ppermute | solution.py:390
  210.6 3.5 %shard_map.265 = (f32[192,768]{1,0:T(8,128)}, bf16[192,768]{1,0:T(8,128)(2,1)}, bf16[192,768]{1,0:T(8,128)(2,1)}) custom-call(s32[2]{0:T(128)} %pad_add_fusion.here, bf16[768,512]{1,0:T(8,128)(2,1)} %get-tuple-element.132.normed, bf16[576,512]{1,0:T(8,128)(2,1)} %get-tuple-element.133.grad_proj, bf16[192,512]{1,0:T(8,128)(2,1)} %get-tuple-element.82.att, ...), custom_call_target="tpu_custom_call" | custom-call | flops 301989888 | bytes 4128776 | tf_op jit(solution)/shard_map/pallas_call | solution.py:69
  214.1 2.4 %collective-permute-start.34 = (bf16[192,768]{1,0:T(8,128)(2,1)}, bf16[192,768]{1,0:T(8,128)(2,1)S(1)}, u32[]{:S(2)}, u32[]{:S(2)}) collective-permute-start(bf16[192,768]{1,0:T(8,128)(2,1)} %get-tuple-element.135), channel_id=1, source_target_pairs={{0,24},{4,28},{8,16},{12,20},{16,8},{20,12},{24,0},{28,4},{1,25},{... | collective-permute-start | bytes 884744 | tf_op jit(solution)/shard_map/ppermute | solution.py:575
  218.8 11.3 %collective-permute-done.33.got_x = bf16[192,768]{1,0:T(8,128)(2,1)S(1)} collective-permute-done((bf16[192,768]{1,0:T(8,128)(2,1)}, bf16[192,768]{1,0:T(8,128)(2,1)S(1)}, u32[]{:S(2)}, u32[]{:S(2)}) %collective-permute-start.33) | collective-permute-done | bytes 294944 | tf_op jit(solution)/shard_map/ppermute | solution.py:574
  231.1 2.4 %shard_map.266 = (f32[192,576]{1,0:T(8,128)}, f32[192,192]{1,0:T(8,128)}) custom-call(s32[2]{0:T(128)} %pad_add_fusion.here, f32[192,768]{1,0:T(8,128)} %get-tuple-element.134.own, bf16[192,768]{1,0:T(8,128)(2,1)} %copy-done.18, bf16[192,768]{1,0:T(8,128)(2,1)} %copy-done.19, bf16[192,768]{1,0:T(8,128)(2,1)} %copy-done.17), custom_call_target="tpu_custom_call" | custom-call | bytes 2064392 | tf_op jit(solution)/shard_map/pallas_call | solution.py:69
  (151 shorter events, 34.2 us)
Async XLA Ops:
  0.6 53.9 %collective-permute-start.1 = (bf16[192,576]{1,0:T(8,128)(2,1)}, bf16[192,576]{1,0:T(8,128)(2,1)S(1)}, u32[]{:S(2)}, u32[]{:S(2)}) collective-permute-start(bf16[192,576]{1,0:T(8,128)(2,1)} %w0.3), channel_id=1, source_target_pairs={{0,4},{4,0},{8,12},{12,8},{1,5},{5,1},{9,13},{13,9},{2,6},{6,2},{1... | collective-permute-start | bytes 663560 | tf_op jit(solution)/shard_map/ppermute | solution.py:390
  1.2 53.9 %collective-permute-start = (bf16[192,576]{1,0:T(8,128)(2,1)}, bf16[192,576]{1,0:T(8,128)(2,1)S(1)}, u32[]{:S(2)}, u32[]{:S(2)}) collective-permute-start(bf16[192,576]{1,0:T(8,128)(2,1)} %w0.3), channel_id=1, source_target_pairs={{0,8},{4,12},{8,0},{12,4},{1,9},{5,13},{9,1},{13,5},{2,10},{6,14},... | collective-permute-start | bytes 663560 | tf_op jit(solution)/shard_map/ppermute | solution.py:390
  3.8 59.2 %collective-permute-start.6 = (bf16[192,768]{1,0:T(8,128)(2,1)}, bf16[192,768]{1,0:T(8,128)(2,1)S(1)}, u32[]{:S(2)}, u32[]{:S(2)}) collective-permute-start(bf16[192,768]{1,0:T(8,128)(2,1)} %u0.1), channel_id=1, source_target_pairs={{0,8},{4,12},{8,0},{12,4},{1,9},{5,13},{9,1},{13,5},{2,10},{6,14},... | collective-permute-start | bytes 884744 | tf_op jit(solution)/shard_map/ppermute | solution.py:390
  3.9 59.4 %collective-permute-start.7 = (bf16[192,768]{1,0:T(8,128)(2,1)}, bf16[192,768]{1,0:T(8,128)(2,1)S(1)}, u32[]{:S(2)}, u32[]{:S(2)}) collective-permute-start(bf16[192,768]{1,0:T(8,128)(2,1)} %u0.1), channel_id=1, source_target_pairs={{0,4},{4,0},{8,12},{12,8},{1,5},{5,1},{9,13},{13,9},{2,6},{6,2},{1... | collective-permute-start | bytes 884744 | tf_op jit(solution)/shard_map/ppermute | solution.py:390
  4.0 59.7 %collective-permute-start.9 = (bf16[192,768]{1,0:T(8,128)(2,1)}, bf16[192,768]{1,0:T(8,128)(2,1)S(1)}, u32[]{:S(2)}, u32[]{:S(2)}) collective-permute-start(bf16[192,768]{1,0:T(8,128)(2,1)} %d0.1), channel_id=1, source_target_pairs={{0,8},{4,12},{8,0},{12,4},{1,9},{5,13},{9,1},{13,5},{2,10},{6,14},... | collective-permute-start | bytes 884744 | tf_op jit(solution)/shard_map/ppermute | solution.py:390
  54.5 9.2 %collective-permute-start.3 = (bf16[768,192]{1,0:T(8,128)(2,1)}, bf16[768,192]{1,0:T(8,128)(2,1)S(1)}, u32[]{:S(2)}, u32[]{:S(2)}) collective-permute-start(bf16[768,192]{1,0:T(8,128)(2,1)} %mix_pack.1.m0), channel_id=1, source_target_pairs={{0,8},{4,12},{8,0},{12,4},{1,9},{5,13},{9,1},{13,5},{2,10},{6,14},... | collective-permute-start | bytes 884744 | tf_op jit(solution)/shard_map/ppermute | solution.py:390
  56.6 26.6 %collective-permute-start.10 = (bf16[192,768]{1,0:T(8,128)(2,1)S(1)}, bf16[192,768]{1,0:T(8,128)(2,1)}, u32[]{:S(2)}, u32[]{:S(2)}) collective-permute-start(bf16[192,768]{1,0:T(8,128)(2,1)S(1)} %copy-done.32), channel_id=1, source_target_pairs={{0,4},{4,0},{8,12},{12,8},{1,5},{5,1},{9,13},{13,9},{2,6},{6,2},{1... | collective-permute-start | bytes 884744 | tf_op jit(solution)/shard_map/ppermute | solution.py:390
  63.0 20.1 %collective-permute-start.4 = (bf16[768,192]{1,0:T(8,128)(2,1)S(1)}, bf16[768,192]{1,0:T(8,128)(2,1)S(1)}, u32[]{:S(2)}, u32[]{:S(2)}) collective-permute-start(bf16[768,192]{1,0:T(8,128)(2,1)S(1)} %copy-done), channel_id=1, source_target_pairs={{0,4},{4,0},{8,12},{12,8},{1,5},{5,1},{9,13},{13,9},{2,6},{6,2},{1... | collective-permute-start | bytes 884744 | tf_op jit(solution)/shard_map/ppermute | solution.py:390
  63.3 19.9 %collective-permute-start.8 = (bf16[192,768]{1,0:T(8,128)(2,1)S(1)}, bf16[192,768]{1,0:T(8,128)(2,1)S(1)}, u32[]{:S(2)}, u32[]{:S(2)}) collective-permute-start(bf16[192,768]{1,0:T(8,128)(2,1)S(1)} %collective-permute-done.6.u1), channel_id=1, source_target_pairs={{0,4},{4,0},{8,12},{12,8},{1,5},{5,1},{9,13},{13,9},{2,6},{6,2},{1... | collective-permute-start | bytes 884744 | tf_op jit(solution)/shard_map/ppermute | solution.py:390
  63.6 19.6 %collective-permute-start.11 = (bf16[192,768]{1,0:T(8,128)(2,1)S(1)}, bf16[192,768]{1,0:T(8,128)(2,1)S(1)}, u32[]{:S(2)}, u32[]{:S(2)}) collective-permute-start(bf16[192,768]{1,0:T(8,128)(2,1)S(1)} %collective-permute-done.9.d1), channel_id=1, source_target_pairs={{0,4},{4,0},{8,12},{12,8},{1,5},{5,1},{9,13},{13,9},{2,6},{6,2},{1... | collective-permute-start | bytes 884744 | tf_op jit(solution)/shard_map/ppermute | solution.py:390
  63.8 20.2 %collective-permute-start.5 = (bf16[768,192]{1,0:T(8,128)(2,1)S(1)}, bf16[768,192]{1,0:T(8,128)(2,1)S(1)}, u32[]{:S(2)}, u32[]{:S(2)}) collective-permute-start(bf16[768,192]{1,0:T(8,128)(2,1)S(1)} %collective-permute-done.3.m1), channel_id=1, source_target_pairs={{0,4},{4,0},{8,12},{12,8},{1,5},{5,1},{9,13},{13,9},{2,6},{6,2},{1... | collective-permute-start | bytes 884744 | tf_op jit(solution)/shard_map/ppermute | solution.py:390
  99.8 10.9 %collective-permute-start.12 = (bf16[768,128]{1,0:T(8,128)(2,1)S(1)}, bf16[768,128]{1,0:T(8,128)(2,1)S(1)}, u32[]{:S(2)}, u32[]{:S(2)}) collective-permute-start(bf16[768,128]{1,0:T(8,128)(2,1)S(1)} %copy-done.40), channel_id=1, source_target_pairs={{0,1},{1,0},{2,3},{3,2},{4,5},{5,4},{6,7},{7,6},{8,9},{9,8},{10,11... | collective-permute-start | bytes 589832 | tf_op jit(solution)/shard_map/ppermute | solution.py:390
  99.9 17.2 %collective-permute-start.13 = (bf16[768,128]{1,0:T(8,128)(2,1)S(1)}, bf16[768,128]{1,0:T(8,128)(2,1)S(1)}, u32[]{:S(2)}, u32[]{:S(2)}) collective-permute-start(bf16[768,128]{1,0:T(8,128)(2,1)S(1)} %copy-done.39), channel_id=1, source_target_pairs={{0,2},{1,3},{2,0},{3,1},{4,6},{5,7},{6,4},{7,5},{8,10},{9,11},{10,... | collective-permute-start | bytes 589832 | tf_op jit(solution)/shard_map/ppermute | solution.py:390
  102.2 15.0 %collective-permute-start.14 = (bf16[768,128]{1,0:T(8,128)(2,1)S(1)}, bf16[768,128]{1,0:T(8,128)(2,1)S(1)}, u32[]{:S(2)}, u32[]{:S(2)}) collective-permute-start(bf16[768,128]{1,0:T(8,128)(2,1)S(1)} %copy-done.38), channel_id=1, source_target_pairs={{0,3},{1,2},{2,1},{3,0},{4,7},{5,6},{6,5},{7,4},{8,11},{9,10},{10,... | collective-permute-start | bytes 589832 | tf_op jit(solution)/shard_map/ppermute | solution.py:390
  117.1 14.5 %collective-permute-start.21 = (bf16[192,1536]{1,0:T(8,128)(2,1)}, bf16[192,1536]{1,0:T(8,128)(2,1)S(1)}, u32[]{:S(2)}, u32[]{:S(2)}) collective-permute-start(bf16[192,1536]{1,0:T(8,128)(2,1)} %get-tuple-element.118), channel_id=1, source_target_pairs={{0,8},{4,12},{8,0},{12,4},{1,9},{5,13},{9,1},{13,5},{2,10},{6,14},... | collective-permute-start | bytes 1769480 | tf_op jit(solution)/shard_map/ppermute | solution.py:390
  123.0 8.8 %collective-permute-start.18 = (bf16[192,128]{1,0:T(8,128)(2,1)}, bf16[192,128]{1,0:T(8,128)(2,1)S(1)}, u32[]{:S(2)}, u32[]{:S(2)}) collective-permute-start(bf16[192,128]{1,0:T(8,128)(2,1)} %get-tuple-element.114), channel_id=1, source_target_pairs={{0,1},{1,0},{2,3},{3,2},{4,5},{5,4},{6,7},{7,6},{8,9},{9,8},{10,11... | collective-permute-start | bytes 147464 | tf_op jit(solution)/shard_map/ppermute | solution.py:390
  127.7 6.6 %collective-permute-start.20 = (bf16[192,128]{1,0:T(8,128)(2,1)}, bf16[192,128]{1,0:T(8,128)(2,1)S(1)}, u32[]{:S(2)}, u32[]{:S(2)}) collective-permute-start(bf16[192,128]{1,0:T(8,128)(2,1)} %get-tuple-element.116), channel_id=1, source_target_pairs={{0,3},{1,2},{2,1},{3,0},{4,7},{5,6},{6,5},{7,4},{8,11},{9,10},{10,... | collective-permute-start | bytes 147464 | tf_op jit(solution)/shard_map/ppermute | solution.py:390
  129.6 19.2 %collective-permute-start.16 = (bf16[384,512]{1,0:T(8,128)(2,1)S(1)}, bf16[384,512]{1,0:T(8,128)(2,1)S(1)}, u32[]{:S(2)}, u32[]{:S(2)}) collective-permute-start(bf16[384,512]{1,0:T(8,128)(2,1)S(1)} %copy-done.31), channel_id=1, source_target_pairs={{0,1},{1,0},{2,3},{3,2},{4,5},{5,4},{6,7},{7,6},{8,9},{9,8},{10,11... | collective-permute-start | bytes 1179656 | tf_op jit(solution)/shard_map/ppermute | solution.py:390
  142.4 10.7 %collective-permute-start.22 = (bf16[208,512]{1,0:T(8,128)(2,1)}, bf16[208,512]{1,0:T(8,128)(2,1)S(1)}, u32[]{:S(2)}, u32[]{:S(2)}) collective-permute-start(bf16[208,512]{1,0:T(8,128)(2,1)} %get-tuple-element.125), channel_id=1, source_target_pairs={{0,1},{1,0},{2,3},{3,2},{4,5},{5,4},{6,7},{7,6},{8,9},{9,8},{10,11... | collective-permute-start | bytes 638984 | tf_op jit(solution)/shard_map/ppermute | solution.py:390
  144.6 27.1 %collective-permute-start.23 = (bf16[208,512]{1,0:T(8,128)(2,1)}, bf16[208,512]{1,0:T(8,128)(2,1)S(1)}, u32[]{:S(2)}, u32[]{:S(2)}) collective-permute-start(bf16[208,512]{1,0:T(8,128)(2,1)} %get-tuple-element.126), channel_id=1, source_target_pairs={{0,2},{1,3},{2,0},{3,1},{4,6},{5,7},{6,4},{7,5},{8,10},{9,11},{10,... | collective-permute-start | bytes 638984 | tf_op jit(solution)/shard_map/ppermute | solution.py:390
  145.0 29.1 %collective-permute-start.24 = (bf16[208,512]{1,0:T(8,128)(2,1)}, bf16[208,512]{1,0:T(8,128)(2,1)S(1)}, u32[]{:S(2)}, u32[]{:S(2)}) collective-permute-start(bf16[208,512]{1,0:T(8,128)(2,1)} %get-tuple-element.127), channel_id=1, source_target_pairs={{0,3},{1,2},{2,1},{3,0},{4,7},{5,6},{6,5},{7,4},{8,11},{9,10},{10,... | collective-permute-start | bytes 638984 | tf_op jit(solution)/shard_map/ppermute | solution.py:390
  147.1 33.4 %collective-permute-start.30 = (bf16[768,128]{1,0:T(8,128)(2,1)S(1)}, bf16[768,128]{1,0:T(8,128)(2,1)S(1)}, u32[]{:S(2)}, u32[]{:S(2)}) collective-permute-start(bf16[768,128]{1,0:T(8,128)(2,1)S(1)} %copy-done.6), channel_id=1, source_target_pairs={{0,3},{1,2},{2,1},{3,0},{4,7},{5,6},{6,5},{7,4},{8,11},{9,10},{10,... | collective-permute-start | bytes 589832 | tf_op jit(solution)/shard_map/ppermute | solution.py:390
  148.8 39.0 %collective-permute-start.29 = (bf16[768,128]{1,0:T(8,128)(2,1)S(1)}, bf16[768,128]{1,0:T(8,128)(2,1)S(1)}, u32[]{:S(2)}, u32[]{:S(2)}) collective-permute-start(bf16[768,128]{1,0:T(8,128)(2,1)S(1)} %copy-done.6), channel_id=1, source_target_pairs={{0,2},{1,3},{2,0},{3,1},{4,6},{5,7},{6,4},{7,5},{8,10},{9,11},{10,... | collective-permute-start | bytes 589832 | tf_op jit(solution)/shard_map/ppermute | solution.py:390
  153.1 34.7 %collective-permute-start.28 = (bf16[768,128]{1,0:T(8,128)(2,1)S(1)}, bf16[768,128]{1,0:T(8,128)(2,1)S(1)}, u32[]{:S(2)}, u32[]{:S(2)}) collective-permute-start(bf16[768,128]{1,0:T(8,128)(2,1)S(1)} %copy-done.6), channel_id=1, source_target_pairs={{0,1},{1,0},{2,3},{3,2},{4,5},{5,4},{6,7},{7,6},{8,9},{9,8},{10,11... | collective-permute-start | bytes 589832 | tf_op jit(solution)/shard_map/ppermute | solution.py:390
  171.8 22.1 %collective-permute-start.17 = (bf16[192,512]{1,0:T(8,128)(2,1)}, bf16[192,512]{1,0:T(8,128)(2,1)S(1)}, u32[]{:S(2)}, u32[]{:S(2)}) collective-permute-start(bf16[192,512]{1,0:T(8,128)(2,1)} %get-tuple-element.109), channel_id=1, source_target_pairs={{0,2},{1,3},{2,0},{3,1},{4,6},{5,7},{6,4},{7,5},{8,10},{9,11},{10,... | collective-permute-start | bytes 589832 | tf_op jit(solution)/shard_map/ppermute | solution.py:390
  179.0 14.2 %collective-permute-start.26 = (f32[8,768]{1,0:T(8,128)S(1)}, f32[8,768]{1,0:T(8,128)S(1)}, u32[]{:S(2)}, u32[]{:S(2)}) collective-permute-start(f32[8,768]{1,0:T(8,128)S(1)} %add.37), channel_id=1, source_target_pairs={{0,8},{4,12},{8,0},{12,4},{1,9},{5,13},{9,1},{13,5},{2,10},{6,14},... | collective-permute-start | bytes 73736 | tf_op jit(solution)/shard_map/ppermute | solution.py:390
  191.7 18.1 %collective-permute-start.31 = (bf16[384,768]{1,0:T(8,128)(2,1)}, bf16[384,768]{1,0:T(8,128)(2,1)S(1)}, u32[]{:S(2)}, u32[]{:S(2)}) collective-permute-start(bf16[384,768]{1,0:T(8,128)(2,1)} %shard_map.264), channel_id=1, source_target_pairs={{0,4},{4,0},{8,12},{12,8},{1,5},{5,1},{9,13},{13,9},{2,6},{6,2},{1... | collective-permute-start | bytes 1769480 | tf_op jit(solution)/shard_map/ppermute | solution.py:390
  191.7 25.8 %collective-permute-start.35 = (bf16[192,1536]{1,0:T(8,128)(2,1)S(1)}, bf16[192,1536]{1,0:T(8,128)(2,1)S(1)}, u32[]{:S(2)}, u32[]{:S(2)}) collective-permute-start(bf16[192,1536]{1,0:T(8,128)(2,1)S(1)} %convert_add_fusion.1), channel_id=1, source_target_pairs={{0,16},{16,0},{1,17},{17,1},{2,18},{18,2},{3,19},{19,3},{4,20},{20... | collective-permute-start | bytes 1769480 | tf_op jit(solution)/shard_map/ppermute | solution.py:390
  193.2 14.8 %collective-permute-start.27 = (f32[8,768]{1,0:T(8,128)S(1)}, f32[8,768]{1,0:T(8,128)S(1)}, u32[]{:S(2)}, u32[]{:S(2)}) collective-permute-start(f32[8,768]{1,0:T(8,128)S(1)} %add.38), channel_id=1, source_target_pairs={{0,16},{16,0},{1,17},{17,1},{2,18},{18,2},{3,19},{19,3},{4,20},{20... | collective-permute-start | bytes 73736 | tf_op jit(solution)/shard_map/ppermute | solution.py:390
  214.1 16.1 %collective-permute-start.34 = (bf16[192,768]{1,0:T(8,128)(2,1)}, bf16[192,768]{1,0:T(8,128)(2,1)S(1)}, u32[]{:S(2)}, u32[]{:S(2)}) collective-permute-start(bf16[192,768]{1,0:T(8,128)(2,1)} %get-tuple-element.135), channel_id=1, source_target_pairs={{0,24},{4,28},{8,16},{12,20},{16,8},{20,12},{24,0},{28,4},{1,25},{... | collective-permute-start | bytes 884744 | tf_op jit(solution)/shard_map/ppermute | solution.py:575
  216.5 13.7 %collective-permute-start.32 = (bf16[192,768]{1,0:T(8,128)(2,1)}, bf16[192,768]{1,0:T(8,128)(2,1)S(1)}, u32[]{:S(2)}, u32[]{:S(2)}) collective-permute-start(bf16[192,768]{1,0:T(8,128)(2,1)} %get-tuple-element.135), channel_id=1, source_target_pairs={{0,8},{4,12},{8,0},{12,4},{1,9},{5,13},{9,1},{13,5},{2,10},{6,14},... | collective-permute-start | bytes 884744 | tf_op jit(solution)/shard_map/ppermute | solution.py:390
  217.0 13.1 %collective-permute-start.33 = (bf16[192,768]{1,0:T(8,128)(2,1)}, bf16[192,768]{1,0:T(8,128)(2,1)S(1)}, u32[]{:S(2)}, u32[]{:S(2)}) collective-permute-start(bf16[192,768]{1,0:T(8,128)(2,1)} %get-tuple-element.136), channel_id=1, source_target_pairs={{0,16},{16,0},{1,17},{17,1},{2,18},{18,2},{3,19},{19,3},{4,20},{20... | collective-permute-start | bytes 884744 | tf_op jit(solution)/shard_map/ppermute | solution.py:574
  (45 other events, 284.2 us)

commit v5 on v4

--- a/solution.py
+++ b/solution.py
@@ -57,23 +57,25 @@
 
 
 def norm_cols(tok_ref, count, which):
-    start = tok_ref.shape[0] // 4 - 128
+    start = tok_ref.shape[0] // 8
     cols = tok_ref[:, count : tok_ref.shape[1]].astype(F32)[:, start:]
     return [cols[:, k : k + 1] + cols[:, k + 5 : k + 6] + cols[:, k + 10 : k + 11] for k in which]
 
 
-def run(kernel, outs, ins, scratch=(), flops=0):
+def run(kernel, outs, ins, scratch=(), flops=0, hold=True):
     specs = [pl.BlockSpec(memory_space=pltpu.SMEM)]
     specs += [pl.BlockSpec(memory_space=pltpu.VMEM)] * (len(ins) - 1)
     size = sum(math.prod(value.shape) * value.dtype.itemsize for value in list(ins) + list(outs))
+    held = [pltpu.with_memory_space_constraint(value, pltpu.VMEM) if hold else value for value in ins[1:]]
     return pl.pallas_call(
         kernel,
-        out_shape=outs,
+        out_shape=[pltpu.VMEM(value.shape, value.dtype) for value in outs],
         in_specs=specs,
         out_specs=[pl.BlockSpec(memory_space=pltpu.VMEM)] * len(outs),
         scratch_shapes=list(scratch),
         cost_estimate=pl.CostEstimate(flops=flops, transcendentals=0, bytes_accessed=size),
-    )(*ins)
+        compiler_params=pltpu.CompilerParams(vmem_limit_bytes=24 * 1024 * 1024),
+    )(ins[0], *held)
 
 
 def shaped(shape, dtype):
@@ -84,7 +86,7 @@
     return jnp.broadcast_to(row, (128, row.shape[1])).T[:, :1]
 
 
-def pack_kernel(here, tok, mix, cot, g1, b1, bm, g2, b2, down, seg, packed, packed_two, down_col, seg_col):
+def pack_kernel(here, tok, mix, g1, b1, bm, g2, b2, down, seg, packed, down_col, seg_col):
     feat, count = tok.shape
     rows = jnp.concatenate([ref[...] for ref in (g1, b1, bm, g2, b2)], axis=0)
     high = rows.astype(BF16).astype(F32)
@@ -92,12 +94,11 @@
     low = rows - high - middle
     used = 3 * rows.shape[0]
     norms = jnp.concatenate([high, middle, low, jnp.zeros((128 - used, feat), F32)], axis=0).T
+    half = feat // 2
+    values = mix[...].astype(F32)
+    values = jnp.where(here[2] == 0, values[:, :half], values[:, half:])
     packed[:, :count] = tok[...]
-    packed[:, count : count + 128] = jnp.concatenate(
-        [mix[:, 128:].astype(F32), norms[:, : 128 - (feat - 128)]], axis=1
-    ).astype(BF16)
-    packed_two[:, :count] = cot[...]
-    packed_two[:, count:] = mix[:, :128]
+    packed[:, count:] = jnp.concatenate([values, norms[:, : 128 - half]], axis=1).astype(BF16)
     down_col[...] = column(down[...])
     seg_col[...] = column(seg[...].astype(F32)).astype(jnp.int32)
 
@@ -135,26 +136,16 @@
             totals[pl.ds(head, 1), cols] = log_total
 
 
-def mix_pack_kernel(tok, cot, out):
-    out[:, :128] = cot[...]
-    out[:, 128:] = tok[:, : out.shape[1] - 128]
-
-
-def mix_pack(tok, cot, feat):
-    width, lanes = tok.shape
-    last = pl.BlockSpec((width, 128), lambda step: (0, lanes // 128 - 1))
-    return pl.pallas_call(
-        mix_pack_kernel,
-        grid=(1,),
-        out_shape=shaped((width, feat), BF16),
-        in_specs=[last, last],
-        out_specs=pl.BlockSpec((width, feat), lambda step: (0, 0)),
-        name="mix_pack",
-    )(tok, cot)
+def mix_pack_kernel(here, own, got, out):
+    half = out.shape[1] // 2
+    mine, other = own[...].astype(F32)[:, :half], got[...].astype(F32)[:, :half]
+    first = jnp.where(here[2] == 0, mine, other)
+    second = jnp.where(here[2] == 0, other, mine)
+    out[...] = jnp.concatenate([first, second], axis=1).astype(BF16)
 
 
 def middle_kernel(
-    order, here, tok, att, m0, m1, m2, m3, u0, u1, u2, u3, d0, d1, d2, d3, cot, row, up,
+    order, here, tok, att, m0, m1, m2, m3, u0, u1, u2, u3, d0, d1, d2, d3, c0, c1, c2, c3, row, up,
     normed, grad_pre, active, grad_final, p1, p2, p3, own_two, own_hat, own_inv, own_hidden, up_sum, down_all,
     up_all, hidden,
 ):
@@ -166,7 +157,9 @@
         up_all[block(here[0] ^ value, feat), :] = piece[...]
     for value, piece in zip(order, (d0, d1, d2, d3)):
         down_all[block(here[0] ^ value, feat), :] = piece[...]
-    grad_final[...] = jnp.where(live, cot[:, :count].astype(F32), 0.0).astype(BF16)
+    for step, piece in enumerate((c0, c1, c2, c3)):
+        masked = jnp.where(live, piece[...].astype(F32), 0.0)
+        grad_final[block(here[1] ^ step, feat), :] = masked.astype(BF16)
     for value, piece in zip(order, (m0, m1, m2, m3)):
         hidden[block(here[0] ^ value, feat), :] = mm_t(piece[...], att[...])
     hidden[...] = hidden[...] + tok[:, :count].astype(F32) + bias_mix
@@ -399,7 +392,7 @@
 
 
 def make_body(n_dp, n_rows, n_cols):
-    assert n_rows == 4 and n_cols == 4
+    assert n_rows == 4 and n_cols == 4 and n_dp % 2 == 0
     far, near = 2, 1
     order = (0, far, near, far ^ near)
 
@@ -442,7 +435,8 @@
         n_hid = up_weight.shape[1]
         heads = n_qkv // (3 * HD)
         head_rows = heads * HD
-        here = jnp.stack([lax.axis_index("rows"), lax.axis_index("cols")]).astype(jnp.int32)
+        here = [lax.axis_index("rows"), lax.axis_index("cols"), lax.axis_index("dp") & 1]
+        here = jnp.stack(here).astype(jnp.int32)
         row = segment_ids.reshape(1, count)
 
         def halve(keep, got):
@@ -452,21 +446,25 @@
         qkv_y = over_rows(qkv_weight, far)
         up_y, down_y = over_rows(up_weight, far), over_rows(down_weight, far)
         qkv_c, up_c, down_c = [over_rows(value, near) for value in (qkv_weight, up_weight, down_weight)]
-        lanes = shaped((feat, count + 128), BF16)
-        packed, packed_two, down_col, seg_col = run(
+        packed, down_col, seg_col = run(
             pack_kernel,
-            (lanes, lanes, shaped((feat, 1), F32), shaped((count, 1), jnp.int32)),
-            (here, tokens, mix_weight, cotangent)
+            (shaped((feat, count + 128), BF16), shaped((feat, 1), F32), shaped((count, 1), jnp.int32)),
+            (here, tokens, mix_weight)
             + tuple(
                 value.reshape(1, -1)
                 for value in (first_gain, first_bias, mix_bias, second_gain, second_bias, down_bias, segment_ids)
             ),
+            hold=False,
         )
         tok = lax.all_gather(packed, "cols", axis=0, tiled=True)
         qkv_yc = over_rows(qkv_y, near)
         w_pieces = (qkv_weight, qkv_y, qkv_c, qkv_yc)
-        cot = lax.all_gather(after(packed_two, tok), "cols", axis=0, tiled=True)
-        mix_all = mix_pack(tok, cot, feat)
+        cot_own = after(cotangent, tok)
+        cot_z = all_over_cols((cot_own,) * 3)
+        mix_half = tok[:, count:]
+        pairs = [(at, at ^ 1) for at in range(n_dp)]
+        mix_got = lax.ppermute(mix_half, "dp", pairs)
+        (mix_all,) = run(mix_pack_kernel, (shaped((width, feat), BF16),), (here, mix_half, mix_got))
         mix_y, mix_c = over_rows(mix_all, far), over_rows(mix_all, near)
         up_yc, down_yc = over_rows(up_y, near), over_rows(down_y, near)
 
@@ -479,7 +477,7 @@
                 shaped((head_rows, count), BF16),
                 shaped((heads, count), F32),
             ),
-            (here, after(tok, mix_all)) + w_pieces + (qv_bias, row, seg_col),
+            (here, tok) + w_pieces + (qv_bias, row, seg_col),
             scratch=(pltpu.VMEM((width, n_qkv), BF16),),
             flops=2 * width * n_qkv * count,
         )
@@ -503,7 +501,9 @@
             + m_pieces
             + (up_weight, up_y, up_c, up_yc)
             + (down_weight, down_y, down_c, down_yc)
-            + (cot, row, up_bias),
+            + (cotangent,)
+            + tuple(cot_z)
+            + (row, up_bias),
             scratch=(pltpu.VMEM((width, n_hid), BF16), pltpu.VMEM((width, count), F32)),
             flops=2 * width * count * (width + 3 * n_hid),
         )
@@ -567,7 +567,6 @@
             scratch=(pltpu.VMEM((2 * feat, count), BF16), pltpu.VMEM((2 * feat, count), BF16)),
             flops=width * count * n_last,
         )
-        pairs = [(at, at ^ 1) for at in range(n_dp)]
         far_dp = [(d * n_rows + r, (d ^ 1) * n_rows + (r ^ far)) for d in range(n_dp) for r in range(n_rows)]
         got_y = over_rows(last_send, far)
         if n_dp > 1:

time: 234 us -> 218 us (0.932)
  waiting for transfers between devices: 66.9 us -> 96.4 us
  Pallas kernels: 55.2 us -> 25.8 us
  blocking collectives: 62.9 us -> 40.2 us
  starting transfers between devices: 34.9 us -> 39.9 us
    pallas_call x14, Pallas kernels: 55.2 us -> 25.8 us  [run(): pl.pallas_call(kernel, out_shape=[pltpu.VMEM(value.shape, value.dtype) fo...]
    ppermute x34 -> x37, waiting for transfers between devices: 55.5 us -> 84.8 us  [swap(): return lax.ppermute(values, axis, [(at, at ^ bit) for at in range(size)])]
    all_gather x1 -> x0, blocking collectives: 21 us -> none  [body(): cot = lax.all_gather(after(packed_two, tok), 'cols', axis=0, tiled=True)]
    ppermute x34 -> x37, starting transfers between devices: 31.9 us -> 36.3 us  [swap(): return lax.ppermute(values, axis, [(at, at ^ bit) for at in range(size)])]
    unnamed x82 -> x39, local copies, waits for them, and re-layouts: 7.12 us -> 8.82 us
  transfers between devices with their start and end apart: 36 -> 40, of which waited for: 12 -> 16; matrix products, arithmetic and copies ran while one was open for 2% -> 3% of each run, Pallas kernels for 16% -> 8%
where the time goes in v5:
time: 218 us
  waiting for transfers between devices  96.4 us (44%)
  blocking collectives  40.2 us (18%)
  starting transfers between devices  39.9 us (18%)
  Pallas kernels  25.8 us (12%)
  local copies, waits for them, and re-layouts  11.7 us (5%)
  other arithmetic  3.01 us (1%)
    ppermute x37, waiting for transfers between devices, swap(): return lax.ppermute(values, axis, [(at, at ^ bit) for at in range(size)])  84.8 us
    ppermute x37, starting transfers between devices, swap(): return lax.ppermute(values, axis, [(at, at ^ bit) for at in range(size)])  36.3 us
    pallas_call x14, Pallas kernels, run(): pl.pallas_call(kernel, out_shape=[pltpu.VMEM(value.shape, value.dtype) fo...  25.8 us
    all_gather x1, blocking collectives, body(): tok = lax.all_gather(packed, 'cols', axis=0, tiled=True)  22.1 us
    all_gather x1, blocking collectives, body(): att = lax.all_gather(attended, 'cols', axis=0, tiled=True)  18.1 us
    ppermute x1, waiting for transfers between devices, body(): got_x = lax.ppermute(own_b, 'dp', pairs)  10 us
    unnamed x39, local copies, waits for them, and re-layouts  8.82 us
  transfers between devices with their start and end apart: 40, of which 16 were waited for; matrix products, arithmetic and copies ran while one was open for 3% of the time, Pallas kernels for 8%

profile of v5, /device:TPU:0, one launch (start us, length us, event | category | flops | bytes accessed | tf_op | source)
XLA Modules:
  0.0 218.0 jit_solution(5621812115742352581)
XLA Ops:
  1.2 2.6 %collective-permute-start = (bf16[192,576]{1,0:T(8,128)(2,1)}, bf16[192,576]{1,0:T(8,128)(2,1)S(1)}, u32[]{:S(2)}, u32[]{:S(2)}) collective-permute-start(bf16[192,576]{1,0:T(8,128)(2,1)} %w0.3), channel_id=1, source_target_pairs={{0,8},{4,12},{8,0},{12,4},{1,9},{5,13},{9,1},{13,5},{2,10},{6,14},... | collective-permute-start | bytes 663560 | tf_op jit(solution)/shard_map/ppermute | solution.py:383
  11.3 22.1 %all_gather.6.tok = bf16[768,640]{1,0:T(8,128)(2,1)S(1)} all-gather(bf16[192,640]{1,0:T(8,128)(2,1)S(1)} %get-tuple-element.75), channel_id=1, replica_groups=mesh['dp'=2,'rows'=4,'cols'=4] {'cols'}, dimensions={0}, use_global_device_ids=true | all-gather | bytes 1228800 | tf_op jit(solution)/shard_map/all_gather | solution.py:459
  33.5 1.6 collective-permute-start.3
  35.0 2.6 %collective-permute-start.15 = (bf16[192,512]{1,0:T(8,128)(2,1)S(1)}, bf16[192,512]{1,0:T(8,128)(2,1)S(1)}, u32[]{:S(2)}, u32[]{:S(2)}) collective-permute-start(bf16[192,512]{1,0:T(8,128)(2,1)S(1)} %copy-done.4), channel_id=1, source_target_pairs={{0,3},{1,2},{2,1},{3,0},{4,7},{5,6},{6,5},{7,4},{8,11},{9,10},{10,... | collective-permute-start | bytes 589832 | tf_op jit(solution)/shard_map/ppermute | solution.py:383
  37.6 1.6 collective-permute-done.3.got
  40.4 3.5 %collective-permute-done.15.c3 = bf16[192,512]{1,0:T(8,128)(2,1)S(1)} collective-permute-done((bf16[192,512]{1,0:T(8,128)(2,1)S(1)}, bf16[192,512]{1,0:T(8,128)(2,1)S(1)}, u32[]{:S(2)}, u32[]{:S(2)}) %collective-permute-start.15) | collective-permute-done | bytes 196640 | tf_op jit(solution)/shard_map/ppermute | solution.py:383
  43.9 9.2 %collective-permute-done.14.c2 = bf16[192,512]{1,0:T(8,128)(2,1)S(1)} collective-permute-done((bf16[192,512]{1,0:T(8,128)(2,1)S(1)}, bf16[192,512]{1,0:T(8,128)(2,1)S(1)}, u32[]{:S(2)}, u32[]{:S(2)}) %collective-permute-start.14) | collective-permute-done | bytes 196640 | tf_op jit(solution)/shard_map/ppermute | solution.py:383
  55.1 3.9 %shard_map.255 = (bf16[768,512]{1,0:T(8,128)(2,1)S(1)}, f32[2,512]{1,0:T(2,128)S(1)}, bf16[576,512]{1,0:T(8,128)(2,1)S(1)}, bf16[192,512]{1,0:T(8,128)(2,1)S(1)}, f32[3,512]{1,0:T(4,128)S(1)}) custom-call(s32[3]{0:T(128)S(1)} %pad_add_fusion.here, bf16[768,640]{1,0:T(8,128)(2,1)S(1)} %all_gather.6.tok, bf16[192,576]{1,0:T(8,128)(2,1)S(1)} %copy-done, ...), custom_call_target="tpu_custom_call" | custom-call | flops 452984832 | bytes 3456524 | tf_op jit(solution)/shard_map/pallas_call | solution.py:70
  59.0 1.8 collective-permute-done.13.c1
  61.4 1.6 collective-permute-done.10.d1
  62.9 6.2 %collective-permute-done.4.m1 = bf16[768,192]{1,0:T(8,128)(2,1)S(1)} collective-permute-done((bf16[768,192]{1,0:T(8,128)(2,1)S(1)}, bf16[768,192]{1,0:T(8,128)(2,1)S(1)}, u32[]{:S(2)}, u32[]{:S(2)}) %collective-permute-start.4) | collective-permute-done | bytes 294944 | tf_op jit(solution)/shard_map/ppermute | solution.py:383
  69.1 18.1 %all_gather.7.att = bf16[768,512]{1,0:T(8,128)(2,1)S(1)} all-gather(bf16[192,512]{1,0:T(8,128)(2,1)S(1)} %get-tuple-element.77.att), channel_id=1, replica_groups=mesh['dp'=2,'rows'=4,'cols'=4] {'cols'}, dimensions={0}, use_global_device_ids=true | all-gather | bytes 983040 | tf_op jit(solution)/shard_map/all_gather | solution.py:484
  87.3 5.3 %shard_map.257 = (bf16[768,512]{1,0:T(8,128)(2,1)S(1)}, bf16[768,512]{1,0:T(8,128)(2,1)S(1)}, bf16[768,512]{1,0:T(8,128)(2,1)S(1)}, bf16[768,512]{1,0:T(8,128)(2...) custom-call(s32[3]{0:T(128)S(1)} %pad_add_fusion.here, ...), custom_call_target="tpu_custom_call" | custom-call | flops 2415919104 | bytes 12214284 | tf_op jit(solution)/shard_map/pallas_call | solution.py:70
  92.6 2.6 %shard_map.258 = (bf16[384,1536]{1,0:T(8,128)(2,1)S(1)}, f32[384,1536]{1,0:T(8,128)S(1)}, bf16[384,512]{1,0:T(8,128)(2,1)S(1)}, f32[384,512]{1,0:T(8,128)S(1)}) custom-call(s32[3]{0:T(128)S(1)} %pad_add_fusion.here, bf16[768,512]{1,0:T(8,128)(2,1)S(1)} %get-tuple-element.81.grad_final, bf16[768,512]{1,0:T(8,128)(2,1)S(1)} %get-tuple-element.82.active, ...), custom_call_target="tpu_custom_call" | custom-call | flops 1811939328 | bytes 9043980 | tf_op jit(solution)/shard_map/pallas_call | solution.py:70
  95.3 2.4 %collective-permute-start.17 = (bf16[768,128]{1,0:T(8,128)(2,1)S(1)}, bf16[768,128]{1,0:T(8,128)(2,1)S(1)}, u32[]{:S(2)}, u32[]{:S(2)}) collective-permute-start(bf16[768,128]{1,0:T(8,128)(2,1)S(1)} %get-tuple-element.88), channel_id=1, source_target_pairs={{0,2},{1,3},{2,0},{3,1},{4,6},{5,7},{6,4},{7,5},{8,10},{9,11},{10,... | collective-permute-start | bytes 589832 | tf_op jit(solution)/shard_map/ppermute | solution.py:383
  97.8 1.9 collective-permute-start.18
  100.5 5.7 %collective-permute-done.16.r1 = bf16[768,128]{1,0:T(8,128)(2,1)S(1)} collective-permute-done((bf16[768,128]{1,0:T(8,128)(2,1)S(1)}, bf16[768,128]{1,0:T(8,128)(2,1)S(1)}, u32[]{:S(2)}, u32[]{:S(2)}) %collective-permute-start.16) | collective-permute-done | bytes 196640 | tf_op jit(solution)/shard_map/ppermute | solution.py:383
  106.2 6.4 %collective-permute-done.17.r2 = bf16[768,128]{1,0:T(8,128)(2,1)S(1)} collective-permute-done((bf16[768,128]{1,0:T(8,128)(2,1)S(1)}, bf16[768,128]{1,0:T(8,128)(2,1)S(1)}, u32[]{:S(2)}, u32[]{:S(2)}) %collective-permute-start.17) | collective-permute-done | bytes 196640 | tf_op jit(solution)/shard_map/ppermute | solution.py:383
  113.1 1.7 shard_map.260
  114.8 4.2 %collective-permute-start.22 = (bf16[192,128]{1,0:T(8,128)(2,1)S(1)}, bf16[192,128]{1,0:T(8,128)(2,1)S(1)}, u32[]{:S(2)}, u32[]{:S(2)}) collective-permute-start(bf16[192,128]{1,0:T(8,128)(2,1)S(1)} %get-tuple-element.110), channel_id=1, source_target_pairs={{0,1},{1,0},{2,3},{3,2},{4,5},{5,4},{6,7},{7,6},{8,9},{9,8},{10,11... | collective-permute-start | bytes 147464 | tf_op jit(solution)/shard_map/ppermute | solution.py:383
  119.6 1.8 collective-permute-start.24
  122.5 3.6 %collective-permute-done.25 = bf16[192,1536]{1,0:T(8,128)(2,1)S(1)} collective-permute-done((bf16[192,1536]{1,0:T(8,128)(2,1)S(1)}, bf16[192,1536]{1,0:T(8,128)(2,1)S(1)}, u32[]{:S(2)}, u32[]{:S(2)}) %collective-permute-start.25) | collective-permute-done | bytes 589856 | tf_op jit(solution)/shard_map/ppermute | solution.py:383
  127.1 4.5 %shard_map.262 = (bf16[576,512]{1,0:T(8,128)(2,1)S(1)}, f32[384,1]{1,0:T(8,128)S(1)}, f32[208,512]{1,0:T(8,128)S(1)}, bf16[208,512]{1,0:T(8,128)(2,1)S(1)}, bf16...) custom-call(s32[3]{0:T(128)S(1)} %pad_add_fusion.here, bf16[768,640]{1,0:T(8,128)(2,1)S(1)} %all_gather.6.tok, ...), custom_call_target="tpu_custom_call" | custom-call | flops 452984832 | bytes 4939276 | tf_op jit(solution)/shard_map/pallas_call | solution.py:70
  131.6 5.4 %collective-permute-start.26 = (bf16[208,512]{1,0:T(8,128)(2,1)S(1)}, bf16[208,512]{1,0:T(8,128)(2,1)S(1)}, u32[]{:S(2)}, u32[]{:S(2)}) collective-permute-start(bf16[208,512]{1,0:T(8,128)(2,1)S(1)} %get-tuple-element.121), channel_id=1, source_target_pairs={{0,1},{1,0},{2,3},{3,2},{4,5},{5,4},{6,7},{7,6},{8,9},{9,8},{10,11... | collective-permute-start | bytes 638984 | tf_op jit(solution)/shard_map/ppermute | solution.py:383
  137.4 2.0 collective-permute-start.28
  139.4 1.8 collective-permute-start.34
  141.9 3.2 %collective-permute-done.26.g1 = bf16[208,512]{1,0:T(8,128)(2,1)S(1)} collective-permute-done((bf16[208,512]{1,0:T(8,128)(2,1)S(1)}, bf16[208,512]{1,0:T(8,128)(2,1)S(1)}, u32[]{:S(2)}, u32[]{:S(2)}) %collective-permute-start.26) | collective-permute-done | bytes 213024 | tf_op jit(solution)/shard_map/ppermute | solution.py:383
  145.8 18.1 %collective-permute-done.27.g2 = bf16[208,512]{1,0:T(8,128)(2,1)S(1)} collective-permute-done((bf16[208,512]{1,0:T(8,128)(2,1)S(1)}, bf16[208,512]{1,0:T(8,128)(2,1)S(1)}, u32[]{:S(2)}, u32[]{:S(2)}) %collective-permute-start.27) | collective-permute-done | bytes 213024 | tf_op jit(solution)/shard_map/ppermute | solution.py:383
  167.3 12.6 %collective-permute-done.33.h2 = bf16[768,128]{1,0:T(8,128)(2,1)S(1)} collective-permute-done((bf16[768,128]{1,0:T(8,128)(2,1)S(1)}, bf16[768,128]{1,0:T(8,128)(2,1)S(1)}, u32[]{:S(2)}, u32[]{:S(2)}) %collective-permute-start.33) | collective-permute-done | bytes 196640 | tf_op jit(solution)/shard_map/ppermute | solution.py:383
  183.5 1.7 add_convert_fusion
  186.0 11.6 %collective-permute-done.31 = f32[8,768]{1,0:T(8,128)S(1)} collective-permute-done((f32[8,768]{1,0:T(8,128)S(1)}, f32[8,768]{1,0:T(8,128)S(1)}, u32[]{:S(2)}, u32[]{:S(2)}) %collective-permute-start.31) | collective-permute-done | bytes 24608 | tf_op jit(solution)/shard_map/ppermute | solution.py:383
  205.5 10.0 %collective-permute-done.37.got_x = bf16[192,768]{1,0:T(8,128)(2,1)S(1)} collective-permute-done((bf16[192,768]{1,0:T(8,128)(2,1)S(1)}, bf16[192,768]{1,0:T(8,128)(2,1)S(1)}, u32[]{:S(2)}, u32[]{:S(2)}) %collective-permute-start.37) | collective-permute-done | bytes 294944 | tf_op jit(solution)/shard_map/ppermute | solution.py:573
  (116 shorter events, 35.7 us)
Async XLA Ops:
  0.6 52.9 %collective-permute-start.1 = (bf16[192,576]{1,0:T(8,128)(2,1)}, bf16[192,576]{1,0:T(8,128)(2,1)S(1)}, u32[]{:S(2)}, u32[]{:S(2)}) collective-permute-start(bf16[192,576]{1,0:T(8,128)(2,1)} %w0.3), channel_id=1, source_target_pairs={{0,4},{4,0},{8,12},{12,8},{1,5},{5,1},{9,13},{13,9},{2,6},{6,2},{1... | collective-permute-start | bytes 663560 | tf_op jit(solution)/shard_map/ppermute | solution.py:383
  1.2 36.4 %collective-permute-start = (bf16[192,576]{1,0:T(8,128)(2,1)}, bf16[192,576]{1,0:T(8,128)(2,1)S(1)}, u32[]{:S(2)}, u32[]{:S(2)}) collective-permute-start(bf16[192,576]{1,0:T(8,128)(2,1)} %w0.3), channel_id=1, source_target_pairs={{0,8},{4,12},{8,0},{12,4},{1,9},{5,13},{9,1},{13,5},{2,10},{6,14},... | collective-permute-start | bytes 663560 | tf_op jit(solution)/shard_map/ppermute | solution.py:383
  37.6 15.4 %collective-permute-start.14 = (bf16[192,512]{1,0:T(8,128)(2,1)S(1)}, bf16[192,512]{1,0:T(8,128)(2,1)S(1)}, u32[]{:S(2)}, u32[]{:S(2)}) collective-permute-start(bf16[192,512]{1,0:T(8,128)(2,1)S(1)} %copy-done.4), channel_id=1, source_target_pairs={{0,2},{1,3},{2,0},{3,1},{4,6},{5,7},{6,4},{7,5},{8,10},{9,11},{10,... | collective-permute-start | bytes 589832 | tf_op jit(solution)/shard_map/ppermute | solution.py:383
  37.6 17.5 %collective-permute-start.2 = (bf16[192,576]{1,0:T(8,128)(2,1)S(1)}, bf16[192,576]{1,0:T(8,128)(2,1)S(1)}, u32[]{:S(2)}, u32[]{:S(2)}) collective-permute-start(bf16[192,576]{1,0:T(8,128)(2,1)S(1)} %collective-permute-done.w1), channel_id=1, source_target_pairs={{0,4},{4,0},{8,12},{12,8},{1,5},{5,1},{9,13},{13,9},{2,6},{6,2},{1... | collective-permute-start | bytes 663560 | tf_op jit(solution)/shard_map/ppermute | solution.py:383
  39.2 21.6 %collective-permute-start.7 = (bf16[192,768]{1,0:T(8,128)(2,1)S(1)}, bf16[192,768]{1,0:T(8,128)(2,1)S(1)}, u32[]{:S(2)}, u32[]{:S(2)}) collective-permute-start(bf16[192,768]{1,0:T(8,128)(2,1)S(1)} %copy-done.14), channel_id=1, source_target_pairs={{0,8},{4,12},{8,0},{12,4},{1,9},{5,13},{9,1},{13,5},{2,10},{6,14},... | collective-permute-start | bytes 884744 | tf_op jit(solution)/shard_map/ppermute | solution.py:383
  43.9 17.4 %collective-permute-start.8 = (bf16[192,768]{1,0:T(8,128)(2,1)S(1)}, bf16[192,768]{1,0:T(8,128)(2,1)S(1)}, u32[]{:S(2)}, u32[]{:S(2)}) collective-permute-start(bf16[192,768]{1,0:T(8,128)(2,1)S(1)} %copy-done.14), channel_id=1, source_target_pairs={{0,4},{4,0},{8,12},{12,8},{1,5},{5,1},{9,13},{13,9},{2,6},{6,2},{1... | collective-permute-start | bytes 884744 | tf_op jit(solution)/shard_map/ppermute | solution.py:383
  53.6 15.6 %collective-permute-start.4 = (bf16[768,192]{1,0:T(8,128)(2,1)S(1)}, bf16[768,192]{1,0:T(8,128)(2,1)S(1)}, u32[]{:S(2)}, u32[]{:S(2)}) collective-permute-start(bf16[768,192]{1,0:T(8,128)(2,1)S(1)} %shard_map.256.m0), channel_id=1, source_target_pairs={{0,8},{4,12},{8,0},{12,4},{1,9},{5,13},{9,1},{13,5},{2,10},{6,14},... | collective-permute-start | bytes 884744 | tf_op jit(solution)/shard_map/ppermute | solution.py:383
  60.8 26.5 %collective-permute-start.11 = (bf16[192,768]{1,0:T(8,128)(2,1)S(1)}, bf16[192,768]{1,0:T(8,128)(2,1)S(1)}, u32[]{:S(2)}, u32[]{:S(2)}) collective-permute-start(bf16[192,768]{1,0:T(8,128)(2,1)S(1)} %copy-done.15), channel_id=1, source_target_pairs={{0,4},{4,0},{8,12},{12,8},{1,5},{5,1},{9,13},{13,9},{2,6},{6,2},{1... | collective-permute-start | bytes 884744 | tf_op jit(solution)/shard_map/ppermute | solution.py:383
  60.8 26.5 %collective-permute-start.5 = (bf16[768,192]{1,0:T(8,128)(2,1)S(1)}, bf16[768,192]{1,0:T(8,128)(2,1)S(1)}, u32[]{:S(2)}, u32[]{:S(2)}) collective-permute-start(bf16[768,192]{1,0:T(8,128)(2,1)S(1)} %shard_map.256.m0), channel_id=1, source_target_pairs={{0,4},{4,0},{8,12},{12,8},{1,5},{5,1},{9,13},{13,9},{2,6},{6,2},{1... | collective-permute-start | bytes 884744 | tf_op jit(solution)/shard_map/ppermute | solution.py:383
  61.3 26.0 %collective-permute-start.9 = (bf16[192,768]{1,0:T(8,128)(2,1)S(1)}, bf16[192,768]{1,0:T(8,128)(2,1)S(1)}, u32[]{:S(2)}, u32[]{:S(2)}) collective-permute-start(bf16[192,768]{1,0:T(8,128)(2,1)S(1)} %collective-permute-done.7.u1), channel_id=1, source_target_pairs={{0,4},{4,0},{8,12},{12,8},{1,5},{5,1},{9,13},{13,9},{2,6},{6,2},{1... | collective-permute-start | bytes 884744 | tf_op jit(solution)/shard_map/ppermute | solution.py:383
  62.9 24.3 %collective-permute-start.12 = (bf16[192,768]{1,0:T(8,128)(2,1)S(1)}, bf16[192,768]{1,0:T(8,128)(2,1)S(1)}, u32[]{:S(2)}, u32[]{:S(2)}) collective-permute-start(bf16[192,768]{1,0:T(8,128)(2,1)S(1)} %collective-permute-done.10.d1), channel_id=1, source_target_pairs={{0,4},{4,0},{8,12},{12,8},{1,5},{5,1},{9,13},{13,9},{2,6},{6,2},{1... | collective-permute-start | bytes 884744 | tf_op jit(solution)/shard_map/ppermute | solution.py:383
  69.1 18.1 %collective-permute-start.6 = (bf16[768,192]{1,0:T(8,128)(2,1)S(1)}, bf16[768,192]{1,0:T(8,128)(2,1)S(1)}, u32[]{:S(2)}, u32[]{:S(2)}) collective-permute-start(bf16[768,192]{1,0:T(8,128)(2,1)S(1)} %collective-permute-done.4.m1), channel_id=1, source_target_pairs={{0,4},{4,0},{8,12},{12,8},{1,5},{5,1},{9,13},{13,9},{2,6},{6,2},{1... | collective-permute-start | bytes 884744 | tf_op jit(solution)/shard_map/ppermute | solution.py:383
  95.3 10.9 %collective-permute-start.16 = (bf16[768,128]{1,0:T(8,128)(2,1)S(1)}, bf16[768,128]{1,0:T(8,128)(2,1)S(1)}, u32[]{:S(2)}, u32[]{:S(2)}) collective-permute-start(bf16[768,128]{1,0:T(8,128)(2,1)S(1)} %get-tuple-element.87), channel_id=1, source_target_pairs={{0,1},{1,0},{2,3},{3,2},{4,5},{5,4},{6,7},{7,6},{8,9},{9,8},{10,11... | collective-permute-start | bytes 589832 | tf_op jit(solution)/shard_map/ppermute | solution.py:383
  95.3 17.2 %collective-permute-start.17 = (bf16[768,128]{1,0:T(8,128)(2,1)S(1)}, bf16[768,128]{1,0:T(8,128)(2,1)S(1)}, u32[]{:S(2)}, u32[]{:S(2)}) collective-permute-start(bf16[768,128]{1,0:T(8,128)(2,1)S(1)} %get-tuple-element.88), channel_id=1, source_target_pairs={{0,2},{1,3},{2,0},{3,1},{4,6},{5,7},{6,4},{7,5},{8,10},{9,11},{10,... | collective-permute-start | bytes 589832 | tf_op jit(solution)/shard_map/ppermute | solution.py:383
  97.8 14.8 %collective-permute-start.18 = (bf16[768,128]{1,0:T(8,128)(2,1)S(1)}, bf16[768,128]{1,0:T(8,128)(2,1)S(1)}, u32[]{:S(2)}, u32[]{:S(2)}) collective-permute-start(bf16[768,128]{1,0:T(8,128)(2,1)S(1)} %get-tuple-element.89), channel_id=1, source_target_pairs={{0,3},{1,2},{2,1},{3,0},{4,7},{5,6},{6,5},{7,4},{8,11},{9,10},{10,... | collective-permute-start | bytes 589832 | tf_op jit(solution)/shard_map/ppermute | solution.py:383
  112.6 13.6 %collective-permute-start.25 = (bf16[192,1536]{1,0:T(8,128)(2,1)S(1)}, bf16[192,1536]{1,0:T(8,128)(2,1)S(1)}, u32[]{:S(2)}, u32[]{:S(2)}) collective-permute-start(bf16[192,1536]{1,0:T(8,128)(2,1)S(1)} %get-tuple-element.114), channel_id=1, source_target_pairs={{0,8},{4,12},{8,0},{12,4},{1,9},{5,13},{9,1},{13,5},{2,10},{6,14},... | collective-permute-start | bytes 1769480 | tf_op jit(solution)/shard_map/ppermute | solution.py:383
  114.8 12.3 %collective-permute-start.22 = (bf16[192,128]{1,0:T(8,128)(2,1)S(1)}, bf16[192,128]{1,0:T(8,128)(2,1)S(1)}, u32[]{:S(2)}, u32[]{:S(2)}) collective-permute-start(bf16[192,128]{1,0:T(8,128)(2,1)S(1)} %get-tuple-element.110), channel_id=1, source_target_pairs={{0,1},{1,0},{2,3},{3,2},{4,5},{5,4},{6,7},{7,6},{8,9},{9,8},{10,11... | collective-permute-start | bytes 147464 | tf_op jit(solution)/shard_map/ppermute | solution.py:383
  121.4 19.8 %collective-permute-start.20 = (bf16[384,512]{1,0:T(8,128)(2,1)S(1)}, bf16[384,512]{1,0:T(8,128)(2,1)S(1)}, u32[]{:S(2)}, u32[]{:S(2)}) collective-permute-start(bf16[384,512]{1,0:T(8,128)(2,1)S(1)} %get-tuple-element.103), channel_id=1, source_target_pairs={{0,1},{1,0},{2,3},{3,2},{4,5},{5,4},{6,7},{7,6},{8,9},{9,8},{10,11... | collective-permute-start | bytes 1179656 | tf_op jit(solution)/shard_map/ppermute | solution.py:383
  131.6 13.5 %collective-permute-start.26 = (bf16[208,512]{1,0:T(8,128)(2,1)S(1)}, bf16[208,512]{1,0:T(8,128)(2,1)S(1)}, u32[]{:S(2)}, u32[]{:S(2)}) collective-permute-start(bf16[208,512]{1,0:T(8,128)(2,1)S(1)} %get-tuple-element.121), channel_id=1, source_target_pairs={{0,1},{1,0},{2,3},{3,2},{4,5},{5,4},{6,7},{7,6},{8,9},{9,8},{10,11... | collective-permute-start | bytes 638984 | tf_op jit(solution)/shard_map/ppermute | solution.py:383
  137.0 26.9 %collective-permute-start.27 = (bf16[208,512]{1,0:T(8,128)(2,1)S(1)}, bf16[208,512]{1,0:T(8,128)(2,1)S(1)}, u32[]{:S(2)}, u32[]{:S(2)}) collective-permute-start(bf16[208,512]{1,0:T(8,128)(2,1)S(1)} %get-tuple-element.122), channel_id=1, source_target_pairs={{0,2},{1,3},{2,0},{3,1},{4,6},{5,7},{6,4},{7,5},{8,10},{9,11},{10,... | collective-permute-start | bytes 638984 | tf_op jit(solution)/shard_map/ppermute | solution.py:383
  137.4 27.5 %collective-permute-start.28 = (bf16[208,512]{1,0:T(8,128)(2,1)S(1)}, bf16[208,512]{1,0:T(8,128)(2,1)S(1)}, u32[]{:S(2)}, u32[]{:S(2)}) collective-permute-start(bf16[208,512]{1,0:T(8,128)(2,1)S(1)} %get-tuple-element.123), channel_id=1, source_target_pairs={{0,3},{1,2},{2,1},{3,0},{4,7},{5,6},{6,5},{7,4},{8,11},{9,10},{10,... | collective-permute-start | bytes 638984 | tf_op jit(solution)/shard_map/ppermute | solution.py:383
  139.4 27.9 %collective-permute-start.34 = (bf16[768,128]{1,0:T(8,128)(2,1)S(1)}, bf16[768,128]{1,0:T(8,128)(2,1)S(1)}, u32[]{:S(2)}, u32[]{:S(2)}) collective-permute-start(bf16[768,128]{1,0:T(8,128)(2,1)S(1)} %get-tuple-element.102.h0), channel_id=1, source_target_pairs={{0,3},{1,2},{2,1},{3,0},{4,7},{5,6},{6,5},{7,4},{8,11},{9,10},{10,... | collective-permute-start | bytes 589832 | tf_op jit(solution)/shard_map/ppermute | solution.py:383
  141.2 38.7 %collective-permute-start.33 = (bf16[768,128]{1,0:T(8,128)(2,1)S(1)}, bf16[768,128]{1,0:T(8,128)(2,1)S(1)}, u32[]{:S(2)}, u32[]{:S(2)}) collective-permute-start(bf16[768,128]{1,0:T(8,128)(2,1)S(1)} %get-tuple-element.102.h0), channel_id=1, source_target_pairs={{0,2},{1,3},{2,0},{3,1},{4,6},{5,7},{6,4},{7,5},{8,10},{9,11},{10,... | collective-permute-start | bytes 589832 | tf_op jit(solution)/shard_map/ppermute | solution.py:383
  145.1 34.8 %collective-permute-start.32 = (bf16[768,128]{1,0:T(8,128)(2,1)S(1)}, bf16[768,128]{1,0:T(8,128)(2,1)S(1)}, u32[]{:S(2)}, u32[]{:S(2)}) collective-permute-start(bf16[768,128]{1,0:T(8,128)(2,1)S(1)} %get-tuple-element.102.h0), channel_id=1, source_target_pairs={{0,1},{1,0},{2,3},{3,2},{4,5},{5,4},{6,7},{7,6},{8,9},{9,8},{10,11... | collective-permute-start | bytes 589832 | tf_op jit(solution)/shard_map/ppermute | solution.py:383
  163.9 19.6 %collective-permute-start.21 = (bf16[192,512]{1,0:T(8,128)(2,1)S(1)}, bf16[192,512]{1,0:T(8,128)(2,1)}, u32[]{:S(2)}, u32[]{:S(2)}) collective-permute-start(bf16[192,512]{1,0:T(8,128)(2,1)S(1)} %get-tuple-element.105), channel_id=1, source_target_pairs={{0,2},{1,3},{2,0},{3,1},{4,6},{5,7},{6,4},{7,5},{8,10},{9,11},{10,... | collective-permute-start | bytes 589832 | tf_op jit(solution)/shard_map/ppermute | solution.py:383
  166.8 15.1 %collective-permute-start.30 = (f32[8,768]{1,0:T(8,128)S(1)}, f32[8,768]{1,0:T(8,128)S(1)}, u32[]{:S(2)}, u32[]{:S(2)}) collective-permute-start(f32[8,768]{1,0:T(8,128)S(1)} %add.37), channel_id=1, source_target_pairs={{0,8},{4,12},{8,0},{12,4},{1,9},{5,13},{9,1},{13,5},{2,10},{6,14},... | collective-permute-start | bytes 73736 | tf_op jit(solution)/shard_map/ppermute | solution.py:383
  181.2 18.1 %collective-permute-start.35 = (bf16[384,768]{1,0:T(8,128)(2,1)S(1)}, bf16[384,768]{1,0:T(8,128)(2,1)S(1)}, u32[]{:S(2)}, u32[]{:S(2)}) collective-permute-start(bf16[384,768]{1,0:T(8,128)(2,1)S(1)} %shard_map.265), channel_id=1, source_target_pairs={{0,4},{4,0},{8,12},{12,8},{1,5},{5,1},{9,13},{13,9},{2,6},{6,2},{1... | collective-permute-start | bytes 1769480 | tf_op jit(solution)/shard_map/ppermute | solution.py:383
  181.3 22.9 %collective-permute-start.39 = (bf16[192,1536]{1,0:T(8,128)(2,1)S(1)}, bf16[192,1536]{1,0:T(8,128)(2,1)S(1)}, u32[]{:S(2)}, u32[]{:S(2)}) collective-permute-start(bf16[192,1536]{1,0:T(8,128)(2,1)S(1)} %copy-done.17), channel_id=1, source_target_pairs={{0,16},{16,0},{1,17},{17,1},{2,18},{18,2},{3,19},{19,3},{4,20},{20... | collective-permute-start | bytes 1769480 | tf_op jit(solution)/shard_map/ppermute | solution.py:383
  181.9 15.6 %collective-permute-start.31 = (f32[8,768]{1,0:T(8,128)S(1)}, f32[8,768]{1,0:T(8,128)S(1)}, u32[]{:S(2)}, u32[]{:S(2)}) collective-permute-start(f32[8,768]{1,0:T(8,128)S(1)} %add.38), channel_id=1, source_target_pairs={{0,16},{16,0},{1,17},{17,1},{2,18},{18,2},{3,19},{19,3},{4,20},{20... | collective-permute-start | bytes 73736 | tf_op jit(solution)/shard_map/ppermute | solution.py:383
  200.6 14.9 %collective-permute-start.38 = (bf16[192,768]{1,0:T(8,128)(2,1)S(1)}, bf16[192,768]{1,0:T(8,128)(2,1)S(1)}, u32[]{:S(2)}, u32[]{:S(2)}) collective-permute-start(bf16[192,768]{1,0:T(8,128)(2,1)S(1)} %get-tuple-element.131), channel_id=1, source_target_pairs={{0,24},{4,28},{8,16},{12,20},{16,8},{20,12},{24,0},{28,4},{1,25},{... | collective-permute-start | bytes 884744 | tf_op jit(solution)/shard_map/ppermute | solution.py:574
  201.2 14.5 %collective-permute-start.36 = (bf16[192,768]{1,0:T(8,128)(2,1)S(1)}, bf16[192,768]{1,0:T(8,128)(2,1)S(1)}, u32[]{:S(2)}, u32[]{:S(2)}) collective-permute-start(bf16[192,768]{1,0:T(8,128)(2,1)S(1)} %get-tuple-element.131), channel_id=1, source_target_pairs={{0,8},{4,12},{8,0},{12,4},{1,9},{5,13},{9,1},{13,5},{2,10},{6,14},... | collective-permute-start | bytes 884744 | tf_op jit(solution)/shard_map/ppermute | solution.py:383
  202.7 12.8 %collective-permute-start.37 = (bf16[192,768]{1,0:T(8,128)(2,1)S(1)}, bf16[192,768]{1,0:T(8,128)(2,1)S(1)}, u32[]{:S(2)}, u32[]{:S(2)}) collective-permute-start(bf16[192,768]{1,0:T(8,128)(2,1)S(1)} %get-tuple-element.132), channel_id=1, source_target_pairs={{0,16},{16,0},{1,17},{17,1},{2,18},{18,2},{3,19},{19,3},{4,20},{20... | collective-permute-start | bytes 884744 | tf_op jit(solution)/shard_map/ppermute | solution.py:573
  (26 other events, 297.5 us)

commit v6 on v5

--- a/solution.py
+++ b/solution.py
@@ -62,7 +62,7 @@
     return [cols[:, k : k + 1] + cols[:, k + 5 : k + 6] + cols[:, k + 10 : k + 11] for k in which]
 
 
-def run(kernel, outs, ins, scratch=(), flops=0, hold=True):
+def run(kernel, outs, ins, scratch=(), flops=0, hold=True, limit=24):
     specs = [pl.BlockSpec(memory_space=pltpu.SMEM)]
     specs += [pl.BlockSpec(memory_space=pltpu.VMEM)] * (len(ins) - 1)
     size = sum(math.prod(value.shape) * value.dtype.itemsize for value in list(ins) + list(outs))
@@ -74,7 +74,7 @@
         out_specs=[pl.BlockSpec(memory_space=pltpu.VMEM)] * len(outs),
         scratch_shapes=list(scratch),
         cost_estimate=pl.CostEstimate(flops=flops, transcendentals=0, bytes_accessed=size),
-        compiler_params=pltpu.CompilerParams(vmem_limit_bytes=24 * 1024 * 1024),
+        compiler_params=pltpu.CompilerParams(vmem_limit_bytes=limit * 1024 * 1024),
     )(ins[0], *held)
 
 
@@ -190,10 +190,9 @@
 
 
 def ff_grads_kernel(
-    order, here, grad_final, active, normed, grad_pre, down_all, send, keep, out_send, out_keep, rows
+    order, here, grad_final, active, normed, grad_pre, send, keep, rows
 ):
     half = keep.shape[0]
-    feat = half // 2
     hid = active.shape[0]
     in_order(order, here, rows, grad_final)
     down = mm_nt(rows[...], active[...])
@@ -203,6 +202,10 @@
     up = mm_nt(rows[...], grad_pre[...])
     keep[:, hid:] = up[:half]
     send[:, hid:] = up[half:].astype(BF16)
+
+
+def out_parts_kernel(here, down_all, active, out_send, out_keep):
+    feat = out_keep.shape[0] // 2
     for step in (0, 2):
         out_keep[pl.ds(step // 2 * feat, feat), :] = mm(down_all[block(here[1] ^ step, feat), :], active[...])
         out = mm(down_all[block(here[1] ^ (step + 1), feat), :], active[...])
@@ -302,37 +305,51 @@
         ref[feat:, :feat] = sums[rows, :].T[:extra].astype(ref.dtype)
 
 
-def last_grads(pair, here, normed, grad_proj, att, pieces, rows, hidden):
-    feat, count = att.shape
-    part = count // len(pieces)
+def last_grads(pair, here, normed, grad_proj, rows):
+    feat = rows.shape[0] // 2
     for at, value in enumerate(pair):
-        source = block(here[0] ^ value, feat)
-        target = pl.ds(at * feat, feat)
-        rows[target, :] = normed[source, :]
-        for step, ref in enumerate(pieces):
-            hidden[target, block(here[1] ^ step, part)] = ref[source, :]
-    return mm_nt(rows[...], grad_proj[...]), mm_nt(hidden[...], att[...])
-
-
-def last_send_kernel(order, here, normed, grad_proj, att, h0, h1, h2, h3, send, rows, hidden):
-    split = grad_proj.shape[0]
-    qkv, mix = last_grads(order[2:], here, normed, grad_proj, att, (h0, h1, h2, h3), rows, hidden)
-    send[:, :split] = qkv.astype(BF16)
-    send[:, split:] = mix.astype(BF16)
-
-
-def last_keep_kernel(order, here, normed, grad_proj, att, h0, h1, h2, h3, got, own, own_b, send, rows, hidden):
-    feat = att.shape[0]
-    split = grad_proj.shape[0]
-    qkv, mix = last_grads(order[:2], here, normed, grad_proj, att, (h0, h1, h2, h3), rows, hidden)
-    qkv += got[:, :split].astype(F32)
-    mix += got[:, split:].astype(F32)
-    own[:, :split] = qkv[:feat]
-    own[:, split:] = mix[:feat]
-    own_b[:, :split] = qkv[:feat].astype(BF16)
-    own_b[:, split:] = mix[:feat].astype(BF16)
-    send[:, :split] = qkv[feat:].astype(BF16)
-    send[:, split:] = mix[feat:].astype(BF16)
+        rows[pl.ds(at * feat, feat), :] = normed[block(here[0] ^ value, feat), :]
+    return mm_nt(rows[...], grad_proj[...])
+
+
+def last_send_kernel(order, here, normed, grad_proj, send, rows):
+    send[...] = last_grads(order[2:], here, normed, grad_proj, rows).astype(BF16)
+
+
+def last_keep_kernel(order, here, normed, grad_proj, got, own, own_b, send, rows):
+    feat = own.shape[0]
+    grad = last_grads(order[:2], here, normed, grad_proj, rows) + got[...].astype(F32)
+    own[...] = grad[:feat]
+    own_b[...] = grad[:feat].astype(BF16)
+    send[...] = grad[feat:].astype(BF16)
+
+
+def mix_send_kernel(order, here, att, grad_hidden_b, send):
+    feat = send.shape[0] // 2
+    own = att[:, block(here[1], grad_hidden_b.shape[1])]
+    for at in (0, 1):
+        rows = grad_hidden_b[block(here[0] ^ order[2 + at], feat), :]
+        send[pl.ds(at * feat, feat), :] = mm_nt(rows, own).astype(BF16)
+
+
+def mix_keep_kernel(order, here, att, grad_hidden_b, got, keep, send):
+    feat = keep.shape[0]
+    own = att[:, block(here[1], grad_hidden_b.shape[1])]
+    for at, out in enumerate((keep, send)):
+        rows = grad_hidden_b[block(here[0] ^ order[at], feat), :]
+        out[...] = (mm_nt(rows, own) + got[pl.ds(at * feat, feat), :].astype(F32)).astype(out.dtype)
+
+
+def mix_turn_kernel(here, grad_mix, own, p1, p2, p3, turned):
+    feat = own.shape[0]
+    turned[...] = grad_mix[...].T
+    own[...] = turned[block(here[1], feat), :]
+    for step, out in enumerate((p1, p2, p3)):
+        out[...] = turned[block(here[1] ^ (step + 1), feat), :].astype(BF16)
+
+
+def mix_sum_kernel(here, own, g1, g2, g3, out):
+    out[...] = own[...] + g1[...].astype(F32) + g2[...].astype(F32) + g3[...].astype(F32)
 
 
 def rest_kernel(here, up_sum, qv_sum, cot, row, rest):
@@ -358,11 +375,8 @@
     sums[:5, :feat] = total[feat : feat + 5, :feat]
 
 
-def last_sum_kernel(here, own, got_y, got_x, got_xy, qkv, mix):
-    split = qkv.shape[1]
-    total = own[...] + got_y[...].astype(F32) + got_x[...].astype(F32) + got_xy[...].astype(F32)
-    qkv[...] = total[:, :split]
-    mix[...] = total[:, split:].T
+def last_sum_kernel(here, own, got_y, got_x, got_xy, qkv):
+    qkv[...] = own[...] + got_y[...].astype(F32) + got_x[...].astype(F32) + got_xy[...].astype(F32)
 
 
 def halve_kernel(here, keep, got, kept, send):
@@ -455,6 +469,7 @@
                 for value in (first_gain, first_bias, mix_bias, second_gain, second_bias, down_bias, segment_ids)
             ),
             hold=False,
+            limit=58,
         )
         tok = lax.all_gather(packed, "cols", axis=0, tiled=True)
         qkv_yc = over_rows(qkv_y, near)
@@ -509,19 +524,24 @@
         )
         got = all_over_cols((p1, p2, p3))
 
-        ff_send, ff_keep, out_send, out_keep = run(
+        ff_send, ff_keep = run(
             functools.partial(ff_grads_kernel, order),
             (
                 shaped((2 * feat, 2 * n_hid), BF16), shaped((2 * feat, 2 * n_hid), F32),
-                shaped((2 * feat, count), BF16), shaped((2 * feat, count), F32),
             ),
-            (here, grad_final, active, normed_two, grad_pre, down_all),
+            (here, grad_final, active, normed_two, grad_pre),
             scratch=(pltpu.VMEM((width, count), BF16),),
-            flops=2 * width * count * 3 * n_hid,
+            flops=2 * width * count * 2 * n_hid,
+        )
+        out_send, out_keep = run(
+            out_parts_kernel,
+            (shaped((2 * feat, count), BF16), shaped((2 * feat, count), F32)),
+            (here, down_all, active),
+            flops=2 * width * count * n_hid,
         )
         ff_keep, ff_send = halve(ff_keep, over_rows(ff_send, near))
-        got[0], got[1], got[2], ff_keep, ff_send, out_send = together(*got, ff_keep, ff_send, out_send)
         ff_got = over_rows(ff_send, far)
+        got[0], got[1], got[2], ff_keep, out_send = together(*got, ff_keep, out_send)
 
         grad_hidden, grad_hidden_b, second, a0, a1, a2, a3 = run(
             functools.partial(second_back_kernel, order),
@@ -534,7 +554,17 @@
             flops=2 * width * part * width,
         )
         b1, b2, b3 = all_over_cols((a1, a2, a3))
-        h_pieces = [grad_hidden_b] + all_over_cols((grad_hidden_b,) * 3)
+        (mix_send,) = run(
+            functools.partial(mix_send_kernel, order), (shaped((2 * feat, width), BF16),),
+            (here, att, grad_hidden_b), flops=width * width * part,
+        )
+        mix_keep, mix_send = run(
+            functools.partial(mix_keep_kernel, order),
+            (shaped((feat, width), F32), shaped((feat, width), BF16)),
+            (here, att, grad_hidden_b, over_rows(mix_send, near)),
+            flops=width * width * part,
+        )
+        mix_got = over_rows(mix_send, far)
         out_got = over_cols(after(out_send, grad_hidden_b), 1)
         ff_sum = ff_keep + ff_got.astype(F32)
         b1, b2, b3, ff_sum = together(b1, b2, b3, ff_sum)
@@ -553,19 +583,19 @@
         )
         got = all_over_cols((s1, s2, s3))
 
-        last_ins = (here, normed_one, grad_proj, attended) + tuple(h_pieces)
-        n_last = n_qkv + feat
+        grad_mix = over_dp(mix_keep + mix_got.astype(F32))
+        last_ins = (here, normed_one, grad_proj)
+        last_rows = (pltpu.VMEM((2 * feat, count), BF16),)
         (last_send,) = run(
-            functools.partial(last_send_kernel, order), (shaped((2 * feat, n_last), BF16),), last_ins,
-            scratch=(pltpu.VMEM((2 * feat, count), BF16), pltpu.VMEM((2 * feat, count), BF16)),
-            flops=width * count * n_last,
+            functools.partial(last_send_kernel, order), (shaped((2 * feat, n_qkv), BF16),), last_ins,
+            scratch=last_rows, flops=width * count * n_qkv,
         )
         own, own_b, last_send = run(
             functools.partial(last_keep_kernel, order),
-            (shaped((feat, n_last), F32), shaped((feat, n_last), BF16), shaped((feat, n_last), BF16)),
+            (shaped((feat, n_qkv), F32), shaped((feat, n_qkv), BF16), shaped((feat, n_qkv), BF16)),
             last_ins + (over_rows(last_send, near),),
-            scratch=(pltpu.VMEM((2 * feat, count), BF16), pltpu.VMEM((2 * feat, count), BF16)),
-            flops=width * count * n_last,
+            scratch=last_rows,
+            flops=width * count * n_qkv,
         )
         far_dp = [(d * n_rows + r, (d ^ 1) * n_rows + (r ^ far)) for d in range(n_dp) for r in range(n_rows)]
         got_y = over_rows(last_send, far)
@@ -574,12 +604,9 @@
             got_xy = lax.ppermute(last_send, ("dp", "rows"), far_dp)
         else:
             got_x = got_xy = jnp.zeros_like(got_y)
-        grad_qkv, grad_mix = run(
-            last_sum_kernel, (shaped((feat, n_qkv), F32), shaped((feat, feat), F32)), (here, own, got_y, got_x, got_xy)
-        )
+        (grad_qkv,) = run(last_sum_kernel, (shaped((feat, n_qkv), F32),), (here, own, got_y, got_x, got_xy))
         for bit in bits_of(n_dp)[1:]:
             grad_qkv = grad_qkv + swap(grad_qkv.astype(BF16), "dp", n_dp, bit).astype(F32)
-            grad_mix = grad_mix + swap(grad_mix.astype(BF16), "dp", n_dp, bit).astype(F32)
 
         (rest,) = run(rest_kernel, (shaped((8, width), F32),), (here, up_sum, qv_sum, cotangent, row))
         grad_tokens, sums = run(
@@ -589,6 +616,15 @@
             for bit in bits_of(size):
                 sums = sums + swap(sums, axis, size, bit)
 
+        square_b = shaped((feat, feat), BF16)
+        mix_own, p1, p2, p3 = run(
+            mix_turn_kernel,
+            (shaped((feat, feat), F32), square_b, square_b, square_b),
+            (here, grad_mix),
+            scratch=(pltpu.VMEM((width, feat), F32),),
+        )
+        got = all_over_cols((p1, p2, p3))
+        (grad_mix,) = run(mix_sum_kernel, (shaped((feat, feat), F32),), (here, mix_own) + tuple(got))
         out_keep, out_send = halve(out_keep, out_got)
         output = own_hidden + down_col + out_keep + over_cols(out_send, 2).astype(F32)
         return (

time: 218 us -> 202 us (0.927)
  waiting for transfers between devices: 96.4 us -> 76.7 us
  local copies, waits for them, and re-layouts: 11.7 us -> 5.17 us
  Pallas kernels: 25.8 us -> 31.7 us
  starting transfers between devices: 39.9 us -> 43.7 us
    ppermute x1, waiting for transfers between devices: 10 us -> 0.01 us  [body(): got_x = lax.ppermute(own_b, 'dp', pairs)]
    ppermute x37 -> x40, waiting for transfers between devices: 84.8 us -> 75.1 us  [swap(): return lax.ppermute(values, axis, [(at, at ^ bit) for at in range(size)])]
    unnamed x39 -> x29, local copies, waits for them, and re-layouts: 8.82 us -> 2.28 us
    pallas_call x14 -> x19, Pallas kernels: 25.8 us -> 31.7 us  [run(): pl.pallas_call(kernel, out_shape=[pltpu.VMEM(value.shape, value.dtype) fo...]
    ppermute x37 -> x40, starting transfers between devices: 36.3 us -> 39.1 us  [swap(): return lax.ppermute(values, axis, [(at, at ^ bit) for at in range(size)])]
  transfers between devices with their start and end apart: 40 -> 43, of which waited for: 16 -> 18; matrix products, arithmetic and copies ran while one was open for 3% -> 4% of each run, Pallas kernels for 8% -> 11%
where the time goes in v6:
time: 202 us
  waiting for transfers between devices  76.7 us (38%)
  starting transfers between devices  43.7 us (22%)
  blocking collectives  40.2 us (20%)
  Pallas kernels  31.7 us (16%)
  local copies, waits for them, and re-layouts  5.17 us (3%)
  other arithmetic  3.63 us (2%)
    ppermute x40, waiting for transfers between devices, swap(): return lax.ppermute(values, axis, [(at, at ^ bit) for at in range(size)])  75.1 us
    ppermute x40, starting transfers between devices, swap(): return lax.ppermute(values, axis, [(at, at ^ bit) for at in range(size)])  39.1 us
    pallas_call x19, Pallas kernels, run(): pl.pallas_call(kernel, out_shape=[pltpu.VMEM(value.shape, value.dtype) fo...  31.7 us
    all_gather x1, blocking collectives, body(): tok = lax.all_gather(packed, 'cols', axis=0, tiled=True)  22.1 us
    all_gather x1, blocking collectives, body(): att = lax.all_gather(attended, 'cols', axis=0, tiled=True)  18.1 us
  transfers between devices with their start and end apart: 43, of which 18 were waited for; matrix products, arithmetic and copies ran while one was open for 4% of the time, Pallas kernels for 11%

profile of v6, /device:TPU:0, one launch (start us, length us, event | category | flops | bytes accessed | tf_op | source)
XLA Modules:
  0.0 202.1 jit_solution(17537198868750292612)
XLA Ops:
  1.2 2.6 %collective-permute-start = (bf16[192,576]{1,0:T(8,128)(2,1)}, bf16[192,576]{1,0:T(8,128)(2,1)S(1)}, u32[]{:S(2)}, u32[]{:S(2)}) collective-permute-start(bf16[192,576]{1,0:T(8,128)(2,1)} %w0.3), channel_id=1, source_target_pairs={{0,8},{4,12},{8,0},{12,4},{1,9},{5,13},{9,1},{13,5},{2,10},{6,14},... | collective-permute-start | bytes 663560 | tf_op jit(solution)/shard_map/ppermute | solution.py:397
  5.8 22.1 %all_gather.6.tok = bf16[768,640]{1,0:T(8,128)(2,1)S(1)} all-gather(bf16[192,640]{1,0:T(8,128)(2,1)S(1)} %get-tuple-element.78), channel_id=1, replica_groups=mesh['dp'=2,'rows'=4,'cols'=4] {'cols'}, dimensions={0}, use_global_device_ids=true | all-gather | bytes 1228800 | tf_op jit(solution)/shard_map/all_gather | solution.py:474
  29.5 2.6 %collective-permute-start.15 = (bf16[192,512]{1,0:T(8,128)(2,1)S(1)}, bf16[192,512]{1,0:T(8,128)(2,1)S(1)}, u32[]{:S(2)}, u32[]{:S(2)}) collective-permute-start(bf16[192,512]{1,0:T(8,128)(2,1)S(1)} %copy-done.3), channel_id=1, source_target_pairs={{0,3},{1,2},{2,1},{3,0},{4,7},{5,6},{6,5},{7,4},{8,11},{9,10},{10,... | collective-permute-start | bytes 589832 | tf_op jit(solution)/shard_map/ppermute | solution.py:397
  34.9 3.5 %collective-permute-done.15.c3 = bf16[192,512]{1,0:T(8,128)(2,1)S(1)} collective-permute-done((bf16[192,512]{1,0:T(8,128)(2,1)S(1)}, bf16[192,512]{1,0:T(8,128)(2,1)S(1)}, u32[]{:S(2)}, u32[]{:S(2)}) %collective-permute-start.15) | collective-permute-done | bytes 196640 | tf_op jit(solution)/shard_map/ppermute | solution.py:397
  38.4 9.2 %collective-permute-done.14.c2 = bf16[192,512]{1,0:T(8,128)(2,1)S(1)} collective-permute-done((bf16[192,512]{1,0:T(8,128)(2,1)S(1)}, bf16[192,512]{1,0:T(8,128)(2,1)S(1)}, u32[]{:S(2)}, u32[]{:S(2)}) %collective-permute-start.14) | collective-permute-done | bytes 196640 | tf_op jit(solution)/shard_map/ppermute | solution.py:397
  49.6 3.8 %shard_map.255 = (bf16[768,512]{1,0:T(8,128)(2,1)S(1)}, f32[2,512]{1,0:T(2,128)S(1)}, bf16[576,512]{1,0:T(8,128)(2,1)S(1)}, bf16[192,512]{1,0:T(8,128)(2,1)S(1)}, f32[3,512]{1,0:T(4,128)S(1)}) custom-call(s32[3]{0:T(128)S(1)} %copy-done.5, bf16[768,640]{1,0:T(8,128)(2,1)S(1)} %all_gather.6.tok, bf16[192,576]{1,0:T(8,128)(2,1)S(1)} %copy-done, ...), custom_call_target="tpu_custom_call" | custom-call | flops 452984832 | bytes 3456524 | tf_op jit(solution)/shard_map/pallas_call | solution.py:70
  53.5 1.8 collective-permute-done.13.c1
  57.4 6.2 %collective-permute-done.4.m1 = bf16[768,192]{1,0:T(8,128)(2,1)S(1)} collective-permute-done((bf16[768,192]{1,0:T(8,128)(2,1)S(1)}, bf16[768,192]{1,0:T(8,128)(2,1)S(1)}, u32[]{:S(2)}, u32[]{:S(2)}) %collective-permute-start.4) | collective-permute-done | bytes 294944 | tf_op jit(solution)/shard_map/ppermute | solution.py:397
  63.6 18.1 %all_gather.7.att = bf16[768,512]{1,0:T(8,128)(2,1)S(1)} all-gather(bf16[192,512]{1,0:T(8,128)(2,1)S(1)} %get-tuple-element.80.att), channel_id=1, replica_groups=mesh['dp'=2,'rows'=4,'cols'=4] {'cols'}, dimensions={0}, use_global_device_ids=true | all-gather | bytes 983040 | tf_op jit(solution)/shard_map/all_gather | solution.py:499
  81.8 5.3 %shard_map.257 = (bf16[768,512]{1,0:T(8,128)(2,1)S(1)}, bf16[768,512]{1,0:T(8,128)(2,1)S(1)}, bf16[768,512]{1,0:T(8,128)(2,1)S(1)}, bf16[768,512]{1,0:T(8,128)(2...) custom-call(s32[3]{0:T(128)S(1)} %copy-done.5, ...), custom_call_target="tpu_custom_call" | custom-call | flops 2415919104 | bytes 12214284 | tf_op jit(solution)/shard_map/pallas_call | solution.py:70
  87.1 2.0 shard_map.259
  89.1 2.8 %collective-permute-done.19.got = bf16[384,1536]{1,0:T(8,128)(2,1)S(1)} collective-permute-done((bf16[384,1536]{1,0:T(8,128)(2,1)S(1)}, bf16[384,1536]{1,0:T(8,128)(2,1)S(1)}, u32[]{:S(2)}, u32[]{:S(2)}) %collective-permute-start.19) | collective-permute-done | bytes 1179680 | tf_op jit(solution)/shard_map/ppermute | solution.py:397
  93.3 2.4 %collective-permute-start.17 = (bf16[768,128]{1,0:T(8,128)(2,1)S(1)}, bf16[768,128]{1,0:T(8,128)(2,1)S(1)}, u32[]{:S(2)}, u32[]{:S(2)}) collective-permute-start(bf16[768,128]{1,0:T(8,128)(2,1)S(1)} %get-tuple-element.88), channel_id=1, source_target_pairs={{0,2},{1,3},{2,0},{3,1},{4,6},{5,7},{6,4},{7,5},{8,10},{9,11},{10,... | collective-permute-start | bytes 589832 | tf_op jit(solution)/shard_map/ppermute | solution.py:397
  95.7 2.0 collective-permute-start.18
  99.0 4.3 %collective-permute-done.16.r1 = bf16[768,128]{1,0:T(8,128)(2,1)S(1)} collective-permute-done((bf16[768,128]{1,0:T(8,128)(2,1)S(1)}, bf16[768,128]{1,0:T(8,128)(2,1)S(1)}, u32[]{:S(2)}, u32[]{:S(2)}) %collective-permute-start.16) | collective-permute-done | bytes 196640 | tf_op jit(solution)/shard_map/ppermute | solution.py:397
  103.3 7.1 %collective-permute-done.17.r2 = bf16[768,128]{1,0:T(8,128)(2,1)S(1)} collective-permute-done((bf16[768,128]{1,0:T(8,128)(2,1)S(1)}, bf16[768,128]{1,0:T(8,128)(2,1)S(1)}, u32[]{:S(2)}, u32[]{:S(2)}) %collective-permute-start.17) | collective-permute-done | bytes 196640 | tf_op jit(solution)/shard_map/ppermute | solution.py:397
  110.4 1.7 shard_map.261
  112.1 3.8 %collective-permute-start.22 = (bf16[192,128]{1,0:T(8,128)(2,1)S(1)}, bf16[192,128]{1,0:T(8,128)(2,1)S(1)}, u32[]{:S(2)}, u32[]{:S(2)}) collective-permute-start(bf16[192,128]{1,0:T(8,128)(2,1)S(1)} %get-tuple-element.112), channel_id=1, source_target_pairs={{0,1},{1,0},{2,3},{3,2},{4,5},{5,4},{6,7},{7,6},{8,9},{9,8},{10,11... | collective-permute-start | bytes 147464 | tf_op jit(solution)/shard_map/ppermute | solution.py:397
  116.5 1.8 collective-permute-start.24
  122.9 4.7 %shard_map.263 = (bf16[576,512]{1,0:T(8,128)(2,1)S(1)}, f32[384,1]{1,0:T(8,128)S(1)}, f32[208,512]{1,0:T(8,128)S(1)}, bf16[208,512]{1,0:T(8,128)(2,1)S(1)}, bf16...) custom-call(s32[3]{0:T(128)S(1)} %copy-done.5, bf16[768,640]{1,0:T(8,128)(2,1)S(1)} %all_gather.6.tok, ...), custom_call_target="tpu_custom_call" | custom-call | flops 452984832 | bytes 4939276 | tf_op jit(solution)/shard_map/pallas_call | solution.py:70
  127.8 2.3 %collective-permute-start.27 = (bf16[208,512]{1,0:T(8,128)(2,1)S(1)}, bf16[208,512]{1,0:T(8,128)(2,1)S(1)}, u32[]{:S(2)}, u32[]{:S(2)}) collective-permute-start(bf16[208,512]{1,0:T(8,128)(2,1)S(1)} %get-tuple-element.124), channel_id=1, source_target_pairs={{0,2},{1,3},{2,0},{3,1},{4,6},{5,7},{6,4},{7,5},{8,10},{9,11},{10,... | collective-permute-start | bytes 638984 | tf_op jit(solution)/shard_map/ppermute | solution.py:397
  130.1 2.0 collective-permute-start.28
  134.3 4.0 %collective-permute-done.26.g1 = bf16[208,512]{1,0:T(8,128)(2,1)S(1)} collective-permute-done((bf16[208,512]{1,0:T(8,128)(2,1)S(1)}, bf16[208,512]{1,0:T(8,128)(2,1)S(1)}, u32[]{:S(2)}, u32[]{:S(2)}) %collective-permute-start.26) | collective-permute-done | bytes 213024 | tf_op jit(solution)/shard_map/ppermute | solution.py:397
  138.3 11.8 %collective-permute-done.27.g2 = bf16[208,512]{1,0:T(8,128)(2,1)S(1)} collective-permute-done((bf16[208,512]{1,0:T(8,128)(2,1)S(1)}, bf16[208,512]{1,0:T(8,128)(2,1)S(1)}, u32[]{:S(2)}, u32[]{:S(2)}) %collective-permute-start.27) | collective-permute-done | bytes 213024 | tf_op jit(solution)/shard_map/ppermute | solution.py:397
  158.9 1.7 add_convert_fusion.1
  161.4 11.6 %collective-permute-done.31 = f32[8,768]{1,0:T(8,128)S(1)} collective-permute-done((f32[8,768]{1,0:T(8,128)S(1)}, f32[8,768]{1,0:T(8,128)S(1)}, u32[]{:S(2)}, u32[]{:S(2)}) %collective-permute-start.31) | collective-permute-done | bytes 24608 | tf_op jit(solution)/shard_map/ppermute | solution.py:397
  176.5 2.5 %collective-permute-start.35 = (bf16[192,576]{1,0:T(8,128)(2,1)S(1)}, bf16[192,576]{1,0:T(8,128)(2,1)S(1)}, u32[]{:S(2)}, u32[]{:S(2)}) collective-permute-start(bf16[192,576]{1,0:T(8,128)(2,1)S(1)} %get-tuple-element.133), channel_id=1, source_target_pairs={{0,24},{4,28},{8,16},{12,20},{16,8},{20,12},{24,0},{28,4},{1,25},{... | collective-permute-start | bytes 663560 | tf_op jit(solution)/shard_map/ppermute | solution.py:604
  180.0 3.6 %collective-permute-done.38 = bf16[192,768]{1,0:T(8,128)(2,1)S(1)} collective-permute-done((bf16[192,768]{1,0:T(8,128)(2,1)S(1)}, bf16[192,768]{1,0:T(8,128)(2,1)S(1)}, u32[]{:S(2)}, u32[]{:S(2)}) %collective-permute-start.38) | collective-permute-done | bytes 294944 | tf_op jit(solution)/shard_map/ppermute | solution.py:397
  184.5 5.2 %collective-permute-start.39 = (bf16[192,192]{1,0:T(8,128)(2,1)S(1)}, bf16[192,192]{1,0:T(8,128)(2,1)S(1)}, u32[]{:S(2)}, u32[]{:S(2)}) collective-permute-start(bf16[192,192]{1,0:T(8,128)(2,1)S(1)} %get-tuple-element.138), channel_id=1, source_target_pairs={{0,1},{1,0},{2,3},{3,2},{4,5},{5,4},{6,7},{7,6},{8,9},{9,8},{10,11... | collective-permute-start | bytes 221192 | tf_op jit(solution)/shard_map/ppermute | solution.py:397
  190.5 2.3 %collective-permute-done.39.g1 = bf16[192,192]{1,0:T(8,128)(2,1)S(1)} collective-permute-done((bf16[192,192]{1,0:T(8,128)(2,1)S(1)}, bf16[192,192]{1,0:T(8,128)(2,1)S(1)}, u32[]{:S(2)}, u32[]{:S(2)}) %collective-permute-start.39) | collective-permute-done | bytes 73760 | tf_op jit(solution)/shard_map/ppermute | solution.py:397
  192.9 2.2 %collective-permute-start.41 = (bf16[192,192]{1,0:T(8,128)(2,1)S(1)}, bf16[192,192]{1,0:T(8,128)(2,1)S(1)}, u32[]{:S(2)}, u32[]{:S(2)}) collective-permute-start(bf16[192,192]{1,0:T(8,128)(2,1)S(1)} %get-tuple-element.140), channel_id=1, source_target_pairs={{0,3},{1,2},{2,1},{3,0},{4,7},{5,6},{6,5},{7,4},{8,11},{9,10},{10,... | collective-permute-start | bytes 221192 | tf_op jit(solution)/shard_map/ppermute | solution.py:397
  197.1 2.3 %collective-permute-done.41.g3 = bf16[192,192]{1,0:T(8,128)(2,1)S(1)} collective-permute-done((bf16[192,192]{1,0:T(8,128)(2,1)S(1)}, bf16[192,192]{1,0:T(8,128)(2,1)S(1)}, u32[]{:S(2)}, u32[]{:S(2)}) %collective-permute-start.41) | collective-permute-done | bytes 73760 | tf_op jit(solution)/shard_map/ppermute | solution.py:397
  (119 shorter events, 41.7 us)
Async XLA Ops:
  0.7 47.4 %collective-permute-start.1 = (bf16[192,576]{1,0:T(8,128)(2,1)}, bf16[192,576]{1,0:T(8,128)(2,1)S(1)}, u32[]{:S(2)}, u32[]{:S(2)}) collective-permute-start(bf16[192,576]{1,0:T(8,128)(2,1)} %w0.3), channel_id=1, source_target_pairs={{0,4},{4,0},{8,12},{12,8},{1,5},{5,1},{9,13},{13,9},{2,6},{6,2},{1... | collective-permute-start | bytes 663560 | tf_op jit(solution)/shard_map/ppermute | solution.py:397
  1.2 30.9 %collective-permute-start = (bf16[192,576]{1,0:T(8,128)(2,1)}, bf16[192,576]{1,0:T(8,128)(2,1)S(1)}, u32[]{:S(2)}, u32[]{:S(2)}) collective-permute-start(bf16[192,576]{1,0:T(8,128)(2,1)} %w0.3), channel_id=1, source_target_pairs={{0,8},{4,12},{8,0},{12,4},{1,9},{5,13},{9,1},{13,5},{2,10},{6,14},... | collective-permute-start | bytes 663560 | tf_op jit(solution)/shard_map/ppermute | solution.py:397
  32.1 15.4 %collective-permute-start.14 = (bf16[192,512]{1,0:T(8,128)(2,1)S(1)}, bf16[192,512]{1,0:T(8,128)(2,1)S(1)}, u32[]{:S(2)}, u32[]{:S(2)}) collective-permute-start(bf16[192,512]{1,0:T(8,128)(2,1)S(1)} %copy-done.3), channel_id=1, source_target_pairs={{0,2},{1,3},{2,0},{3,1},{4,6},{5,7},{6,4},{7,5},{8,10},{9,11},{10,... | collective-permute-start | bytes 589832 | tf_op jit(solution)/shard_map/ppermute | solution.py:397
  32.1 17.5 %collective-permute-start.2 = (bf16[192,576]{1,0:T(8,128)(2,1)S(1)}, bf16[192,576]{1,0:T(8,128)(2,1)S(1)}, u32[]{:S(2)}, u32[]{:S(2)}) collective-permute-start(bf16[192,576]{1,0:T(8,128)(2,1)S(1)} %collective-permute-done.w1), channel_id=1, source_target_pairs={{0,4},{4,0},{8,12},{12,8},{1,5},{5,1},{9,13},{13,9},{2,6},{6,2},{1... | collective-permute-start | bytes 663560 | tf_op jit(solution)/shard_map/ppermute | solution.py:397
  33.7 21.6 %collective-permute-start.7 = (bf16[192,768]{1,0:T(8,128)(2,1)S(1)}, bf16[192,768]{1,0:T(8,128)(2,1)S(1)}, u32[]{:S(2)}, u32[]{:S(2)}) collective-permute-start(bf16[192,768]{1,0:T(8,128)(2,1)S(1)} %copy-done.8), channel_id=1, source_target_pairs={{0,8},{4,12},{8,0},{12,4},{1,9},{5,13},{9,1},{13,5},{2,10},{6,14},... | collective-permute-start | bytes 884744 | tf_op jit(solution)/shard_map/ppermute | solution.py:397
  38.4 17.4 %collective-permute-start.8 = (bf16[192,768]{1,0:T(8,128)(2,1)S(1)}, bf16[192,768]{1,0:T(8,128)(2,1)S(1)}, u32[]{:S(2)}, u32[]{:S(2)}) collective-permute-start(bf16[192,768]{1,0:T(8,128)(2,1)S(1)} %copy-done.8), channel_id=1, source_target_pairs={{0,4},{4,0},{8,12},{12,8},{1,5},{5,1},{9,13},{13,9},{2,6},{6,2},{1... | collective-permute-start | bytes 884744 | tf_op jit(solution)/shard_map/ppermute | solution.py:397
  47.5 9.9 %collective-permute-start.10 = (bf16[192,768]{1,0:T(8,128)(2,1)S(1)}, bf16[192,768]{1,0:T(8,128)(2,1)S(1)}, u32[]{:S(2)}, u32[]{:S(2)}) collective-permute-start(bf16[192,768]{1,0:T(8,128)(2,1)S(1)} %copy-done.10), channel_id=1, source_target_pairs={{0,8},{4,12},{8,0},{12,4},{1,9},{5,13},{9,1},{13,5},{2,10},{6,14},... | collective-permute-start | bytes 884744 | tf_op jit(solution)/shard_map/ppermute | solution.py:397
  48.0 15.6 %collective-permute-start.4 = (bf16[768,192]{1,0:T(8,128)(2,1)S(1)}, bf16[768,192]{1,0:T(8,128)(2,1)S(1)}, u32[]{:S(2)}, u32[]{:S(2)}) collective-permute-start(bf16[768,192]{1,0:T(8,128)(2,1)S(1)} %shard_map.256.m0), channel_id=1, source_target_pairs={{0,8},{4,12},{8,0},{12,4},{1,9},{5,13},{9,1},{13,5},{2,10},{6,14},... | collective-permute-start | bytes 884744 | tf_op jit(solution)/shard_map/ppermute | solution.py:397
  55.2 26.5 %collective-permute-start.11 = (bf16[192,768]{1,0:T(8,128)(2,1)S(1)}, bf16[192,768]{1,0:T(8,128)(2,1)S(1)}, u32[]{:S(2)}, u32[]{:S(2)}) collective-permute-start(bf16[192,768]{1,0:T(8,128)(2,1)S(1)} %copy-done.10), channel_id=1, source_target_pairs={{0,4},{4,0},{8,12},{12,8},{1,5},{5,1},{9,13},{13,9},{2,6},{6,2},{1... | collective-permute-start | bytes 884744 | tf_op jit(solution)/shard_map/ppermute | solution.py:397
  55.2 26.5 %collective-permute-start.5 = (bf16[768,192]{1,0:T(8,128)(2,1)S(1)}, bf16[768,192]{1,0:T(8,128)(2,1)S(1)}, u32[]{:S(2)}, u32[]{:S(2)}) collective-permute-start(bf16[768,192]{1,0:T(8,128)(2,1)S(1)} %shard_map.256.m0), channel_id=1, source_target_pairs={{0,4},{4,0},{8,12},{12,8},{1,5},{5,1},{9,13},{13,9},{2,6},{6,2},{1... | collective-permute-start | bytes 884744 | tf_op jit(solution)/shard_map/ppermute | solution.py:397
  55.8 26.0 %collective-permute-start.9 = (bf16[192,768]{1,0:T(8,128)(2,1)S(1)}, bf16[192,768]{1,0:T(8,128)(2,1)S(1)}, u32[]{:S(2)}, u32[]{:S(2)}) collective-permute-start(bf16[192,768]{1,0:T(8,128)(2,1)S(1)} %collective-permute-done.7.u1), channel_id=1, source_target_pairs={{0,4},{4,0},{8,12},{12,8},{1,5},{5,1},{9,13},{13,9},{2,6},{6,2},{1... | collective-permute-start | bytes 884744 | tf_op jit(solution)/shard_map/ppermute | solution.py:397
  57.4 24.3 %collective-permute-start.12 = (bf16[192,768]{1,0:T(8,128)(2,1)S(1)}, bf16[192,768]{1,0:T(8,128)(2,1)S(1)}, u32[]{:S(2)}, u32[]{:S(2)}) collective-permute-start(bf16[192,768]{1,0:T(8,128)(2,1)S(1)} %collective-permute-done.10.d1), channel_id=1, source_target_pairs={{0,4},{4,0},{8,12},{12,8},{1,5},{5,1},{9,13},{13,9},{2,6},{6,2},{1... | collective-permute-start | bytes 884744 | tf_op jit(solution)/shard_map/ppermute | solution.py:397
  63.6 18.1 %collective-permute-start.6 = (bf16[768,192]{1,0:T(8,128)(2,1)S(1)}, bf16[768,192]{1,0:T(8,128)(2,1)S(1)}, u32[]{:S(2)}, u32[]{:S(2)}) collective-permute-start(bf16[768,192]{1,0:T(8,128)(2,1)S(1)} %collective-permute-done.4.m1), channel_id=1, source_target_pairs={{0,4},{4,0},{8,12},{12,8},{1,5},{5,1},{9,13},{13,9},{2,6},{6,2},{1... | collective-permute-start | bytes 884744 | tf_op jit(solution)/shard_map/ppermute | solution.py:397
  92.7 28.3 %collective-permute-start.25 = (bf16[192,1536]{1,0:T(8,128)(2,1)S(1)}, bf16[192,1536]{1,0:T(8,128)(2,1)S(1)}, u32[]{:S(2)}, u32[]{:S(2)}) collective-permute-start(bf16[192,1536]{1,0:T(8,128)(2,1)S(1)} %get-tuple-element.116), channel_id=1, source_target_pairs={{0,8},{4,12},{8,0},{12,4},{1,9},{5,13},{9,1},{13,5},{2,10},{6,14},... | collective-permute-start | bytes 1769480 | tf_op jit(solution)/shard_map/ppermute | solution.py:397
  93.3 10.0 %collective-permute-start.16 = (bf16[768,128]{1,0:T(8,128)(2,1)S(1)}, bf16[768,128]{1,0:T(8,128)(2,1)S(1)}, u32[]{:S(2)}, u32[]{:S(2)}) collective-permute-start(bf16[768,128]{1,0:T(8,128)(2,1)S(1)} %get-tuple-element.87), channel_id=1, source_target_pairs={{0,1},{1,0},{2,3},{3,2},{4,5},{5,4},{6,7},{7,6},{8,9},{9,8},{10,11... | collective-permute-start | bytes 589832 | tf_op jit(solution)/shard_map/ppermute | solution.py:397
  93.3 17.1 %collective-permute-start.17 = (bf16[768,128]{1,0:T(8,128)(2,1)S(1)}, bf16[768,128]{1,0:T(8,128)(2,1)S(1)}, u32[]{:S(2)}, u32[]{:S(2)}) collective-permute-start(bf16[768,128]{1,0:T(8,128)(2,1)S(1)} %get-tuple-element.88), channel_id=1, source_target_pairs={{0,2},{1,3},{2,0},{3,1},{4,6},{5,7},{6,4},{7,5},{8,10},{9,11},{10,... | collective-permute-start | bytes 589832 | tf_op jit(solution)/shard_map/ppermute | solution.py:397
  95.7 14.7 %collective-permute-start.18 = (bf16[768,128]{1,0:T(8,128)(2,1)S(1)}, bf16[768,128]{1,0:T(8,128)(2,1)S(1)}, u32[]{:S(2)}, u32[]{:S(2)}) collective-permute-start(bf16[768,128]{1,0:T(8,128)(2,1)S(1)} %get-tuple-element.89), channel_id=1, source_target_pairs={{0,3},{1,2},{2,1},{3,0},{4,7},{5,6},{6,5},{7,4},{8,11},{9,10},{10,... | collective-permute-start | bytes 589832 | tf_op jit(solution)/shard_map/ppermute | solution.py:397
  112.1 9.9 %collective-permute-start.22 = (bf16[192,128]{1,0:T(8,128)(2,1)S(1)}, bf16[192,128]{1,0:T(8,128)(2,1)S(1)}, u32[]{:S(2)}, u32[]{:S(2)}) collective-permute-start(bf16[192,128]{1,0:T(8,128)(2,1)S(1)} %get-tuple-element.112), channel_id=1, source_target_pairs={{0,1},{1,0},{2,3},{3,2},{4,5},{5,4},{6,7},{7,6},{8,9},{9,8},{10,11... | collective-permute-start | bytes 147464 | tf_op jit(solution)/shard_map/ppermute | solution.py:397
  118.3 13.8 %collective-permute-start.20 = (bf16[384,512]{1,0:T(8,128)(2,1)S(1)}, bf16[384,512]{1,0:T(8,128)(2,1)S(1)}, u32[]{:S(2)}, u32[]{:S(2)}) collective-permute-start(bf16[384,512]{1,0:T(8,128)(2,1)S(1)} %get-tuple-element.105), channel_id=1, source_target_pairs={{0,1},{1,0},{2,3},{3,2},{4,5},{5,4},{6,7},{7,6},{8,9},{9,8},{10,11... | collective-permute-start | bytes 1179656 | tf_op jit(solution)/shard_map/ppermute | solution.py:397
  121.1 32.6 %collective-permute-start.36 = (bf16[384,768]{1,0:T(8,128)(2,1)}, bf16[384,768]{1,0:T(8,128)(2,1)}, u32[]{:S(2)}, u32[]{:S(2)}) collective-permute-start(bf16[384,768]{1,0:T(8,128)(2,1)} %shard_map.269), channel_id=1, source_target_pairs={{0,4},{4,0},{8,12},{12,8},{1,5},{5,1},{9,13},{13,9},{2,6},{6,2},{1... | collective-permute-start | bytes 1769480 | tf_op jit(solution)/shard_map/ppermute | solution.py:397
  127.6 10.7 %collective-permute-start.26 = (bf16[208,512]{1,0:T(8,128)(2,1)S(1)}, bf16[208,512]{1,0:T(8,128)(2,1)S(1)}, u32[]{:S(2)}, u32[]{:S(2)}) collective-permute-start(bf16[208,512]{1,0:T(8,128)(2,1)S(1)} %get-tuple-element.123), channel_id=1, source_target_pairs={{0,1},{1,0},{2,3},{3,2},{4,5},{5,4},{6,7},{7,6},{8,9},{9,8},{10,11... | collective-permute-start | bytes 638984 | tf_op jit(solution)/shard_map/ppermute | solution.py:397
  127.8 22.4 %collective-permute-start.27 = (bf16[208,512]{1,0:T(8,128)(2,1)S(1)}, bf16[208,512]{1,0:T(8,128)(2,1)S(1)}, u32[]{:S(2)}, u32[]{:S(2)}) collective-permute-start(bf16[208,512]{1,0:T(8,128)(2,1)S(1)} %get-tuple-element.124), channel_id=1, source_target_pairs={{0,2},{1,3},{2,0},{3,1},{4,6},{5,7},{6,4},{7,5},{8,10},{9,11},{10,... | collective-permute-start | bytes 638984 | tf_op jit(solution)/shard_map/ppermute | solution.py:397
  130.1 20.1 %collective-permute-start.28 = (bf16[208,512]{1,0:T(8,128)(2,1)S(1)}, bf16[208,512]{1,0:T(8,128)(2,1)S(1)}, u32[]{:S(2)}, u32[]{:S(2)}) collective-permute-start(bf16[208,512]{1,0:T(8,128)(2,1)S(1)} %get-tuple-element.125), channel_id=1, source_target_pairs={{0,3},{1,2},{2,1},{3,0},{4,7},{5,6},{6,5},{7,4},{8,11},{9,10},{10,... | collective-permute-start | bytes 638984 | tf_op jit(solution)/shard_map/ppermute | solution.py:397
  133.4 25.5 %collective-permute-start.21 = (bf16[192,512]{1,0:T(8,128)(2,1)}, bf16[192,512]{1,0:T(8,128)(2,1)}, u32[]{:S(2)}, u32[]{:S(2)}) collective-permute-start(bf16[192,512]{1,0:T(8,128)(2,1)} %get-tuple-element.107), channel_id=1, source_target_pairs={{0,2},{1,3},{2,0},{3,1},{4,6},{5,7},{6,4},{7,5},{8,10},{9,11},{10,... | collective-permute-start | bytes 589832 | tf_op jit(solution)/shard_map/ppermute | solution.py:397
  155.0 18.6 %collective-permute-start.37 = (bf16[192,768]{1,0:T(8,128)(2,1)S(1)}, bf16[192,768]{1,0:T(8,128)(2,1)S(1)}, u32[]{:S(2)}, u32[]{:S(2)}) collective-permute-start(bf16[192,768]{1,0:T(8,128)(2,1)S(1)} %get-tuple-element.136), channel_id=1, source_target_pairs={{0,8},{4,12},{8,0},{12,4},{1,9},{5,13},{9,1},{13,5},{2,10},{6,14},... | collective-permute-start | bytes 884744 | tf_op jit(solution)/shard_map/ppermute | solution.py:397
  156.7 18.8 %collective-permute-start.32 = (bf16[384,576]{1,0:T(8,128)(2,1)S(1)}, bf16[384,576]{1,0:T(8,128)(2,1)S(1)}, u32[]{:S(2)}, u32[]{:S(2)}) collective-permute-start(bf16[384,576]{1,0:T(8,128)(2,1)S(1)} %shard_map.266), channel_id=1, source_target_pairs={{0,4},{4,0},{8,12},{12,8},{1,5},{5,1},{9,13},{13,9},{2,6},{6,2},{1... | collective-permute-start | bytes 1327112 | tf_op jit(solution)/shard_map/ppermute | solution.py:397
  156.7 33.0 %collective-permute-start.42 = (bf16[192,1536]{1,0:T(8,128)(2,1)S(1)}, bf16[192,1536]{1,0:T(8,128)(2,1)S(1)}, u32[]{:S(2)}, u32[]{:S(2)}) collective-permute-start(bf16[192,1536]{1,0:T(8,128)(2,1)S(1)} %copy-done.12), channel_id=1, source_target_pairs={{0,16},{16,0},{1,17},{17,1},{2,18},{18,2},{3,19},{19,3},{4,20},{20... | collective-permute-start | bytes 1769480 | tf_op jit(solution)/shard_map/ppermute | solution.py:397
  157.3 15.6 %collective-permute-start.31 = (f32[8,768]{1,0:T(8,128)S(1)}, f32[8,768]{1,0:T(8,128)S(1)}, u32[]{:S(2)}, u32[]{:S(2)}) collective-permute-start(f32[8,768]{1,0:T(8,128)S(1)} %add.44), channel_id=1, source_target_pairs={{0,16},{16,0},{1,17},{17,1},{2,18},{18,2},{3,19},{19,3},{4,20},{20... | collective-permute-start | bytes 73736 | tf_op jit(solution)/shard_map/ppermute | solution.py:397
  173.7 9.9 %collective-permute-start.38 = (bf16[192,768]{1,0:T(8,128)(2,1)S(1)}, bf16[192,768]{1,0:T(8,128)(2,1)S(1)}, u32[]{:S(2)}, u32[]{:S(2)}) collective-permute-start(bf16[192,768]{1,0:T(8,128)(2,1)S(1)} %add_convert_fusion), channel_id=1, source_target_pairs={{0,16},{16,0},{1,17},{17,1},{2,18},{18,2},{3,19},{19,3},{4,20},{20... | collective-permute-start | bytes 884744 | tf_op jit(solution)/shard_map/ppermute | solution.py:397
  176.5 24.2 %collective-permute-start.35 = (bf16[192,576]{1,0:T(8,128)(2,1)S(1)}, bf16[192,576]{1,0:T(8,128)(2,1)S(1)}, u32[]{:S(2)}, u32[]{:S(2)}) collective-permute-start(bf16[192,576]{1,0:T(8,128)(2,1)S(1)} %get-tuple-element.133), channel_id=1, source_target_pairs={{0,24},{4,28},{8,16},{12,20},{16,8},{20,12},{24,0},{28,4},{1,25},{... | collective-permute-start | bytes 663560 | tf_op jit(solution)/shard_map/ppermute | solution.py:604
  179.0 21.7 %collective-permute-start.33 = (bf16[192,576]{1,0:T(8,128)(2,1)S(1)}, bf16[192,576]{1,0:T(8,128)(2,1)S(1)}, u32[]{:S(2)}, u32[]{:S(2)}) collective-permute-start(bf16[192,576]{1,0:T(8,128)(2,1)S(1)} %get-tuple-element.133), channel_id=1, source_target_pairs={{0,8},{4,12},{8,0},{12,4},{1,9},{5,13},{9,1},{13,5},{2,10},{6,14},... | collective-permute-start | bytes 663560 | tf_op jit(solution)/shard_map/ppermute | solution.py:397
  179.5 21.2 %collective-permute-start.34 = (bf16[192,576]{1,0:T(8,128)(2,1)S(1)}, bf16[192,576]{1,0:T(8,128)(2,1)S(1)}, u32[]{:S(2)}, u32[]{:S(2)}) collective-permute-start(bf16[192,576]{1,0:T(8,128)(2,1)S(1)} %get-tuple-element.134), channel_id=1, source_target_pairs={{0,16},{16,0},{1,17},{17,1},{2,18},{18,2},{3,19},{19,3},{4,20},{20... | collective-permute-start | bytes 663560 | tf_op jit(solution)/shard_map/ppermute | solution.py:603
  (24 other events, 422.4 us)

commit v7 on v6

--- a/solution.py
+++ b/solution.py
@@ -9,6 +9,8 @@
 from jax.sharding import PartitionSpec as P
 
 
+COLS = "cols"
+ROWS = "rows"
 HD = 64
 MAXLEN = 256
 EPS = 1e-05
@@ -62,14 +64,14 @@
     return [cols[:, k : k + 1] + cols[:, k + 5 : k + 6] + cols[:, k + 10 : k + 11] for k in which]
 
 
-def run(kernel, outs, ins, scratch=(), flops=0, hold=True, limit=24):
+def run(kernel, outs, ins, scratch=(), flops=0, hold=True, limit=24, final=False):
     specs = [pl.BlockSpec(memory_space=pltpu.SMEM)]
     specs += [pl.BlockSpec(memory_space=pltpu.VMEM)] * (len(ins) - 1)
     size = sum(math.prod(value.shape) * value.dtype.itemsize for value in list(ins) + list(outs))
     held = [pltpu.with_memory_space_constraint(value, pltpu.VMEM) if hold else value for value in ins[1:]]
     return pl.pallas_call(
         kernel,
-        out_shape=[pltpu.VMEM(value.shape, value.dtype) for value in outs],
+        out_shape=list(outs) if final else [pltpu.VMEM(value.shape, value.dtype) for value in outs],
         in_specs=specs,
         out_specs=[pl.BlockSpec(memory_space=pltpu.VMEM)] * len(outs),
         scratch_shapes=list(scratch),
@@ -365,6 +367,12 @@
     rest[...] = total.T[:8]
 
 
+def sums_out_kernel(here, sums, got, *outs):
+    total = sums[...] + got[...]
+    for row, out in enumerate(outs):
+        out[...] = total[row : row + 1, : out.shape[1]]
+
+
 def token_sum_kernel(here, s0, g1, g2, g3, rest, out, sums):
     feat = out.shape[0]
     total = s0[...]
@@ -379,6 +387,10 @@
     qkv[...] = own[...] + got_y[...].astype(F32) + got_x[...].astype(F32) + got_xy[...].astype(F32)
 
 
+def output_kernel(here, own_hidden, down_col, keep, got, out):
+    out[...] = (own_hidden[...] + down_col[...] + keep[...] + got[...].astype(F32)).astype(BF16)
+
+
 def halve_kernel(here, keep, got, kept, send):
     half = kept.shape[0]
     kept[...] = keep[:half] + got[:half].astype(F32)
@@ -411,10 +423,10 @@
     order = (0, far, near, far ^ near)
 
     def over_rows(value, bit):
-        return swap(value, "rows", n_rows, bit)
+        return swap(value, ROWS, n_rows, bit)
 
     def over_cols(value, bit):
-        return swap(value, "cols", n_cols, bit)
+        return swap(value, COLS, n_cols, bit)
 
     def all_over_cols(values):
         return [over_cols(value, bit) for value, bit in zip(values, (1, 2, 3))]
@@ -449,7 +461,7 @@
         n_hid = up_weight.shape[1]
         heads = n_qkv // (3 * HD)
         head_rows = heads * HD
-        here = [lax.axis_index("rows"), lax.axis_index("cols"), lax.axis_index("dp") & 1]
+        here = [lax.axis_index(ROWS), lax.axis_index(COLS), lax.axis_index("dp") & 1]
         here = jnp.stack(here).astype(jnp.int32)
         row = segment_ids.reshape(1, count)
 
@@ -471,7 +483,7 @@
             hold=False,
             limit=58,
         )
-        tok = lax.all_gather(packed, "cols", axis=0, tiled=True)
+        tok = lax.all_gather(packed, COLS, axis=0, tiled=True)
         qkv_yc = over_rows(qkv_y, near)
         w_pieces = (qkv_weight, qkv_y, qkv_c, qkv_yc)
         cot_own = after(cotangent, tok)
@@ -496,7 +508,7 @@
             scratch=(pltpu.VMEM((width, n_qkv), BF16),),
             flops=2 * width * n_qkv * count,
         )
-        att = lax.all_gather(attended, "cols", axis=0, tiled=True)
+        att = lax.all_gather(attended, COLS, axis=0, tiled=True)
         mix_yc = over_rows(mix_y, near)
         m_pieces = (mix_all, mix_y, mix_c, mix_yc)
 
@@ -541,7 +553,7 @@
         )
         ff_keep, ff_send = halve(ff_keep, over_rows(ff_send, near))
         ff_got = over_rows(ff_send, far)
-        got[0], got[1], got[2], ff_keep, out_send = together(*got, ff_keep, out_send)
+        got[0], got[1], got[2], ff_keep = together(*got, ff_keep)
 
         grad_hidden, grad_hidden_b, second, a0, a1, a2, a3 = run(
             functools.partial(second_back_kernel, order),
@@ -565,7 +577,7 @@
             flops=width * width * part,
         )
         mix_got = over_rows(mix_send, far)
-        out_got = over_cols(after(out_send, grad_hidden_b), 1)
+        out_got = over_cols(out_send, 1)
         ff_sum = ff_keep + ff_got.astype(F32)
         b1, b2, b3, ff_sum = together(b1, b2, b3, ff_sum)
         grad_ff = over_dp(ff_sum)
@@ -601,20 +613,28 @@
         got_y = over_rows(last_send, far)
         if n_dp > 1:
             got_x = lax.ppermute(own_b, "dp", pairs)
-            got_xy = lax.ppermute(last_send, ("dp", "rows"), far_dp)
+            got_xy = lax.ppermute(last_send, ("dp", ROWS), far_dp)
         else:
             got_x = got_xy = jnp.zeros_like(got_y)
-        (grad_qkv,) = run(last_sum_kernel, (shaped((feat, n_qkv), F32),), (here, own, got_y, got_x, got_xy))
+        (grad_qkv,) = run(last_sum_kernel, (shaped((feat, n_qkv), F32),), (here, own, got_y, got_x, got_xy), final=True)
         for bit in bits_of(n_dp)[1:]:
             grad_qkv = grad_qkv + swap(grad_qkv.astype(BF16), "dp", n_dp, bit).astype(F32)
 
-        (rest,) = run(rest_kernel, (shaped((8, width), F32),), (here, up_sum, qv_sum, cotangent, row))
+        (rest,) = run(rest_kernel, (shaped((8, width), F32),), (here, up_sum, qv_sum, cotangent, row), hold=False)
         grad_tokens, sums = run(
             token_sum_kernel, (shaped((feat, count), F32), shaped((8, width), F32)), (here, s0) + tuple(got) + (rest,)
         )
-        for axis, size in (("rows", n_rows), ("dp", n_dp)):
-            for bit in bits_of(size):
-                sums = sums + swap(sums, axis, size, bit)
+        steps = [(ROWS, n_rows, bit) for bit in bits_of(n_rows)] + [("dp", n_dp, bit) for bit in bits_of(n_dp)]
+        for axis, size, bit in steps:
+            sums_got = swap(sums, axis, size, bit)
+            if (axis, size, bit) != steps[-1]:
+                sums = sums + sums_got
+        lengths = (feat, feat, feat, feat, feat, n_hid, 2 * head_rows, feat)
+        sums = run(
+            sums_out_kernel, tuple(shaped((1, length), F32) for length in lengths), (here, sums, sums_got),
+            final=True,
+        )
+        sums = [value.reshape(-1) for value in sums]
 
         square_b = shaped((feat, feat), BF16)
         mix_own, p1, p2, p3 = run(
@@ -624,24 +644,28 @@
             scratch=(pltpu.VMEM((width, feat), F32),),
         )
         got = all_over_cols((p1, p2, p3))
-        (grad_mix,) = run(mix_sum_kernel, (shaped((feat, feat), F32),), (here, mix_own) + tuple(got))
+        (grad_mix,) = run(mix_sum_kernel, (shaped((feat, feat), F32),), (here, mix_own) + tuple(got), final=True)
         out_keep, out_send = halve(out_keep, out_got)
-        output = own_hidden + down_col + out_keep + over_cols(out_send, 2).astype(F32)
+        (output,) = run(
+            output_kernel, (shaped((feat, count), BF16),),
+            (here, own_hidden, down_col, out_keep, over_cols(out_send, 2)),
+            final=True,
+        )
         return (
-            output.astype(BF16),
+            output,
             grad_tokens,
-            sums[3, :feat],
-            sums[4, :feat],
+            sums[3],
+            sums[4],
             grad_qkv,
-            sums[6, : 2 * head_rows],
+            sums[6],
             grad_mix,
-            sums[2, :feat],
-            sums[0, :feat],
-            sums[1, :feat],
+            sums[2],
+            sums[0],
+            sums[1],
             grad_ff[:, n_hid:],
-            sums[5, :n_hid],
+            sums[5],
             grad_ff[:, :n_hid],
-            sums[7, :feat],
+            sums[7],
         )
 
     return body
@@ -649,43 +673,43 @@
 
 def solution(mesh):
     sizes = mesh.shape
-    body = make_body(sizes["dp"], sizes["rows"], sizes["cols"])
+    body = make_body(sizes["dp"], sizes[ROWS], sizes[COLS])
 
     return jax.shard_map(
         body,
         mesh=mesh,
         in_specs=(
-            P("cols", ("dp", "rows")),
-            P(("dp", "rows")),
-            P("cols"),
-            P("cols"),
-            P("rows", "cols"),
-            P("cols"),
-            P("cols", "rows"),
-            P("cols"),
-            P("cols"),
-            P("cols"),
-            P("rows", "cols"),
-            P("cols"),
-            P("rows", "cols"),
-            P("cols"),
-            P("cols", ("dp", "rows")),
+            P(COLS, ("dp", ROWS)),
+            P(("dp", ROWS)),
+            P(COLS),
+            P(COLS),
+            P(ROWS, COLS),
+            P(COLS),
+            P(COLS, ROWS),
+            P(COLS),
+            P(COLS),
+            P(COLS),
+            P(ROWS, COLS),
+            P(COLS),
+            P(ROWS, COLS),
+            P(COLS),
+            P(COLS, ("dp", ROWS)),
         ),
         out_specs=(
-            P("cols", ("dp", "rows")),
-            P("cols", ("dp", "rows")),
-            P("cols"),
-            P("cols"),
-            P("rows", "cols"),
-            P("cols"),
-            P("cols", "rows"),
-            P("cols"),
-            P("cols"),
-            P("cols"),
-            P("rows", "cols"),
-            P("cols"),
-            P("rows", "cols"),
-            P("cols"),
+            P(COLS, ("dp", ROWS)),
+            P(COLS, ("dp", ROWS)),
+            P(COLS),
+            P(COLS),
+            P(ROWS, COLS),
+            P(COLS),
+            P(COLS, ROWS),
+            P(COLS),
+            P(COLS),
+            P(COLS),
+            P(ROWS, COLS),
+            P(COLS),
+            P(ROWS, COLS),
+            P(COLS),
         ),
         check_vma=False,
     )

time: 202 us -> 193 us (0.955)
  waiting for transfers between devices: 76.7 us -> 67 us
  local copies, waits for them, and re-layouts: 5.17 us -> 1.89 us
    ppermute x40, waiting for transfers between devices: 75.1 us -> 65.4 us  [swap(): return lax.ppermute(values, axis, [(at, at ^ bit) for at in range(size)])]
    add x2, other arithmetic: 0.21 us -> 2.26 us  [over_dp(): value = value + swap(value.astype(BF16), 'dp', n_dp, bit).astype(F32)]
    pallas_call x19 -> x21, Pallas kernels: 31.7 us -> 33.7 us  [run(): pl.pallas_call(kernel, out_shape=list(outs) if final else [pltpu.VMEM(val...]
  transfers between devices with their start and end apart: 43 -> 43, of which waited for: 18 -> 19; matrix products, arithmetic and copies ran while one was open for 4% -> 3% of each run, Pallas kernels for 11% -> 12%
where the time goes in v7:
time: 193 us
  waiting for transfers between devices  67 us (35%)
  starting transfers between devices  44.7 us (23%)
  blocking collectives  40.2 us (21%)
  Pallas kernels  33.7 us (17%)
  other arithmetic  4.27 us (2%)
    ppermute x40, waiting for transfers between devices, swap(): return lax.ppermute(values, axis, [(at, at ^ bit) for at in range(size)])  65.4 us
    ppermute x40, starting transfers between devices, swap(): return lax.ppermute(values, axis, [(at, at ^ bit) for at in range(size)])  40.1 us
    pallas_call x21, Pallas kernels, run(): pl.pallas_call(kernel, out_shape=list(outs) if final else [pltpu.VMEM(val...  33.7 us
    all_gather x1, blocking collectives, body(): tok = lax.all_gather(packed, COLS, axis=0, tiled=True)  22.1 us
    all_gather x1, blocking collectives, body(): att = lax.all_gather(attended, COLS, axis=0, tiled=True)  18.1 us
  transfers between devices with their start and end apart: 43, of which 19 were waited for; matrix products, arithmetic and copies ran while one was open for 3% of the time, Pallas kernels for 12%

profile of v7, /device:TPU:0, one launch (start us, length us, event | category | flops | bytes accessed | tf_op | source)
XLA Modules:
  0.0 192.7 jit_solution(7791615828826734950)
XLA Ops:
  1.2 2.6 %collective-permute-start = (bf16[192,576]{1,0:T(8,128)(2,1)}, bf16[192,576]{1,0:T(8,128)(2,1)S(1)}, u32[]{:S(2)}, u32[]{:S(2)}) collective-permute-start(bf16[192,576]{1,0:T(8,128)(2,1)} %w0.3), channel_id=1, source_target_pairs={{0,8},{4,12},{8,0},{12,4},{1,9},{5,13},{9,1},{13,5},{2,10},{6,14},... | collective-permute-start | bytes 663560 | tf_op jit(solution)/shard_map/ppermute | solution.py:409
  5.8 22.1 %all_gather.6.tok = bf16[768,640]{1,0:T(8,128)(2,1)S(1)} all-gather(bf16[192,640]{1,0:T(8,128)(2,1)S(1)} %get-tuple-element.84), channel_id=1, replica_groups=mesh['dp'=2,'rows'=4,'cols'=4] {'cols'}, dimensions={0}, use_global_device_ids=true | all-gather | bytes 1228800 | tf_op jit(solution)/shard_map/all_gather | solution.py:486
  29.5 2.6 %collective-permute-start.15 = (bf16[192,512]{1,0:T(8,128)(2,1)S(1)}, bf16[192,512]{1,0:T(8,128)(2,1)S(1)}, u32[]{:S(2)}, u32[]{:S(2)}) collective-permute-start(bf16[192,512]{1,0:T(8,128)(2,1)S(1)} %copy-done.1), channel_id=1, source_target_pairs={{0,3},{1,2},{2,1},{3,0},{4,7},{5,6},{6,5},{7,4},{8,11},{9,10},{10,... | collective-permute-start | bytes 589832 | tf_op jit(solution)/shard_map/ppermute | solution.py:409
  34.9 3.5 %collective-permute-done.15.c3 = bf16[192,512]{1,0:T(8,128)(2,1)S(1)} collective-permute-done((bf16[192,512]{1,0:T(8,128)(2,1)S(1)}, bf16[192,512]{1,0:T(8,128)(2,1)S(1)}, u32[]{:S(2)}, u32[]{:S(2)}) %collective-permute-start.15) | collective-permute-done | bytes 196640 | tf_op jit(solution)/shard_map/ppermute | solution.py:409
  38.4 9.2 %collective-permute-done.14.c2 = bf16[192,512]{1,0:T(8,128)(2,1)S(1)} collective-permute-done((bf16[192,512]{1,0:T(8,128)(2,1)S(1)}, bf16[192,512]{1,0:T(8,128)(2,1)S(1)}, u32[]{:S(2)}, u32[]{:S(2)}) %collective-permute-start.14) | collective-permute-done | bytes 196640 | tf_op jit(solution)/shard_map/ppermute | solution.py:409
  49.6 3.8 %shard_map.255 = (bf16[768,512]{1,0:T(8,128)(2,1)S(1)}, f32[2,512]{1,0:T(2,128)S(1)}, bf16[576,512]{1,0:T(8,128)(2,1)S(1)}, bf16[192,512]{1,0:T(8,128)(2,1)S(1)}, f32[3,512]{1,0:T(4,128)S(1)}) custom-call(s32[3]{0:T(128)S(1)} %copy-done.2, bf16[768,640]{1,0:T(8,128)(2,1)S(1)} %all_gather.6.tok, bf16[192,576]{1,0:T(8,128)(2,1)S(1)} %copy-done, ...), custom_call_target="tpu_custom_call" | custom-call | flops 452984832 | bytes 3456524 | tf_op jit(solution)/shard_map/pallas_call | solution.py:72
  53.5 1.8 collective-permute-done.13.c1
  55.8 1.6 collective-permute-done.10.d1
  57.4 6.2 %collective-permute-done.4.m1 = bf16[768,192]{1,0:T(8,128)(2,1)S(1)} collective-permute-done((bf16[768,192]{1,0:T(8,128)(2,1)S(1)}, bf16[768,192]{1,0:T(8,128)(2,1)S(1)}, u32[]{:S(2)}, u32[]{:S(2)}) %collective-permute-start.4) | collective-permute-done | bytes 294944 | tf_op jit(solution)/shard_map/ppermute | solution.py:409
  63.6 18.1 %all_gather.7.att = bf16[768,512]{1,0:T(8,128)(2,1)S(1)} all-gather(bf16[192,512]{1,0:T(8,128)(2,1)S(1)} %get-tuple-element.86.att), channel_id=1, replica_groups=mesh['dp'=2,'rows'=4,'cols'=4] {'cols'}, dimensions={0}, use_global_device_ids=true | all-gather | bytes 983040 | tf_op jit(solution)/shard_map/all_gather | solution.py:511
  81.8 5.3 %shard_map.257 = (bf16[768,512]{1,0:T(8,128)(2,1)S(1)}, bf16[768,512]{1,0:T(8,128)(2,1)S(1)}, bf16[768,512]{1,0:T(8,128)(2,1)S(1)}, bf16[768,512]{1,0:T(8,128)(2...) custom-call(s32[3]{0:T(128)S(1)} %copy-done.2, ...), custom_call_target="tpu_custom_call" | custom-call | flops 2415919104 | bytes 12214284 | tf_op jit(solution)/shard_map/pallas_call | solution.py:72
  87.1 2.0 %shard_map.261 = (bf16[384,1536]{1,0:T(8,128)(2,1)S(1)}, f32[384,1536]{1,0:T(8,128)S(1)}) custom-call(s32[3]{0:T(128)S(1)} %copy-done.2, bf16[768,512]{1,0:T(8,128)(2,1)S(1)} %get-tuple-element.103.grad_final, bf16[768,512]{1,0:T(8,128)(2,1)S(1)} %get-tuple-element.91.active, bf16[768,512]{1,0:T(8,128)(2,1)S(1)} %get-tuple-element.104.normed, ...), custom_call_target="tpu_custom_call" | custom-call | flops 1207959552 | bytes 6684684 | tf_op jit(solution)/shard_map/pallas_call | solution.py:72
  89.2 2.4 %collective-permute-start.19 = (bf16[768,128]{1,0:T(8,128)(2,1)S(1)}, bf16[768,128]{1,0:T(8,128)(2,1)S(1)}, u32[]{:S(2)}, u32[]{:S(2)}) collective-permute-start(bf16[768,128]{1,0:T(8,128)(2,1)S(1)} %get-tuple-element.101), channel_id=1, source_target_pairs={{0,2},{1,3},{2,0},{3,1},{4,6},{5,7},{6,4},{7,5},{8,10},{9,11},{10,... | collective-permute-start | bytes 589832 | tf_op jit(solution)/shard_map/ppermute | solution.py:409
  91.6 2.0 %collective-permute-start.20 = (bf16[768,128]{1,0:T(8,128)(2,1)S(1)}, bf16[768,128]{1,0:T(8,128)(2,1)S(1)}, u32[]{:S(2)}, u32[]{:S(2)}) collective-permute-start(bf16[768,128]{1,0:T(8,128)(2,1)S(1)} %get-tuple-element.102), channel_id=1, source_target_pairs={{0,3},{1,2},{2,1},{3,0},{4,7},{5,6},{6,5},{7,4},{8,11},{9,10},{10,... | collective-permute-start | bytes 589832 | tf_op jit(solution)/shard_map/ppermute | solution.py:409
  94.3 5.7 %collective-permute-done.18.r1 = bf16[768,128]{1,0:T(8,128)(2,1)S(1)} collective-permute-done((bf16[768,128]{1,0:T(8,128)(2,1)S(1)}, bf16[768,128]{1,0:T(8,128)(2,1)S(1)}, u32[]{:S(2)}, u32[]{:S(2)}) %collective-permute-start.18) | collective-permute-done | bytes 196640 | tf_op jit(solution)/shard_map/ppermute | solution.py:409
  100.1 6.4 %collective-permute-done.19.r2 = bf16[768,128]{1,0:T(8,128)(2,1)S(1)} collective-permute-done((bf16[768,128]{1,0:T(8,128)(2,1)S(1)}, bf16[768,128]{1,0:T(8,128)(2,1)S(1)}, u32[]{:S(2)}, u32[]{:S(2)}) %collective-permute-start.19) | collective-permute-done | bytes 196640 | tf_op jit(solution)/shard_map/ppermute | solution.py:409
  106.4 1.7 shard_map.263
  111.0 4.2 %collective-permute-start.16 = (bf16[384,512]{1,0:T(8,128)(2,1)S(1)}, bf16[384,512]{1,0:T(8,128)(2,1)S(1)}, u32[]{:S(2)}, u32[]{:S(2)}) collective-permute-start(bf16[384,512]{1,0:T(8,128)(2,1)S(1)} %get-tuple-element.93), channel_id=1, source_target_pairs={{0,1},{1,0},{2,3},{3,2},{4,5},{5,4},{6,7},{7,6},{8,9},{9,8},{10,11... | collective-permute-start | bytes 1179656 | tf_op jit(solution)/shard_map/ppermute | solution.py:409
  115.3 2.5 %collective-permute-start.23 = (bf16[192,128]{1,0:T(8,128)(2,1)S(1)}, bf16[192,128]{1,0:T(8,128)(2,1)S(1)}, u32[]{:S(2)}, u32[]{:S(2)}) collective-permute-start(bf16[192,128]{1,0:T(8,128)(2,1)S(1)} %get-tuple-element.116), channel_id=1, source_target_pairs={{0,2},{1,3},{2,0},{3,1},{4,6},{5,7},{6,4},{7,5},{8,10},{9,11},{10,... | collective-permute-start | bytes 147464 | tf_op jit(solution)/shard_map/ppermute | solution.py:409
  117.8 1.8 collective-permute-start.24
  120.4 4.4 %collective-permute-done.25 = bf16[192,1536]{1,0:T(8,128)(2,1)S(1)} collective-permute-done((bf16[192,1536]{1,0:T(8,128)(2,1)S(1)}, bf16[192,1536]{1,0:T(8,128)(2,1)S(1)}, u32[]{:S(2)}, u32[]{:S(2)}) %collective-permute-start.25) | collective-permute-done | bytes 589856 | tf_op jit(solution)/shard_map/ppermute | solution.py:409
  126.7 2.8 %collective-permute-done.24.a3 = bf16[192,128]{1,0:T(8,128)(2,1)S(1)} collective-permute-done((bf16[192,128]{1,0:T(8,128)(2,1)S(1)}, bf16[192,128]{1,0:T(8,128)(2,1)S(1)}, u32[]{:S(2)}, u32[]{:S(2)}) %collective-permute-start.24) | collective-permute-done | bytes 49184 | tf_op jit(solution)/shard_map/ppermute | solution.py:409
  129.5 4.7 %shard_map.264 = (bf16[576,512]{1,0:T(8,128)(2,1)S(1)}, f32[384,1]{1,0:T(8,128)S(1)}, f32[208,512]{1,0:T(8,128)S(1)}, bf16[208,512]{1,0:T(8,128)(2,1)S(1)}, bf16...) custom-call(s32[3]{0:T(128)S(1)} %copy-done.2, bf16[768,640]{1,0:T(8,128)(2,1)S(1)} %all_gather.6.tok, ...), custom_call_target="tpu_custom_call" | custom-call | flops 452984832 | bytes 4939276 | tf_op jit(solution)/shard_map/pallas_call | solution.py:72
  134.4 2.2 %collective-permute-start.27 = (bf16[208,512]{1,0:T(8,128)(2,1)S(1)}, bf16[208,512]{1,0:T(8,128)(2,1)S(1)}, u32[]{:S(2)}, u32[]{:S(2)}) collective-permute-start(bf16[208,512]{1,0:T(8,128)(2,1)S(1)} %get-tuple-element.127), channel_id=1, source_target_pairs={{0,2},{1,3},{2,0},{3,1},{4,6},{5,7},{6,4},{7,5},{8,10},{9,11},{10,... | collective-permute-start | bytes 638984 | tf_op jit(solution)/shard_map/ppermute | solution.py:409
  136.7 2.0 %collective-permute-start.28 = (bf16[208,512]{1,0:T(8,128)(2,1)S(1)}, bf16[208,512]{1,0:T(8,128)(2,1)S(1)}, u32[]{:S(2)}, u32[]{:S(2)}) collective-permute-start(bf16[208,512]{1,0:T(8,128)(2,1)S(1)} %get-tuple-element.128), channel_id=1, source_target_pairs={{0,3},{1,2},{2,1},{3,0},{4,7},{5,6},{6,5},{7,4},{8,11},{9,10},{10,... | collective-permute-start | bytes 638984 | tf_op jit(solution)/shard_map/ppermute | solution.py:409
  140.5 3.3 %collective-permute-done.26.g1 = bf16[208,512]{1,0:T(8,128)(2,1)S(1)} collective-permute-done((bf16[208,512]{1,0:T(8,128)(2,1)S(1)}, bf16[208,512]{1,0:T(8,128)(2,1)S(1)}, u32[]{:S(2)}, u32[]{:S(2)}) %collective-permute-start.26) | collective-permute-done | bytes 213024 | tf_op jit(solution)/shard_map/ppermute | solution.py:409
  144.9 9.8 %collective-permute-done.27.g2 = bf16[208,512]{1,0:T(8,128)(2,1)S(1)} collective-permute-done((bf16[208,512]{1,0:T(8,128)(2,1)S(1)}, bf16[208,512]{1,0:T(8,128)(2,1)S(1)}, u32[]{:S(2)}, u32[]{:S(2)}) %collective-permute-start.27) | collective-permute-done | bytes 213024 | tf_op jit(solution)/shard_map/ppermute | solution.py:409
  159.1 2.3 %collective-permute-done.30 = f32[8,768]{1,0:T(8,128)S(1)} collective-permute-done((f32[8,768]{1,0:T(8,128)S(1)}, f32[8,768]{1,0:T(8,128)S(1)}, u32[]{:S(2)}, u32[]{:S(2)}) %collective-permute-start.30) | collective-permute-done | bytes 24608 | tf_op jit(solution)/shard_map/ppermute | solution.py:409
  161.9 1.7 collective-permute-done.17.got
  174.6 5.8 %collective-permute-start.39 = (bf16[192,192]{1,0:T(8,128)(2,1)S(1)}, bf16[192,192]{1,0:T(8,128)(2,1)S(1)}, u32[]{:S(2)}, u32[]{:S(2)}) collective-permute-start(bf16[192,192]{1,0:T(8,128)(2,1)S(1)} %get-tuple-element.145), channel_id=1, source_target_pairs={{0,1},{1,0},{2,3},{3,2},{4,5},{5,4},{6,7},{7,6},{8,9},{9,8},{10,11... | collective-permute-start | bytes 221192 | tf_op jit(solution)/shard_map/ppermute | solution.py:409
  183.5 2.3 %collective-permute-start.41 = (bf16[192,192]{1,0:T(8,128)(2,1)S(1)}, bf16[192,192]{1,0:T(8,128)(2,1)S(1)}, u32[]{:S(2)}, u32[]{:S(2)}) collective-permute-start(bf16[192,192]{1,0:T(8,128)(2,1)S(1)} %get-tuple-element.147), channel_id=1, source_target_pairs={{0,3},{1,2},{2,1},{3,0},{4,7},{5,6},{6,5},{7,4},{8,11},{9,10},{10,... | collective-permute-start | bytes 221192 | tf_op jit(solution)/shard_map/ppermute | solution.py:409
  187.4 2.6 %collective-permute-done.41.g3 = bf16[192,192]{1,0:T(8,128)(2,1)S(1)} collective-permute-done((bf16[192,192]{1,0:T(8,128)(2,1)S(1)}, bf16[192,192]{1,0:T(8,128)(2,1)S(1)}, u32[]{:S(2)}, u32[]{:S(2)}) %collective-permute-start.41) | collective-permute-done | bytes 73760 | tf_op jit(solution)/shard_map/ppermute | solution.py:409
  (105 shorter events, 42.5 us)
Async XLA Ops:
  0.7 47.4 %collective-permute-start.1 = (bf16[192,576]{1,0:T(8,128)(2,1)}, bf16[192,576]{1,0:T(8,128)(2,1)S(1)}, u32[]{:S(2)}, u32[]{:S(2)}) collective-permute-start(bf16[192,576]{1,0:T(8,128)(2,1)} %w0.3), channel_id=1, source_target_pairs={{0,4},{4,0},{8,12},{12,8},{1,5},{5,1},{9,13},{13,9},{2,6},{6,2},{1... | collective-permute-start | bytes 663560 | tf_op jit(solution)/shard_map/ppermute | solution.py:409
  1.2 30.9 %collective-permute-start = (bf16[192,576]{1,0:T(8,128)(2,1)}, bf16[192,576]{1,0:T(8,128)(2,1)S(1)}, u32[]{:S(2)}, u32[]{:S(2)}) collective-permute-start(bf16[192,576]{1,0:T(8,128)(2,1)} %w0.3), channel_id=1, source_target_pairs={{0,8},{4,12},{8,0},{12,4},{1,9},{5,13},{9,1},{13,5},{2,10},{6,14},... | collective-permute-start | bytes 663560 | tf_op jit(solution)/shard_map/ppermute | solution.py:409
  32.1 15.4 %collective-permute-start.14 = (bf16[192,512]{1,0:T(8,128)(2,1)S(1)}, bf16[192,512]{1,0:T(8,128)(2,1)S(1)}, u32[]{:S(2)}, u32[]{:S(2)}) collective-permute-start(bf16[192,512]{1,0:T(8,128)(2,1)S(1)} %copy-done.1), channel_id=1, source_target_pairs={{0,2},{1,3},{2,0},{3,1},{4,6},{5,7},{6,4},{7,5},{8,10},{9,11},{10,... | collective-permute-start | bytes 589832 | tf_op jit(solution)/shard_map/ppermute | solution.py:409
  32.1 17.5 %collective-permute-start.2 = (bf16[192,576]{1,0:T(8,128)(2,1)S(1)}, bf16[192,576]{1,0:T(8,128)(2,1)S(1)}, u32[]{:S(2)}, u32[]{:S(2)}) collective-permute-start(bf16[192,576]{1,0:T(8,128)(2,1)S(1)} %collective-permute-done.w1), channel_id=1, source_target_pairs={{0,4},{4,0},{8,12},{12,8},{1,5},{5,1},{9,13},{13,9},{2,6},{6,2},{1... | collective-permute-start | bytes 663560 | tf_op jit(solution)/shard_map/ppermute | solution.py:409
  33.7 21.6 %collective-permute-start.7 = (bf16[192,768]{1,0:T(8,128)(2,1)S(1)}, bf16[192,768]{1,0:T(8,128)(2,1)S(1)}, u32[]{:S(2)}, u32[]{:S(2)}) collective-permute-start(bf16[192,768]{1,0:T(8,128)(2,1)S(1)} %copy-done.5), channel_id=1, source_target_pairs={{0,8},{4,12},{8,0},{12,4},{1,9},{5,13},{9,1},{13,5},{2,10},{6,14},... | collective-permute-start | bytes 884744 | tf_op jit(solution)/shard_map/ppermute | solution.py:409
  38.4 17.4 %collective-permute-start.8 = (bf16[192,768]{1,0:T(8,128)(2,1)S(1)}, bf16[192,768]{1,0:T(8,128)(2,1)S(1)}, u32[]{:S(2)}, u32[]{:S(2)}) collective-permute-start(bf16[192,768]{1,0:T(8,128)(2,1)S(1)} %copy-done.5), channel_id=1, source_target_pairs={{0,4},{4,0},{8,12},{12,8},{1,5},{5,1},{9,13},{13,9},{2,6},{6,2},{1... | collective-permute-start | bytes 884744 | tf_op jit(solution)/shard_map/ppermute | solution.py:409
  47.5 9.9 %collective-permute-start.10 = (bf16[192,768]{1,0:T(8,128)(2,1)S(1)}, bf16[192,768]{1,0:T(8,128)(2,1)S(1)}, u32[]{:S(2)}, u32[]{:S(2)}) collective-permute-start(bf16[192,768]{1,0:T(8,128)(2,1)S(1)} %copy-done.6), channel_id=1, source_target_pairs={{0,8},{4,12},{8,0},{12,4},{1,9},{5,13},{9,1},{13,5},{2,10},{6,14},... | collective-permute-start | bytes 884744 | tf_op jit(solution)/shard_map/ppermute | solution.py:409
  48.0 15.6 %collective-permute-start.4 = (bf16[768,192]{1,0:T(8,128)(2,1)S(1)}, bf16[768,192]{1,0:T(8,128)(2,1)S(1)}, u32[]{:S(2)}, u32[]{:S(2)}) collective-permute-start(bf16[768,192]{1,0:T(8,128)(2,1)S(1)} %shard_map.256.m0), channel_id=1, source_target_pairs={{0,8},{4,12},{8,0},{12,4},{1,9},{5,13},{9,1},{13,5},{2,10},{6,14},... | collective-permute-start | bytes 884744 | tf_op jit(solution)/shard_map/ppermute | solution.py:409
  55.2 26.5 %collective-permute-start.11 = (bf16[192,768]{1,0:T(8,128)(2,1)S(1)}, bf16[192,768]{1,0:T(8,128)(2,1)S(1)}, u32[]{:S(2)}, u32[]{:S(2)}) collective-permute-start(bf16[192,768]{1,0:T(8,128)(2,1)S(1)} %copy-done.6), channel_id=1, source_target_pairs={{0,4},{4,0},{8,12},{12,8},{1,5},{5,1},{9,13},{13,9},{2,6},{6,2},{1... | collective-permute-start | bytes 884744 | tf_op jit(solution)/shard_map/ppermute | solution.py:409
  55.2 26.5 %collective-permute-start.5 = (bf16[768,192]{1,0:T(8,128)(2,1)S(1)}, bf16[768,192]{1,0:T(8,128)(2,1)S(1)}, u32[]{:S(2)}, u32[]{:S(2)}) collective-permute-start(bf16[768,192]{1,0:T(8,128)(2,1)S(1)} %shard_map.256.m0), channel_id=1, source_target_pairs={{0,4},{4,0},{8,12},{12,8},{1,5},{5,1},{9,13},{13,9},{2,6},{6,2},{1... | collective-permute-start | bytes 884744 | tf_op jit(solution)/shard_map/ppermute | solution.py:409
  55.8 26.0 %collective-permute-start.9 = (bf16[192,768]{1,0:T(8,128)(2,1)S(1)}, bf16[192,768]{1,0:T(8,128)(2,1)S(1)}, u32[]{:S(2)}, u32[]{:S(2)}) collective-permute-start(bf16[192,768]{1,0:T(8,128)(2,1)S(1)} %collective-permute-done.7.u1), channel_id=1, source_target_pairs={{0,4},{4,0},{8,12},{12,8},{1,5},{5,1},{9,13},{13,9},{2,6},{6,2},{1... | collective-permute-start | bytes 884744 | tf_op jit(solution)/shard_map/ppermute | solution.py:409
  57.4 24.3 %collective-permute-start.12 = (bf16[192,768]{1,0:T(8,128)(2,1)S(1)}, bf16[192,768]{1,0:T(8,128)(2,1)S(1)}, u32[]{:S(2)}, u32[]{:S(2)}) collective-permute-start(bf16[192,768]{1,0:T(8,128)(2,1)S(1)} %collective-permute-done.10.d1), channel_id=1, source_target_pairs={{0,4},{4,0},{8,12},{12,8},{1,5},{5,1},{9,13},{13,9},{2,6},{6,2},{1... | collective-permute-start | bytes 884744 | tf_op jit(solution)/shard_map/ppermute | solution.py:409
  63.6 18.1 %collective-permute-start.6 = (bf16[768,192]{1,0:T(8,128)(2,1)S(1)}, bf16[768,192]{1,0:T(8,128)(2,1)S(1)}, u32[]{:S(2)}, u32[]{:S(2)}) collective-permute-start(bf16[768,192]{1,0:T(8,128)(2,1)S(1)} %collective-permute-done.4.m1), channel_id=1, source_target_pairs={{0,4},{4,0},{8,12},{12,8},{1,5},{5,1},{9,13},{13,9},{2,6},{6,2},{1... | collective-permute-start | bytes 884744 | tf_op jit(solution)/shard_map/ppermute | solution.py:409
  89.1 10.9 %collective-permute-start.18 = (bf16[768,128]{1,0:T(8,128)(2,1)S(1)}, bf16[768,128]{1,0:T(8,128)(2,1)S(1)}, u32[]{:S(2)}, u32[]{:S(2)}) collective-permute-start(bf16[768,128]{1,0:T(8,128)(2,1)S(1)} %get-tuple-element.100), channel_id=1, source_target_pairs={{0,1},{1,0},{2,3},{3,2},{4,5},{5,4},{6,7},{7,6},{8,9},{9,8},{10,11... | collective-permute-start | bytes 589832 | tf_op jit(solution)/shard_map/ppermute | solution.py:409
  89.2 17.2 %collective-permute-start.19 = (bf16[768,128]{1,0:T(8,128)(2,1)S(1)}, bf16[768,128]{1,0:T(8,128)(2,1)S(1)}, u32[]{:S(2)}, u32[]{:S(2)}) collective-permute-start(bf16[768,128]{1,0:T(8,128)(2,1)S(1)} %get-tuple-element.101), channel_id=1, source_target_pairs={{0,2},{1,3},{2,0},{3,1},{4,6},{5,7},{6,4},{7,5},{8,10},{9,11},{10,... | collective-permute-start | bytes 589832 | tf_op jit(solution)/shard_map/ppermute | solution.py:409
  91.6 14.8 %collective-permute-start.20 = (bf16[768,128]{1,0:T(8,128)(2,1)S(1)}, bf16[768,128]{1,0:T(8,128)(2,1)S(1)}, u32[]{:S(2)}, u32[]{:S(2)}) collective-permute-start(bf16[768,128]{1,0:T(8,128)(2,1)S(1)} %get-tuple-element.102), channel_id=1, source_target_pairs={{0,3},{1,2},{2,1},{3,0},{4,7},{5,6},{6,5},{7,4},{8,11},{9,10},{10,... | collective-permute-start | bytes 589832 | tf_op jit(solution)/shard_map/ppermute | solution.py:409
  109.1 15.7 %collective-permute-start.25 = (bf16[192,1536]{1,0:T(8,128)(2,1)S(1)}, bf16[192,1536]{1,0:T(8,128)(2,1)S(1)}, u32[]{:S(2)}, u32[]{:S(2)}) collective-permute-start(bf16[192,1536]{1,0:T(8,128)(2,1)S(1)} %get-tuple-element.119), channel_id=1, source_target_pairs={{0,8},{4,12},{8,0},{12,4},{1,9},{5,13},{9,1},{13,5},{2,10},{6,14},... | collective-permute-start | bytes 1769480 | tf_op jit(solution)/shard_map/ppermute | solution.py:409
  111.0 28.8 %collective-permute-start.16 = (bf16[384,512]{1,0:T(8,128)(2,1)S(1)}, bf16[384,512]{1,0:T(8,128)(2,1)S(1)}, u32[]{:S(2)}, u32[]{:S(2)}) collective-permute-start(bf16[384,512]{1,0:T(8,128)(2,1)S(1)} %get-tuple-element.93), channel_id=1, source_target_pairs={{0,1},{1,0},{2,3},{3,2},{4,5},{5,4},{6,7},{7,6},{8,9},{9,8},{10,11... | collective-permute-start | bytes 1179656 | tf_op jit(solution)/shard_map/ppermute | solution.py:409
  115.2 11.5 %collective-permute-start.22 = (bf16[192,128]{1,0:T(8,128)(2,1)S(1)}, bf16[192,128]{1,0:T(8,128)(2,1)S(1)}, u32[]{:S(2)}, u32[]{:S(2)}) collective-permute-start(bf16[192,128]{1,0:T(8,128)(2,1)S(1)} %get-tuple-element.115), channel_id=1, source_target_pairs={{0,1},{1,0},{2,3},{3,2},{4,5},{5,4},{6,7},{7,6},{8,9},{9,8},{10,11... | collective-permute-start | bytes 147464 | tf_op jit(solution)/shard_map/ppermute | solution.py:409
  115.3 11.5 %collective-permute-start.23 = (bf16[192,128]{1,0:T(8,128)(2,1)S(1)}, bf16[192,128]{1,0:T(8,128)(2,1)S(1)}, u32[]{:S(2)}, u32[]{:S(2)}) collective-permute-start(bf16[192,128]{1,0:T(8,128)(2,1)S(1)} %get-tuple-element.116), channel_id=1, source_target_pairs={{0,2},{1,3},{2,0},{3,1},{4,6},{5,7},{6,4},{7,5},{8,10},{9,11},{10,... | collective-permute-start | bytes 147464 | tf_op jit(solution)/shard_map/ppermute | solution.py:409
  117.8 11.7 %collective-permute-start.24 = (bf16[192,128]{1,0:T(8,128)(2,1)S(1)}, bf16[192,128]{1,0:T(8,128)(2,1)S(1)}, u32[]{:S(2)}, u32[]{:S(2)}) collective-permute-start(bf16[192,128]{1,0:T(8,128)(2,1)S(1)} %get-tuple-element.117), channel_id=1, source_target_pairs={{0,3},{1,2},{2,1},{3,0},{4,7},{5,6},{6,5},{7,4},{8,11},{9,10},{10,... | collective-permute-start | bytes 147464 | tf_op jit(solution)/shard_map/ppermute | solution.py:409
  124.8 15.0 %collective-permute-start.37 = (bf16[192,768]{1,0:T(8,128)(2,1)S(1)}, bf16[192,768]{1,0:T(8,128)(2,1)S(1)}, u32[]{:S(2)}, u32[]{:S(2)}) collective-permute-start(bf16[192,768]{1,0:T(8,128)(2,1)S(1)} %get-tuple-element.143), channel_id=1, source_target_pairs={{0,8},{4,12},{8,0},{12,4},{1,9},{5,13},{9,1},{13,5},{2,10},{6,14},... | collective-permute-start | bytes 884744 | tf_op jit(solution)/shard_map/ppermute | solution.py:409
  134.2 9.5 %collective-permute-start.26 = (bf16[208,512]{1,0:T(8,128)(2,1)S(1)}, bf16[208,512]{1,0:T(8,128)(2,1)S(1)}, u32[]{:S(2)}, u32[]{:S(2)}) collective-permute-start(bf16[208,512]{1,0:T(8,128)(2,1)S(1)} %get-tuple-element.126), channel_id=1, source_target_pairs={{0,1},{1,0},{2,3},{3,2},{4,5},{5,4},{6,7},{7,6},{8,9},{9,8},{10,11... | collective-permute-start | bytes 638984 | tf_op jit(solution)/shard_map/ppermute | solution.py:409
  134.4 20.3 %collective-permute-start.27 = (bf16[208,512]{1,0:T(8,128)(2,1)S(1)}, bf16[208,512]{1,0:T(8,128)(2,1)S(1)}, u32[]{:S(2)}, u32[]{:S(2)}) collective-permute-start(bf16[208,512]{1,0:T(8,128)(2,1)S(1)} %get-tuple-element.127), channel_id=1, source_target_pairs={{0,2},{1,3},{2,0},{3,1},{4,6},{5,7},{6,4},{7,5},{8,10},{9,11},{10,... | collective-permute-start | bytes 638984 | tf_op jit(solution)/shard_map/ppermute | solution.py:409
  136.7 19.0 %collective-permute-start.28 = (bf16[208,512]{1,0:T(8,128)(2,1)S(1)}, bf16[208,512]{1,0:T(8,128)(2,1)S(1)}, u32[]{:S(2)}, u32[]{:S(2)}) collective-permute-start(bf16[208,512]{1,0:T(8,128)(2,1)S(1)} %get-tuple-element.128), channel_id=1, source_target_pairs={{0,3},{1,2},{2,1},{3,0},{4,7},{5,6},{6,5},{7,4},{8,11},{9,10},{10,... | collective-permute-start | bytes 638984 | tf_op jit(solution)/shard_map/ppermute | solution.py:409
  139.7 28.4 %collective-permute-start.32 = (bf16[384,576]{1,0:T(8,128)(2,1)S(1)}, bf16[384,576]{1,0:T(8,128)(2,1)S(1)}, u32[]{:S(2)}, u32[]{:S(2)}) collective-permute-start(bf16[384,576]{1,0:T(8,128)(2,1)S(1)} %shard_map.268), channel_id=1, source_target_pairs={{0,4},{4,0},{8,12},{12,8},{1,5},{5,1},{9,13},{13,9},{2,6},{6,2},{1... | collective-permute-start | bytes 1327112 | tf_op jit(solution)/shard_map/ppermute | solution.py:409
  139.8 40.6 %collective-permute-start.42 = (bf16[192,1536]{1,0:T(8,128)(2,1)S(1)}, bf16[192,1536]{1,0:T(8,128)(2,1)}, u32[]{:S(2)}, u32[]{:S(2)}) collective-permute-start(bf16[192,1536]{1,0:T(8,128)(2,1)S(1)} %convert_add_fusion.1), channel_id=1, source_target_pairs={{0,16},{16,0},{1,17},{17,1},{2,18},{18,2},{3,19},{19,3},{4,20},{20... | collective-permute-start | bytes 1769480 | tf_op jit(solution)/shard_map/ppermute | solution.py:409
  143.8 28.9 %collective-permute-start.38 = (bf16[192,768]{1,0:T(8,128)(2,1)S(1)}, bf16[192,768]{1,0:T(8,128)(2,1)}, u32[]{:S(2)}, u32[]{:S(2)}) collective-permute-start(bf16[192,768]{1,0:T(8,128)(2,1)S(1)} %add_convert_fusion), channel_id=1, source_target_pairs={{0,16},{16,0},{1,17},{17,1},{2,18},{18,2},{3,19},{19,3},{4,20},{20... | collective-permute-start | bytes 884744 | tf_op jit(solution)/shard_map/ppermute | solution.py:409
  154.7 9.0 %collective-permute-start.17 = (bf16[192,512]{1,0:T(8,128)(2,1)S(1)}, bf16[192,512]{1,0:T(8,128)(2,1)S(1)}, u32[]{:S(2)}, u32[]{:S(2)}) collective-permute-start(bf16[192,512]{1,0:T(8,128)(2,1)S(1)} %get-tuple-element.95), channel_id=1, source_target_pairs={{0,2},{1,3},{2,0},{3,1},{4,6},{5,7},{6,4},{7,5},{8,10},{9,11},{10,... | collective-permute-start | bytes 589832 | tf_op jit(solution)/shard_map/ppermute | solution.py:409
  169.1 22.1 %collective-permute-start.35 = (bf16[192,576]{1,0:T(8,128)(2,1)S(1)}, bf16[192,576]{1,0:T(8,128)(2,1)S(1)}, u32[]{:S(2)}, u32[]{:S(2)}) collective-permute-start(bf16[192,576]{1,0:T(8,128)(2,1)S(1)} %get-tuple-element.138), channel_id=1, source_target_pairs={{0,24},{4,28},{8,16},{12,20},{16,8},{20,12},{24,0},{28,4},{1,25},{... | collective-permute-start | bytes 663560 | tf_op jit(solution)/shard_map/ppermute | solution.py:616
  170.7 20.6 %collective-permute-start.33 = (bf16[192,576]{1,0:T(8,128)(2,1)S(1)}, bf16[192,576]{1,0:T(8,128)(2,1)S(1)}, u32[]{:S(2)}, u32[]{:S(2)}) collective-permute-start(bf16[192,576]{1,0:T(8,128)(2,1)S(1)} %get-tuple-element.138), channel_id=1, source_target_pairs={{0,8},{4,12},{8,0},{12,4},{1,9},{5,13},{9,1},{13,5},{2,10},{6,14},... | collective-permute-start | bytes 663560 | tf_op jit(solution)/shard_map/ppermute | solution.py:409
  171.2 20.1 %collective-permute-start.34 = (bf16[192,576]{1,0:T(8,128)(2,1)S(1)}, bf16[192,576]{1,0:T(8,128)(2,1)S(1)}, u32[]{:S(2)}, u32[]{:S(2)}) collective-permute-start(bf16[192,576]{1,0:T(8,128)(2,1)S(1)} %get-tuple-element.139), channel_id=1, source_target_pairs={{0,16},{16,0},{1,17},{17,1},{2,18},{18,2},{3,19},{19,3},{4,20},{20... | collective-permute-start | bytes 663560 | tf_op jit(solution)/shard_map/ppermute | solution.py:615
  (19 other events, 362.5 us)
